TPU v7x, 32 devices: a whole 2x2x4 slice. The times are simulated.
32 devices in a mesh: dp: 8 (over z, x), mp: 4 (over y, core).
Axes of the slice: x: 2, y: 2, z: 4, core: 2. Of those that a mesh axis runs over, the one named last changes fastest.
Arguments:
- token_ids: int32 [16, 1024], P('dp'), may hold values from 0 to 30719
- type_ids: int32 [16, 1024], P('dp'), may hold values from 0 to 1, as said below
- mask_pos: int32 [16, 256], P('dp'), may hold values from 1 to 1023, as said below
- mask_valid: int32 [16, 256], P('dp'), may hold values from 0 to 1, as said below
- mlm_labels: int32 [16, 256], P('dp'), may hold values from 0 to 30719
- nsp_labels: int32 [16], P('dp'), may hold values from 0 to 1
- word_table: float32 [30720, 768], P(('mp', 'dp')), may hold values from -0.4375 to 0.4375
- word_m: float32 [30720, 768], P(('mp', 'dp')), may hold values from -5.722046e-06 to 5.722046e-06
- word_v: float32 [30720, 768], P(('mp', 'dp')), may hold values from 3.8244378e-14 to 6.1191005e-13
- attn_weight: float32 [768, 4, 768], P('dp', None, 'mp')
- attn_m: float32 [768, 4, 768], P('dp', None, 'mp'), may hold values from -5.722046e-06 to 5.722046e-06
- attn_v: float32 [768, 4, 768], P('dp', None, 'mp'), may hold values from 3.8244378e-14 to 6.1191005e-13
- ff_weight: float32 [768, 2, 3072], P('dp', None, 'mp'), may hold values from -0.21875 to 0.21875
- ff_m: float32 [768, 2, 3072], P('dp', None, 'mp'), may hold values from -5.722046e-06 to 5.722046e-06
- ff_v: float32 [768, 2, 3072], P('dp', None, 'mp'), may hold values from 3.8244378e-14 to 6.1191005e-13
- side_weight: float32 [2560, 768], P('dp'), may hold values from -0.21875 to 0.21875
- side_m: float32 [2560, 768], P('dp'), may hold values from -5.722046e-06 to 5.722046e-06
- side_v: float32 [2560, 768], P('dp'), may hold values from 3.8244378e-14 to 6.1191005e-13
- vectors: float32 [16, 768], P(None, 'dp')
- vec_m: float32 [16, 768], P(None, 'dp'), may hold values from -2.2888184e-05 to 2.2888184e-05
- vec_v: float32 [16, 768], P(None, 'dp'), may hold values from 6.1191005e-13 to 9.790561e-12
- split_bias: float32 [6, 768], P(None, 'mp'), may hold values from -1.25 to 1.25
- split_m: float32 [6, 768], P(None, 'mp'), may hold values from -2.2888184e-05 to 2.2888184e-05
- split_v: float32 [6, 768], P(None, 'mp'), may hold values from 6.1191005e-13 to 9.790561e-12
- decoder_bias: float32 [30720], P('mp'), may hold values from -3 to 3
- decoder_m: float32 [30720], P('mp'), may hold values from -2.2888184e-05 to 2.2888184e-05
- decoder_v: float32 [30720], P('mp'), may hold values from 6.1191005e-13 to 9.790561e-12
Outputs:
- total_loss: float32 [], replicated
- grad_norm: float32 [], replicated
- new_word: float32 [30720, 768], P(('mp', 'dp'))
- new_word_m: float32 [30720, 768], P(('mp', 'dp'))
- new_word_v: float32 [30720, 768], P(('mp', 'dp'))
- new_attn: float32 [768, 4, 768], P('dp', None, 'mp')
- new_attn_m: float32 [768, 4, 768], P('dp', None, 'mp')
- new_attn_v: float32 [768, 4, 768], P('dp', None, 'mp')
- new_ff: float32 [768, 2, 3072], P('dp', None, 'mp')
- new_ff_m: float32 [768, 2, 3072], P('dp', None, 'mp')
- new_ff_v: float32 [768, 2, 3072], P('dp', None, 'mp')
- new_side: float32 [2560, 768], P('dp')
- new_side_m: float32 [2560, 768], P('dp')
- new_side_v: float32 [2560, 768], P('dp')
- new_vec: float32 [16, 768], P(None, 'dp')
- new_vec_m: float32 [16, 768], P(None, 'dp')
- new_vec_v: float32 [16, 768], P(None, 'dp')
- new_split: float32 [6, 768], P(None, 'mp')
- new_split_m: float32 [6, 768], P(None, 'mp')
- new_split_v: float32 [6, 768], P(None, 'mp')
- new_decoder: float32 [30720], P('mp')
- new_decoder_m: float32 [30720], P('mp')
- new_decoder_v: float32 [30720], P('mp')
Inputs may be any that keep to these rules, and one draw needn't show every extreme that they name: `type_ids`: 0 up to a split point and 1 from it on; the split lies between 256 and 768. `mask_pos`: slots of one sequence hold distinct positions, never 0; slots beyond a sequence's count hold positions too, without effect. `mask_valid`: each sequence's valid slots come first; counts vary from sequence to sequence, between 1 and 256; in every draw one sequence has all 256 slots valid.
All inputs are finite; a program needn't handle non-finite values.
Results may differ from a plain program's by a relative error of at most 0.012.
The roundings to bfloat16 on the way count: a program that leaves them out, or rounds other values in their place, can miss the bound.
Values may be sent and summed in bfloat16 or wider, within the bound.
A program may use at most 256 MiB of HBM per device.

v0:
```python
import math

import jax
import jax.numpy as jnp
from jax import lax
from jax.sharding import PartitionSpec as P

D = 768
HEAD_DIM = 64


beta_one = 0.9
beta_two = 0.999
adam_eps = 1e-06
learn_rate = 0.2
decay_rate = 0.01
step_count = 10
max_norm = 0.05
norm_eps = 1e-12
highest = lax.Precision.HIGHEST


def merged(part, axis, combine):
    gathered = jax.tree.map(lambda a: lax.all_gather(a, axis), part)

    def take(source):
        return jax.tree.map(lambda a: lax.dynamic_index_in_dim(a, source, 0, False), gathered)

    return lax.fori_loop(
        1, lax.axis_size(axis), lambda source, state: combine(state, take(source)), take(0)
    )


def layer_norm(inputs, norm_gain, norm_shift):
    center = inputs - jnp.mean(inputs, axis=-1, keepdims=True)
    spread = jnp.mean(center * center, axis=-1, keepdims=True)
    return center * lax.rsqrt(spread + norm_eps) * norm_gain + norm_shift


def gelu_exact(inputs):
    return jax.nn.gelu(inputs, approximate=False)


def norm_backward(inputs, norm_gain, norm_shift, upstream):
    _, pullback = jax.vjp(layer_norm, inputs, norm_gain, norm_shift)
    return pullback(upstream)


def gelu_backward(inputs, upstream):
    _, pullback = jax.vjp(gelu_exact, inputs)
    return pullback(upstream)[0]


def adam_step(weight, moment, square, gradient, clip_scale, decays):
    gradient = gradient * clip_scale
    moment = beta_one * moment + (1 - beta_one) * gradient
    square = beta_two * square + (1 - beta_two) * gradient * gradient
    mean_hat = moment / (1 - beta_one**step_count)
    var_hat = square / (1 - beta_two**step_count)
    change = mean_hat / (jnp.sqrt(var_hat) + adam_eps)
    if decays:
        change = change + decay_rate * weight
    return (weight - learn_rate * change, moment, square)


def merge_stats(left_part, right_part):
    row_top = jnp.maximum(left_part[0], right_part[0])
    row_total = left_part[1] * jnp.exp(left_part[0] - row_top) + right_part[1] * jnp.exp(
        right_part[0] - row_top
    )
    return (row_top, row_total, left_part[2] + right_part[2])


def layer_forward(hidden0, attn_full, ffw_full, vec_rows, split_local):
    batch_size, length = (hidden0.shape[0], hidden0.shape[1])
    head_count = attn_full.shape[2] // HEAD_DIM
    score_scale = 1.0 / math.sqrt(HEAD_DIM)
    hidden0_b = hidden0.astype(jnp.bfloat16)
    packed = jnp.einsum(
        "bsd,dch->bsch", hidden0_b, attn_full[:, :3, :], preferred_element_type=jnp.float32
    )
    head_shape = (batch_size, length, head_count, HEAD_DIM)
    queries = (packed[:, :, 0] + split_local[0]).astype(jnp.bfloat16).reshape(head_shape)
    key_rows = packed[:, :, 1].astype(jnp.bfloat16).reshape(head_shape)
    value_rows = (packed[:, :, 2] + split_local[1]).astype(jnp.bfloat16).reshape(head_shape)
    scores = (
        jnp.einsum("bqhe,bkhe->bhqk", queries, key_rows, preferred_element_type=jnp.float32)
        * score_scale
    )
    row_top = jnp.max(scores, axis=-1, keepdims=True)
    exp_scores = jnp.exp(scores - row_top)
    row_total = jnp.sum(exp_scores, axis=-1, keepdims=True)
    attn_probs = exp_scores / row_total
    log_norm = row_top + jnp.log(row_total)
    mixed_heads = jnp.einsum(
        "bhqk,bkhe->bqhe",
        attn_probs.astype(jnp.bfloat16),
        value_rows,
        preferred_element_type=jnp.float32,
    )
    mixed_heads = mixed_heads.reshape(batch_size, length, head_count * HEAD_DIM).astype(
        jnp.bfloat16
    )
    attn_part = jnp.einsum(
        "bsh,dh->bsd", mixed_heads, attn_full[:, 3, :], preferred_element_type=jnp.float32
    )
    resid1 = hidden0 + (lax.psum(attn_part, "mp") + vec_rows[2])
    hidden1 = layer_norm(resid1, vec_rows[3], vec_rows[4])
    hidden1_b = hidden1.astype(jnp.bfloat16)
    ff_bias = split_local[2:6].T.reshape(-1)
    upward = (
        jnp.einsum("bsd,df->bsf", hidden1_b, ffw_full[:, 0, :], preferred_element_type=jnp.float32)
        + ff_bias
    )
    active = gelu_exact(upward).astype(jnp.bfloat16)
    ffn_part = jnp.einsum(
        "bsf,df->bsd", active, ffw_full[:, 1, :], preferred_element_type=jnp.float32
    )
    resid2 = hidden1 + (lax.psum(ffn_part, "mp") + vec_rows[5])
    hidden2 = layer_norm(resid2, vec_rows[6], vec_rows[7])
    kept_state = (
        hidden0_b,
        queries,
        key_rows,
        value_rows,
        log_norm,
        mixed_heads,
        resid1,
        hidden1_b,
        upward,
        active,
        resid2,
    )
    return (hidden2, kept_state)


def layer_backward(grad_top, kept_state, attn_full, ffw_full, vec_rows):
    (
        hidden0_b,
        queries,
        key_rows,
        value_rows,
        log_norm,
        mixed_heads,
        resid1,
        hidden1_b,
        upward,
        active,
        resid2,
    ) = kept_state
    score_scale = 1.0 / math.sqrt(HEAD_DIM)
    grad_r2, grad_g2, grad_s2 = norm_backward(resid2, vec_rows[6], vec_rows[7], grad_top)
    ffn_grad_b = grad_r2.astype(jnp.bfloat16)
    out_bias_two = jnp.sum(ffn_grad_b.astype(jnp.float32), axis=(0, 1))
    ffw_grad_one = jnp.einsum("bsd,bsf->df", ffn_grad_b, active, preferred_element_type=jnp.float32)
    grad_active = jnp.einsum(
        "bsd,df->bsf", ffn_grad_b, ffw_full[:, 1, :], preferred_element_type=jnp.float32
    )
    grad_up = gelu_backward(upward, grad_active).astype(jnp.bfloat16)
    ff_bias_grad = jnp.sum(grad_up.astype(jnp.float32), axis=(0, 1))
    ffw_grad_zero = jnp.einsum(
        "bsd,bsf->df", hidden1_b, grad_up, preferred_element_type=jnp.float32
    )
    hidden1_part = jnp.einsum(
        "bsf,df->bsd", grad_up, ffw_full[:, 0, :], preferred_element_type=jnp.float32
    )
    ffw_grad = jnp.stack([ffw_grad_zero, ffw_grad_one], axis=1)
    grad_h1 = grad_r2 + lax.psum(hidden1_part, "mp")
    grad_r1, grad_g1, grad_s1 = norm_backward(resid1, vec_rows[3], vec_rows[4], grad_h1)
    attn_grad_b = grad_r1.astype(jnp.bfloat16)
    out_bias_one = jnp.sum(attn_grad_b.astype(jnp.float32), axis=(0, 1))
    attn_grad_out = jnp.einsum(
        "bsd,bsh->dh", attn_grad_b, mixed_heads, preferred_element_type=jnp.float32
    )
    grad_mixed = jnp.einsum(
        "bsd,dh->bsh", attn_grad_b, attn_full[:, 3, :], preferred_element_type=jnp.float32
    )
    grad_mixed = grad_mixed.astype(jnp.bfloat16).reshape(queries.shape)
    scores = (
        jnp.einsum("bqhe,bkhe->bhqk", queries, key_rows, preferred_element_type=jnp.float32)
        * score_scale
    )
    attn_probs = jnp.exp(scores - log_norm)
    grad_probs = jnp.einsum(
        "bqhe,bkhe->bhqk", grad_mixed, value_rows, preferred_element_type=jnp.float32
    )
    grad_values = jnp.einsum(
        "bhqk,bqhe->bkhe",
        attn_probs.astype(jnp.bfloat16),
        grad_mixed,
        preferred_element_type=jnp.float32,
    ).astype(jnp.bfloat16)
    row_dot = jnp.sum(grad_probs * attn_probs, axis=-1, keepdims=True)
    grad_scores = (attn_probs * (grad_probs - row_dot)).astype(jnp.bfloat16)
    grad_queries = (
        jnp.einsum("bhqk,bkhe->bqhe", grad_scores, key_rows, preferred_element_type=jnp.float32)
        * score_scale
    ).astype(jnp.bfloat16)
    grad_keys = (
        jnp.einsum("bhqk,bqhe->bkhe", grad_scores, queries, preferred_element_type=jnp.float32)
        * score_scale
    ).astype(jnp.bfloat16)
    flat_shape = (queries.shape[0], queries.shape[1], queries.shape[2] * HEAD_DIM)
    grad_packed = jnp.stack(
        [
            grad_queries.reshape(flat_shape),
            grad_keys.reshape(flat_shape),
            grad_values.reshape(flat_shape),
        ],
        axis=2,
    )
    attn_grad_in = jnp.einsum(
        "bsd,bsch->dch", hidden0_b, grad_packed, preferred_element_type=jnp.float32
    )
    packed_sums = jnp.sum(grad_packed.astype(jnp.float32), axis=(0, 1))
    hidden0_part = jnp.einsum(
        "bsch,dch->bsd", grad_packed, attn_full[:, :3, :], preferred_element_type=jnp.float32
    )
    grad_h0 = grad_r1 + lax.psum(hidden0_part.astype(jnp.bfloat16), "mp").astype(jnp.float32)
    attn_grad = jnp.concatenate([attn_grad_in, attn_grad_out[:, None, :]], axis=1)
    split_grad = jnp.concatenate(
        [packed_sums[0:1], packed_sums[2:3], ff_bias_grad.reshape(-1, 4).T], axis=0
    )
    vec_parts = (out_bias_one, grad_g1, grad_s1, out_bias_two, grad_g2, grad_s2)
    return (grad_h0, attn_grad, ffw_grad, vec_parts, split_grad)


def body(
    token_ids,
    type_ids,
    mask_pos,
    mask_valid,
    mlm_labels,
    nsp_labels,
    word_table,
    word_m,
    word_v,
    attn_weight,
    attn_m,
    attn_v,
    ff_weight,
    ff_m,
    ff_v,
    side_weight,
    side_m,
    side_v,
    vectors,
    vec_m,
    vec_v,
    split_bias,
    split_m,
    split_v,
    decoder_bias,
    decoder_m,
    decoder_v,
):
    mp_rank = lax.axis_index("mp")
    dp_size = lax.axis_size("dp")
    mp_size = lax.axis_size("mp")
    validity = mask_valid.astype(jnp.float32)
    word_full, attn_full, ffw_full, side_full, vec_full = (
        lax.all_gather(word_table.astype(jnp.bfloat16), "dp", axis=0, tiled=True),
        lax.all_gather(attn_weight.astype(jnp.bfloat16), "dp", axis=0, tiled=True),
        lax.all_gather(ff_weight.astype(jnp.bfloat16), "dp", axis=0, tiled=True),
        lax.all_gather(side_weight.astype(jnp.bfloat16), "dp", axis=0, tiled=True),
        lax.all_gather(vectors.astype(jnp.bfloat16), "dp", axis=1, tiled=True),
    )
    vec_rows = vec_full.astype(jnp.float32)
    total_count = lax.psum(jnp.sum(validity), "dp")
    total_seqs = jnp.float32(token_ids.shape[0] * dp_size)
    vocab_local = word_full.shape[0]
    shifted = token_ids - mp_rank * vocab_local
    inside = (shifted >= 0) & (shifted < vocab_local)
    safe_ids = jnp.where(inside, shifted, 0)
    looked = jnp.where(inside[..., None], word_full[safe_ids], jnp.zeros((), jnp.bfloat16))
    embedded = lax.psum(looked, "mp").astype(jnp.float32)
    position_rows = side_full[2 * D :].astype(jnp.float32)
    embedded = (
        embedded
        + position_rows[None]
        + jnp.where(type_ids[..., None] == 0, vec_rows[12], vec_rows[13])
    )
    hidden0 = layer_norm(embedded, vec_rows[0], vec_rows[1])
    hidden2, kept_state = layer_forward(hidden0, attn_full, ffw_full, vec_rows, split_bias)
    batch_size, slot_count = mask_pos.shape
    row_count = batch_size * slot_count
    batch_index = lax.broadcasted_iota(jnp.int32, (batch_size, slot_count), 0)
    picked_b = hidden2[batch_index, mask_pos].reshape(row_count, D).astype(jnp.bfloat16)
    dense_w = side_full[D : 2 * D]
    dense_out = jnp.dot(picked_b, dense_w, preferred_element_type=jnp.float32) + vec_rows[8]
    act_dense = gelu_exact(dense_out)
    head_rows = layer_norm(act_dense, vec_rows[9], vec_rows[10])
    head_b = head_rows.astype(jnp.bfloat16)
    logits = (
        jnp.einsum("rd,vd->rv", head_b, word_full, preferred_element_type=jnp.float32)
        + decoder_bias
    )
    label_local = mlm_labels.reshape(-1) - mp_rank * vocab_local
    hit_rows = label_local[:, None] == lax.broadcasted_iota(jnp.int32, (row_count, vocab_local), 1)
    row_top = jnp.max(logits, axis=1)
    row_total = jnp.sum(jnp.exp(logits - row_top[:, None]), axis=1)
    row_target = jnp.sum(jnp.where(hit_rows, logits, 0.0), axis=1)
    top_all, total_all, target_all = merged((row_top, row_total, row_target), "mp", merge_stats)
    log_total = top_all + jnp.log(total_all)
    valid_rows = validity.reshape(-1)
    mlm_sum = -jnp.sum(valid_rows * (target_all - log_total))
    weight_rows = valid_rows / total_count
    grad_logits = (
        (jnp.exp(logits - log_total[:, None]) - hit_rows.astype(jnp.float32)) * weight_rows[:, None]
    ).astype(jnp.bfloat16)
    decoder_grad = jnp.sum(grad_logits.astype(jnp.float32), axis=0)
    word_grad = jnp.einsum("rv,rd->vd", grad_logits, head_b, preferred_element_type=jnp.float32)
    head_part = jnp.dot(grad_logits, word_full, preferred_element_type=jnp.float32)
    grad_head = lax.psum(head_part, "mp")
    grad_act, grad_g9, grad_s9 = norm_backward(act_dense, vec_rows[9], vec_rows[10], grad_head)
    grad_dense = gelu_backward(dense_out, grad_act).astype(jnp.bfloat16)
    dense_bias_grad = jnp.sum(grad_dense.astype(jnp.float32), axis=0)
    dense_grad = jnp.einsum("rd,re->de", picked_b, grad_dense, preferred_element_type=jnp.float32)
    grad_picked = jnp.einsum("re,de->rd", grad_dense, dense_w, preferred_element_type=jnp.float32)
    grad_top = (
        jnp.zeros_like(hidden2)
        .at[batch_index, mask_pos]
        .add(grad_picked.reshape(batch_size, slot_count, D))
    )
    cls_rows = hidden2[:, 0].astype(jnp.bfloat16)
    pooler_w = side_full[:D]
    pooled = jnp.tanh(
        jnp.dot(cls_rows, pooler_w, preferred_element_type=jnp.float32) + vec_rows[11]
    )
    classes = vec_rows[14:16]
    nsp_logp = jax.nn.log_softmax(jnp.dot(pooled, classes.T, precision=highest), axis=-1)
    pick_nsp = nsp_labels[:, None] == lax.broadcasted_iota(jnp.int32, (batch_size, 2), 1)
    nsp_sum = -jnp.sum(jnp.where(pick_nsp, nsp_logp, 0.0))
    grad_nsp = (jnp.exp(nsp_logp) - pick_nsp.astype(jnp.float32)) / total_seqs
    class_grad = jnp.dot(grad_nsp.T, pooled, precision=highest)
    grad_pre = jnp.dot(grad_nsp, classes, precision=highest) * (1.0 - pooled * pooled)
    pooler_bias_grad = jnp.sum(grad_pre, axis=0)
    pooler_grad = jnp.dot(cls_rows.astype(jnp.float32).T, grad_pre, precision=highest)
    grad_top = grad_top.at[:, 0].add(
        jnp.dot(grad_pre, pooler_w.astype(jnp.float32).T, precision=highest)
    )
    grad_h0, attn_grad, ffw_grad, vec_parts, split_grad = layer_backward(
        grad_top, kept_state, attn_full, ffw_full, vec_rows
    )
    grad_x0, grad_g0, grad_s0 = norm_backward(embedded, vec_rows[0], vec_rows[1], grad_h0)
    word_grad = word_grad + jnp.zeros((vocab_local, D), jnp.float32).at[safe_ids.reshape(-1)].add(
        jnp.where(inside.reshape(-1)[:, None], grad_x0.reshape(-1, D), 0.0)
    )
    position_grad = jnp.sum(grad_x0, axis=0)
    type_zero = jnp.sum(jnp.where(type_ids[..., None] == 0, grad_x0, 0.0), axis=(0, 1))
    type_one = jnp.sum(jnp.where(type_ids[..., None] == 1, grad_x0, 0.0), axis=(0, 1))
    side_grad = jnp.concatenate([pooler_grad, dense_grad, position_grad], axis=0)
    vec_grad = jnp.stack(
        [
            grad_g0,
            grad_s0,
            vec_parts[0],
            vec_parts[1],
            vec_parts[2],
            vec_parts[3],
            vec_parts[4],
            vec_parts[5],
            dense_bias_grad,
            grad_g9,
            grad_s9,
            pooler_bias_grad,
            type_zero,
            type_one,
            class_grad[0],
            class_grad[1],
        ],
        axis=0,
    )
    word_red, attn_red, ffw_red, side_red, vec_red = (
        lax.psum_scatter(word_grad, "dp", scatter_dimension=0, tiled=True),
        lax.psum_scatter(attn_grad, "dp", scatter_dimension=0, tiled=True),
        lax.psum_scatter(ffw_grad, "dp", scatter_dimension=0, tiled=True),
        lax.psum_scatter(side_grad, "dp", scatter_dimension=0, tiled=True),
        lax.psum_scatter(vec_grad, "dp", scatter_dimension=1, tiled=True),
    )
    split_red, decoder_red = lax.psum((split_grad, decoder_grad), "dp")
    own_square = (
        jnp.sum(word_red * word_red)
        + jnp.sum(attn_red * attn_red)
        + jnp.sum(ffw_red * ffw_red)
        + (jnp.sum(side_red * side_red) + jnp.sum(vec_red * vec_red)) / mp_size
        + (jnp.sum(split_red * split_red) + jnp.sum(decoder_red * decoder_red)) / dp_size
    )
    loss_part = (mlm_sum / total_count + nsp_sum / total_seqs) / mp_size
    grad_square, total_loss = lax.psum((own_square, loss_part), ("dp", "mp"))
    grad_norm = jnp.sqrt(grad_square)
    clip_scale = max_norm / jnp.maximum(grad_norm, max_norm)
    word_new = adam_step(word_table, word_m, word_v, word_red, clip_scale, True)
    attn_new = adam_step(attn_weight, attn_m, attn_v, attn_red, clip_scale, True)
    ff_new = adam_step(ff_weight, ff_m, ff_v, ffw_red, clip_scale, True)
    side_new = adam_step(side_weight, side_m, side_v, side_red, clip_scale, True)
    vec_new = adam_step(vectors, vec_m, vec_v, vec_red, clip_scale, False)
    split_new = adam_step(split_bias, split_m, split_v, split_red, clip_scale, False)
    decoder_new = adam_step(decoder_bias, decoder_m, decoder_v, decoder_red, clip_scale, False)
    return (
        total_loss,
        grad_norm,
        word_new[0],
        word_new[1],
        word_new[2],
        attn_new[0],
        attn_new[1],
        attn_new[2],
        ff_new[0],
        ff_new[1],
        ff_new[2],
        side_new[0],
        side_new[1],
        side_new[2],
        vec_new[0],
        vec_new[1],
        vec_new[2],
        split_new[0],
        split_new[1],
        split_new[2],
        decoder_new[0],
        decoder_new[1],
        decoder_new[2],
    )


def solution(mesh):
    placed = (
        P("dp", None),
        P("dp", None),
        P("dp", None),
        P("dp", None),
        P("dp", None),
        P("dp"),
        P(("mp", "dp"), None),
        P(("mp", "dp"), None),
        P(("mp", "dp"), None),
        P("dp", None, "mp"),
        P("dp", None, "mp"),
        P("dp", None, "mp"),
        P("dp", None, "mp"),
        P("dp", None, "mp"),
        P("dp", None, "mp"),
        P("dp", None),
        P("dp", None),
        P("dp", None),
        P(None, "dp"),
        P(None, "dp"),
        P(None, "dp"),
        P(None, "mp"),
        P(None, "mp"),
        P(None, "mp"),
        P("mp"),
        P("mp"),
        P("mp"),
    )
    return jax.shard_map(
        body,
        mesh=mesh,
        in_specs=placed,
        out_specs=(
            P(),
            P(),
            P(("mp", "dp"), None),
            P(("mp", "dp"), None),
            P(("mp", "dp"), None),
            P("dp", None, "mp"),
            P("dp", None, "mp"),
            P("dp", None, "mp"),
            P("dp", None, "mp"),
            P("dp", None, "mp"),
            P("dp", None, "mp"),
            P("dp", None),
            P("dp", None),
            P("dp", None),
            P(None, "dp"),
            P(None, "dp"),
            P(None, "dp"),
            P(None, "mp"),
            P(None, "mp"),
            P(None, "mp"),
            P("mp"),
            P("mp"),
            P("mp"),
        ),
        check_vma=False,
    )
```

profile of v0, /device:TPU:0, one launch (start us, length us, event | category | flops | bytes accessed | tf_op | source)
XLA Modules:
  0.0 2109.4 jit_solution(18084089695242035304)
XLA Ops:
  13.9 166.2 %all-gather.12.cloned.1.call-done = bf16[7680,768]{1,0:T(8,128)(2,1)} async-done(((bf16[960,768]{1,0:T(8,128)(2,1)}), bf16[7680,768]{1,0:T(8,128)(2,1)}) %all-gather.12.cloned.1.call-update) | async-done | bytes 11796496 | tf_op jit(solution)/shard_map/all_gather | solution.py:262
  180.0 14.3 gather_fusion
  196.5 31.0 %all-gather.3 = bf16[8,96,16]{1,2,0:T(8,128)(2,1)S(1)} all-gather(bf16[1,96,16]{1,2,0:T(8,128)(2,1)S(1)} %convert_bitcast_fusion), channel_id=1, replica_groups=mesh['dp'=8,'mp'=4] {'dp'}, dimensions={0}, use_global_device_ids=true | all-gather | bytes 27648 | tf_op jit(solution)/shard_map/all_gather | solution.py:266
  236.1 60.0 %all-gather.14.cloned.1.call-done = bf16[2560,768]{1,0:T(8,128)(2,1)} async-done(((bf16[320,768]{1,0:T(8,128)(2,1)}), bf16[2560,768]{1,0:T(8,128)(2,1)}) %all-gather.14.cloned.1.call-update) | async-done | bytes 3932176 | tf_op jit(solution)/shard_map/all_gather | solution.py:265
  297.8 67.7 %all-reduce.9.cloned.1.call-done = bf16[2,1024,768]{2,1,0:T(8,128)(2,1)} async-done(((bf16[2,1024,768]{2,1,0:T(8,128)(2,1)}), bf16[2,1024,768]{2,1,0:T(8,128)(2,1)}) %all-reduce.9.cloned.1.call-update) | async-done | bytes 3145744 | tf_op jit(solution)/shard_map/psum | solution.py:276
  375.2 10.1 multiply_reduce_fusion.1
  385.3 10.6 fusion
  395.9 11.0 fusion.26
  414.0 117.4 %all-reduce.11.cloned.1.call-done = f32[2,1024,768]{2,1,0:T(8,128)} async-done(((f32[2,1024,768]{2,1,0:T(8,128)}), f32[2,1024,768]{2,1,0:T(8,128)}) %all-reduce.11.cloned.1.call-update) | async-done | bytes 6291472 | tf_op jit(solution)/shard_map/psum | solution.py:107
  531.5 5.7 fusion.101
  540.7 45.4 %all-gather.18.cloned.1.call-done = bf16[768,2,768]{2,0,1:T(8,128)(2,1)} async-done(((bf16[96,2,768]{2,0,1:T(8,128)(2,1)}), bf16[768,2,768]{2,0,1:T(8,128)(2,1)}) %all-gather.18.cloned.1.call-update) | async-done | bytes 2359312 | tf_op jit(solution)/shard_map/all_gather | solution.py:264
  586.1 7.7 fusion.25
  593.9 15.6 multiply_convert_fusion.2
  617.1 20.0 psum.80
  638.3 95.8 %all-reduce.13.cloned.1.call-done = f32[2,1024,768]{2,1,0:T(8,128)} async-done(((f32[2,1024,768]{2,1,0:T(8,128)}), f32[2,1024,768]{2,1,0:T(8,128)}) %all-reduce.13.cloned.1.call-update) | async-done | bytes 6291472 | tf_op jit(solution)/shard_map/psum | solution.py:119
  734.1 5.6 fusion.99
  744.2 10.1 gather_fusion.1
  754.3 7.1 fusion.97
  762.5 9.3 add_reduce_fusion
  771.9 9.0 select_reduce_fusion
  798.1 9.5 convert_reduce_fusion
  810.9 10.4 fusion.106
  826.2 38.3 %all-reduce.15.cloned.1.call-done = f32[512,768]{1,0:T(8,128)} async-done(((f32[512,768]{1,0:T(8,128)}), f32[512,768]{1,0:T(8,128)}) %all-reduce.15.cloned.1.call-update) | async-done | bytes 1572880 | tf_op jit(solution)/shard_map/psum | solution.py:314
  877.4 68.8 %scatter_fusion = f32[2,1024,768]{2,1,0:T(8,128)} fusion(f32[2,1024,768]{2,1,0:T(8,128)} %broadcast.466, s32[512]{0:T(512)S(1)} %bitcast.187, f32[512,768]{1,0:T(8,128)S(1)} %fusion.37), kind=kCustom, calls=%fused_computation.2 | custom fusion | flops 393216 | bytes 4722688 | tf_op jit(solution)/shard_map/scatter-add | solution.py:323
  948.5 5.9 multiply_reduce_fusion.2
  964.0 6.4 convert_reduce_fusion.1
  977.0 119.6 %all-reduce.17.cloned.1.call-done = f32[2,1024,768]{2,1,0:T(8,128)} async-done(((f32[2,1024,768]{2,1,0:T(8,128)}), f32[2,1024,768]{2,1,0:T(8,128)}) %all-reduce.17.cloned.1.call-update) | async-done | bytes 6291472 | tf_op jit(solution)/shard_map/psum | solution.py:168
  1096.5 8.1 multiply_reduce_fusion.3
  1112.4 20.0 multiply_reduce_fusion
  1132.4 17.3 multiply_convert_fusion
  1153.0 6.3 multiply_convert_fusion.3
  1159.3 13.7 fusion.27
  1173.0 6.4 bitcast_convert_fusion
  1182.7 6.2 convolution_bitcast_fusion.2
  1188.9 59.4 %all-reduce.19.cloned.1.call-done = bf16[2,1024,768]{2,1,0:T(8,128)(2,1)} async-done(((bf16[2,1024,768]{2,1,0:T(8,128)(2,1)}), bf16[2,1024,768]{2,1,0:T(8,128)(2,1)}) %all-reduce.19.cloned.1.call-update) | async-done | bytes 3145744 | tf_op jit(solution)/shard_map/psum | solution.py:219
  1248.3 6.9 fusion.85
  1259.4 7.1 select_reduce_fusion.1
  1271.7 5.7 convolution_bitcast_fusion
  1277.3 6.0 convolution_bitcast_fusion.1
  1294.2 14.5 fusion.83
  1313.6 30.2 %scatter_fusion.1 = f32[7680,768]{1,0:T(8,128)} fusion(f32[7680,768]{1,0:T(8,128)} %fusion.83, s32[2048]{0:T(1024)S(1)} %bitcast.232, f32[2048,768]{1,0:T(8,128)} %bitcast_select_fusion), kind=kCustom, calls=%fused_computation.3 | custom fusion | flops 1572864 | bytes 18882560 | tf_op jit(solution)/shard_map/scatter-add | solution.py:346
  1350.3 38.2 %all-reduce.1 = (f32[6,192]{1,0:T(8,128)S(1)}, f32[7680]{0:T(1024)S(1)}) all-reduce(f32[6,192]{1,0:T(8,128)S(1)} %pad_maximum_fusion.4, f32[7680]{0:T(1024)S(1)} %copy-done.59), channel_id=1, replica_groups=mesh['dp'=8,'mp'=4] {'dp'}, use_global_device_ids=true, to_apply=%region_66.67 | all-reduce | flops 8832 | bytes 70656 | tf_op jit(solution)/shard_map/psum | solution.py:381
  1392.6 10.5 reduce-scatter.16.cloned.1.call-done
  1404.9 96.7 %reduce-scatter.12.cloned.1.call-done = f32[96,2,768]{2,0,1:T(8,128)} async-done(((f32[768,2,768]{2,0,1:T(8,128)}), f32[96,2,768]{2,0,1:T(8,128)}) %reduce-scatter.12.cloned.1.call-update) | async-done | bytes 589840 | tf_op jit(solution)/shard_map/reduce_scatter | solution.py:377
  1503.5 141.6 %reduce-scatter.14.cloned.1.call-done = f32[320,768]{1,0:T(8,128)} async-done(((f32[2560,768]{1,0:T(8,128)}), f32[320,768]{1,0:T(8,128)}) %reduce-scatter.14.cloned.1.call-update) | async-done | bytes 983056 | tf_op jit(solution)/shard_map/reduce_scatter | solution.py:378
  1648.4 380.0 %reduce-scatter.10.cloned.1.call-done = f32[960,768]{1,0:T(8,128)} async-done(((f32[7680,768]{1,0:T(8,128)}), f32[960,768]{1,0:T(8,128)}) %reduce-scatter.10.cloned.1.call-update) | async-done | bytes 2949136 | tf_op jit(solution)/shard_map/reduce_scatter | solution.py:375
  2035.5 39.5 %all-reduce = (f32[]{:T(128)}, f32[]{:T(128)}) all-reduce(f32[]{:T(128)S(6)} %div.236, f32[]{:T(128)S(6)} %add.501), channel_id=1, replica_groups=mesh['dp'=8,'mp'=4] {'dp','mp'}, use_global_device_ids=true, to_apply=%region_24.25 | all-reduce | flops 2 | bytes 16 | tf_op jit(solution)/shard_map/psum | solution.py:390
  2095.7 5.7 multiply_subtract_fusion
  (467 shorter events, 186.5 us)
Async XLA Ops:
  7.2 172.8 %all-gather.12.cloned.1.call-start = ((), (), s32[]{:S(2)}) async-start(), calls=%async_computation.5 | async-start | bytes 13271040 | tf_op jit(solution)/shard_map/all_gather | solution.py:262
  10.4 219.2 %all-gather.16.cloned.1.call-start = ((), (), s32[]{:S(2)}) async-start(), calls=%async_computation.8 | async-start | bytes 1769472 | tf_op jit(solution)/shard_map/all_gather | solution.py:263
  12.3 283.9 %all-gather.14.cloned.1.call-start = ((), (), s32[]{:S(2)}) async-start(), calls=%async_computation.7 | async-start | bytes 4423680 | tf_op jit(solution)/shard_map/all_gather | solution.py:265
  13.2 352.3 %all-reduce.9.cloned.1.call-start = ((), (), s32[]{:S(2)}) async-start(), calls=%async_computation.6 | async-start | bytes 6291456 | tf_op jit(solution)/shard_map/psum | solution.py:276
  13.3 181.2 %copy-start.78 = (pred[2,1024]{1,0:T(4,128)(4,1)}, pred[2,1024]{1,0:T(4,128)(4,1)S(1)}, u32[]{:S(2)}) copy-start(pred[2,1024]{1,0:T(4,128)(4,1)S(1)} %compare_and_fusion) | copy-start | bytes 6148
  196.4 335.1 %all-reduce.11.cloned.1.call-start = ((), (), s32[]{:S(2)}) async-start(), calls=%async_computation.9 | async-start | bytes 12582912 | tf_op jit(solution)/shard_map/psum | solution.py:107
  227.7 147.5 %copy-start.76 = (f32[3,64]{1,0:T(4,128)}, f32[3,64]{1,0:T(4,128)S(1)}, u32[]{:S(2)}) copy-start(f32[3,64]{1,0:T(4,128)S(1)} %add.453) | copy-start | bytes 2308
  229.0 302.4 %copy-start.49 = (f32[768]{0:T(1024)}, f32[768]{0:T(1024)S(1)}, u32[]{:S(2)}) copy-start(f32[768]{0:T(1024)S(1)} %get-tuple-element.318) | copy-start | bytes 9220
  229.0 302.4 %copy-start.51 = (f32[768]{0:T(1024)}, f32[768]{0:T(1024)S(1)}, u32[]{:S(2)}) copy-start(f32[768]{0:T(1024)S(1)} %get-tuple-element.319) | copy-start | bytes 9220
  229.0 302.4 %copy-start.57 = (f32[768]{0:T(1024)}, f32[768]{0:T(1024)S(1)}, u32[]{:S(2)}) copy-start(f32[768]{0:T(1024)S(1)} %get-tuple-element.317) | copy-start | bytes 9220
  229.0 505.1 %copy-start.71 = (f32[768]{0:T(1024)}, f32[768]{0:T(1024)S(1)}, u32[]{:S(2)}) copy-start(f32[768]{0:T(1024)S(1)} %get-tuple-element.314) | copy-start | bytes 9220
  229.6 301.8 %copy-start.53 = (pred[2,1024]{1,0:T(4,128)(4,1)}, pred[2,1024]{1,0:T(4,128)(4,1)S(1)}, u32[]{:S(2)}) copy-start(pred[2,1024]{1,0:T(4,128)(4,1)S(1)} %get-tuple-element.394) | copy-start | bytes 6148
  236.1 170.9 %copy-start.40 = (bf16[768,1,192]{0,2,1:T(8,128)(2,1)}, bf16[768,1,192]{0,2,1:T(8,128)(2,1)S(1)}, u32[]{:S(2)}) copy-start(bf16[768,1,192]{0,2,1:T(8,128)(2,1)S(1)} %copy.162) | copy-start | bytes 884740
  297.8 233.7 %copy-start = (f32[1024,768]{1,0:T(8,128)}, f32[1024,768]{1,0:T(8,128)S(1)}, u32[]{:S(2)}) copy-start(f32[1024,768]{1,0:T(8,128)S(1)} %slice_convert_fusion.1) | copy-start | bytes 9437188
  368.5 163.0 %copy-start.45 = (f32[2,1024]{1,0:T(2,128)}, f32[2,1024]{1,0:T(2,128)S(1)}, u32[]{:S(2)}) copy-start(f32[2,1024]{1,0:T(2,128)S(1)} %broadcast_multiply_fusion.2) | copy-start | bytes 24580
  370.5 161.0 %copy-start.55 = (f32[2,1024]{1,0:T(2,128)}, f32[2,1024]{1,0:T(2,128)S(1)}, u32[]{:S(2)}) copy-start(f32[2,1024]{1,0:T(2,128)S(1)} %fusion.62) | copy-start | bytes 24580
  411.6 119.9 %copy-start.109 = (f32[768]{0:T(1024)S(1)}, f32[768]{0:T(1024)}, u32[]{:S(2)}) copy-start(f32[768]{0:T(1024)} %get-tuple-element.315) | copy-start | bytes 9220
  411.6 174.5 %all-gather.18.cloned.1.call-start = ((), (), s32[]{:S(2)}) async-start(), calls=%async_computation.10 | async-start | bytes 2654208 | tf_op jit(solution)/shard_map/all_gather | solution.py:264
  413.5 320.6 %all-reduce.13.cloned.1.call-start = ((), (), s32[]{:S(2)}) async-start(), calls=%async_computation.11 | async-start | bytes 12582912 | tf_op jit(solution)/shard_map/psum | solution.py:119
  414.0 179.9 %copy-start.101 = (f32[768]{0:T(1024)}, f32[768]{0:T(1024)S(1)}, u32[]{:S(2)}) copy-start(f32[768]{0:T(1024)S(1)} %add.464) | copy-start | bytes 9220
  537.2 48.9 %copy-start.106 = (f32[768]{0:T(1024)S(1)}, f32[768]{0:T(1024)}, u32[]{:S(2)}) copy-start(f32[768]{0:T(1024)} %get-tuple-element.313) | copy-start | bytes 9220
  615.8 118.3 %copy-start.108 = (f32[768]{0:T(1024)S(1)}, f32[768]{0:T(1024)}, u32[]{:S(2)}) copy-start(f32[768]{0:T(1024)} %get-tuple-element.312) | copy-start | bytes 9220
  615.8 248.7 %all-reduce.15.cloned.1.call-start = ((), (), s32[]{:S(2)}) async-start(), calls=%async_computation.12 | async-start | bytes 3145728 | tf_op jit(solution)/shard_map/psum | solution.py:314
  810.8 53.7 %copy-start.11 = (f32[512,768]{1,0:T(8,128)S(1)}, f32[512,768]{1,0:T(8,128)}, u32[]{:S(2)}) copy-start(f32[512,768]{1,0:T(8,128)} %copy-done.10) | copy-start | bytes 4718596
  810.8 53.7 %copy-start.67 = (f32[768]{0:T(1024)S(1)}, f32[768]{0:T(1024)}, u32[]{:S(2)}) copy-start(f32[768]{0:T(1024)} %get-tuple-element.308) | copy-start | bytes 9220
  810.9 53.6 %copy-start.74 = (f32[512]{0:T(512)S(1)}, f32[512]{0:T(512)}, u32[]{:S(2)}) copy-start(f32[512]{0:T(512)} %copy-done.73) | copy-start | bytes 6148
  821.3 45.2 %copy-start.98 = (f32[512]{0:T(512)S(1)}, f32[512]{0:T(512)}, u32[]{:S(2)}) copy-start(f32[512]{0:T(512)} %copy-done.97) | copy-start | bytes 6148
  821.3 45.2 %copy-start.93 = (f32[512]{0:T(512)S(1)}, f32[512]{0:T(512)}, u32[]{:S(2)}) copy-start(f32[512]{0:T(512)} %copy-done.92) | copy-start | bytes 6148
  821.3 275.2 %all-reduce.17.cloned.1.call-start = ((), (), s32[]{:S(2)}) async-start(), calls=%async_computation.13 | async-start | bytes 12582912 | tf_op jit(solution)/shard_map/psum | solution.py:168
  877.4 71.1 %copy-start.70 = (f32[768]{0:T(1024)S(1)}, f32[768]{0:T(1024)}, u32[]{:S(2)}) copy-start(f32[768]{0:T(1024)} %get-tuple-element.311) | copy-start | bytes 9220
  976.6 119.9 %copy-start.72 = (f32[768]{0:T(1024)S(1)}, f32[768]{0:T(1024)}, u32[]{:S(2)}) copy-start(f32[768]{0:T(1024)} %copy-done.71) | copy-start | bytes 9220
  976.7 271.6 %all-reduce.19.cloned.1.call-start = ((), (), s32[]{:S(2)}) async-start(), calls=%async_computation.14 | async-start | bytes 6291456 | tf_op jit(solution)/shard_map/psum | solution.py:219
  1179.4 211.7 %reduce-scatter.18.cloned.1.call-start = ((), (), s32[]{:S(2)}) async-start(), calls=%async_computation.19 | async-start | bytes 442368
  1182.7 65.6 %copy-start.1 = (f32[1024,768]{1,0:T(8,128)S(1)}, f32[1024,768]{1,0:T(8,128)}, u32[]{:S(2)}) copy-start(f32[1024,768]{1,0:T(8,128)} %copy-done) | copy-start | bytes 9437188
  1182.7 65.6 %copy-start.46 = (f32[2,1024]{1,0:T(2,128)S(1)}, f32[2,1024]{1,0:T(2,128)}, u32[]{:S(2)}) copy-start(f32[2,1024]{1,0:T(2,128)} %copy-done.45) | copy-start | bytes 24580
  1182.7 65.6 %copy-start.50 = (f32[768]{0:T(1024)S(1)}, f32[768]{0:T(1024)}, u32[]{:S(2)}) copy-start(f32[768]{0:T(1024)} %copy-done.49) | copy-start | bytes 9220
  1182.7 65.6 %copy-start.52 = (f32[768]{0:T(1024)S(1)}, f32[768]{0:T(1024)}, u32[]{:S(2)}) copy-start(f32[768]{0:T(1024)} %copy-done.51) | copy-start | bytes 9220
  1182.7 65.6 %copy-start.54 = (pred[2,1024]{1,0:T(4,128)(4,1)S(1)}, pred[2,1024]{1,0:T(4,128)(4,1)}, u32[]{:S(2)}) copy-start(pred[2,1024]{1,0:T(4,128)(4,1)} %copy-done.53) | copy-start | bytes 6148
  1182.7 65.6 %copy-start.58 = (f32[768]{0:T(1024)S(1)}, f32[768]{0:T(1024)}, u32[]{:S(2)}) copy-start(f32[768]{0:T(1024)} %copy-done.57) | copy-start | bytes 9220
  1188.9 66.4 %copy-start.63 = (f32[2,1024]{1,0:T(2,128)S(1)}, f32[2,1024]{1,0:T(2,128)}, u32[]{:S(2)}) copy-start(f32[2,1024]{1,0:T(2,128)} %copy-done.62) | copy-start | bytes 24580
  1188.9 66.4 %copy-start.56 = (f32[2,1024]{1,0:T(2,128)S(1)}, f32[2,1024]{1,0:T(2,128)}, u32[]{:S(2)}) copy-start(f32[2,1024]{1,0:T(2,128)} %copy-done.55) | copy-start | bytes 24580
  1267.5 135.6 %reduce-scatter.16.cloned.1.call-start = ((), (), s32[]{:S(2)}) async-start(), calls=%async_computation.18 | async-start | bytes 2654208
  1271.4 230.2 %reduce-scatter.12.cloned.1.call-start = ((), (), s32[]{:S(2)}) async-start(), calls=%async_computation.16 | async-start | bytes 5308416 | tf_op jit(solution)/shard_map/reduce_scatter | solution.py:377
  1285.9 359.1 %reduce-scatter.14.cloned.1.call-start = ((), (), s32[]{:S(2)}) async-start(), calls=%async_computation.17 | async-start | bytes 8847360 | tf_op jit(solution)/shard_map/reduce_scatter | solution.py:378
  1292.8 735.6 %reduce-scatter.10.cloned.1.call-start = ((), (), s32[]{:S(2)}) async-start(), calls=%async_computation.15 | async-start | bytes 26542080 | tf_op jit(solution)/shard_map/reduce_scatter | solution.py:375
  1344.8 731.0 %copy-start.37 = (f32[96,2,768]{2,1,0:T(2,128)S(1)}, f32[96,2,768]{2,1,0:T(2,128)}, u32[]{:S(2)}) copy-start(f32[96,2,768]{2,1,0:T(2,128)} %param.43) | copy-start | bytes 1769476
  1350.3 725.5 %copy-start.43 = (f32[96,2,768]{2,1,0:T(2,128)S(1)}, f32[96,2,768]{2,1,0:T(2,128)}, u32[]{:S(2)}) copy-start(f32[96,2,768]{2,1,0:T(2,128)} %param.44) | copy-start | bytes 1769476
  1350.3 725.5 %copy-start.44 = (f32[96,2,768]{2,1,0:T(2,128)S(1)}, f32[96,2,768]{2,1,0:T(2,128)}, u32[]{:S(2)}) copy-start(f32[96,2,768]{2,1,0:T(2,128)} %param.45) | copy-start | bytes 1769476
  (101 other events, 819.5 us)
Sparse Core Ops, SparseCore 0:
  10.8 169.2 all-gather.11
  182.8 42.5 all-gather.15
  228.2 67.9 all-gather.13
  298.4 67.0 all-reduce.8
  411.7 119.6 all-reduce.10
  534.1 52.0 all-gather.17
  615.9 118.1 all-reduce.12
  821.4 43.0 all-reduce.14
  976.8 119.6 all-reduce.16
  1179.5 68.7 all-reduce.18
  1267.7 62.3 reduce-scatter.17
  1333.9 69.1 reduce-scatter.15
  1406.8 94.8 reduce-scatter.11
  1505.1 139.8 reduce-scatter.13
  1648.8 379.5 reduce-scatter.9
where the time goes:
time: 2120 us; the launch traced here: 2110 us
  waiting for transfers between devices  1400 us (66%)
  other arithmetic  284 us (13%)
  matrix products  172 us (8%)
  blocking collectives  144 us (7%)
  local copies, waits for them, and re-layouts  83.9 us (4%)
  between operations  24.5 us (1%)
    reduce_scatter x1, waiting for transfers between devices, body(): lax.psum_scatter(word_grad, 'dp', scatter_dimension=0, tiled=True)  380 us
    all_gather x1, waiting for transfers between devices, body(): lax.all_gather(word_table.astype(jnp.bfloat16), 'dp', axis=0, tiled=True)  166 us
    reduce_scatter x1, waiting for transfers between devices, body(): lax.psum_scatter(side_grad, 'dp', scatter_dimension=0, tiled=True)  142 us
    psum x1, waiting for transfers between devices, layer_backward(): grad_h1 = grad_r2 + lax.psum(hidden1_part, 'mp')  120 us
    psum x1, waiting for transfers between devices, layer_forward(): resid1 = hidden0 + (lax.psum(attn_part, 'mp') + vec_rows[2])  117 us
    reduce_scatter x1, waiting for transfers between devices, body(): lax.psum_scatter(ffw_grad, 'dp', scatter_dimension=0, tiled=True)  96.7 us
    psum x1, waiting for transfers between devices, layer_forward(): resid2 = hidden1 + (lax.psum(ffn_part, 'mp') + vec_rows[5])  95.8 us
    scatter-add x1, other arithmetic, body(): grad_top = jnp.zeros_like(hidden2).at[batch_index, mask_pos].add(grad_pic...  68.8 us
  transfers between devices with their start and end apart: 15, of which 13 were waited for; matrix products, arithmetic and copies ran while one was open for 7% of the time, Pallas kernels for 0%

commit v1 on v0

v1 whole, which is shorter than its diff:
```python
import functools
import math

import jax
import jax.numpy as jnp
from jax import lax
from jax.sharding import Mesh, PartitionSpec as P

D = 768
HEAD_DIM = 64


beta_one = 0.9
beta_two = 0.999
adam_eps = 1e-06
learn_rate = 0.2
decay_rate = 0.01
step_count = 10
max_norm = 0.05
norm_eps = 1e-12
highest = lax.Precision.HIGHEST


def layer_norm(inputs, norm_gain, norm_shift):
    center = inputs - jnp.mean(inputs, axis=-1, keepdims=True)
    spread = jnp.mean(center * center, axis=-1, keepdims=True)
    return center * lax.rsqrt(spread + norm_eps) * norm_gain + norm_shift


def gelu_exact(inputs):
    return jax.nn.gelu(inputs, approximate=False)


def norm_backward(inputs, norm_gain, norm_shift, upstream):
    _, pullback = jax.vjp(layer_norm, inputs, norm_gain, norm_shift)
    return pullback(upstream)


def gelu_backward(inputs, upstream):
    _, pullback = jax.vjp(gelu_exact, inputs)
    return pullback(upstream)[0]


def adam_step(weight, moment, square, gradient, clip_scale, decays):
    gradient = gradient * clip_scale
    moment = beta_one * moment + (1 - beta_one) * gradient
    square = beta_two * square + (1 - beta_two) * gradient * gradient
    mean_hat = moment / (1 - beta_one**step_count)
    var_hat = square / (1 - beta_two**step_count)
    change = mean_hat / (jnp.sqrt(var_hat) + adam_eps)
    if decays:
        change = change + decay_rate * weight
    return (weight - learn_rate * change, moment, square)


def comm_all_gather(value, axes):
    return lax.all_gather(value, axes, axis=0, tiled=True)


def comm_scatter_sum(value, axes):
    return lax.psum_scatter(value, axes, scatter_dimension=0, tiled=True)


def attention_forward(queries, key_rows, value_rows):
    score_scale = 1.0 / math.sqrt(HEAD_DIM)
    length, width = queries.shape
    heads = width // HEAD_DIM
    q3 = queries.reshape(length, heads, HEAD_DIM)
    k3 = key_rows.reshape(-1, heads, HEAD_DIM)
    v3 = value_rows.reshape(-1, heads, HEAD_DIM)
    scores = jnp.einsum("qhe,khe->hqk", q3, k3, preferred_element_type=jnp.float32) * score_scale
    row_top = jnp.max(scores, axis=-1, keepdims=True)
    exp_scores = jnp.exp(scores - row_top)
    row_total = jnp.sum(exp_scores, axis=-1, keepdims=True)
    attn_probs = exp_scores / row_total
    log_norm = row_top + jnp.log(row_total)
    mixed = jnp.einsum(
        "hqk,khe->qhe", attn_probs.astype(jnp.bfloat16), v3, preferred_element_type=jnp.float32
    )
    return mixed.reshape(length, width).astype(jnp.bfloat16), log_norm


def attention_backward(queries, key_rows, value_rows, log_norm, grad_mixed):
    score_scale = 1.0 / math.sqrt(HEAD_DIM)
    length, width = queries.shape
    heads = width // HEAD_DIM
    q3 = queries.reshape(length, heads, HEAD_DIM)
    k3 = key_rows.reshape(-1, heads, HEAD_DIM)
    v3 = value_rows.reshape(-1, heads, HEAD_DIM)
    g3 = grad_mixed.reshape(length, heads, HEAD_DIM)
    scores = jnp.einsum("qhe,khe->hqk", q3, k3, preferred_element_type=jnp.float32) * score_scale
    attn_probs = jnp.exp(scores - log_norm)
    grad_probs = jnp.einsum("qhe,khe->hqk", g3, v3, preferred_element_type=jnp.float32)
    grad_values = jnp.einsum(
        "hqk,qhe->khe", attn_probs.astype(jnp.bfloat16), g3, preferred_element_type=jnp.float32
    )
    row_dot = jnp.sum(grad_probs * attn_probs, axis=-1, keepdims=True)
    grad_scores = (attn_probs * (grad_probs - row_dot)).astype(jnp.bfloat16)
    grad_queries = (
        jnp.einsum("hqk,khe->qhe", grad_scores, k3, preferred_element_type=jnp.float32)
        * score_scale
    )
    grad_keys = (
        jnp.einsum("hqk,qhe->khe", grad_scores, q3, preferred_element_type=jnp.float32)
        * score_scale
    )
    return (
        grad_queries.reshape(length, width),
        grad_keys.reshape(-1, width),
        grad_values.reshape(-1, width),
    )


def step(sizes, *args):
    (
        token_ids, type_ids, mask_pos, mask_valid, mlm_labels, nsp_labels,
        word_table, word_m, word_v, attn_weight, attn_m, attn_v,
        ff_weight, ff_m, ff_v, side_weight, side_m, side_v,
        vectors, vec_m, vec_v, split_bias, split_m, split_v,
        decoder_bias, decoder_m, decoder_v,
    ) = args
    z_size, x_size, y_size, c_size = sizes
    dp_size, mp_size = z_size * x_size, y_size * c_size
    z_at, x_at, y_at, c_at = (lax.axis_index(a) for a in ("z", "x", "y", "c"))
    dp_rank, mp_rank = z_at * x_size + x_at, y_at * c_size + c_at
    every = ("z", "x", "y", "c")
    mp_first = ("y", "c", "z", "x")
    plane = ("x", "y", "c")
    batch_size, length = token_ids.shape
    slots = mask_pos.shape[1]
    own_len, own_slots = length // c_size, slots // c_size
    vocab_own = word_table.shape[0]
    attn_cols, ff_cols = attn_weight.shape[2], ff_weight.shape[2]
    rows_own = attn_weight.shape[0]
    low = jnp.bfloat16

    def mine(rows, size):
        row = lax.dynamic_index_in_dim(rows, y_at, 0, False)
        return lax.dynamic_slice_in_dim(row, c_at * size, size, 0)

    own_ids = mine(token_ids, own_len)
    own_types = mine(type_ids, own_len)
    seq_pos = lax.dynamic_index_in_dim(mask_pos, y_at, 0, False)
    own_pos = mine(mask_pos, own_slots)
    own_valid = mine(mask_valid, own_slots)
    own_labels = mine(mlm_labels, own_slots)
    first_core = (c_at == 0).astype(jnp.float32)

    word_plane = comm_all_gather(word_table.astype(low), plane)
    ints = comm_all_gather(jnp.concatenate([own_ids, own_labels, own_valid])[None], "z")
    z_ids, z_labels, z_valid = (
        ints[:, :own_len],
        ints[:, own_len : own_len + own_slots],
        ints[:, own_len + own_slots :],
    )
    total_count = lax.psum(jnp.sum(mask_valid.astype(jnp.float32)), ("z", "x"))
    total_seqs = jnp.float32(batch_size * dp_size)
    attn_blocks = comm_all_gather(
        attn_weight.astype(low).reshape(rows_own, 4 * attn_cols), mp_first
    ).reshape(mp_size, D, 4 * attn_cols)
    ff_blocks = comm_all_gather(
        ff_weight.astype(low).reshape(rows_own, 2 * ff_cols), mp_first
    ).reshape(mp_size, D, 2 * ff_cols)
    side_rows = side_weight.shape[0] // mp_size
    side_full = comm_all_gather(
        lax.dynamic_slice_in_dim(side_weight.astype(low), mp_rank * side_rows, side_rows, 0), every
    )
    vec_rows = (
        comm_all_gather(vectors.astype(low)[None], ("z", "x"))
        .transpose(1, 0, 2)
        .reshape(vectors.shape[0], D)
        .astype(jnp.float32)
    )
    stripe = vocab_own * x_size
    bias_mine = lax.dynamic_slice_in_dim(decoder_bias, z_at * stripe, stripe, 0)
    mp_small = comm_all_gather(
        jnp.concatenate([bias_mine, split_bias.reshape(-1)])[None], ("y", "c")
    )
    bias_plane = (
        mp_small[:, :stripe].reshape(mp_size, x_size, vocab_own).transpose(1, 0, 2).reshape(-1)
    )
    split_full = mp_small[:, stripe:].reshape(mp_size, 6, attn_cols)

    def plane_index(ids):
        block = ids // stripe
        offset = ids % stripe
        inside = block % z_size == z_at
        at = ((offset // vocab_own) * mp_size + block // z_size) * vocab_own + offset % vocab_own
        return inside, at

    flat_ids = z_ids.reshape(-1)
    inside, at = plane_index(flat_ids)
    looked = jnp.where(inside[:, None], word_plane[jnp.where(inside, at, 0)], jnp.zeros((), low))
    embedded = comm_scatter_sum(looked, "z").astype(jnp.float32)
    position_rows = lax.dynamic_slice_in_dim(side_full, 2 * D + c_at * own_len, own_len, 0)
    embedded = (
        embedded
        + position_rows.astype(jnp.float32)
        + jnp.where(own_types[:, None] == 0, vec_rows[12], vec_rows[13])
    )
    hidden0 = layer_norm(embedded, vec_rows[0], vec_rows[1])
    hidden0_b = hidden0.astype(low)

    qkv_blocks = attn_blocks[:, :, : 3 * attn_cols]
    out_blocks = attn_blocks[:, :, 3 * attn_cols :]
    packed = jnp.einsum("td,mde->tme", hidden0_b, qkv_blocks, preferred_element_type=jnp.float32)
    packed = packed.reshape(own_len, mp_size, 3, attn_cols)
    queries = (packed[:, :, 0] + split_full[:, 0]).astype(low).reshape(own_len, D)
    own_keys = packed[:, :, 1].astype(low).reshape(own_len, D)
    own_values = (packed[:, :, 2] + split_full[:, 1]).astype(low).reshape(own_len, D)
    both = comm_all_gather(jnp.stack([own_keys, own_values])[None], "c")
    key_rows = both[:, 0].reshape(-1, D)
    value_rows = both[:, 1].reshape(-1, D)
    mixed, log_norm = attention_forward(queries, key_rows, value_rows)
    attn_out = jnp.einsum(
        "tme,mde->td",
        mixed.reshape(own_len, mp_size, attn_cols),
        out_blocks,
        preferred_element_type=jnp.float32,
    )
    resid1 = hidden0 + (attn_out + vec_rows[2])
    hidden1 = layer_norm(resid1, vec_rows[3], vec_rows[4])
    hidden1_b = hidden1.astype(low)
    ff_bias = split_full[:, 2:6].transpose(0, 2, 1).reshape(mp_size, ff_cols)
    ff_in, ff_out = ff_blocks[:, :, :ff_cols], ff_blocks[:, :, ff_cols:]
    upward = jnp.einsum("td,mdf->mtf", hidden1_b, ff_in, preferred_element_type=jnp.float32)
    upward = upward + ff_bias[:, None]
    active = gelu_exact(upward).astype(low)
    ffn_out = jnp.einsum("mtf,mdf->td", active, ff_out, preferred_element_type=jnp.float32)
    resid2 = hidden1 + (ffn_out + vec_rows[5])
    hidden2 = layer_norm(resid2, vec_rows[6], vec_rows[7])

    hidden2_seq = comm_all_gather(hidden2.astype(low), "c")
    picked_b = hidden2_seq[own_pos]
    dense_w = side_full[D : 2 * D]
    dense_out = jnp.dot(picked_b, dense_w, preferred_element_type=jnp.float32) + vec_rows[8]
    act_dense = gelu_exact(dense_out)
    head_rows = layer_norm(act_dense, vec_rows[9], vec_rows[10])
    head_b = comm_all_gather(head_rows.astype(low), "z")
    row_count = head_b.shape[0]
    logits = (
        jnp.einsum("rd,vd->rv", head_b, word_plane, preferred_element_type=jnp.float32)
        + bias_plane
    )
    label_in, label_at = plane_index(z_labels.reshape(-1))
    label_at = jnp.where(label_in, label_at, -1)
    hit_rows = label_at[:, None] == lax.broadcasted_iota(jnp.int32, logits.shape, 1)
    row_top = jnp.max(logits, axis=1)
    row_total = jnp.sum(jnp.exp(logits - row_top[:, None]), axis=1)
    row_target = jnp.sum(jnp.where(hit_rows, logits, 0.0), axis=1)
    stats = comm_all_gather(jnp.stack([row_top, row_total, row_target])[None], "z")
    top_all = jnp.max(stats[:, 0], axis=0)
    total_all = jnp.sum(stats[:, 1] * jnp.exp(stats[:, 0] - top_all), axis=0)
    target_all = jnp.sum(stats[:, 2], axis=0)
    log_total = top_all + jnp.log(total_all)
    valid_rows = z_valid.reshape(-1).astype(jnp.float32)
    mlm_sum = -jnp.sum(valid_rows * (target_all - log_total))
    weight_rows = valid_rows / total_count
    grad_logits = (
        (jnp.exp(logits - log_total[:, None]) - hit_rows.astype(jnp.float32)) * weight_rows[:, None]
    ).astype(low)
    decoder_part = jnp.sum(grad_logits.astype(jnp.float32), axis=0)
    head_part = jnp.dot(grad_logits, word_plane, preferred_element_type=jnp.float32)
    grad_head = comm_scatter_sum(head_part, "z")
    grad_act, grad_g9, grad_s9 = norm_backward(act_dense, vec_rows[9], vec_rows[10], grad_head)
    grad_dense = gelu_backward(dense_out, grad_act).astype(low)
    dense_bias_grad = jnp.sum(grad_dense.astype(jnp.float32), axis=0)
    dense_grad = jnp.einsum("rd,re->de", picked_b, grad_dense, preferred_element_type=jnp.float32)
    grad_picked = jnp.einsum("re,de->rd", grad_dense, dense_w, preferred_element_type=jnp.float32)
    seq_picked = comm_all_gather(grad_picked, "c")
    place = (
        seq_pos[None, :]
        == c_at * own_len + lax.broadcasted_iota(jnp.int32, (own_len, slots), 0)
    ).astype(jnp.float32)
    grad_top = jnp.dot(place, seq_picked, precision=highest)

    cls_row = hidden2_seq[0:1]
    pooler_w = side_full[:D]
    pooled = jnp.tanh(jnp.dot(cls_row, pooler_w, preferred_element_type=jnp.float32) + vec_rows[11])
    classes = vec_rows[14:16]
    nsp_logp = jax.nn.log_softmax(jnp.dot(pooled, classes.T, precision=highest), axis=-1)
    own_nsp = lax.dynamic_slice_in_dim(nsp_labels, y_at, 1, 0)
    pick_nsp = own_nsp[:, None] == lax.broadcasted_iota(jnp.int32, (1, 2), 1)
    nsp_sum = -jnp.sum(jnp.where(pick_nsp, nsp_logp, 0.0)) * first_core
    grad_nsp = (jnp.exp(nsp_logp) - pick_nsp.astype(jnp.float32)) / total_seqs * first_core
    class_grad = grad_nsp[0][:, None] * pooled
    grad_pre = jnp.dot(grad_nsp, classes, precision=highest) * (1.0 - pooled * pooled)
    pooler_bias_grad = grad_pre[0]
    pooler_grad = cls_row.astype(jnp.float32).T * grad_pre
    grad_cls = jnp.dot(grad_pre, pooler_w.astype(jnp.float32).T, precision=highest)
    first_row = lax.broadcasted_iota(jnp.int32, (own_len, 1), 0) == 0
    grad_top = grad_top + jnp.where(first_row, grad_cls, 0.0)

    grad_r2, grad_g2, grad_s2 = norm_backward(resid2, vec_rows[6], vec_rows[7], grad_top)
    ffn_grad_b = grad_r2.astype(low)
    out_bias_two = jnp.sum(ffn_grad_b.astype(jnp.float32), axis=0)
    ff_out_grad = jnp.einsum("td,mtf->mdf", ffn_grad_b, active, preferred_element_type=jnp.float32)
    grad_active = jnp.einsum("td,mdf->mtf", ffn_grad_b, ff_out, preferred_element_type=jnp.float32)
    grad_up = gelu_backward(upward, grad_active).astype(low)
    ff_bias_grad = jnp.sum(grad_up.astype(jnp.float32), axis=1)
    ff_in_grad = jnp.einsum("td,mtf->mdf", hidden1_b, grad_up, preferred_element_type=jnp.float32)
    hidden1_part = jnp.einsum("mtf,mdf->td", grad_up, ff_in, preferred_element_type=jnp.float32)
    ff_grad = jnp.concatenate([ff_in_grad, ff_out_grad], axis=2).astype(low)
    ff_red = comm_scatter_sum(ff_grad.reshape(mp_size * D, 2 * ff_cols), mp_first)
    grad_h1 = grad_r2 + hidden1_part
    grad_r1, grad_g1, grad_s1 = norm_backward(resid1, vec_rows[3], vec_rows[4], grad_h1)
    attn_grad_b = grad_r1.astype(low)
    out_bias_one = jnp.sum(attn_grad_b.astype(jnp.float32), axis=0)
    mixed_blocks = mixed.reshape(own_len, mp_size, attn_cols)
    attn_grad_out = jnp.einsum(
        "td,tme->mde", attn_grad_b, mixed_blocks, preferred_element_type=jnp.float32
    )
    grad_mixed = jnp.einsum(
        "td,mde->tme", attn_grad_b, out_blocks, preferred_element_type=jnp.float32
    )
    grad_mixed = grad_mixed.astype(low).reshape(own_len, D)
    grad_q, part_k, part_v = attention_backward(
        queries, key_rows, value_rows, log_norm, grad_mixed
    )
    part_kv = jnp.concatenate([part_k, part_v], axis=1)
    grad_kv = comm_scatter_sum(part_kv, "c").astype(low)
    grad_packed = jnp.stack(
        [
            grad_q.astype(low).reshape(own_len, mp_size, attn_cols),
            grad_kv[:, :D].reshape(own_len, mp_size, attn_cols),
            grad_kv[:, D:].reshape(own_len, mp_size, attn_cols),
        ],
        axis=2,
    ).reshape(own_len, mp_size, 3 * attn_cols)
    attn_grad_in = jnp.einsum(
        "td,tme->mde", hidden0_b, grad_packed, preferred_element_type=jnp.float32
    )
    packed_sums = jnp.sum(grad_packed.astype(jnp.float32), axis=0).reshape(mp_size, 3, attn_cols)
    hidden0_part = jnp.einsum(
        "tme,mde->td", grad_packed, qkv_blocks, preferred_element_type=jnp.float32
    )
    attn_grad = jnp.concatenate([attn_grad_in, attn_grad_out], axis=2).astype(low)
    attn_red = comm_scatter_sum(attn_grad.reshape(mp_size * D, 4 * attn_cols), mp_first)
    grad_h0 = grad_r1 + hidden0_part
    grad_x0, grad_g0, grad_s0 = norm_backward(embedded, vec_rows[0], vec_rows[1], grad_h0)

    all_x0 = comm_all_gather(grad_x0.astype(low), "z")
    onehot = (
        jnp.where(inside, at, -1)[None, :]
        == lax.broadcasted_iota(jnp.int32, (word_plane.shape[0], flat_ids.shape[0]), 0)
    ).astype(low)
    word_grad = jnp.einsum("rv,rd->vd", grad_logits, head_b, preferred_element_type=jnp.float32)
    word_grad = word_grad + jnp.dot(onehot, all_x0, preferred_element_type=jnp.float32)
    word_red = comm_scatter_sum(word_grad.astype(low), plane).astype(jnp.float32)

    position_grad = lax.dynamic_update_slice_in_dim(
        jnp.zeros((length, D), low), grad_x0.astype(low), c_at * own_len, 0
    )
    side_grad = jnp.concatenate([pooler_grad.astype(low), dense_grad.astype(low), position_grad], axis=0)
    side_quarter = comm_scatter_sum(side_grad, every)
    side_red = comm_all_gather(side_quarter, ("y", "c")).astype(jnp.float32)
    type_zero = jnp.sum(jnp.where(own_types[:, None] == 0, grad_x0, 0.0), axis=0)
    type_one = jnp.sum(jnp.where(own_types[:, None] == 1, grad_x0, 0.0), axis=0)
    vec_grad = jnp.stack(
        [
            grad_g0, grad_s0, out_bias_one, grad_g1, grad_s1, out_bias_two, grad_g2, grad_s2,
            dense_bias_grad, grad_g9, grad_s9, pooler_bias_grad, type_zero, type_one,
            class_grad[0], class_grad[1],
        ],
        axis=0,
    )
    split_grad = jnp.concatenate(
        [
            packed_sums[:, 0:1],
            packed_sums[:, 2:3],
            ff_bias_grad.reshape(mp_size, attn_cols, 4).transpose(0, 2, 1),
        ],
        axis=1,
    )
    small = lax.psum(jnp.concatenate([vec_grad.reshape(-1), split_grad.reshape(-1)]), every)
    vec_all = small[: vec_grad.size].reshape(vec_grad.shape)
    split_all = small[vec_grad.size :].reshape(split_grad.shape)
    vec_cols = vectors.shape[1]
    vec_red = lax.dynamic_slice_in_dim(vec_all, dp_rank * vec_cols, vec_cols, 1)
    split_red = lax.dynamic_index_in_dim(split_all, mp_rank, 0, False)
    decoder_own = comm_scatter_sum(decoder_part, plane)
    decoder_red = comm_all_gather(decoder_own, ("z", "x"))
    word_f, attn_f, ff_f = (
        word_red,
        attn_red.astype(jnp.float32).reshape(attn_weight.shape),
        ff_red.astype(jnp.float32).reshape(ff_weight.shape),
    )
    own_square = (
        jnp.sum(word_f * word_f)
        + jnp.sum(attn_f * attn_f)
        + jnp.sum(ff_f * ff_f)
        + jnp.sum(side_red * side_red) / mp_size
        + jnp.sum(vec_red * vec_red) / mp_size
        + (jnp.sum(split_red * split_red) + jnp.sum(decoder_red * decoder_red)) / dp_size
    )
    loss_part = mlm_sum / total_count / z_size + nsp_sum / total_seqs
    grad_square, total_loss = lax.psum((own_square, loss_part), every)
    grad_norm = jnp.sqrt(grad_square)
    clip_scale = max_norm / jnp.maximum(grad_norm, max_norm)
    return (
        total_loss,
        grad_norm,
        *adam_step(word_table, word_m, word_v, word_f, clip_scale, True),
        *adam_step(attn_weight, attn_m, attn_v, attn_f, clip_scale, True),
        *adam_step(ff_weight, ff_m, ff_v, ff_f, clip_scale, True),
        *adam_step(side_weight, side_m, side_v, side_red, clip_scale, True),
        *adam_step(vectors, vec_m, vec_v, vec_red, clip_scale, False),
        *adam_step(split_bias, split_m, split_v, split_red, clip_scale, False),
        *adam_step(decoder_bias, decoder_m, decoder_v, decoder_red, clip_scale, False),
    )


def solution(mesh):
    dp_size, mp_size = mesh.shape["dp"], mesh.shape["mp"]
    x_size = 2 if dp_size % 2 == 0 else 1
    c_size = 2 if mp_size % 2 == 0 else 1
    sizes = (dp_size // x_size, x_size, mp_size // c_size, c_size)
    fine = Mesh(mesh.devices.reshape(sizes), ("z", "x", "y", "c"))
    dp, mp = ("z", "x"), ("y", "c")
    word = P(("y", "c", "z", "x"), None)
    cube = P(dp, None, mp)
    kinds = (
        [P(dp, None)] * 5
        + [P(dp)]
        + [word] * 3
        + [cube] * 6
        + [P(dp, None)] * 3
        + [P(None, dp)] * 3
        + [P(None, mp)] * 3
        + [P(mp)] * 3
    )
    return jax.shard_map(
        functools.partial(step, sizes),
        mesh=fine,
        in_specs=tuple(kinds),
        out_specs=(P(), P(), *kinds[6:]),
        check_vma=False,
    )
```

time: 2120 us -> 1390 us (0.66)
  waiting for transfers between devices: 1400 us -> 679 us
  other arithmetic: 284 us -> 133 us
  blocking collectives: 144 us -> 214 us
  matrix products: 172 us -> 219 us
  local copies, waits for them, and re-layouts: 83.9 us -> 110 us
    psum x6 -> x1, waiting for transfers between devices: 498 us -> 123 us  [step(): lax.psum(jnp.concatenate([vec_grad.reshape(-1), split_grad.reshape(-1)]),...]
    reduce_scatter x3 -> x6, waiting for transfers between devices: 618 us -> 297 us  [comm_scatter_sum(): return lax.psum_scatter(value, axes, scatter_dimension=0, tiled=True)]
    all_gather x4 -> x7, waiting for transfers between devices: 272 us -> 157 us  [comm_all_gather(): return lax.all_gather(value, axes, axis=0, tiled=True)]
    scatter-add x2 -> x0, other arithmetic: 99 us -> none  [the longest x1 68.8 us: body(): grad_top = jnp.zeros_like(hidden2).at[batch_index, mask_pos].add(grad_pic...]
    unnamed x17 -> x16, waiting for transfers between devices: 10.8 us -> 103 us
    unnamed x0 -> x2, blocking collectives: none -> 62.8 us
    dot_general x30 -> x29, matrix products: 172 us -> 218 us  [the longest x1 34.7 us: step(): jnp.dot(onehot, all_x0, preferred_element_type=jnp.float32)]
    all_gather x4 -> x7, blocking collectives: 46.7 us -> 90.5 us  [comm_all_gather(): return lax.all_gather(value, axes, axis=0, tiled=True)]
  transfers between devices with their start and end apart: 15 -> 15, of which waited for: 13 -> 13; matrix products, arithmetic and copies ran while one was open for 7% -> 18% of each run, Pallas kernels for 0% -> 0%
where the time goes in v1:
time: 1390 us; the launch traced here: 1380 us
  waiting for transfers between devices  679 us (49%)
  matrix products  219 us (16%)
  blocking collectives  214 us (15%)
  other arithmetic  133 us (10%)
  local copies, waits for them, and re-layouts  110 us (8%)
  between operations  26.8 us (2%)
    reduce_scatter x6, waiting for transfers between devices, comm_scatter_sum(): return lax.psum_scatter(value, axes, scatter_dimension=0, tiled=True)  297 us
    all_gather x7, waiting for transfers between devices, comm_all_gather(): return lax.all_gather(value, axes, axis=0, tiled=True)  157 us
    psum x1, waiting for transfers between devices, step(): lax.psum(jnp.concatenate([vec_grad.reshape(-1), split_grad.reshape(-1)]),...  123 us
    unnamed x16, waiting for transfers between devices  103 us
    all_gather x7, blocking collectives, comm_all_gather(): return lax.all_gather(value, axes, axis=0, tiled=True)  90.5 us
    unnamed x2, blocking collectives  62.8 us
    psum x1, blocking collectives, step(): grad_square, total_loss = lax.psum((own_square, loss_part), every)  39.6 us
    dot_general x1, matrix products, step(): jnp.dot(onehot, all_x0, preferred_element_type=jnp.float32)  34.7 us
  transfers between devices with their start and end apart: 15, of which 13 were waited for; matrix products, arithmetic and copies ran while one was open for 18% of the time, Pallas kernels for 0%

profile of v1, /device:TPU:0, one launch (start us, length us, event | category | flops | bytes accessed | tf_op | source)
XLA Modules:
  0.0 1381.4 jit_solution(4666855828200933366)
XLA Ops:
  13.8 14.8 %all-gather.5 = s32[4,1,768]{2,1,0:T(1,128)S(1)} all-gather(s32[1,1,768]{2,1,0:T(1,128)S(1)} %reshape.886), channel_id=2, replica_groups=mesh['z'=4,'x'=2,'y'=2,'c'=2] {'z'}, dimensions={0}, use_global_device_ids=true | all-gather | bytes 15360 | tf_op jit(solution)/shard_map/all_gather | solution.py:57
  29.2 52.7 %all-gather.15.cloned.1.call-done = bf16[7680,768]{1,0:T(8,128)(2,1)} async-done(((bf16[960,768]{1,0:T(8,128)(2,1)}), bf16[7680,768]{1,0:T(8,128)(2,1)}) %all-gather.15.cloned.1.call-update) | async-done | bytes 11796496 | tf_op jit(solution)/shard_map/all_gather | solution.py:57
  81.9 14.3 %gather_fusion = bf16[2048,768]{1,0:T(8,128)(2,1)S(1)} fusion(bf16[7680,768]{1,0:T(8,128)(2,1)} %all-gather.15.cloned.1.call-done, s32[2048]{0:T(1024)S(1)} %broadcast_clamp_fusion), kind=kCustom, calls=%fused_computation | custom fusion | bytes 6299648 | tf_op jit(solution)/shard_map/gather | solution.py:193
  100.1 30.8 %all-gather.1 = bf16[128,96]{1,0:T(8,128)(2,1)S(1)} all-gather(bf16[16,96]{1,0:T(8,128)(2,1)S(1)} %convert_element_type.198), channel_id=3, replica_groups=mesh['z'=4,'x'=2,'y'=2,'c'=2] {'z','x'}, dimensions={0}, use_global_device_ids=true | all-gather | bytes 27648 | tf_op jit(solution)/shard_map/all_gather | solution.py:57
  133.3 5.3 all-gather.2
  140.2 6.3 all-gather.17.cloned.1.call-done
  146.5 61.4 %reduce-scatter.10.cloned.1.call-done = bf16[512,768]{1,0:T(8,128)(2,1)} async-done(((bf16[2048,768]{1,0:T(8,128)(2,1)}), bf16[512,768]{1,0:T(8,128)(2,1)}) %reduce-scatter.10.cloned.1.call-update) | async-done | bytes 786448 | tf_op jit(solution)/shard_map/reduce_scatter | solution.py:61
  211.8 63.1 %all-gather.19.cloned.1.call-done = bf16[3072,768]{1,0:T(8,128)(2,1)} async-done(((bf16[96,768]{1,0:T(8,128)(2,1)}), bf16[3072,768]{1,0:T(8,128)(2,1)}) %all-gather.19.cloned.1.call-update) | async-done | bytes 4718608 | tf_op jit(solution)/shard_map/all_gather | solution.py:57
  274.9 4.9 fusion.40
  302.0 5.2 copy.120
  307.2 3.8 reshape_reshape_squeeze.8
  311.0 10.3 multiply_reduce_fusion.1
  321.3 11.3 fusion.2
  332.6 10.9 fusion.59
  347.8 31.3 %all-gather.21.cloned.1.call-done = bf16[3072,1536]{1,0:T(8,128)(2,1)} async-done(((bf16[96,1536]{1,0:T(8,128)(2,1)}), bf16[3072,1536]{1,0:T(8,128)(2,1)}) %all-gather.21.cloned.1.call-update) | async-done | bytes 9437200 | tf_op jit(solution)/shard_map/all_gather | solution.py:57
  379.1 20.6 %fusion.18 = (bf16[4,512,768]{2,1,0:T(8,128)(2,1)S(1)}, f32[4,512,768]{2,1,0:T(8,128)}, f32[512,4,768]{2,0,1:T(8,128)}) fusion(f32[4,768]{1,0:T(4,128)S(1)} %copy-done.101, bf16[4,768,1536]{2,1,0:T(8,128)(2,1)} %bitcast.377, f32[512,768]{1,0:T(8,128)S(1)} %get-tuple-element.130, f32[768]{0:T(1024)S(1)} %copy-done.124, f32[768]{0:T(1024)S(1)} %copy-done.93, ...), kind=kOutput, calls=%fused_computation.43 | convolution fusion | flops 2521694208 | bytes 22042624 | tf_op jit(solution)/shard_map/td,mdf->mtf/dot_general | solution.py:226
  399.8 5.3 fusion.170
  407.5 20.9 %psum.28 = f32[]{:T(128)} all-reduce(f32[]{:T(128)} %convert_reduce_fusion.6), channel_id=1, replica_groups=mesh['z'=4,'x'=2,'y'=2,'c'=2] {'z','x'}, use_global_device_ids=true, to_apply=%region_19.20 | all-reduce | flops 1 | bytes 8 | tf_op jit(solution)/shard_map/psum | solution.py:156
  439.2 16.7 %all_gather.54 = bf16[512,768]{1,0:T(8,128)(2,1)} all-gather(bf16[128,768]{1,0:T(8,128)(2,1)S(1)} %add_convert_fusion.7), channel_id=1, replica_groups=mesh['z'=4,'x'=2,'y'=2,'c'=2] {'z'}, dimensions={0}, use_global_device_ids=true | all-gather | bytes 983040 | tf_op jit(solution)/shard_map/all_gather | solution.py:57
  455.9 14.7 %add_reduce_fusion = (f32[512]{0:T(512)}, f32[512,7680]{1,0:T(8,128)}) fusion(f32[7680]{0:T(1024)} %add.673, bf16[512,768]{1,0:T(8,128)(2,1)} %all_gather.54, bf16[7680,768]{1,0:T(8,128)(2,1)} %all-gather.15.cloned.1.call-done), kind=kOutput, calls=%fused_computation.19 | convolution fusion | flops 6047661568 | bytes 28344320 | tf_op jit(solution)/shard_map/rd,vd->rv/dot_general | solution.py:242
  470.6 9.9 exponential_reduce_fusion
  482.1 13.3 all-gather.6
  496.7 8.1 convert_reduce_fusion
  508.0 7.4 fusion.175
  540.2 9.0 reduce-scatter.12.cloned.1.call-done
  564.3 9.1 convert_reduce_fusion.1
  579.7 20.2 %multiply_reduce_fusion = (f32[12,512]{1,0:T(8,128)S(1)}, f32[12,512,1024]{2,1,0:T(8,128)}) fusion(f32[12,512,1024]{2,1,0:T(8,128)} %get-tuple-element.128, f32[12,512]{1,0:T(8,128)S(1)} %copy-done.36, bf16[512,12,64]{0,2,1:T(8,128)(2,1)S(1)} %bitcast.330, bf16[1024,12,64]{0,2,1:T(8,128)(2,1)S(1)} %copy-done.13), kind=kOutput, calls=%fused_computation.6 | convolution fusion | flops 830466048 | bytes 52740096 | tf_op jit(solution)/shard_map/qhe,khe->hqk/dot_general | solution.py:93
  599.9 10.2 fusion.4
  610.1 17.5 %multiply_convert_fusion = bf16[12,512,1024]{2,1,0:T(8,128)(2,1)S(1)} fusion(f32[12,512,1024]{2,1,0:T(8,128)} %get-tuple-element.142, f32[12,512,1024]{2,1,0:T(8,128)} %get-tuple-element.128, f32[12,512]{1,0:T(8,128)S(1)} %get-tuple-element.141, f32[12,512]{1,0:T(8,128)S(1)} %copy-done.36), kind=kLoop, calls=%fused_computation.5 | loop fusion | flops 31457280 | bytes 62963712 | tf_op jit(solution)/shard_map/convert_element_type | solution.py:98
  636.9 9.5 multiply_convert_fusion.3
  654.3 6.0 multiply_reduce_fusion.4
  665.0 5.1 convolution_convert_fusion
  673.4 4.2 pad_maximum_fusion
  717.8 6.7 copy.141
  725.6 14.4 %fusion.174 = f32[7680,768]{1,0:T(8,128)} fusion(bf16[512,7680]{1,0:T(8,128)(2,1)} %copy-done.9, bf16[512,768]{1,0:T(8,128)(2,1)S(1)} %copy-done.31), kind=kOutput, calls=%fused_computation.371 | convolution fusion | flops 6039797760 | bytes 32243712 | tf_op jit(solution)/shard_map/rv,rd->vd/dot_general | solution.py:347
  740.1 34.7 %add_convert_fusion = bf16[7680,768]{1,0:T(8,128)(2,1)} fusion(f32[7680,768]{1,0:T(8,128)} %fusion.174, bf16[2048,768]{1,0:T(8,128)(2,1)} %all-gather.25.cloned.1.call-done, s32[2048]{0:T(1024)S(1)} %fusion.101), kind=kOutput, calls=%fused_computation.10 | convolution fusion | flops 24186716160 | bytes 38543360 | tf_op jit(solution)/shard_map/dot_general | solution.py:348
  779.8 26.4 %all-reduce.1 = f32[7680]{0:T(1024)S(1)} all-reduce(f32[7680]{0:T(1024)S(1)} %copy-done.42), channel_id=14, replica_groups=mesh['z'=4,'x'=2,'y'=2,'c'=2] {'x','y','c'}, use_global_device_ids=true, to_apply=%region_62.63.clone | all-reduce | flops 7680 | bytes 61440
  806.4 36.4 %all-reduce = f32[7680]{0:T(1024)S(1)} all-reduce(f32[7680]{0:T(1024)S(1)} %dynamic-slice_dynamic-update-slice_fusion), channel_id=1, replica_groups=mesh['z'=4,'x'=2,'y'=2,'c'=2] {'z','x'}, use_global_device_ids=true, to_apply=%add | all-reduce | flops 7680 | bytes 61440
  843.4 27.6 %reduce-scatter.18.cloned.1.call-done = bf16[96,1536]{1,0:T(8,128)(2,1)} async-done(((bf16[3072,1536]{1,0:T(8,128)(2,1)}), bf16[96,1536]{1,0:T(8,128)(2,1)}) %reduce-scatter.18.cloned.1.call-update) | async-done | bytes 294928 | tf_op jit(solution)/shard_map/reduce_scatter | solution.py:61
  872.8 122.9 %all-reduce.5.cloned.1.call-done = f32[16896]{0:T(1024)} async-done(((f32[16896]{0:T(1024)}), f32[16896]{0:T(1024)}) %all-reduce.5.cloned.1.call-update) | async-done | bytes 67600 | tf_op jit(solution)/shard_map/psum | solution.py:375
  1000.6 107.8 %reduce-scatter.20.cloned.1.call-done = bf16[80,768]{1,0:T(8,128)(2,1)} async-done(((bf16[2560,768]{1,0:T(8,128)(2,1)}), bf16[80,768]{1,0:T(8,128)(2,1)}) %reduce-scatter.20.cloned.1.call-update) | async-done | bytes 122896 | tf_op jit(solution)/shard_map/reduce_scatter | solution.py:61
  1108.4 7.2 all_gather.58
  1117.2 103.0 %reduce-scatter.22.cloned.1.call-done = bf16[96,768]{1,0:T(8,128)(2,1)} async-done(((bf16[3072,768]{1,0:T(8,128)(2,1)}), bf16[96,768]{1,0:T(8,128)(2,1)}) %reduce-scatter.22.cloned.1.call-update) | async-done | bytes 147472
  1222.0 88.9 %reduce-scatter.16.cloned.1.call-done = bf16[960,768]{1,0:T(8,128)(2,1)} async-done(((bf16[7680,768]{1,0:T(8,128)(2,1)}), bf16[960,768]{1,0:T(8,128)(2,1)}) %reduce-scatter.16.cloned.1.call-update) | async-done | bytes 1474576 | tf_op jit(solution)/shard_map/reduce_scatter | solution.py:61
  1315.6 39.6 %all-reduce.2 = (f32[]{:T(128)}, f32[]{:T(128)}) all-reduce(f32[]{:T(128)S(6)} %add.683, f32[]{:T(128)S(6)} %add.703), channel_id=1, replica_groups=mesh['z'=4,'x'=2,'y'=2,'c'=2] {'z','x','y','c'}, use_global_device_ids=true, to_apply=%region_23.24 | all-reduce | flops 2 | bytes 16 | tf_op jit(solution)/shard_map/psum | solution.py:397
  1358.7 4.0 multiply_subtract_fusion.1
  1362.7 4.7 multiply_subtract_fusion.2
  1369.1 4.2 multiply_subtract_fusion
  (546 shorter events, 191.8 us)
Async XLA Ops:
  7.2 74.7 %all-gather.15.cloned.1.call-start = ((), (), s32[]{:S(2)}) async-start(), calls=%async_computation.7 | async-start | bytes 13271040 | tf_op jit(solution)/shard_map/all_gather | solution.py:57
  10.4 136.2 %all-gather.17.cloned.1.call-start = ((), (), s32[]{:S(2)}) async-start(), calls=%async_computation.9 | async-start | bytes 4055040 | tf_op jit(solution)/shard_map/all_gather | solution.py:57
  12.1 195.9 %reduce-scatter.10.cloned.1.call-start = ((), (), s32[]{:S(2)}) async-start(), calls=%async_computation.8 | async-start | bytes 3932160 | tf_op jit(solution)/shard_map/reduce_scatter | solution.py:61
  28.7 67.6 %copy-start.80 = (pred[1,4,4,128]{3,1,2,0:T(4,128)(4,1)}, pred[1,4,4,128]{3,1,2,0:T(4,128)(4,1)S(1)}, u32[]{:S(2)}) copy-start(pred[1,4,4,128]{3,1,2,0:T(4,128)(4,1)S(1)} %copy.152) | copy-start | bytes 6148
  98.1 34.3 %copy-start.61 = (f32[6,192]{1,0:T(8,128)S(1)}, f32[6,192]{1,0:T(8,128)}, u32[]{:S(2)}) copy-start(f32[6,192]{1,0:T(8,128)} %param.48) | copy-start | bytes 13828
  98.2 176.8 %all-gather.19.cloned.1.call-start = ((), (), s32[]{:S(2)}) async-start(), calls=%async_computation.10 | async-start | bytes 4866048 | tf_op jit(solution)/shard_map/all_gather | solution.py:57
  100.1 192.9 %all-gather.27.cloned.1.call-start = ((), (), s32[]{:S(2)}) async-start(), calls=%async_computation.20 | async-start | bytes 4718592 | tf_op jit(solution)/shard_map/all_gather | solution.py:57
  132.2 211.3 %copy-start.49 = (f32[768]{0:T(1024)}, f32[768]{0:T(1024)S(1)}, u32[]{:S(2)}) copy-start(f32[768]{0:T(1024)S(1)} %squeeze.31) | copy-start | bytes 9220
  132.3 147.6 %copy-start.51 = (f32[768]{0:T(1024)}, f32[768]{0:T(1024)S(1)}, u32[]{:S(2)}) copy-start(f32[768]{0:T(1024)S(1)} %squeeze.32) | copy-start | bytes 9220
  132.4 147.5 %copy-start.82 = (f32[768]{0:T(1024)}, f32[768]{0:T(1024)S(1)}, u32[]{:S(2)}) copy-start(f32[768]{0:T(1024)S(1)} %mul.817) | copy-start | bytes 9220
  132.5 147.4 %copy-start.121 = (f32[768]{0:T(1024)}, f32[768]{0:T(1024)S(1)}, u32[]{:S(2)}) copy-start(f32[768]{0:T(1024)S(1)} %add.635) | copy-start | bytes 9220
  140.2 139.7 %copy-start.95 = (pred[512]{0:T(512)(128)(4,1)}, pred[512]{0:T(512)(128)(4,1)S(1)}, u32[]{:S(2)}) copy-start(pred[512]{0:T(512)(128)(4,1)S(1)} %get-tuple-element.45) | copy-start | bytes 1540
  208.0 67.0 %copy-start.10 = (bf16[512,768]{1,0:T(8,128)(2,1)S(1)}, bf16[512,768]{1,0:T(8,128)(2,1)}, u32[]{:S(2)}) copy-start(bf16[512,768]{1,0:T(8,128)(2,1)} %reduce-scatter.10.cloned.1.call-done) | copy-start | bytes 2359300
  209.8 70.1 %copy-start.65 = (f32[512]{0:T(512)}, f32[512]{0:T(512)S(1)}, u32[]{:S(2)}) copy-start(f32[512]{0:T(512)S(1)} %broadcast_multiply_fusion.3) | copy-start | bytes 6148
  211.8 68.2 %copy-start.74 = (f32[512]{0:T(512)}, f32[512]{0:T(512)S(1)}, u32[]{:S(2)}) copy-start(f32[512]{0:T(512)S(1)} %multiply_reduce_fusion.10) | copy-start | bytes 6148
  211.8 68.1 %copy-start.104 = (f32[512]{0:T(512)}, f32[512]{0:T(512)S(1)}, u32[]{:S(2)}) copy-start(f32[512]{0:T(512)S(1)} %fusion.126) | copy-start | bytes 6148
  280.3 30.7 %copy-start.4 = (f32[512,4,1,192]{0,3,2,1:T(8,128)}, f32[512,4,1,192]{0,3,2,1:T(8,128)S(1)}, u32[]{:S(2)}) copy-start(f32[512,4,1,192]{0,3,2,1:T(8,128)S(1)} %get-tuple-element.94) | copy-start | bytes 4718596
  282.4 96.7 %all-gather.21.cloned.1.call-start = ((), (), s32[]{:S(2)}) async-start(), calls=%async_computation.11 | async-start | bytes 9732096 | tf_op jit(solution)/shard_map/all_gather | solution.py:57
  284.5 147.5 %all-gather.23.cloned.1.call-start = ((), (), s32[]{:S(2)}) async-start(), calls=%async_computation.12 | async-start | bytes 2359296 | tf_op jit(solution)/shard_map/all_gather | solution.py:57
  284.8 26.2 %copy-start.43 = (f32[12,64]{1,0:T(8,128)}, f32[12,64]{1,0:T(8,128)S(1)}, u32[]{:S(2)}) copy-start(f32[12,64]{1,0:T(8,128)S(1)} %add.642) | copy-start | bytes 9220
  343.6 35.5 %copy-start.93 = (f32[768]{0:T(1024)S(1)}, f32[768]{0:T(1024)}, u32[]{:S(2)}) copy-start(f32[768]{0:T(1024)} %mul.825) | copy-start | bytes 9220
  343.6 35.4 %copy-start.101 = (f32[4,768]{1,0:T(4,128)S(1)}, f32[4,768]{1,0:T(4,128)}, u32[]{:S(2)}) copy-start(f32[4,768]{1,0:T(4,128)} %add.653) | copy-start | bytes 36868
  343.7 35.4 %copy-start.124 = (f32[768]{0:T(1024)S(1)}, f32[768]{0:T(1024)}, u32[]{:S(2)}) copy-start(f32[768]{0:T(1024)} %add.650) | copy-start | bytes 9220
  347.5 52.3 %copy-start.14 = (f32[512,768]{1,0:T(8,128)}, f32[512,768]{1,0:T(8,128)S(1)}, u32[]{:S(2)}) copy-start(f32[512,768]{1,0:T(8,128)S(1)} %get-tuple-element.130) | copy-start | bytes 4718596
  347.5 52.3 %copy-start.69 = (f32[512]{0:T(512)}, f32[512]{0:T(512)S(1)}, u32[]{:S(2)}) copy-start(f32[512]{0:T(512)S(1)} %broadcast_multiply_fusion.2) | copy-start | bytes 6148
  347.8 52.0 %copy-start.76 = (f32[512]{0:T(512)}, f32[512]{0:T(512)S(1)}, u32[]{:S(2)}) copy-start(f32[512]{0:T(512)S(1)} %multiply_reduce_fusion.9) | copy-start | bytes 6148
  347.8 52.0 %copy-start.108 = (f32[512]{0:T(512)}, f32[512]{0:T(512)S(1)}, u32[]{:S(2)}) copy-start(f32[512]{0:T(512)S(1)} %fusion.127) | copy-start | bytes 6148
  406.8 142.3 %reduce-scatter.12.cloned.1.call-start = ((), (), s32[]{:S(2)}) async-start(), calls=%async_computation.13 | async-start | bytes 1966080 | tf_op jit(solution)/shard_map/reduce_scatter | solution.py:61
  470.6 37.3 %slice-start = ((s8[11796480]{0:T(1024)(128)(4,1)}), s8[4194304]{0:T(1024)(128)(4,1)S(1)}, s32[]{:S(2)}) async-start(s8[11796480]{0:T(1024)(128)(4,1)} %bitcast.323), calls=%async_computation.22 | async-start | bytes 8388608
  470.6 37.3 %slice-start.1 = ((s8[11796480]{0:T(1024)(128)(4,1)}), s8[4194304]{0:T(1024)(128)(4,1)S(1)}, s32[]{:S(2)}) async-start(s8[11796480]{0:T(1024)(128)(4,1)} %bitcast.323), calls=%async_computation.23 | async-start | bytes 8388608
  515.4 133.0 %reduce-scatter.14.cloned.1.call-start = ((), (), s32[]{:S(2)}) async-start(), calls=%async_computation.14 | async-start | bytes 9437184 | tf_op jit(solution)/shard_map/reduce_scatter | solution.py:61
  523.1 28.4 %copy-start.118 = (f32[128]{0:T(128)S(1)}, f32[128]{0:T(128)}, u32[]{:S(2)}) copy-start(f32[128]{0:T(128)} %copy-done.117) | copy-start | bytes 1540
  635.6 104.5 %all-gather.25.cloned.1.call-start = ((), (), s32[]{:S(2)}) async-start(), calls=%async_computation.15 | async-start | bytes 3932160 | tf_op jit(solution)/shard_map/all_gather | solution.py:57
  664.9 206.1 %reduce-scatter.18.cloned.1.call-start = ((), (), s32[]{:S(2)}) async-start(), calls=%async_computation.17 | async-start | bytes 9732096 | tf_op jit(solution)/shard_map/reduce_scatter | solution.py:61
  677.6 318.1 %all-reduce.5.cloned.1.call-start = ((), (), s32[]{:S(2)}) async-start(), calls=%async_computation.19 | async-start | bytes 139264 | tf_op jit(solution)/shard_map/psum | solution.py:375
  705.3 403.1 %reduce-scatter.20.cloned.1.call-start = ((), (), s32[]{:S(2)}) async-start(), calls=%async_computation.18 | async-start | bytes 4055040 | tf_op jit(solution)/shard_map/reduce_scatter | solution.py:61
  708.8 511.4 %reduce-scatter.22.cloned.1.call-start = ((), (), s32[]{:S(2)}) async-start(), calls=%async_computation.21 | async-start | bytes 4866048
  724.5 586.3 %reduce-scatter.16.cloned.1.call-start = ((), (), s32[]{:S(2)}) async-start(), calls=%async_computation.16 | async-start | bytes 13271040 | tf_op jit(solution)/shard_map/reduce_scatter | solution.py:61
  871.0 484.9 %copy-start.29 = (bf16[96,1536]{1,0:T(8,128)(2,1)S(1)}, bf16[96,1536]{1,0:T(8,128)(2,1)}, u32[]{:S(2)}) copy-start(bf16[96,1536]{1,0:T(8,128)(2,1)} %reduce-scatter.18.cloned.1.call-done) | copy-start | bytes 884740
  1115.6 241.0 %copy-start.54 = (f32[7680]{0:T(1024)S(1)}, f32[7680]{0:T(1024)}, u32[]{:S(2)}) copy-start(f32[7680]{0:T(1024)} %param.51) | copy-start | bytes 92164
  1115.6 241.0 %copy-start.59 = (f32[7680]{0:T(1024)S(1)}, f32[7680]{0:T(1024)}, u32[]{:S(2)}) copy-start(f32[7680]{0:T(1024)} %param.52) | copy-start | bytes 92164
  1115.6 241.0 %copy-start.60 = (f32[7680]{0:T(1024)S(1)}, f32[7680]{0:T(1024)}, u32[]{:S(2)}) copy-start(f32[7680]{0:T(1024)} %param.53) | copy-start | bytes 92164
  1116.4 240.8 %copy-start.62 = (f32[6,192]{1,0:T(8,128)S(1)}, f32[6,192]{1,0:T(8,128)}, u32[]{:S(2)}) copy-start(f32[6,192]{1,0:T(8,128)} %param.48) | copy-start | bytes 13828
  1116.4 240.8 %copy-start.111 = (f32[6,192]{1,0:T(8,128)S(1)}, f32[6,192]{1,0:T(8,128)}, u32[]{:S(2)}) copy-start(f32[6,192]{1,0:T(8,128)} %param.49) | copy-start | bytes 13828
  1116.5 240.8 %copy-start.112 = (f32[6,192]{1,0:T(8,128)S(1)}, f32[6,192]{1,0:T(8,128)}, u32[]{:S(2)}) copy-start(f32[6,192]{1,0:T(8,128)} %param.50) | copy-start | bytes 13828
  1116.5 241.5 %copy-start.64 = (f32[16,96]{1,0:T(8,128)S(1)}, f32[16,96]{1,0:T(8,128)}, u32[]{:S(2)}) copy-start(f32[16,96]{1,0:T(8,128)} %param.45) | copy-start | bytes 18436
  1116.5 241.5 %copy-start.113 = (f32[16,96]{1,0:T(8,128)S(1)}, f32[16,96]{1,0:T(8,128)}, u32[]{:S(2)}) copy-start(f32[16,96]{1,0:T(8,128)} %param.46) | copy-start | bytes 18436
  1116.5 241.5 %copy-start.114 = (f32[16,96]{1,0:T(8,128)S(1)}, f32[16,96]{1,0:T(8,128)}, u32[]{:S(2)}) copy-start(f32[16,96]{1,0:T(8,128)} %param.47) | copy-start | bytes 18436
  (122 other events, 862.8 us)
Sparse Core Ops, SparseCore 0:
  10.5 71.3 all-gather.14
  85.4 61.0 all-gather.16
  148.8 59.0 reduce-scatter.9
  211.4 63.5 all-gather.18
  282.5 10.4 all-gather.26
  296.4 82.6 all-gather.20
  406.9 8.3 all-gather.22
  515.5 33.5 reduce-scatter.11
  635.7 12.6 reduce-scatter.13
  665.0 64.7 all-gather.24
  735.7 135.2 reduce-scatter.17
  877.0 118.6 all-reduce.4
  1001.1 107.2 reduce-scatter.19
  1113.7 106.4 reduce-scatter.21
  1223.6 87.2 reduce-scatter.15

commit v2 on v1

--- a/solution.py
+++ b/solution.py
@@ -4,6 +4,8 @@
 import jax
 import jax.numpy as jnp
 from jax import lax
+from jax.experimental import pallas as pl
+from jax.experimental.pallas import tpu as pltpu
 from jax.sharding import Mesh, PartitionSpec as P
 
 D = 768
@@ -59,6 +61,274 @@
 
 def comm_scatter_sum(value, axes):
     return lax.psum_scatter(value, axes, scatter_dimension=0, tiled=True)
+
+
+MESH = pl.DeviceIdType.MESH
+BIG, FAST = pl.ANY, pltpu.VMEM
+
+
+class Links:
+    def __init__(self, sizes):
+        self.sizes = dict(zip(("z", "x", "y", "c"), sizes))
+        self.used = 0
+
+    def next_id(self):
+        self.used += 1
+        return self.used - 1
+
+    def count(self, axes):
+        return math.prod(self.sizes[a] for a in axes)
+
+    def place(self, axes):
+        at = 0
+        for a in axes:
+            at = at * self.sizes[a] + lax.axis_index(a)
+        return at
+
+    def target(self, axes, flat):
+        where = {}
+        for a in reversed(axes):
+            where[a] = lax.rem(flat, self.sizes[a])
+            flat = lax.div(flat, self.sizes[a])
+        return where
+
+    def greet(self, groups):
+        barrier = pltpu.get_barrier_semaphore()
+        total = 0
+        for axes in groups:
+            size, me = self.count(axes), self.place(axes)
+            for r in range(1, size):
+                pl.semaphore_signal(
+                    barrier,
+                    inc=1,
+                    device_id=self.target(axes, lax.rem(me + r, size)),
+                    device_id_type=MESH,
+                )
+            total += size - 1
+        pl.semaphore_wait(barrier, total)
+
+    def call(self, kernel, outs, spaces, out_spaces, scratch, values, wire, name):
+        result = pl.pallas_call(
+            kernel,
+            out_shape=outs,
+            in_specs=[pl.BlockSpec(memory_space=m) for m in spaces],
+            out_specs=[pl.BlockSpec(memory_space=m) for m in out_spaces],
+            scratch_shapes=scratch,
+            compiler_params=pltpu.CompilerParams(
+                collective_id=self.next_id(),
+                has_side_effects=True,
+                vmem_limit_bytes=40 * 2**20,
+            ),
+            cost_estimate=pl.CostEstimate(flops=0, bytes_accessed=wire, transcendentals=0),
+            name=name,
+        )(*values)
+        return result
+
+    def exchange(self, name, *moves):
+        outs, transfers = [], 0
+        for kind, axes, dim, _, value in moves:
+            size = self.count(axes)
+            shape = value.shape
+            if kind == "gather":
+                shape = (size, *shape)
+            elif kind == "swap":
+                shape = shape[:dim] + shape[dim + 1 :]
+            elif kind == "spread":
+                shape = (size - 1, *shape[1:])
+            outs.append(jax.ShapeDtypeStruct(shape, value.dtype))
+            transfers += size - 1
+        spaces = [m[3] for m in moves]
+        groups = list(dict.fromkeys(m[1] for m in moves))
+
+        def kernel(*refs):
+            ins, dests = refs[: len(moves)], refs[len(moves) : 2 * len(moves)]
+            sends, lands, own_sems = refs[2 * len(moves) :]
+            self.greet(groups)
+            started, slot = [], 0
+            for (kind, axes, dim, _, _), source, dest in zip(moves, ins, dests):
+                size, me = self.count(axes), self.place(axes)
+                for r in range(1, size):
+                    peer = lax.rem(me + r, size)
+                    if kind == "gather":
+                        src, dst = source, dest.at[me]
+                    elif kind == "swap":
+                        src, dst = source.at[(slice(None),) * dim + (peer,)], dest
+                    elif kind == "spread":
+                        src, dst = source.at[peer], dest.at[r - 1]
+                    else:
+                        src, dst = source, dest
+                    copy = pltpu.make_async_remote_copy(
+                        src_ref=src,
+                        dst_ref=dst,
+                        send_sem=sends.at[slot],
+                        recv_sem=lands.at[slot],
+                        device_id=self.target(axes, peer),
+                        device_id_type=MESH,
+                    )
+                    copy.start()
+                    started.append(copy)
+                    slot += 1
+            for number, ((kind, axes, _, _, _), source, dest) in enumerate(zip(moves, ins, dests)):
+                if kind == "gather":
+                    copy = pltpu.make_async_copy(
+                        source, dest.at[self.place(axes)], own_sems.at[number]
+                    )
+                    copy.start()
+                    started.append(copy)
+            for copy in started:
+                copy.wait()
+
+        return self.call(
+            kernel,
+            outs,
+            spaces,
+            spaces,
+            [
+                pltpu.SemaphoreType.DMA((transfers,)),
+                pltpu.SemaphoreType.DMA((transfers,)),
+                pltpu.SemaphoreType.DMA((len(moves),)),
+            ],
+            [m[4] for m in moves],
+            sum(2 * math.prod(o.shape) * o.dtype.itemsize for o in outs),
+            name,
+        )
+
+    def combine(self, name, value):
+        pairs = [a for a in ("c", "x", "y") if self.sizes[a] > 1]
+        depth = self.sizes["z"]
+        steps = len(pairs)
+
+        def kernel(x_ref, out_ref, sums, land, sends, lands):
+            self.greet([(a,) for a in pairs] + [("z",)])
+            me = lax.axis_index("z")
+            for i, a in enumerate(pairs):
+                source = x_ref if i == 0 else sums.at[i - 1]
+                copy = pltpu.make_async_remote_copy(
+                    src_ref=source,
+                    dst_ref=land.at[i],
+                    send_sem=sends.at[i],
+                    recv_sem=lands.at[i],
+                    device_id={a: 1 - lax.axis_index(a)},
+                    device_id_type=MESH,
+                )
+                copy.start()
+                copy.wait()
+                sums[i] = source[...] + land[i]
+            out_ref[me] = sums[steps - 1]
+            started = []
+            for r in range(1, depth):
+                copy = pltpu.make_async_remote_copy(
+                    src_ref=sums.at[steps - 1],
+                    dst_ref=out_ref.at[me],
+                    send_sem=sends.at[steps + r - 1],
+                    recv_sem=lands.at[steps + r - 1],
+                    device_id={"z": lax.rem(me + r, depth)},
+                    device_id_type=MESH,
+                )
+                copy.start()
+                started.append(copy)
+            for copy in started:
+                copy.wait()
+
+        return self.call(
+            kernel,
+            [jax.ShapeDtypeStruct((depth, *value.shape), value.dtype)],
+            [FAST],
+            [FAST],
+            [
+                pltpu.VMEM((steps, *value.shape), value.dtype),
+                pltpu.VMEM((steps, *value.shape), value.dtype),
+                pltpu.SemaphoreType.DMA((steps + depth - 1,)),
+                pltpu.SemaphoreType.DMA((steps + depth - 1,)),
+            ],
+            [value],
+            16 * value.size * 4,
+            name,
+        )[0]
+
+    def gather_plane(self, name, value):
+        rows, width = value.shape
+        parts = 4 if rows % 64 == 0 else 1
+        head = (parts + 1) // 2
+        value = value.reshape(parts, rows // parts, width)
+        shape = (*(self.sizes[a] for a in ("x", "y", "c")), *value.shape)
+
+        def kernel(own, out, sends, lands, own_sem):
+            self.greet([("x",), ("y",), ("c",)])
+            x, y, c = (lax.axis_index(a) for a in ("x", "y", "c"))
+            by_x, by_y, by_c = {"x": 1 - x}, {"y": 1 - y}, {"c": 1 - c}
+            started = []
+
+            def send(src, place, part, slot, peer):
+                copy = pltpu.make_async_remote_copy(
+                    src_ref=src,
+                    dst_ref=out.at[(*place, part)],
+                    send_sem=sends.at[len(started)],
+                    recv_sem=lands.at[slot, part],
+                    device_id=peer,
+                    device_id_type=MESH,
+                )
+                copy.start()
+                started.append(copy)
+
+            def arrived(place, part, slot):
+                landed = out.at[(*place, part)]
+                pltpu.make_async_remote_copy(
+                    src_ref=landed,
+                    dst_ref=landed,
+                    send_sem=sends.at[0],
+                    recv_sem=lands.at[slot, part],
+                    device_id=by_c,
+                    device_id_type=MESH,
+                ).wait_recv()
+                return landed
+
+            me, at_x, at_y, at_xy = (x, y, c), (1 - x, y, c), (x, 1 - y, c), (1 - x, 1 - y, c)
+            for part in range(parts):
+                send(own.at[part], me, part, 0, by_x)
+                send(own.at[part], me, part, 1, by_y)
+            for part in range(parts):
+                send(own.at[part], me, part, 3, by_c)
+            local = pltpu.make_async_copy(own, out.at[me], own_sem.at[0])
+            local.start()
+            for part in range(parts):
+                landed = arrived(at_x, part, 0)
+                if part < head:
+                    send(landed, at_x, part, 2, by_y)
+                send(landed, at_x, part, 4, by_c)
+                landed = arrived(at_y, part, 1)
+                if part >= head:
+                    send(landed, at_y, part, 2, by_x)
+                send(landed, at_y, part, 5, by_c)
+            for part in range(parts):
+                landed = arrived(at_xy, part, 2)
+                send(landed, at_xy, part, 6, by_c)
+            for slot, place in ((3, me), (4, at_x), (5, at_y), (6, at_xy)):
+                for part in range(parts):
+                    arrived((place[0], place[1], 1 - c), part, slot)
+            for copy in started:
+                copy.wait_send()
+            local.wait()
+
+        return self.call(
+            kernel,
+            [jax.ShapeDtypeStruct(shape, value.dtype)],
+            [BIG],
+            [BIG],
+            [
+                pltpu.SemaphoreType.DMA((7 * parts,)),
+                pltpu.SemaphoreType.DMA((7, parts)),
+                pltpu.SemaphoreType.DMA((1,)),
+            ],
+            [value],
+            4 * math.prod(shape),
+            name,
+        )[0].reshape(-1, width)
+
+
+def lanes(flat):
+    padded = jnp.pad(flat, (0, -flat.size % 1024))
+    return padded.reshape(-1, 128)
 
 
 def attention_forward(queries, key_rows, value_rows):
@@ -133,6 +403,7 @@
     attn_cols, ff_cols = attn_weight.shape[2], ff_weight.shape[2]
     rows_own = attn_weight.shape[0]
     low = jnp.bfloat16
+    links = Links(sizes)
 
     def mine(rows, size):
         row = lax.dynamic_index_in_dim(rows, y_at, 0, False)
@@ -146,40 +417,53 @@
     own_labels = mine(mlm_labels, own_slots)
     first_core = (c_at == 0).astype(jnp.float32)
 
-    word_plane = comm_all_gather(word_table.astype(low), plane)
-    ints = comm_all_gather(jnp.concatenate([own_ids, own_labels, own_valid])[None], "z")
-    z_ids, z_labels, z_valid = (
-        ints[:, :own_len],
-        ints[:, own_len : own_len + own_slots],
-        ints[:, own_len + own_slots :],
-    )
-    total_count = lax.psum(jnp.sum(mask_valid.astype(jnp.float32)), ("z", "x"))
-    total_seqs = jnp.float32(batch_size * dp_size)
+    side_rows = side_weight.shape[0] // mp_size
+    side_full = comm_all_gather(
+        lax.dynamic_slice_in_dim(side_weight.astype(low), mp_rank * side_rows, side_rows, 0), every
+    )
     attn_blocks = comm_all_gather(
         attn_weight.astype(low).reshape(rows_own, 4 * attn_cols), mp_first
     ).reshape(mp_size, D, 4 * attn_cols)
     ff_blocks = comm_all_gather(
         ff_weight.astype(low).reshape(rows_own, 2 * ff_cols), mp_first
     ).reshape(mp_size, D, 2 * ff_cols)
-    side_rows = side_weight.shape[0] // mp_size
-    side_full = comm_all_gather(
-        lax.dynamic_slice_in_dim(side_weight.astype(low), mp_rank * side_rows, side_rows, 0), every
-    )
+    vec_cols = vectors.shape[1]
+    stripe = vocab_own * x_size
+    bias_mine = lax.dynamic_slice_in_dim(decoder_bias, z_at * stripe, stripe, 0)
+    int_count = own_len + 2 * own_slots
+    ints, vec_parts, counts, mp_small = links.exchange(
+        "small_gather",
+        ("gather", ("z",), 0, FAST, lanes(jnp.concatenate([own_ids, own_labels, own_valid]))),
+        ("gather", ("z", "x"), 0, FAST, jnp.pad(vectors.astype(low), ((0, 0), (0, 128 - vec_cols)))),
+        (
+            "gather",
+            ("z", "x"),
+            0,
+            FAST,
+            jnp.full((8, 128), jnp.sum(mask_valid.astype(jnp.float32))),
+        ),
+        ("gather", ("y", "c"), 0, FAST, lanes(jnp.concatenate([bias_mine, split_bias.reshape(-1)]))),
+    )
+    ints = ints.reshape(z_size, -1)[:, :int_count]
+    z_ids, z_labels, z_valid = (
+        ints[:, :own_len],
+        ints[:, own_len : own_len + own_slots],
+        ints[:, own_len + own_slots :],
+    )
+    total_count = jnp.sum(counts[:, 0, 0])
+    total_seqs = jnp.float32(batch_size * dp_size)
     vec_rows = (
-        comm_all_gather(vectors.astype(low)[None], ("z", "x"))
+        vec_parts[:, :, :vec_cols]
         .transpose(1, 0, 2)
         .reshape(vectors.shape[0], D)
         .astype(jnp.float32)
     )
-    stripe = vocab_own * x_size
-    bias_mine = lax.dynamic_slice_in_dim(decoder_bias, z_at * stripe, stripe, 0)
-    mp_small = comm_all_gather(
-        jnp.concatenate([bias_mine, split_bias.reshape(-1)])[None], ("y", "c")
-    )
+    mp_small = mp_small.reshape(mp_size, -1)
+    word_plane = links.gather_plane("word_gather", word_table.astype(low))
     bias_plane = (
         mp_small[:, :stripe].reshape(mp_size, x_size, vocab_own).transpose(1, 0, 2).reshape(-1)
     )
-    split_full = mp_small[:, stripe:].reshape(mp_size, 6, attn_cols)
+    split_full = mp_small[:, stripe : stripe + 6 * attn_cols].reshape(mp_size, 6, attn_cols)
 
     def plane_index(ids):
         block = ids // stripe
@@ -191,7 +475,10 @@
     flat_ids = z_ids.reshape(-1)
     inside, at = plane_index(flat_ids)
     looked = jnp.where(inside[:, None], word_plane[jnp.where(inside, at, 0)], jnp.zeros((), low))
-    embedded = comm_scatter_sum(looked, "z").astype(jnp.float32)
+    looked = looked.reshape(z_size, own_len, D)
+    (found,) = links.exchange("token_spread", ("spread", ("z",), 0, BIG, looked))
+    embedded = lax.dynamic_index_in_dim(looked, z_at, 0, False).astype(jnp.float32)
+    embedded = embedded + jnp.sum(found.astype(jnp.float32), axis=0)
     position_rows = lax.dynamic_slice_in_dim(side_full, 2 * D + c_at * own_len, own_len, 0)
     embedded = (
         embedded
@@ -208,9 +495,11 @@
     queries = (packed[:, :, 0] + split_full[:, 0]).astype(low).reshape(own_len, D)
     own_keys = packed[:, :, 1].astype(low).reshape(own_len, D)
     own_values = (packed[:, :, 2] + split_full[:, 1]).astype(low).reshape(own_len, D)
-    both = comm_all_gather(jnp.stack([own_keys, own_values])[None], "c")
-    key_rows = both[:, 0].reshape(-1, D)
-    value_rows = both[:, 1].reshape(-1, D)
+    other_keys, other_values = links.exchange(
+        "key_trade", ("trade", ("c",), 0, FAST, own_keys), ("trade", ("c",), 0, FAST, own_values)
+    )
+    key_rows = jnp.concatenate([own_keys, other_keys])
+    value_rows = jnp.concatenate([own_values, other_values])
     mixed, log_norm = attention_forward(queries, key_rows, value_rows)
     attn_out = jnp.einsum(
         "tme,mde->td",
@@ -230,13 +519,17 @@
     resid2 = hidden1 + (ffn_out + vec_rows[5])
     hidden2 = layer_norm(resid2, vec_rows[6], vec_rows[7])
 
-    hidden2_seq = comm_all_gather(hidden2.astype(low), "c")
-    picked_b = hidden2_seq[own_pos]
+    hidden2_b = hidden2.astype(low)
+    (other_h2,) = links.exchange("hidden_trade", ("trade", ("c",), 0, FAST, hidden2_b))
+    picked_b = jnp.concatenate([hidden2_b, other_h2])[
+        own_pos % own_len + jnp.where(own_pos // own_len == c_at, 0, own_len)
+    ]
     dense_w = side_full[D : 2 * D]
     dense_out = jnp.dot(picked_b, dense_w, preferred_element_type=jnp.float32) + vec_rows[8]
     act_dense = gelu_exact(dense_out)
     head_rows = layer_norm(act_dense, vec_rows[9], vec_rows[10])
-    head_b = comm_all_gather(head_rows.astype(low), "z")
+    (head_b,) = links.exchange("head_gather", ("gather", ("z",), 0, FAST, head_rows.astype(low)))
+    head_b = head_b.reshape(-1, D)
     row_count = head_b.shape[0]
     logits = (
         jnp.einsum("rd,vd->rv", head_b, word_plane, preferred_element_type=jnp.float32)
@@ -248,7 +541,8 @@
     row_top = jnp.max(logits, axis=1)
     row_total = jnp.sum(jnp.exp(logits - row_top[:, None]), axis=1)
     row_target = jnp.sum(jnp.where(hit_rows, logits, 0.0), axis=1)
-    stats = comm_all_gather(jnp.stack([row_top, row_total, row_target])[None], "z")
+    stats = jnp.pad(jnp.stack([row_top, row_total, row_target]), ((0, 5), (0, 0)))
+    (stats,) = links.exchange("stat_gather", ("gather", ("z",), 0, FAST, stats))
     top_all = jnp.max(stats[:, 0], axis=0)
     total_all = jnp.sum(stats[:, 1] * jnp.exp(stats[:, 0] - top_all), axis=0)
     target_all = jnp.sum(stats[:, 2], axis=0)
@@ -261,20 +555,26 @@
     ).astype(low)
     decoder_part = jnp.sum(grad_logits.astype(jnp.float32), axis=0)
     head_part = jnp.dot(grad_logits, word_plane, preferred_element_type=jnp.float32)
-    grad_head = comm_scatter_sum(head_part, "z")
+    head_part = head_part.reshape(z_size, own_slots, D)
+    (head_others,) = links.exchange("head_spread", ("spread", ("z",), 0, FAST, head_part.astype(low)))
+    grad_head = lax.dynamic_index_in_dim(head_part, z_at, 0, False) + jnp.sum(
+        head_others.astype(jnp.float32), axis=0
+    )
     grad_act, grad_g9, grad_s9 = norm_backward(act_dense, vec_rows[9], vec_rows[10], grad_head)
     grad_dense = gelu_backward(dense_out, grad_act).astype(low)
     dense_bias_grad = jnp.sum(grad_dense.astype(jnp.float32), axis=0)
     dense_grad = jnp.einsum("rd,re->de", picked_b, grad_dense, preferred_element_type=jnp.float32)
     grad_picked = jnp.einsum("re,de->rd", grad_dense, dense_w, preferred_element_type=jnp.float32)
-    seq_picked = comm_all_gather(grad_picked, "c")
+    (other_picked,) = links.exchange("picked_trade", ("trade", ("c",), 0, FAST, grad_picked))
+    seq_picked = jnp.concatenate([grad_picked, other_picked])
+    other_pos = lax.dynamic_slice_in_dim(seq_pos, (1 - c_at) * own_slots, own_slots, 0)
     place = (
-        seq_pos[None, :]
+        jnp.concatenate([own_pos, other_pos])[None, :]
         == c_at * own_len + lax.broadcasted_iota(jnp.int32, (own_len, slots), 0)
     ).astype(jnp.float32)
     grad_top = jnp.dot(place, seq_picked, precision=highest)
 
-    cls_row = hidden2_seq[0:1]
+    cls_row = hidden2_b[0:1]
     pooler_w = side_full[:D]
     pooled = jnp.tanh(jnp.dot(cls_row, pooler_w, preferred_element_type=jnp.float32) + vec_rows[11])
     classes = vec_rows[14:16]
@@ -317,13 +617,18 @@
     grad_q, part_k, part_v = attention_backward(
         queries, key_rows, value_rows, log_norm, grad_mixed
     )
-    part_kv = jnp.concatenate([part_k, part_v], axis=1)
-    grad_kv = comm_scatter_sum(part_kv, "c").astype(low)
+    from_k, from_v = links.exchange(
+        "key_grad_trade",
+        ("trade", ("c",), 0, FAST, part_k[own_len:]),
+        ("trade", ("c",), 0, FAST, part_v[own_len:]),
+    )
+    grad_k = (part_k[:own_len] + from_k).astype(low)
+    grad_v = (part_v[:own_len] + from_v).astype(low)
     grad_packed = jnp.stack(
         [
             grad_q.astype(low).reshape(own_len, mp_size, attn_cols),
-            grad_kv[:, :D].reshape(own_len, mp_size, attn_cols),
-            grad_kv[:, D:].reshape(own_len, mp_size, attn_cols),
+            grad_k.reshape(own_len, mp_size, attn_cols),
+            grad_v.reshape(own_len, mp_size, attn_cols),
         ],
         axis=2,
     ).reshape(own_len, mp_size, 3 * attn_cols)
@@ -335,7 +640,7 @@
         "tme,mde->td", grad_packed, qkv_blocks, preferred_element_type=jnp.float32
     )
     attn_grad = jnp.concatenate([attn_grad_in, attn_grad_out], axis=2).astype(low)
-    attn_red = comm_scatter_sum(attn_grad.reshape(mp_size * D, 4 * attn_cols), mp_first)
+    attn_grad = attn_grad.reshape(y_size, c_size, z_size, x_size, rows_own, 4 * attn_cols)
     grad_h0 = grad_r1 + hidden0_part
     grad_x0, grad_g0, grad_s0 = norm_backward(embedded, vec_rows[0], vec_rows[1], grad_h0)
 
@@ -352,8 +657,37 @@
         jnp.zeros((length, D), low), grad_x0.astype(low), c_at * own_len, 0
     )
     side_grad = jnp.concatenate([pooler_grad.astype(low), dense_grad.astype(low), position_grad], axis=0)
-    side_quarter = comm_scatter_sum(side_grad, every)
-    side_red = comm_all_gather(side_quarter, ("y", "c")).astype(jnp.float32)
+    side_grad = side_grad.reshape(z_size, x_size, y_size, c_size, side_rows, D)
+
+    def joined(value, at, dim, received):
+        kept = lax.dynamic_index_in_dim(value, at, dim, False)
+        return (kept.astype(jnp.float32) + received.astype(jnp.float32)).astype(low)
+
+    from_a, from_s = links.exchange(
+        "grad_swap_c", ("swap", ("c",), 1, BIG, attn_grad), ("swap", ("c",), 3, BIG, side_grad)
+    )
+    attn_grad, side_grad = joined(attn_grad, c_at, 1, from_a), joined(side_grad, c_at, 3, from_s)
+    from_a, from_s = links.exchange(
+        "grad_swap_xy", ("swap", ("x",), 2, BIG, attn_grad), ("swap", ("y",), 2, BIG, side_grad)
+    )
+    attn_grad, side_grad = joined(attn_grad, x_at, 2, from_a), joined(side_grad, y_at, 2, from_s)
+    from_a, from_s = links.exchange(
+        "grad_swap_yx", ("swap", ("y",), 0, BIG, attn_grad), ("swap", ("x",), 1, BIG, side_grad)
+    )
+    attn_grad, side_grad = joined(attn_grad, y_at, 0, from_a), joined(side_grad, x_at, 1, from_s)
+    from_a, from_s = links.exchange(
+        "grad_spread_z", ("spread", ("z",), 0, BIG, attn_grad), ("spread", ("z",), 0, BIG, side_grad)
+    )
+
+    def total(value, received):
+        kept = lax.dynamic_index_in_dim(value, z_at, 0, False).astype(jnp.float32)
+        return kept + jnp.sum(received.astype(jnp.float32), axis=0)
+
+    attn_red, side_quarter = total(attn_grad, from_a), total(side_grad, from_s)
+    (side_red,) = links.exchange(
+        "side_gather", ("gather", ("y", "c"), 0, FAST, side_quarter.astype(low))
+    )
+    side_red = side_red.reshape(side_weight.shape).astype(jnp.float32)
     type_zero = jnp.sum(jnp.where(own_types[:, None] == 0, grad_x0, 0.0), axis=0)
     type_one = jnp.sum(jnp.where(own_types[:, None] == 1, grad_x0, 0.0), axis=0)
     vec_grad = jnp.stack(
@@ -372,17 +706,25 @@
         ],
         axis=1,
     )
-    small = lax.psum(jnp.concatenate([vec_grad.reshape(-1), split_grad.reshape(-1)]), every)
-    vec_all = small[: vec_grad.size].reshape(vec_grad.shape)
-    split_all = small[vec_grad.size :].reshape(split_grad.shape)
-    vec_cols = vectors.shape[1]
+    small = links.combine(
+        "small_sum",
+        lanes(jnp.concatenate([vec_grad.reshape(-1), split_grad.reshape(-1), decoder_part])),
+    ).reshape(z_size, -1)
+    narrow = vec_grad.size + split_grad.size
+    summed = jnp.sum(small[:, :narrow], axis=0)
+    vec_all = summed[: vec_grad.size].reshape(vec_grad.shape)
+    split_all = summed[vec_grad.size :].reshape(split_grad.shape)
     vec_red = lax.dynamic_slice_in_dim(vec_all, dp_rank * vec_cols, vec_cols, 1)
     split_red = lax.dynamic_index_in_dim(split_all, mp_rank, 0, False)
-    decoder_own = comm_scatter_sum(decoder_part, plane)
-    decoder_red = comm_all_gather(decoder_own, ("z", "x"))
+    decoder_red = lax.dynamic_index_in_dim(
+        small[:, narrow : narrow + decoder_part.size].reshape(z_size, x_size, mp_size, vocab_own),
+        mp_rank,
+        2,
+        False,
+    ).reshape(-1)
     word_f, attn_f, ff_f = (
         word_red,
-        attn_red.astype(jnp.float32).reshape(attn_weight.shape),
+        attn_red.reshape(attn_weight.shape),
         ff_red.astype(jnp.float32).reshape(ff_weight.shape),
     )
     own_square = (
@@ -394,7 +736,11 @@
         + (jnp.sum(split_red * split_red) + jnp.sum(decoder_red * decoder_red)) / dp_size
     )
     loss_part = mlm_sum / total_count / z_size + nsp_sum / total_seqs
-    grad_square, total_loss = lax.psum((own_square, loss_part), every)
+    ends = jnp.where(
+        lax.broadcasted_iota(jnp.int32, (8, 128), 0) == 0, own_square, loss_part
+    )
+    ends = jnp.sum(links.combine("norm_sum", ends), axis=0)
+    grad_square, total_loss = ends[0, 0], ends[1, 0]
     grad_norm = jnp.sqrt(grad_square)
     clip_scale = max_norm / jnp.maximum(grad_norm, max_norm)
     return (

time: 1390 us -> 922 us (0.66)
  waiting for transfers between devices: 679 us -> 110 us
  Pallas kernels: 0 us -> 322 us
  blocking collectives: 214 us -> 0 us
    pallas_call x0 -> x17, Pallas kernels: none -> 322 us  [call(): pl.pallas_call(kernel, out_shape=outs, in_specs=[pl.BlockSpec(memory_spac...]
    reduce_scatter x6 -> x2, waiting for transfers between devices: 297 us -> 51.2 us  [comm_scatter_sum(): return lax.psum_scatter(value, axes, scatter_dimension=0, tiled=True)]
    psum x1 -> x0, waiting for transfers between devices: 123 us -> none  [step(): lax.psum(jnp.concatenate([vec_grad.reshape(-1), split_grad.reshape(-1)]),...]
    unnamed x16 -> x6, waiting for transfers between devices: 103 us -> 0.1 us
    all_gather x7 -> x4, waiting for transfers between devices: 157 us -> 58.4 us  [comm_all_gather(): return lax.all_gather(value, axes, axis=0, tiled=True)]
    all_gather x7 -> x0, blocking collectives: 90.5 us -> none  [comm_all_gather(): return lax.all_gather(value, axes, axis=0, tiled=True)]
    unnamed x2 -> x0, blocking collectives: 62.8 us -> none
    psum x2 -> x0, blocking collectives: 60.5 us -> none  [the longest x1 39.6 us: step(): grad_square, total_loss = lax.psum((own_square, loss_part), every)]
  transfers between devices with their start and end apart: 15 -> 6, of which waited for: 13 -> 3; matrix products, arithmetic and copies ran while one was open for 18% -> 22% of each run, Pallas kernels for 0% -> 28%
where the time goes in v2:
time: 922 us; the launch traced here: 911 us
  Pallas kernels  322 us (35%)
  matrix products  221 us (24%)
  other arithmetic  133 us (14%)
  waiting for transfers between devices  110 us (12%)
  local copies, waits for them, and re-layouts  99.6 us (11%)
  between operations  25.8 us (3%)
    pallas_call x17, Pallas kernels, call(): pl.pallas_call(kernel, out_shape=outs, in_specs=[pl.BlockSpec(memory_spac...  322 us
    all_gather x4, waiting for transfers between devices, comm_all_gather(): return lax.all_gather(value, axes, axis=0, tiled=True)  58.4 us
    reduce_scatter x2, waiting for transfers between devices, comm_scatter_sum(): return lax.psum_scatter(value, axes, scatter_dimension=0, tiled=True)  51.2 us
    dot_general x1, matrix products, step(): jnp.dot(onehot, all_x0, preferred_element_type=jnp.float32)  34.6 us
    unnamed x304, local copies, waits for them, and re-layouts  28.8 us
    convert_element_type x1, other arithmetic, attention_backward(): grad_scores = (attn_probs * (grad_probs - row_dot)).astype(jnp.bfloat16)  22 us
    dot_general x1, matrix products, step(): jnp.einsum('td,mdf->mtf', hidden1_b, ff_in, preferred_element_type=jnp.fl...  21 us
    dot_general x1, matrix products, attention_backward(): jnp.einsum('qhe,khe->hqk', g3, v3, preferred_element_type=jnp.float32)  20.1 us
  transfers between devices with their start and end apart: 6, of which 3 were waited for; matrix products, arithmetic and copies ran while one was open for 22% of the time, Pallas kernels for 28%

profile of v2, /device:TPU:0, one launch (start us, length us, event | category | flops | bytes accessed | tf_op | source)
XLA Modules:
  0.0 910.8 jit_solution(13806220329229794079)
XLA Ops:
  16.8 10.3 %small_gather.1 = (s32[4,8,128]{2,1,0:T(8,128)S(1)}, bf16[8,16,128]{2,1,0:T(8,128)(2,1)S(1)}, f32[8,8,128]{2,1,0:T(8,128)S(1)}, f32[4,24,128]{2,1,0:T(8,128)S(1)}) custom-call(s32[8,128]{1,0:T(8,128)S(1)} %pad_bitcast_fusion.refs_0_, bf16[16,128]{1,0:T(8,128)(2,1)S(1)} %pad.13.refs_1_, f32[8,128]{1,0:T(8,128)S(1)} %broadcast_in_dim.154.refs_2_, ...), custom_call_target="tpu_custom_call" | custom-call | bytes 262144 | tf_op jit(solution)/shard_map/small_gather/pallas_call | solution.py:111
  30.6 62.7 %word_gather.1 = bf16[2,2,2,4,240,768]{5,4,3,2,1,0:T(8,128)(2,1)S(1)} custom-call(bf16[4,240,768]{2,1,0:T(8,128)(2,1)S(1)} %bitcast.405), custom_call_target="tpu_custom_call" | custom-call | bytes 23592960 | tf_op jit(solution)/shard_map/word_gather/pallas_call | solution.py:111
  93.3 4.2 copy-done
  97.8 16.0 %gather_fusion = bf16[2048,768]{1,0:T(8,128)(2,1)} fusion(bf16[7680,768]{1,0:T(8,128)(2,1)} %bitcast.398, s32[2048]{0:T(1024)S(1)} %broadcast_clamp_fusion), kind=kCustom, calls=%fused_computation | custom fusion | bytes 6299648 | tf_op jit(solution)/shard_map/gather | solution.py:477
  115.9 68.2 %token_spread.1 = bf16[3,512,768]{2,1,0:T(8,128)(2,1)S(1)} custom-call(bf16[4,512,768]{2,1,0:T(8,128)(2,1)S(1)} %broadcast_select_fusion.refs_0_), custom_call_target="tpu_custom_call" | custom-call | bytes 4718592 | tf_op jit(solution)/shard_map/token_spread/pallas_call | solution.py:111
  207.6 4.4 fusion.42
  228.9 11.9 %multiply_reduce_fusion.1 = (f32[12,512]{1,0:T(8,128)S(1)}, f32[12,512,1024]{2,1,0:T(8,128)}) fusion(bf16[512,12,64]{0,2,1:T(8,128)(2,1)} %bitcast.422, bf16[512,12,64]{0,2,1:T(8,128)(2,1)} %bitcast.418, f32[512,12,64]{0,2,1:T(8,128)S(1)} %bitcast.413, f32[12,64]{1,0:T(8,128)S(1)} %add.740), kind=kOutput, calls=%fused_computation.12 | convolution fusion | flops 821815296 | bytes 28339200 | tf_op jit(solution)/shard_map/qhe,khe->hqk/dot_general | solution.py:341
  240.8 11.1 %fusion.2 = f32[12,512]{1,0:T(8,128)S(1)} fusion(f32[12,512,1024]{2,1,0:T(8,128)} %get-tuple-element.167, f32[12,512]{1,0:T(8,128)S(1)} %get-tuple-element.166), kind=kLoop, calls=%fused_computation.11 | loop fusion | flops 18868224 | bytes 25214976 | tf_op jit(solution)/shard_map/reduce_sum | solution.py:344
  251.9 11.8 %fusion.70 = bf16[12,64,512]{2,1,0:T(8,128)(2,1)S(1)} fusion(f32[12,512,1024]{2,1,0:T(8,128)} %get-tuple-element.167, f32[12,512]{1,0:T(8,128)S(1)} %fusion.2, f32[12,512]{1,0:T(8,128)S(1)} %get-tuple-element.166, bf16[512,12,64]{0,2,1:T(8,128)(2,1)S(1)} %bitcast.437, bf16[512,12,64]{0,2,1:T(8,128)(2,1)S(1)} %add_convert_fusion.6), kind=kOutput, calls=%fused_computation.148 | convolution fusion | flops 834011136 | bytes 27574272 | tf_op jit(solution)/shard_map/hqk,khe->qhe/dot_general | solution.py:347
  263.8 3.6 fusion.197
  268.5 19.5 %all-gather.9.cloned.1.call-done = bf16[3072,1536]{1,0:T(8,128)(2,1)} async-done(((bf16[96,1536]{1,0:T(8,128)(2,1)}), bf16[3072,1536]{1,0:T(8,128)(2,1)}) %all-gather.9.cloned.1.call-update) | async-done | bytes 9437200 | tf_op jit(solution)/shard_map/all_gather | solution.py:59
  288.0 21.0 %fusion.18 = (bf16[4,512,768]{2,1,0:T(8,128)(2,1)S(1)}, f32[4,512,768]{2,1,0:T(8,128)}, f32[512,4,768]{2,0,1:T(8,128)}) fusion(f32[4,768]{1,0:T(4,128)S(1)} %add.751, bf16[4,768,1536]{2,1,0:T(8,128)(2,1)} %bitcast.472, f32[512,768]{1,0:T(8,128)S(1)} %get-tuple-element.169, f32[768]{0:T(1024)S(1)} %add.748, f32[768]{0:T(1024)S(1)} %mul.833, ...), kind=kOutput, calls=%fused_computation.42 | convolution fusion | flops 2521694208 | bytes 22042624 | tf_op jit(solution)/shard_map/td,mdf->mtf/dot_general | solution.py:515
  323.4 17.3 %head_gather.1 = bf16[4,128,768]{2,1,0:T(8,128)(2,1)S(1)} custom-call(bf16[128,768]{1,0:T(8,128)(2,1)S(1)} %add_convert_fusion.11.refs_0_), custom_call_target="tpu_custom_call" | custom-call | bytes 1572864 | tf_op jit(solution)/shard_map/head_gather/pallas_call | solution.py:111
  340.7 14.9 %add_reduce_fusion = (f32[512]{0:T(512)}, f32[512,7680]{1,0:T(8,128)}) fusion(f32[7680]{0:T(1024)} %add.773, bf16[512,768]{1,0:T(8,128)(2,1)S(1)} %bitcast.407, bf16[7680,768]{1,0:T(8,128)(2,1)} %bitcast.399), kind=kOutput, calls=%fused_computation.19 | convolution fusion | flops 6047661568 | bytes 28344320 | tf_op jit(solution)/shard_map/rd,vd->rv/dot_general | solution.py:535
  355.7 9.4 %exponential_reduce_fusion = (f32[512]{0:T(512)S(1)}, f32[512]{0:T(512)S(1)}) fusion(f32[512,7680]{1,0:T(8,128)} %get-tuple-element.175, f32[512]{0:T(512)} %get-tuple-element.174, f32[7680]{0:T(1024)} %add.773, s32[512]{0:T(512)} %fusion.139), kind=kLoop, calls=%fused_computation.18 | loop fusion | flops 23591936 | bytes 15767552 | tf_op jit(solution)/shard_map/reduce_sum | solution.py:542
  365.1 8.5 stat_gather.1
  375.8 9.9 %convert_reduce_fusion = (f32[7680]{0:T(1024)}, bf16[512,7680]{1,0:T(8,128)(2,1)S(1)}) fusion(f32[512]{0:T(512)S(1)} %get-tuple-element.157, s32[512]{0:T(512)S(1)} %copy-done.75, f32[512]{0:T(512)S(1)} %get-tuple-element.133, f32[512,7680]{1,0:T(8,128)} %get-tuple-element.175, f32[7680]{0:T(1024)S(1)} %copy-done.60), kind=kLoop, calls=%fused_computation.14 | loop fusion | flops 35381760 | bytes 23660544 | tf_op jit(solution)/shard_map/reduce_sum | solution.py:556
  385.7 6.2 fusion.200
  392.0 15.6 %head_spread.1 = bf16[3,128,768]{2,1,0:T(8,128)(2,1)S(1)} custom-call(bf16[4,128,768]{2,1,0:T(8,128)(2,1)S(1)} %get-tuple-element.178.refs_0_), custom_call_target="tpu_custom_call" | custom-call | bytes 1179648 | tf_op jit(solution)/shard_map/head_spread/pallas_call | solution.py:111
  426.1 10.0 %convert_reduce_fusion.1 = (f32[4,768]{1,0:T(4,128)}, bf16[4,512,768]{2,1,0:T(8,128)(2,1)S(1)}) fusion(f32[4,512,768]{2,1,0:T(8,128)} %get-tuple-element.138, bf16[4,768,1536]{2,1,0:T(8,128)(2,1)} %bitcast.473, bf16[512,768]{1,0:T(8,128)(2,1)S(1)} %get-tuple-element.116, f32[512,4,768]{2,0,1:T(8,128)} %get-tuple-element.170, f32[4,768]{1,0:T(4,128)S(1)} %copy-done.99), kind=kOutput, calls=%fused_computation.43 | convolution fusion | flops 2442654720 | bytes 21258240 | tf_op jit(solution)/shard_map/td,mdf->mtf/dot_general | solution.py:598
  436.1 3.6 multiply_reduce_fusion.3
  443.1 20.1 %multiply_reduce_fusion = (f32[12,512]{1,0:T(8,128)S(1)}, f32[12,512,1024]{2,1,0:T(8,128)}) fusion(f32[12,512,1024]{2,1,0:T(8,128)} %get-tuple-element.167, f32[12,512]{1,0:T(8,128)S(1)} %copy-done.55, bf16[512,12,64]{0,2,1:T(8,128)(2,1)S(1)} %bitcast.424, bf16[512,12,64]{0,2,1:T(8,128)(2,1)S(1)} %bitcast.438, bf16[512,12,64]{0,2,1:T(8,128)(2,1)S(1)} %copy-done.39), kind=kOutput, calls=%fused_computation.6 | convolution fusion | flops 833611776 | bytes 52740096 | tf_op jit(solution)/shard_map/qhe,khe->hqk/dot_general | solution.py:363
  463.3 22.0 %multiply_convert_fusion = bf16[12,512,1024]{2,1,0:T(8,128)(2,1)} fusion(f32[12,512,1024]{2,1,0:T(8,128)} %get-tuple-element.183, f32[12,512,1024]{2,1,0:T(8,128)} %get-tuple-element.167, f32[12,512]{1,0:T(8,128)S(1)} %get-tuple-element.182, f32[12,512]{1,0:T(8,128)S(1)} %copy-done.55), kind=kLoop, calls=%fused_computation.5 | loop fusion | flops 31457280 | bytes 62963712 | tf_op jit(solution)/shard_map/convert_element_type | solution.py:368
  485.3 9.5 %multiply_convert_fusion.3 = bf16[12,64,512]{2,1,0:T(8,128)(2,1)} fusion(bf16[12,512,1024]{2,1,0:T(8,128)(2,1)} %multiply_convert_fusion, bf16[512,12,64]{0,2,1:T(8,128)(2,1)S(1)} %bitcast.423, bf16[512,12,64]{0,2,1:T(8,128)(2,1)S(1)} %bitcast.419), kind=kOutput, calls=%fused_computation.129 | convolution fusion | flops 809238528 | bytes 14942208 | tf_op jit(solution)/shard_map/hqk,khe->qhe/dot_general | solution.py:370
  494.8 7.0 multiply_bitcast_fusion
  501.8 12.5 %fusion.55 = f32[1024,12,64]{0,2,1:T(8,128)} fusion(bf16[512,12,64]{0,2,1:T(8,128)(2,1)S(1)} %bitcast.425, f32[12,512,1024]{2,1,0:T(8,128)} %get-tuple-element.167, f32[12,512]{1,0:T(8,128)S(1)} %copy-done.55), kind=kOutput, calls=%fused_computation.104 | convolution fusion | flops 824180736 | bytes 29122560 | tf_op jit(solution)/shard_map/hqk,qhe->khe/dot_general | solution.py:364
  516.2 4.0 fusion.194
  525.2 5.7 key_grad_trade.1
  544.3 5.1 multiply_reduce_fusion.4
  553.6 5.2 convolution_convert_fusion
  562.0 4.2 pad_maximum_fusion
  567.4 14.1 %fusion.203 = f32[7680,768]{1,0:T(8,128)} fusion(bf16[512,7680]{1,0:T(8,128)(2,1)} %copy-done.20, bf16[512,768]{1,0:T(8,128)(2,1)S(1)} %bitcast.408), kind=kOutput, calls=%fused_computation.452 | convolution fusion | flops 6039797760 | bytes 32243712 | tf_op jit(solution)/shard_map/rv,rd->vd/dot_general | solution.py:652
  581.5 38.9 %all-gather.11.cloned.1.call-done = bf16[2048,768]{1,0:T(8,128)(2,1)} async-done(((bf16[512,768]{1,0:T(8,128)(2,1)}), bf16[2048,768]{1,0:T(8,128)(2,1)}) %all-gather.11.cloned.1.call-update) | async-done | bytes 3145744 | tf_op jit(solution)/shard_map/all_gather | solution.py:59
  620.4 34.6 %add_convert_fusion = bf16[7680,768]{1,0:T(8,128)(2,1)} fusion(f32[7680,768]{1,0:T(8,128)} %fusion.203, bf16[2048,768]{1,0:T(8,128)(2,1)} %all-gather.11.cloned.1.call-done, s32[2048]{0:T(1024)S(1)} %fusion.119), kind=kOutput, calls=%fused_computation.10 | convolution fusion | flops 24186716160 | bytes 38543360 | tf_op jit(solution)/shard_map/dot_general | solution.py:653
  659.5 20.6 %small_sum.1 = f32[4,192,128]{2,1,0:T(8,128)S(1)} custom-call(f32[192,128]{1,0:T(8,128)S(1)} %maximum_bitcast_fusion.x_ref), custom_call_target="tpu_custom_call" | custom-call | bytes 1572864 | tf_op jit(solution)/shard_map/small_sum/pallas_call | solution.py:111
  682.1 5.6 convert_bitcast_fusion
  687.8 6.2 copy.194
  698.3 3.9 pad_maximum_fusion.1
  704.5 7.4 grad_swap_c.1
  715.7 32.4 %grad_swap_xy.1 = (bf16[2,4,96,768]{3,2,1,0:T(8,128)(2,1)S(1)}, bf16[4,2,80,768]{3,2,1,0:T(8,128)(2,1)S(1)}) custom-call(bf16[2,4,2,96,768]{4,3,2,1,0:T(8,128)(2,1)S(1)} %copy.201.refs_0_, bf16[4,2,2,80,768]{4,3,2,1,0:T(8,128)(2,1)S(1)} %copy.202.refs_1_), custom_call_target="tpu_custom_call" | custom-call | bytes 4325376 | tf_op jit(solution)/shard_map/grad_swap_xy/pallas_call | solution.py:111
  748.8 16.9 %grad_swap_yx.1 = (bf16[4,96,768]{2,1,0:T(8,128)(2,1)S(1)}, bf16[4,80,768]{2,1,0:T(8,128)(2,1)S(1)}) custom-call(bf16[2,4,96,768]{3,2,1,0:T(8,128)(2,1)S(1)} %fusion.51.refs_0_, bf16[4,2,80,768]{3,2,1,0:T(8,128)(2,1)S(1)} %copy.204.refs_1_), custom_call_target="tpu_custom_call" | custom-call | bytes 2162688 | tf_op jit(solution)/shard_map/grad_swap_yx/pallas_call | solution.py:111
  766.0 30.0 %grad_spread_z.1 = (bf16[3,96,768]{2,1,0:T(8,128)(2,1)S(1)}, bf16[3,80,768]{2,1,0:T(8,128)(2,1)S(1)}) custom-call(bf16[4,96,768]{2,1,0:T(8,128)(2,1)S(1)} %fusion.73.refs_0_, bf16[4,80,768]{2,1,0:T(8,128)(2,1)S(1)} %fusion.84.refs_1_), custom_call_target="tpu_custom_call" | custom-call | bytes 1622016 | tf_op jit(solution)/shard_map/grad_spread_z/pallas_call | solution.py:111
  796.1 6.5 side_gather.1
  813.2 51.2 %reduce-scatter.3.cloned.1.call-done = bf16[960,768]{1,0:T(8,128)(2,1)} async-done(((bf16[7680,768]{1,0:T(8,128)(2,1)}), bf16[960,768]{1,0:T(8,128)(2,1)}) %reduce-scatter.3.cloned.1.call-update) | async-done | bytes 1474576 | tf_op jit(solution)/shard_map/reduce_scatter | solution.py:63
  869.2 12.5 %norm_sum.1 = f32[4,8,128]{2,1,0:T(8,128)S(1)} custom-call(f32[8,128]{1,0:T(8,128)S(1)} %iota.41.x_ref), custom_call_target="tpu_custom_call" | custom-call | bytes 65536 | tf_op jit(solution)/shard_map/norm_sum/pallas_call | solution.py:111
  888.1 4.1 multiply_subtract_fusion.1
  892.1 4.5 multiply_subtract_fusion.2
  898.4 4.3 multiply_subtract_fusion
  (537 shorter events, 155.6 us)
Async XLA Ops:
  7.2 193.4 %all-gather.5.cloned.1.call-start = ((), (), s32[]{:S(2)}) async-start(), calls=%async_computation.2 | async-start | bytes 4055040 | tf_op jit(solution)/shard_map/all_gather | solution.py:59
  8.9 195.3 %all-gather.7.cloned.1.call-start = ((), (), s32[]{:S(2)}) async-start(), calls=%async_computation.3 | async-start | bytes 4866048 | tf_op jit(solution)/shard_map/all_gather | solution.py:59
  10.9 277.1 %all-gather.9.cloned.1.call-start = ((), (), s32[]{:S(2)}) async-start(), calls=%async_computation.4 | async-start | bytes 9732096 | tf_op jit(solution)/shard_map/all_gather | solution.py:59
  13.0 607.4 %all-gather.11.cloned.1.call-start = ((), (), s32[]{:S(2)}) async-start(), calls=%async_computation.5 | async-start | bytes 3932160 | tf_op jit(solution)/shard_map/all_gather | solution.py:59
  27.4 169.4 %copy-start.63 = (s32[1,4,8,128]{3,1,2,0:T(4,128)}, s32[1,4,8,128]{3,1,2,0:T(4,128)S(1)}, u32[]{:S(2)}) copy-start(s32[1,4,8,128]{3,1,2,0:T(4,128)S(1)} %copy.257) | copy-start | bytes 49156
  115.9 76.5 %copy-start.133 = (s32[2]{0:T(128)S(1)}, s32[2]{0:T(128)}, u32[]{:S(2)}) copy-start(s32[2]{0:T(128)} %param.32) | copy-start | bytes 28
  115.9 78.9 %copy-start.128 = (s32[2,256]{1,0:T(2,128)S(1)}, s32[2,256]{1,0:T(2,128)}, u32[]{:S(2)}) copy-start(s32[2,256]{1,0:T(2,128)} %param.29) | copy-start | bytes 6148
  186.0 77.8 %copy-start.91 = (f32[768]{0:T(1024)}, f32[768]{0:T(1024)S(1)}, u32[]{:S(2)}) copy-start(f32[768]{0:T(1024)S(1)} %mul.826) | copy-start | bytes 9220
  186.0 77.7 %copy-start.117 = (f32[768]{0:T(1024)}, f32[768]{0:T(1024)S(1)}, u32[]{:S(2)}) copy-start(f32[768]{0:T(1024)S(1)} %add.731) | copy-start | bytes 9220
  186.1 42.8 %copy-start.64 = (f32[12,64]{1,0:T(8,128)}, f32[12,64]{1,0:T(8,128)S(1)}, u32[]{:S(2)}) copy-start(f32[12,64]{1,0:T(8,128)S(1)} %add.740) | copy-start | bytes 9220
  186.3 122.8 %copy-start.93 = (f32[768]{0:T(1024)}, f32[768]{0:T(1024)S(1)}, u32[]{:S(2)}) copy-start(f32[768]{0:T(1024)S(1)} %mul.833) | copy-start | bytes 9220
  186.3 122.7 %copy-start.119 = (f32[768]{0:T(1024)}, f32[768]{0:T(1024)S(1)}, u32[]{:S(2)}) copy-start(f32[768]{0:T(1024)S(1)} %add.748) | copy-start | bytes 9220
  188.5 99.5 %copy-start.98 = (f32[4,768]{1,0:T(4,128)}, f32[4,768]{1,0:T(4,128)S(1)}, u32[]{:S(2)}) copy-start(f32[4,768]{1,0:T(4,128)S(1)} %add.751) | copy-start | bytes 36868
  202.8 61.0 %copy-start.71 = (f32[512]{0:T(512)}, f32[512]{0:T(512)S(1)}, u32[]{:S(2)}) copy-start(f32[512]{0:T(512)S(1)} %broadcast_multiply_fusion.3) | copy-start | bytes 6148
  204.2 59.5 %copy-start.103 = (f32[512]{0:T(512)}, f32[512]{0:T(512)S(1)}, u32[]{:S(2)}) copy-start(f32[512]{0:T(512)S(1)} %fusion.148) | copy-start | bytes 6148
  228.9 23.0 %copy-start.38 = (bf16[512,12,64]{0,2,1:T(8,128)(2,1)}, bf16[512,12,64]{0,2,1:T(8,128)(2,1)S(1)}, u32[]{:S(2)}) copy-start(bf16[512,12,64]{0,2,1:T(8,128)(2,1)S(1)} %add_convert_fusion.6) | copy-start | bytes 2359300
  240.8 11.1 %copy-start.36 = (bf16[512,768]{0,1:T(8,128)(2,1)S(1)}, bf16[512,768]{0,1:T(8,128)(2,1)}, u32[]{:S(2)}) copy-start(bf16[512,768]{0,1:T(8,128)(2,1)} %copy.180) | copy-start | bytes 2359300
  251.9 11.9 %copy-start.12 = (f32[512,768]{1,0:T(8,128)S(1)}, f32[512,768]{1,0:T(8,128)}, u32[]{:S(2)}) copy-start(f32[512,768]{1,0:T(8,128)} %copy-done.10) | copy-start | bytes 4718596
  267.4 41.7 %copy-start.22 = (f32[512,768]{1,0:T(8,128)}, f32[512,768]{1,0:T(8,128)S(1)}, u32[]{:S(2)}) copy-start(f32[512,768]{1,0:T(8,128)S(1)} %get-tuple-element.169) | copy-start | bytes 4718596
  267.7 41.3 %copy-start.78 = (f32[512]{0:T(512)}, f32[512]{0:T(512)S(1)}, u32[]{:S(2)}) copy-start(f32[512]{0:T(512)S(1)} %multiply_reduce_fusion.9) | copy-start | bytes 6148
  267.7 41.4 %copy-start.105 = (f32[512]{0:T(512)}, f32[512]{0:T(512)S(1)}, u32[]{:S(2)}) copy-start(f32[512]{0:T(512)S(1)} %fusion.149) | copy-start | bytes 6148
  288.0 21.1 %copy-start.132 = (bf16[3072,1536]{1,0:T(8,128)(2,1)S(1)}, bf16[3072,1536]{1,0:T(8,128)(2,1)}, u32[]{:S(2)}) copy-start(bf16[3072,1536]{1,0:T(8,128)(2,1)} %all-gather.9.cloned.1.call-done) | copy-start | bytes 28311556
  312.6 100.6 %copy-start.2 = (bf16[512,768]{1,0:T(8,128)(2,1)}, bf16[512,768]{1,0:T(8,128)(2,1)S(1)}, u32[]{:S(2)}) copy-start(bf16[512,768]{1,0:T(8,128)(2,1)S(1)} %add_convert_fusion.3.refs_0_) | copy-start | bytes 2359300
  340.7 15.0 %copy-start.5 = (bf16[4,128,768]{2,1,0:T(8,128)(2,1)}, bf16[4,128,768]{2,1,0:T(8,128)(2,1)S(1)}, u32[]{:S(2)}) copy-start(bf16[4,128,768]{2,1,0:T(8,128)(2,1)S(1)} %head_gather.1) | copy-start | bytes 2359300
  355.7 20.1 %copy-start.60 = (f32[7680]{0:T(1024)S(1)}, f32[7680]{0:T(1024)}, u32[]{:S(2)}) copy-start(f32[7680]{0:T(1024)} %add.773) | copy-start | bytes 92164
  355.7 20.1 %copy-start.75 = (s32[512]{0:T(512)S(1)}, s32[512]{0:T(512)}, u32[]{:S(2)}) copy-start(s32[512]{0:T(512)} %fusion.139) | copy-start | bytes 6148
  355.7 30.0 %slice-start = ((s8[11796480]{0:T(1024)(128)(4,1)}), s8[4194304]{0:T(1024)(128)(4,1)S(1)}, s32[]{:S(2)}) async-start(s8[11796480]{0:T(1024)(128)(4,1)} %bitcast.400), calls=%async_computation.8 | async-start | bytes 8388608
  355.7 30.0 %slice-start.1 = ((s8[11796480]{0:T(1024)(128)(4,1)}), s8[3407872]{0:T(1024)(128)(4,1)S(1)}, s32[]{:S(2)}) async-start(s8[11796480]{0:T(1024)(128)(4,1)} %bitcast.400), calls=%async_computation.9 | async-start | bytes 6815744
  385.7 22.1 %copy-start.96 = (f32[128]{0:T(128)S(1)}, f32[128]{0:T(128)}, u32[]{:S(2)}) copy-start(f32[128]{0:T(128)} %copy-done.95) | copy-start | bytes 1540
  392.0 16.5 %copy-start.131 = (f32[128]{0:T(128)S(1)}, f32[128]{0:T(128)}, u32[]{:S(2)}) copy-start(f32[128]{0:T(128)} %copy-done.130) | copy-start | bytes 1540
  392.0 16.5 %copy-start.111 = (f32[128]{0:T(128)S(1)}, f32[128]{0:T(128)}, u32[]{:S(2)}) copy-start(f32[128]{0:T(128)} %copy-done.110) | copy-start | bytes 1540
  392.0 17.3 %copy-start.56 = (f32[128,768]{1,0:T(8,128)S(1)}, f32[128,768]{1,0:T(8,128)}, u32[]{:S(2)}) copy-start(f32[128,768]{1,0:T(8,128)} %get-tuple-element.136) | copy-start | bytes 1179652
  392.0 17.3 %copy-start.57 = (f32[128,768]{1,0:T(8,128)S(1)}, f32[128,768]{1,0:T(8,128)}, u32[]{:S(2)}) copy-start(f32[128,768]{1,0:T(8,128)} %get-tuple-element.173) | copy-start | bytes 1179652
  392.0 18.9 %copy-start.32 = (bf16[2560,768]{1,0:T(8,128)(2,1)S(1)}, bf16[2560,768]{1,0:T(8,128)(2,1)}, u32[]{:S(2)}) copy-start(bf16[2560,768]{1,0:T(8,128)(2,1)} %all-gather.5.cloned.1.call-done) | copy-start | bytes 11796484
  410.2 12.3 %copy-start.74 = (f32[512]{0:T(512)S(1)}, f32[512]{0:T(512)}, u32[]{:S(2)}) copy-start(f32[512]{0:T(512)} %copy-done.73) | copy-start | bytes 6148
  410.2 12.3 %copy-start.125 = (s32[512]{0:T(512)S(1)}, s32[512]{0:T(512)}, u32[]{:S(2)}) copy-start(s32[512]{0:T(512)} %iota_add_fusion) | copy-start | bytes 6148
  410.2 12.3 %copy-start.129 = (s32[256]{0:T(256)S(1)}, s32[256]{0:T(256)}, u32[]{:S(2)}) copy-start(s32[256]{0:T(256)} %pad_add_fusion.1) | copy-start | bytes 3076
  410.2 12.3 %copy-start.136 = (pred[512]{0:T(512)(128)(4,1)S(1)}, pred[512]{0:T(512)(128)(4,1)}, u32[]{:S(2)}) copy-start(pred[512]{0:T(512)(128)(4,1)} %iota_compare_fusion.6) | copy-start | bytes 1540
  424.6 11.5 %slice-start.3 = ((s8[9437184]{0:T(1024)(128)(4,1)}), s8[4194304]{0:T(1024)(128)(4,1)S(1)}, s32[]{:S(2)}) async-start(s8[9437184]{0:T(1024)(128)(4,1)} %bitcast.475), calls=%async_computation.11 | async-start | bytes 8388608
  463.3 22.0 %copy-start.18 = (bf16[512,4,1,192]{0,3,1,2:T(8,128)(2,1)S(1)}, bf16[512,4,1,192]{0,3,1,2:T(8,128)(2,1)}, u32[]{:S(2)}) copy-start(bf16[512,4,1,192]{0,3,1,2:T(8,128)(2,1)} %copy-done.17) | copy-start | bytes 2359300
  463.3 22.0 %copy-start.21 = (bf16[512,768]{0,1:T(8,128)(2,1)S(1)}, bf16[512,768]{0,1:T(8,128)(2,1)}, u32[]{:S(2)}) copy-start(bf16[512,768]{0,1:T(8,128)(2,1)} %copy.181) | copy-start | bytes 2359300
  553.5 258.0 %reduce-scatter.5.cloned.1.call-start = ((), (), s32[]{:S(2)}) async-start(), calls=%async_computation.7 | async-start | bytes 9732096 | tf_op jit(solution)/shard_map/reduce_scatter | solution.py:63
  566.3 298.2 %reduce-scatter.3.cloned.1.call-start = ((), (), s32[]{:S(2)}) async-start(), calls=%async_computation.6 | async-start | bytes 13271040 | tf_op jit(solution)/shard_map/reduce_scatter | solution.py:63
  658.1 24.1 %copy-start.118 = (f32[768]{0:T(1024)S(1)}, f32[768]{0:T(1024)}, u32[]{:S(2)}) copy-start(f32[768]{0:T(1024)} %copy-done.117) | copy-start | bytes 9220
  765.9 42.8 %copy-start.61 = (f32[4,2,4,960]{3,2,1,0:T(4,128)S(1)}, f32[4,2,4,960]{3,2,1,0:T(4,128)}, u32[]{:S(2)}) copy-start(f32[4,2,4,960]{3,2,1,0:T(4,128)} %reshape.1005) | copy-start | bytes 368644
  810.7 75.9 %copy-start.66 = (f32[7680]{0:T(1024)S(1)}, f32[7680]{0:T(1024)}, u32[]{:S(2)}) copy-start(f32[7680]{0:T(1024)} %param.51) | copy-start | bytes 92164
  811.4 71.9 %copy-start.47 = (bf16[96,1536]{1,0:T(8,128)(2,1)S(1)}, bf16[96,1536]{1,0:T(8,128)(2,1)}, u32[]{:S(2)}) copy-start(bf16[96,1536]{1,0:T(8,128)(2,1)} %reduce-scatter.5.cloned.1.call-done) | copy-start | bytes 884740
  888.0 10.3 %copy-start.40 = (f32[960,768]{1,0:T(8,128)S(1)}, f32[960,768]{1,0:T(8,128)}, u32[]{:S(2)}) copy-start(f32[960,768]{1,0:T(8,128)} %param.34) | copy-start | bytes 8847364
  (104 other events, 418.0 us)
Sparse Core Ops, SparseCore 0:
  11.5 72.7 all-gather.4
  87.9 104.0 all-gather.6
  195.5 92.4 all-gather.8
  553.6 66.8 all-gather.10
  626.2 146.2 reduce-scatter.4
  775.9 88.5 reduce-scatter.2

commit v3 on v2

--- a/solution.py
+++ b/solution.py
@@ -4,6 +4,7 @@
 import jax
 import jax.numpy as jnp
 from jax import lax
+from jax.experimental.layout import Layout, with_layout_constraint
 from jax.experimental import pallas as pl
 from jax.experimental.pallas import tpu as pltpu
 from jax.sharding import Mesh, PartitionSpec as P
@@ -29,18 +30,22 @@
     return center * lax.rsqrt(spread + norm_eps) * norm_gain + norm_shift
 
 
+def normal_cdf(inputs):
+    return 0.5 + 0.5 * lax.erf(inputs * math.sqrt(0.5))
+
+
 def gelu_exact(inputs):
-    return jax.nn.gelu(inputs, approximate=False)
+    return inputs * normal_cdf(inputs)
+
+
+def gelu_slope(inputs):
+    density = jnp.exp(-0.5 * inputs * inputs) * (1.0 / math.sqrt(2.0 * math.pi))
+    return normal_cdf(inputs) + inputs * density
 
 
 def norm_backward(inputs, norm_gain, norm_shift, upstream):
     _, pullback = jax.vjp(layer_norm, inputs, norm_gain, norm_shift)
     return pullback(upstream)
-
-
-def gelu_backward(inputs, upstream):
-    _, pullback = jax.vjp(gelu_exact, inputs)
-    return pullback(upstream)[0]
 
 
 def adam_step(weight, moment, square, gradient, clip_scale, decays):
@@ -326,59 +331,119 @@
         )[0].reshape(-1, width)
 
 
+def row_major(value):
+    return with_layout_constraint(value, Layout(major_to_minor=tuple(range(value.ndim))))
+
+
 def lanes(flat):
     padded = jnp.pad(flat, (0, -flat.size % 1024))
     return padded.reshape(-1, 128)
 
 
-def attention_forward(queries, key_rows, value_rows):
-    score_scale = 1.0 / math.sqrt(HEAD_DIM)
+HEAD_SCALE = math.log2(math.e) / math.sqrt(HEAD_DIM)
+PAIR = 2 * HEAD_DIM
+ROWS = 256
+
+
+def dots(left, right, left_dim, right_dim):
+    return lax.dot_general(
+        left, right, (((left_dim,), (right_dim,)), ((), ())), preferred_element_type=jnp.float32
+    )
+
+
+def half_lanes(value, half):
+    lane = lax.broadcasted_iota(jnp.int32, value.shape, 1)
+    return jnp.where((lane >= HEAD_DIM) == (half == 1), value, jnp.zeros((), value.dtype))
+
+
+def forward_kernel(q_ref, k0_ref, k1_ref, v0_ref, v1_ref, out_ref, norm_ref):
+    keys = jnp.concatenate([k0_ref[...], k1_ref[...]], axis=0)
+    values = jnp.concatenate([v0_ref[...], v1_ref[...]], axis=0)
+    for start in range(0, q_ref.shape[0], ROWS):
+        rows = pl.ds(start, ROWS)
+        queries = q_ref[rows, :]
+        halves = []
+        for half in range(2):
+            scores = dots(keys, half_lanes(queries, half), 1, 1)
+            top = jnp.max(scores, axis=0, keepdims=True)
+            powers = jnp.exp2((scores - top) * HEAD_SCALE)
+            total = jnp.sum(powers, axis=0, keepdims=True)
+            probs = (powers * (1.0 / total)).astype(jnp.bfloat16)
+            norm_ref[0, half : half + 1, rows] = top * HEAD_SCALE + jnp.log2(total)
+            mixed = dots(values, probs, 0, 0)
+            halves.append(mixed[half * HEAD_DIM : (half + 1) * HEAD_DIM])
+        out_ref[rows, :] = jnp.concatenate(halves, axis=0).T.astype(out_ref.dtype)
+
+
+def attention_forward(queries, keys, values):
     length, width = queries.shape
-    heads = width // HEAD_DIM
-    q3 = queries.reshape(length, heads, HEAD_DIM)
-    k3 = key_rows.reshape(-1, heads, HEAD_DIM)
-    v3 = value_rows.reshape(-1, heads, HEAD_DIM)
-    scores = jnp.einsum("qhe,khe->hqk", q3, k3, preferred_element_type=jnp.float32) * score_scale
-    row_top = jnp.max(scores, axis=-1, keepdims=True)
-    exp_scores = jnp.exp(scores - row_top)
-    row_total = jnp.sum(exp_scores, axis=-1, keepdims=True)
-    attn_probs = exp_scores / row_total
-    log_norm = row_top + jnp.log(row_total)
-    mixed = jnp.einsum(
-        "hqk,khe->qhe", attn_probs.astype(jnp.bfloat16), v3, preferred_element_type=jnp.float32
-    )
-    return mixed.reshape(length, width).astype(jnp.bfloat16), log_norm
-
-
-def attention_backward(queries, key_rows, value_rows, log_norm, grad_mixed):
-    score_scale = 1.0 / math.sqrt(HEAD_DIM)
+    pairs = width // PAIR
+    block = pl.BlockSpec((length, PAIR), lambda i: (0, i))
+    flops = 8 * length * length * width
+    return pl.pallas_call(
+        forward_kernel,
+        grid=(pairs,),
+        out_shape=[
+            jax.ShapeDtypeStruct((length, width), queries.dtype),
+            jax.ShapeDtypeStruct((pairs, 2, length), jnp.float32),
+        ],
+        in_specs=[block] * 5,
+        out_specs=[block, pl.BlockSpec((1, 2, length), lambda i: (i, 0, 0))],
+        cost_estimate=pl.CostEstimate(
+            flops=2 * flops, bytes_accessed=16 * length * width, transcendentals=flops // 256
+        ),
+        name="attention_forward",
+    )(queries, *keys, *values)
+
+
+def backward_kernel(
+    q_ref, k0_ref, k1_ref, v0_ref, v1_ref, norm_ref, g_ref, dq_ref, dk0_ref, dk1_ref, dv0_ref, dv1_ref
+):
+    own = k0_ref.shape[0]
+    keys = jnp.concatenate([k0_ref[...], k1_ref[...]], axis=0)
+    values = jnp.concatenate([v0_ref[...], v1_ref[...]], axis=0)
+    grad_keys = grad_values = 0.0
+    for start in range(0, q_ref.shape[0], ROWS):
+        rows = pl.ds(start, ROWS)
+        halves = []
+        for half in range(2):
+            queries = half_lanes(q_ref[rows, :], half)
+            upstream = half_lanes(g_ref[rows, :], half)
+            scores = dots(keys, queries, 1, 1)
+            probs = jnp.exp2(scores * HEAD_SCALE - norm_ref[0, half : half + 1, rows])
+            grad_probs = dots(values, upstream, 1, 1)
+            row_dot = jnp.sum(grad_probs * probs, axis=0, keepdims=True)
+            grad_scores = (probs * (grad_probs - row_dot)).astype(jnp.bfloat16)
+            grad_values = grad_values + dots(probs.astype(jnp.bfloat16), upstream, 1, 0)
+            grad_keys = grad_keys + dots(grad_scores, queries, 1, 0)
+            grad_queries = dots(keys, grad_scores, 0, 0)
+            halves.append(grad_queries[half * HEAD_DIM : (half + 1) * HEAD_DIM])
+        grad_queries = jnp.concatenate(halves, axis=0) * (1.0 / math.sqrt(HEAD_DIM))
+        dq_ref[rows, :] = grad_queries.T.astype(dq_ref.dtype)
+    grad_keys = grad_keys * (1.0 / math.sqrt(HEAD_DIM))
+    dk0_ref[...] = grad_keys[:own]
+    dk1_ref[...] = grad_keys[own:]
+    dv0_ref[...] = grad_values[:own]
+    dv1_ref[...] = grad_values[own:]
+
+
+def attention_backward(queries, keys, values, log_norm, grad_mixed):
     length, width = queries.shape
-    heads = width // HEAD_DIM
-    q3 = queries.reshape(length, heads, HEAD_DIM)
-    k3 = key_rows.reshape(-1, heads, HEAD_DIM)
-    v3 = value_rows.reshape(-1, heads, HEAD_DIM)
-    g3 = grad_mixed.reshape(length, heads, HEAD_DIM)
-    scores = jnp.einsum("qhe,khe->hqk", q3, k3, preferred_element_type=jnp.float32) * score_scale
-    attn_probs = jnp.exp(scores - log_norm)
-    grad_probs = jnp.einsum("qhe,khe->hqk", g3, v3, preferred_element_type=jnp.float32)
-    grad_values = jnp.einsum(
-        "hqk,qhe->khe", attn_probs.astype(jnp.bfloat16), g3, preferred_element_type=jnp.float32
-    )
-    row_dot = jnp.sum(grad_probs * attn_probs, axis=-1, keepdims=True)
-    grad_scores = (attn_probs * (grad_probs - row_dot)).astype(jnp.bfloat16)
-    grad_queries = (
-        jnp.einsum("hqk,khe->qhe", grad_scores, k3, preferred_element_type=jnp.float32)
-        * score_scale
-    )
-    grad_keys = (
-        jnp.einsum("hqk,qhe->khe", grad_scores, q3, preferred_element_type=jnp.float32)
-        * score_scale
-    )
-    return (
-        grad_queries.reshape(length, width),
-        grad_keys.reshape(-1, width),
-        grad_values.reshape(-1, width),
-    )
+    pairs = width // PAIR
+    block = pl.BlockSpec((length, PAIR), lambda i: (0, i))
+    flops = 20 * length * length * width
+    wide = jax.ShapeDtypeStruct((length, width), jnp.float32)
+    return pl.pallas_call(
+        backward_kernel,
+        grid=(pairs,),
+        out_shape=[jax.ShapeDtypeStruct((length, width), queries.dtype)] + [wide] * 4,
+        in_specs=[block] * 5 + [pl.BlockSpec((1, 2, length), lambda i: (i, 0, 0)), block],
+        out_specs=[block] * 5,
+        cost_estimate=pl.CostEstimate(
+            flops=2 * flops, bytes_accessed=32 * length * width, transcendentals=flops // 640
+        ),
+        name="attention_backward",
+    )(queries, *keys, *values, log_norm, grad_mixed)
 
 
 def step(sizes, *args):
@@ -498,9 +563,8 @@
     other_keys, other_values = links.exchange(
         "key_trade", ("trade", ("c",), 0, FAST, own_keys), ("trade", ("c",), 0, FAST, own_values)
     )
-    key_rows = jnp.concatenate([own_keys, other_keys])
-    value_rows = jnp.concatenate([own_values, other_values])
-    mixed, log_norm = attention_forward(queries, key_rows, value_rows)
+    keys, values = (own_keys, other_keys), (own_values, other_values)
+    mixed, log_norm = attention_forward(queries, keys, values)
     attn_out = jnp.einsum(
         "tme,mde->td",
         mixed.reshape(own_len, mp_size, attn_cols),
@@ -561,7 +625,7 @@
         head_others.astype(jnp.float32), axis=0
     )
     grad_act, grad_g9, grad_s9 = norm_backward(act_dense, vec_rows[9], vec_rows[10], grad_head)
-    grad_dense = gelu_backward(dense_out, grad_act).astype(low)
+    grad_dense = (grad_act * gelu_slope(dense_out)).astype(low)
     dense_bias_grad = jnp.sum(grad_dense.astype(jnp.float32), axis=0)
     dense_grad = jnp.einsum("rd,re->de", picked_b, grad_dense, preferred_element_type=jnp.float32)
     grad_picked = jnp.einsum("re,de->rd", grad_dense, dense_w, preferred_element_type=jnp.float32)
@@ -596,12 +660,19 @@
     out_bias_two = jnp.sum(ffn_grad_b.astype(jnp.float32), axis=0)
     ff_out_grad = jnp.einsum("td,mtf->mdf", ffn_grad_b, active, preferred_element_type=jnp.float32)
     grad_active = jnp.einsum("td,mdf->mtf", ffn_grad_b, ff_out, preferred_element_type=jnp.float32)
-    grad_up = gelu_backward(upward, grad_active).astype(low)
+    grad_up = (grad_active * gelu_slope(upward)).astype(low)
     ff_bias_grad = jnp.sum(grad_up.astype(jnp.float32), axis=1)
     ff_in_grad = jnp.einsum("td,mtf->mdf", hidden1_b, grad_up, preferred_element_type=jnp.float32)
     hidden1_part = jnp.einsum("mtf,mdf->td", grad_up, ff_in, preferred_element_type=jnp.float32)
-    ff_grad = jnp.concatenate([ff_in_grad, ff_out_grad], axis=2).astype(low)
-    ff_red = comm_scatter_sum(ff_grad.reshape(mp_size * D, 2 * ff_cols), mp_first)
+    ff_grad = jnp.stack(
+        [
+            row_major(g.astype(low)).reshape(mp_size * dp_size, rows_own, ff_cols)
+            for g in (ff_in_grad, ff_out_grad)
+        ],
+        axis=1,
+    )
+    ff_grad, hidden1_part = lax.optimization_barrier((ff_grad, hidden1_part))
+    ff_red = comm_scatter_sum(ff_grad.reshape(-1, ff_cols), mp_first)
     grad_h1 = grad_r2 + hidden1_part
     grad_r1, grad_g1, grad_s1 = norm_backward(resid1, vec_rows[3], vec_rows[4], grad_h1)
     attn_grad_b = grad_r1.astype(low)
@@ -614,19 +685,19 @@
         "td,mde->tme", attn_grad_b, out_blocks, preferred_element_type=jnp.float32
     )
     grad_mixed = grad_mixed.astype(low).reshape(own_len, D)
-    grad_q, part_k, part_v = attention_backward(
-        queries, key_rows, value_rows, log_norm, grad_mixed
+    grad_q, own_k, part_k, own_v, part_v = attention_backward(
+        queries, keys, values, log_norm, grad_mixed
     )
     from_k, from_v = links.exchange(
         "key_grad_trade",
-        ("trade", ("c",), 0, FAST, part_k[own_len:]),
-        ("trade", ("c",), 0, FAST, part_v[own_len:]),
-    )
-    grad_k = (part_k[:own_len] + from_k).astype(low)
-    grad_v = (part_v[:own_len] + from_v).astype(low)
+        ("trade", ("c",), 0, FAST, part_k),
+        ("trade", ("c",), 0, FAST, part_v),
+    )
+    grad_k = (own_k + from_k).astype(low)
+    grad_v = (own_v + from_v).astype(low)
     grad_packed = jnp.stack(
         [
-            grad_q.astype(low).reshape(own_len, mp_size, attn_cols),
+            grad_q.reshape(own_len, mp_size, attn_cols),
             grad_k.reshape(own_len, mp_size, attn_cols),
             grad_v.reshape(own_len, mp_size, attn_cols),
         ],
@@ -644,37 +715,52 @@
     grad_h0 = grad_r1 + hidden0_part
     grad_x0, grad_g0, grad_s0 = norm_backward(embedded, vec_rows[0], vec_rows[1], grad_h0)
 
-    all_x0 = comm_all_gather(grad_x0.astype(low), "z")
+    position_grad = lax.dynamic_update_slice_in_dim(
+        jnp.zeros((length, D), low), grad_x0.astype(low), c_at * own_len, 0
+    )
+    side_grad = jnp.concatenate([pooler_grad.astype(low), dense_grad.astype(low), position_grad], axis=0)
+    side_grad = side_grad.reshape(z_size, x_size, y_size, c_size, side_rows, D)
+
+    def joined(value, at, dim, received):
+        kept = lax.dynamic_index_in_dim(value, at, dim, False)
+        return (kept.astype(jnp.float32) + received.astype(jnp.float32)).astype(low)
+
+    x0_b = grad_x0.astype(low)
+    cut_one, cut_two = own_len // 8, 5 * own_len // 8
+    from_a, from_s, x0_one = links.exchange(
+        "grad_swap_c",
+        ("swap", ("c",), 1, BIG, attn_grad),
+        ("swap", ("c",), 3, BIG, side_grad),
+        ("gather", ("z",), 0, BIG, x0_b[:cut_one]),
+    )
+    attn_grad, side_grad = joined(attn_grad, c_at, 1, from_a), joined(side_grad, c_at, 3, from_s)
+    from_a, from_s, x0_two = links.exchange(
+        "grad_swap_xy",
+        ("swap", ("x",), 2, BIG, attn_grad),
+        ("swap", ("y",), 2, BIG, side_grad),
+        ("gather", ("z",), 0, BIG, x0_b[cut_one:cut_two]),
+    )
+    attn_grad, side_grad = joined(attn_grad, x_at, 2, from_a), joined(side_grad, y_at, 2, from_s)
+    from_a, from_s, x0_three = links.exchange(
+        "grad_swap_yx",
+        ("swap", ("y",), 0, BIG, attn_grad),
+        ("swap", ("x",), 1, BIG, side_grad),
+        ("gather", ("z",), 0, BIG, x0_b[cut_two:]),
+    )
+    attn_grad, side_grad = joined(attn_grad, y_at, 0, from_a), joined(side_grad, x_at, 1, from_s)
+
+    ff_red, x0_three = lax.optimization_barrier((ff_red, x0_three))
+    all_x0 = jnp.concatenate([x0_one, x0_two, x0_three], axis=1).reshape(-1, D)
     onehot = (
         jnp.where(inside, at, -1)[None, :]
         == lax.broadcasted_iota(jnp.int32, (word_plane.shape[0], flat_ids.shape[0]), 0)
     ).astype(low)
     word_grad = jnp.einsum("rv,rd->vd", grad_logits, head_b, preferred_element_type=jnp.float32)
     word_grad = word_grad + jnp.dot(onehot, all_x0, preferred_element_type=jnp.float32)
-    word_red = comm_scatter_sum(word_grad.astype(low), plane).astype(jnp.float32)
-
-    position_grad = lax.dynamic_update_slice_in_dim(
-        jnp.zeros((length, D), low), grad_x0.astype(low), c_at * own_len, 0
-    )
-    side_grad = jnp.concatenate([pooler_grad.astype(low), dense_grad.astype(low), position_grad], axis=0)
-    side_grad = side_grad.reshape(z_size, x_size, y_size, c_size, side_rows, D)
-
-    def joined(value, at, dim, received):
-        kept = lax.dynamic_index_in_dim(value, at, dim, False)
-        return (kept.astype(jnp.float32) + received.astype(jnp.float32)).astype(low)
-
-    from_a, from_s = links.exchange(
-        "grad_swap_c", ("swap", ("c",), 1, BIG, attn_grad), ("swap", ("c",), 3, BIG, side_grad)
-    )
-    attn_grad, side_grad = joined(attn_grad, c_at, 1, from_a), joined(side_grad, c_at, 3, from_s)
-    from_a, from_s = links.exchange(
-        "grad_swap_xy", ("swap", ("x",), 2, BIG, attn_grad), ("swap", ("y",), 2, BIG, side_grad)
-    )
-    attn_grad, side_grad = joined(attn_grad, x_at, 2, from_a), joined(side_grad, y_at, 2, from_s)
-    from_a, from_s = links.exchange(
-        "grad_swap_yx", ("swap", ("y",), 0, BIG, attn_grad), ("swap", ("x",), 1, BIG, side_grad)
-    )
-    attn_grad, side_grad = joined(attn_grad, y_at, 0, from_a), joined(side_grad, x_at, 1, from_s)
+    word_grad, attn_grad, side_grad = lax.optimization_barrier(
+        (word_grad.astype(low), attn_grad, side_grad)
+    )
+    word_red = comm_scatter_sum(word_grad, plane).astype(jnp.float32)
     from_a, from_s = links.exchange(
         "grad_spread_z", ("spread", ("z",), 0, BIG, attn_grad), ("spread", ("z",), 0, BIG, side_grad)
     )
@@ -684,10 +770,6 @@
         return kept + jnp.sum(received.astype(jnp.float32), axis=0)
 
     attn_red, side_quarter = total(attn_grad, from_a), total(side_grad, from_s)
-    (side_red,) = links.exchange(
-        "side_gather", ("gather", ("y", "c"), 0, FAST, side_quarter.astype(low))
-    )
-    side_red = side_red.reshape(side_weight.shape).astype(jnp.float32)
     type_zero = jnp.sum(jnp.where(own_types[:, None] == 0, grad_x0, 0.0), axis=0)
     type_one = jnp.sum(jnp.where(own_types[:, None] == 1, grad_x0, 0.0), axis=0)
     vec_grad = jnp.stack(
@@ -706,10 +788,16 @@
         ],
         axis=1,
     )
+    late = lanes(jnp.concatenate([vec_grad.reshape(-1), split_grad.reshape(-1), decoder_part]))
+    late, side_quarter = lax.optimization_barrier((late, side_quarter))
     small = links.combine(
         "small_sum",
-        lanes(jnp.concatenate([vec_grad.reshape(-1), split_grad.reshape(-1), decoder_part])),
+        late,
     ).reshape(z_size, -1)
+    (side_red,) = links.exchange(
+        "side_gather", ("gather", ("y", "c"), 0, FAST, side_quarter.astype(low))
+    )
+    side_red = side_red.reshape(side_weight.shape).astype(jnp.float32)
     narrow = vec_grad.size + split_grad.size
     summed = jnp.sum(small[:, :narrow], axis=0)
     vec_all = summed[: vec_grad.size].reshape(vec_grad.shape)
@@ -725,7 +813,9 @@
     word_f, attn_f, ff_f = (
         word_red,
         attn_red.reshape(attn_weight.shape),
-        ff_red.astype(jnp.float32).reshape(ff_weight.shape),
+        lax.optimization_barrier(
+            ff_red.astype(jnp.float32).reshape(2, rows_own, ff_cols).transpose(1, 0, 2)
+        ),
     )
     own_square = (
         jnp.sum(word_f * word_f)

time: 922 us -> 829 us (0.90)
  matrix products: 221 us -> 129 us
  Pallas kernels: 322 us -> 407 us
  waiting for transfers between devices: 110 us -> 57.2 us
  other arithmetic: 133 us -> 98.7 us
    dot_general x6 -> x0, matrix products: 72.8 us -> none  [the longest x1 20.1 us: attention_backward(): jnp.einsum('qhe,khe->hqk', g3, v3, preferred_element_type=jnp.float32)]
    pallas_call x0 -> x2, Pallas kernels: none -> 46.1 us  [the longest x1 23.7 us: attention_backward(): pl.pallas_call(backward_kernel, grid=(pairs,), out_shape=[jax.ShapeDtypeS...]
    pallas_call x17, Pallas kernels: 322 us -> 361 us  [call(): pl.pallas_call(kernel, out_shape=outs, in_specs=[pl.BlockSpec(memory_spac...]
    reduce_scatter x2, waiting for transfers between devices: 51.2 us -> 20 us  [comm_scatter_sum(): return lax.psum_scatter(value, axes, scatter_dimension=0, tiled=True)]
    all_gather x4 -> x3, waiting for transfers between devices: 58.4 us -> 37.2 us  [comm_all_gather(): return lax.all_gather(value, axes, axis=0, tiled=True)]
    convert_element_type x4 -> x3, other arithmetic: 25.6 us -> 4.58 us  [the longest x1 2.43 us: step(): grad_v = (own_v + from_v).astype(low)]
    dot_general x1, matrix products: 21 us -> 6.88 us  [step(): jnp.einsum('td,mdf->mtf', hidden1_b, ff_in, preferred_element_type=jnp.fl...]
    slice x8 -> x6, local copies, waits for them, and re-layouts: 14.2 us -> 2.24 us  [the longest x1 2.04 us: step(): packed[:, :, 2] + split_full[:, 1]]
  transfers between devices with their start and end apart: 6 -> 5, of which waited for: 3 -> 2; matrix products, arithmetic and copies ran while one was open for 22% -> 17% of each run, Pallas kernels for 28% -> 43%
where the time goes in v3:
time: 829 us; the launch traced here: 819 us
  Pallas kernels  407 us (49%)
  matrix products  129 us (16%)
  local copies, waits for them, and re-layouts  101 us (12%)
  other arithmetic  98.7 us (12%)
  waiting for transfers between devices  57.2 us (7%)
  between operations  25.4 us (3%)
    pallas_call x17, Pallas kernels, call(): pl.pallas_call(kernel, out_shape=outs, in_specs=[pl.BlockSpec(memory_spac...  361 us
    all_gather x3, waiting for transfers between devices, comm_all_gather(): return lax.all_gather(value, axes, axis=0, tiled=True)  37.2 us
    unnamed x304, local copies, waits for them, and re-layouts  37 us
    dot_general x1, matrix products, step(): jnp.dot(onehot, all_x0, preferred_element_type=jnp.float32)  33.8 us
    pallas_call x1, Pallas kernels, attention_backward(): pl.pallas_call(backward_kernel, grid=(pairs,), out_shape=[jax.ShapeDtypeS...  23.7 us
    pallas_call x1, Pallas kernels, attention_forward(): pl.pallas_call(forward_kernel, grid=(pairs,), out_shape=[jax.ShapeDtypeSt...  22.3 us
    reduce_scatter x2, waiting for transfers between devices, comm_scatter_sum(): return lax.psum_scatter(value, axes, scatter_dimension=0, tiled=True)  20 us
  transfers between devices with their start and end apart: 5, of which 2 were waited for; matrix products, arithmetic and copies ran while one was open for 17% of the time, Pallas kernels for 43%

profile of v3, /device:TPU:0, one launch (start us, length us, event | category | flops | bytes accessed | tf_op | source)
XLA Modules:
  0.0 818.7 jit_solution(17137354554152969419)
XLA Ops:
  16.8 10.3 %small_gather.1 = (s32[4,8,128]{2,1,0:T(8,128)S(1)}, bf16[8,16,128]{2,1,0:T(8,128)(2,1)S(1)}, f32[8,8,128]{2,1,0:T(8,128)S(1)}, f32[4,24,128]{2,1,0:T(8,128)S(1)}) custom-call(s32[8,128]{1,0:T(8,128)S(1)} %pad_bitcast_fusion.refs_0_, bf16[16,128]{1,0:T(8,128)(2,1)S(1)} %pad.13.refs_1_, f32[8,128]{1,0:T(8,128)S(1)} %broadcast_in_dim.151.refs_2_, ...), custom_call_target="tpu_custom_call" | custom-call | bytes 262144 | tf_op jit(solution)/shard_map/small_gather/pallas_call | solution.py:116
  30.4 62.7 %word_gather.1 = bf16[2,2,2,4,240,768]{5,4,3,2,1,0:T(8,128)(2,1)S(1)} custom-call(bf16[4,240,768]{2,1,0:T(8,128)(2,1)S(1)} %bitcast.330), custom_call_target="tpu_custom_call" | custom-call | bytes 23592960 | tf_op jit(solution)/shard_map/word_gather/pallas_call | solution.py:116
  93.1 4.4 copy-done
  97.6 16.0 %gather_fusion = bf16[2048,768]{1,0:T(8,128)(2,1)} fusion(bf16[7680,768]{1,0:T(8,128)(2,1)} %bitcast.323, s32[2048]{0:T(1024)S(1)} %broadcast_clamp_fusion), kind=kCustom, calls=%fused_computation | custom fusion | bytes 6299648 | tf_op jit(solution)/shard_map/gather | solution.py:542
  115.7 68.2 %token_spread.1 = bf16[3,512,768]{2,1,0:T(8,128)(2,1)S(1)} custom-call(bf16[4,512,768]{2,1,0:T(8,128)(2,1)S(1)} %broadcast_select_fusion.refs_0_), custom_call_target="tpu_custom_call" | custom-call | bytes 4718592 | tf_op jit(solution)/shard_map/token_spread/pallas_call | solution.py:116
  197.3 3.3 convert_reduce_fusion.3
  204.3 4.9 fusion.23
  213.6 3.4 copy.202
  217.1 3.5 key_trade.1
  222.0 22.3 %attention_forward.1 = (bf16[512,768]{1,0:T(8,128)(2,1)}, f32[6,2,512]{2,1,0:T(2,128)}) custom-call(bf16[512,768]{1,0:T(8,128)(2,1)} %add_convert_fusion.5.q_ref, bf16[512,768]{1,0:T(8,128)(2,1)} %copy-done.2, bf16[512,768]{1,0:T(8,128)(2,1)} %copy-done.9, bf16[512,768]{1,0:T(8,128)(2,1)} %copy-done.3, bf16[512,768]{1,0:T(8,128)(2,1)} %copy-done.10), custom_call_target="tpu_custom_call" | custom-call | flops 3221225472 | bytes 6291456 | tf_op jit(solution)/shard_map/attention_forward/pallas_call | solution.py:383
  246.7 3.6 fusion.165
  250.7 37.1 %all-gather.8.cloned.1.call-done = bf16[3072,1536]{1,0:T(8,128)(2,1)} async-done(((bf16[96,1536]{1,0:T(8,128)(2,1)}), bf16[3072,1536]{1,0:T(8,128)(2,1)}) %all-gather.8.cloned.1.call-update) | async-done | bytes 9437200 | tf_op jit(solution)/shard_map/all_gather | solution.py:64
  287.8 6.9 fusion.11
  294.7 5.4 fusion.166
  310.8 17.3 %head_gather.1 = bf16[4,128,768]{2,1,0:T(8,128)(2,1)S(1)} custom-call(bf16[128,768]{1,0:T(8,128)(2,1)S(1)} %add_convert_fusion.9.refs_0_), custom_call_target="tpu_custom_call" | custom-call | bytes 1572864 | tf_op jit(solution)/shard_map/head_gather/pallas_call | solution.py:116
  328.1 15.0 %add_reduce_fusion = (f32[512]{0:T(512)}, f32[512,7680]{1,0:T(8,128)}) fusion(f32[7680]{0:T(1024)} %add.774, bf16[512,768]{1,0:T(8,128)(2,1)S(1)} %bitcast.332, bf16[7680,768]{1,0:T(8,128)(2,1)} %bitcast.324), kind=kOutput, calls=%fused_computation.11 | convolution fusion | flops 6047661568 | bytes 28344320 | tf_op jit(solution)/shard_map/rd,vd->rv/dot_general | solution.py:599
  343.1 9.5 %exponential_reduce_fusion = (f32[512]{0:T(512)S(1)}, f32[512]{0:T(512)S(1)}) fusion(f32[512,7680]{1,0:T(8,128)} %get-tuple-element.298, f32[512]{0:T(512)} %get-tuple-element.297, f32[7680]{0:T(1024)} %add.774, s32[512]{0:T(512)} %fusion.113), kind=kLoop, calls=%fused_computation.10 | loop fusion | flops 23591936 | bytes 15767552 | tf_op jit(solution)/shard_map/reduce_sum | solution.py:606
  352.6 8.3 %stat_gather.1 = f32[4,8,512]{2,1,0:T(8,128)S(1)} custom-call(f32[8,512]{1,0:T(8,128)S(1)} %select_maximum_fusion.refs_0_), custom_call_target="tpu_custom_call" | custom-call | bytes 131072 | tf_op jit(solution)/shard_map/stat_gather/pallas_call | solution.py:116
  362.9 10.1 %convert_reduce_fusion = (f32[7680]{0:T(1024)}, bf16[512,7680]{1,0:T(8,128)(2,1)S(1)}) fusion(f32[512]{0:T(512)S(1)} %get-tuple-element.281, s32[512]{0:T(512)S(1)} %copy-done.67, f32[512]{0:T(512)S(1)} %get-tuple-element.264, f32[512,7680]{1,0:T(8,128)} %get-tuple-element.298, f32[7680]{0:T(1024)S(1)} %copy-done.45), kind=kLoop, calls=%fused_computation.6 | loop fusion | flops 35381760 | bytes 23660544 | tf_op jit(solution)/shard_map/reduce_sum | solution.py:620
  373.0 6.2 fusion.168
  379.3 15.6 %head_spread.1 = bf16[3,128,768]{2,1,0:T(8,128)(2,1)S(1)} custom-call(bf16[4,128,768]{2,1,0:T(8,128)(2,1)S(1)} %get-tuple-element.301.refs_0_), custom_call_target="tpu_custom_call" | custom-call | bytes 1179648 | tf_op jit(solution)/shard_map/head_spread/pallas_call | solution.py:116
  414.5 4.5 convolution_convert_fusion
  420.8 6.1 convert_reduce_fusion.1
  426.9 4.9 convolution_convert_fusion.1
  431.8 3.8 fusion.40
  435.6 8.2 %pad_maximum_fusion = bf16[32,2,96,768]{3,2,1,0:T(8,128)(2,1)} fusion(bf16[32,1,96,768]{3,2,1,0:T(8,128)(2,1)} %bitcast.345, bf16[32,1,96,768]{3,2,1,0:T(8,128)(2,1)} %bitcast.346), kind=kLoop, calls=%fused_computation.13 | loop fusion | flops 4718592 | bytes 18874368 | tf_op jit(solution)/shard_map/stack | solution.py:667
  445.2 3.3 slice.257
  450.1 3.3 multiply_reduce_fusion.1
  457.3 23.7 %attention_backward.1 = (bf16[512,768]{1,0:T(8,128)(2,1)}, f32[512,768]{1,0:T(8,128)}, f32[512,768]{1,0:T(8,128)}, f32[512,768]{1,0:T(8,128)}, f32[512,768]{1,0:T(8,128)}) custom-call(bf16[512,768]{1,0:T(8,128)(2,1)} %add_convert_fusion.5.q_ref, bf16[512,768]{1,0:T(8,128)(2,1)} %copy-done.2, bf16[512,768]{1,0:T(8,128)(2,1)} %copy-done.9, ...), custom_call_target="tpu_custom_call" | custom-call | flops 8053063680 | bytes 12582912 | tf_op jit(solution)/shard_map/attention_backward/pallas_call | solution.py:436
  484.0 6.3 key_grad_trade.1
  500.7 5.7 multiply_reduce_fusion.2
  510.0 4.1 convert_bitcast_fusion
  514.0 6.1 copy.224
  522.1 2.6 concatenate.42
  524.7 4.6 copy.226
  529.3 3.9 pad_maximum_fusion.1
  535.5 17.9 %grad_swap_c.1 = (bf16[2,4,2,96,768]{4,3,2,1,0:T(8,128)(2,1)S(1)}, bf16[4,2,2,80,768]{4,3,2,1,0:T(8,128)(2,1)S(1)}, bf16[4,64,768]{2,1,0:T(8,128)(2,1)S(1)}) custom-call(bf16[2,2,4,2,96,768]{5,4,3,2,1,0:T(8,128)(2,1)S(1)} %copy.227.refs_0_, bf16[4,2,2,2,80,768]{5,4,3,2,1,0:T(8,128)(2,1)S(1)} %bitcast.328, bf16[64,768]{1,0:T(8,128)(2,1)S(1)} %slice.278.refs_2_), custom_call_target="tpu_custom_call" | custom-call | bytes 9437184 | tf_op jit(solution)/shard_map/grad_swap_c/pallas_call | solution.py:116
  557.2 34.9 %grad_swap_xy.1 = (bf16[2,4,96,768]{3,2,1,0:T(8,128)(2,1)S(1)}, bf16[4,2,80,768]{3,2,1,0:T(8,128)(2,1)S(1)}, bf16[4,256,768]{2,1,0:T(8,128)(2,1)S(1)}) custom-call(bf16[2,4,2,96,768]{4,3,2,1,0:T(8,128)(2,1)S(1)} %copy.231.refs_0_, bf16[4,2,2,80,768]{4,3,2,1,0:T(8,128)(2,1)S(1)} %copy.232.refs_1_, bf16[256,768]{1,0:T(8,128)(2,1)S(1)} %slice.279.refs_2_), custom_call_target="tpu_custom_call" | custom-call | bytes 7471104 | tf_op jit(solution)/shard_map/grad_swap_xy/pallas_call | solution.py:116
  592.7 34.9 %grad_swap_yx.1 = (bf16[4,96,768]{2,1,0:T(8,128)(2,1)S(1)}, bf16[4,80,768]{2,1,0:T(8,128)(2,1)S(1)}, bf16[4,192,768]{2,1,0:T(8,128)(2,1)S(1)}) custom-call(bf16[2,4,96,768]{3,2,1,0:T(8,128)(2,1)S(1)} %fusion.34.refs_0_, bf16[4,2,80,768]{3,2,1,0:T(8,128)(2,1)S(1)} %copy.234.refs_1_, bf16[192,768]{1,0:T(8,128)(2,1)S(1)} %slice.280.refs_2_), custom_call_target="tpu_custom_call" | custom-call | bytes 4521984 | tf_op jit(solution)/shard_map/grad_swap_yx/pallas_call | solution.py:116
  629.2 11.1 %fusion.171 = f32[7680,768]{1,0:T(8,128)} fusion(bf16[512,7680]{1,0:T(8,128)(2,1)S(1)} %bitcast.342, bf16[512,768]{1,0:T(8,128)(2,1)S(1)} %bitcast.333), kind=kOutput, calls=%fused_computation.397 | convolution fusion | flops 6039797760 | bytes 32243712 | tf_op jit(solution)/shard_map/rv,rd->vd/dot_general | solution.py:758
  641.8 33.8 %add_convert_fusion = bf16[7680,768]{1,0:T(8,128)(2,1)} fusion(f32[7680,768]{1,0:T(8,128)} %fusion.171, bf16[2048,768]{1,0:T(8,128)(2,1)S(1)} %bitcast.349, s32[2048]{0:T(1024)S(1)} %copy-done.104), kind=kOutput, calls=%fused_computation.5 | convolution fusion | flops 24186716160 | bytes 38543360 | tf_op jit(solution)/shard_map/dot_general | solution.py:759
  681.2 28.7 %grad_spread_z.1 = (bf16[3,96,768]{2,1,0:T(8,128)(2,1)S(1)}, bf16[3,80,768]{2,1,0:T(8,128)(2,1)S(1)}) custom-call(bf16[4,96,768]{2,1,0:T(8,128)(2,1)S(1)} %fusion.50.refs_0_, bf16[4,80,768]{2,1,0:T(8,128)(2,1)S(1)} %fusion.59.refs_1_), custom_call_target="tpu_custom_call" | custom-call | bytes 1622016 | tf_op jit(solution)/shard_map/grad_spread_z/pallas_call | solution.py:116
  710.0 26.8 %small_sum.1 = f32[4,192,128]{2,1,0:T(8,128)S(1)} custom-call(f32[192,128]{1,0:T(8,128)S(1)} %maximum_bitcast_fusion.x_ref), custom_call_target="tpu_custom_call" | custom-call | bytes 1572864 | tf_op jit(solution)/shard_map/small_sum/pallas_call | solution.py:116
  738.9 8.8 %side_gather.1 = bf16[4,80,768]{2,1,0:T(8,128)(2,1)S(1)} custom-call(bf16[80,768]{1,0:T(8,128)(2,1)S(1)} %convert_add_fusion.7.refs_0_), custom_call_target="tpu_custom_call" | custom-call | bytes 983040 | tf_op jit(solution)/shard_map/side_gather/pallas_call | solution.py:116
  754.0 20.0 %reduce-scatter.5.cloned.1.call-done = bf16[960,768]{1,0:T(8,128)(2,1)} async-done(((bf16[7680,768]{1,0:T(8,128)(2,1)}), bf16[960,768]{1,0:T(8,128)(2,1)}) %reduce-scatter.5.cloned.1.call-update) | async-done | bytes 1474576 | tf_op jit(solution)/shard_map/reduce_scatter | solution.py:68
  774.0 2.7 fusion.28
  778.8 12.6 %norm_sum.1 = f32[4,8,128]{2,1,0:T(8,128)S(1)} custom-call(f32[8,128]{1,0:T(8,128)S(1)} %iota.41.x_ref), custom_call_target="tpu_custom_call" | custom-call | bytes 65536 | tf_op jit(solution)/shard_map/norm_sum/pallas_call | solution.py:116
  806.5 4.2 multiply_subtract_fusion
  (528 shorter events, 131.8 us)
Async XLA Ops:
  7.2 7.5 copy-start.119
  7.2 193.4 %all-gather.4.cloned.1.call-start = ((), (), s32[]{:S(2)}) async-start(), calls=%async_computation.2 | async-start | bytes 4055040 | tf_op jit(solution)/shard_map/all_gather | solution.py:64
  8.9 195.3 %all-gather.6.cloned.1.call-start = ((), (), s32[]{:S(2)}) async-start(), calls=%async_computation.3 | async-start | bytes 4866048 | tf_op jit(solution)/shard_map/all_gather | solution.py:64
  10.9 276.9 %all-gather.8.cloned.1.call-start = ((), (), s32[]{:S(2)}) async-start(), calls=%async_computation.4 | async-start | bytes 9732096 | tf_op jit(solution)/shard_map/all_gather | solution.py:64
  13.0 627.3 %reduce-scatter.3.cloned.1.call-start = ((), (), s32[]{:S(2)}) async-start(), calls=%async_computation.5 | async-start | bytes 9732096 | tf_op jit(solution)/shard_map/reduce_scatter | solution.py:68
  27.1 169.6 %copy-start.48 = (s32[1,4,8,128]{3,1,2,0:T(4,128)}, s32[1,4,8,128]{3,1,2,0:T(4,128)S(1)}, u32[]{:S(2)}) copy-start(s32[1,4,8,128]{3,1,2,0:T(4,128)S(1)} %copy.304) | copy-start | bytes 49156
  115.7 76.6 %copy-start.130 = (s32[2]{0:T(128)S(1)}, s32[2]{0:T(128)}, u32[]{:S(2)}) copy-start(s32[2]{0:T(128)} %param.32) | copy-start | bytes 28
  115.7 79.1 %copy-start.125 = (s32[2,256]{1,0:T(2,128)S(1)}, s32[2,256]{1,0:T(2,128)}, u32[]{:S(2)}) copy-start(s32[2,256]{1,0:T(2,128)} %param.29) | copy-start | bytes 6148
  185.8 60.9 %copy-start.87 = (f32[768]{0:T(1024)}, f32[768]{0:T(1024)S(1)}, u32[]{:S(2)}) copy-start(f32[768]{0:T(1024)S(1)} %mul.790) | copy-start | bytes 9220
  185.8 60.9 %copy-start.114 = (f32[768]{0:T(1024)}, f32[768]{0:T(1024)S(1)}, u32[]{:S(2)}) copy-start(f32[768]{0:T(1024)S(1)} %add.732) | copy-start | bytes 9220
  186.3 108.3 %copy-start.116 = (f32[768]{0:T(1024)}, f32[768]{0:T(1024)S(1)}, u32[]{:S(2)}) copy-start(f32[768]{0:T(1024)S(1)} %add.746) | copy-start | bytes 9220
  188.5 99.3 %copy-start.93 = (f32[4,768]{1,0:T(4,128)}, f32[4,768]{1,0:T(4,128)S(1)}, u32[]{:S(2)}) copy-start(f32[4,768]{1,0:T(4,128)S(1)} %add.749) | copy-start | bytes 36868
  202.8 43.9 %copy-start.61 = (f32[512]{0:T(512)}, f32[512]{0:T(512)S(1)}, u32[]{:S(2)}) copy-start(f32[512]{0:T(512)S(1)} %broadcast_multiply_fusion.3) | copy-start | bytes 6148
  204.2 42.5 %copy-start.97 = (f32[512]{0:T(512)}, f32[512]{0:T(512)S(1)}, u32[]{:S(2)}) copy-start(f32[512]{0:T(512)S(1)} %fusion.122) | copy-start | bytes 6148
  222.0 24.7 %copy-start.13 = (f32[512,768]{1,0:T(8,128)S(1)}, f32[512,768]{1,0:T(8,128)}, u32[]{:S(2)}) copy-start(f32[512,768]{1,0:T(8,128)} %copy-done.12) | copy-start | bytes 4718596
  250.3 44.4 %copy-start.15 = (f32[512,768]{1,0:T(8,128)}, f32[512,768]{1,0:T(8,128)S(1)}, u32[]{:S(2)}) copy-start(f32[512,768]{1,0:T(8,128)S(1)} %get-tuple-element.291) | copy-start | bytes 4718596
  250.6 44.0 %copy-start.70 = (f32[512]{0:T(512)}, f32[512]{0:T(512)S(1)}, u32[]{:S(2)}) copy-start(f32[512]{0:T(512)S(1)} %multiply_reduce_fusion.7) | copy-start | bytes 6148
  250.6 44.0 %copy-start.63 = (f32[512]{0:T(512)}, f32[512]{0:T(512)S(1)}, u32[]{:S(2)}) copy-start(f32[512]{0:T(512)S(1)} %fusion.123) | copy-start | bytes 6148
  287.8 6.9 copy-start.129
  328.1 15.0 %copy-start.7 = (bf16[4,128,768]{2,1,0:T(8,128)(2,1)}, bf16[4,128,768]{2,1,0:T(8,128)(2,1)S(1)}, u32[]{:S(2)}) copy-start(bf16[4,128,768]{2,1,0:T(8,128)(2,1)S(1)} %head_gather.1) | copy-start | bytes 2359300
  343.1 9.5 %copy-start.99 = (f32[512]{0:T(512)S(1)}, f32[512]{0:T(512)}, u32[]{:S(2)}) copy-start(f32[512]{0:T(512)} %get-tuple-element.297) | copy-start | bytes 6148
  343.1 19.8 %copy-start.45 = (f32[7680]{0:T(1024)S(1)}, f32[7680]{0:T(1024)}, u32[]{:S(2)}) copy-start(f32[7680]{0:T(1024)} %add.774) | copy-start | bytes 92164
  343.1 19.8 %copy-start.67 = (s32[512]{0:T(512)S(1)}, s32[512]{0:T(512)}, u32[]{:S(2)}) copy-start(s32[512]{0:T(512)} %fusion.113) | copy-start | bytes 6148
  343.1 29.9 %slice-start = ((s8[11796480]{0:T(1024)(128)(4,1)}), s8[4194304]{0:T(1024)(128)(4,1)S(1)}, s32[]{:S(2)}) async-start(s8[11796480]{0:T(1024)(128)(4,1)} %bitcast.325), calls=%async_computation.7 | async-start | bytes 8388608
  343.1 29.9 %slice-start.1 = ((s8[11796480]{0:T(1024)(128)(4,1)}), s8[3407872]{0:T(1024)(128)(4,1)S(1)}, s32[]{:S(2)}) async-start(s8[11796480]{0:T(1024)(128)(4,1)} %bitcast.325), calls=%async_computation.8 | async-start | bytes 6815744
  362.9 10.1 %slice-start.2 = ((s8[11796480]{0:T(1024)(128)(4,1)}), s8[4194304]{0:T(1024)(128)(4,1)S(1)}, s32[]{:S(2)}) async-start(s8[11796480]{0:T(1024)(128)(4,1)} %bitcast.325), calls=%async_computation.9 | async-start | bytes 8388608
  379.3 15.7 %copy-start.90 = (f32[128]{0:T(128)S(1)}, f32[128]{0:T(128)}, u32[]{:S(2)}) copy-start(f32[128]{0:T(128)} %copy-done.89) | copy-start | bytes 1540
  379.3 16.5 %copy-start.128 = (f32[128]{0:T(128)S(1)}, f32[128]{0:T(128)}, u32[]{:S(2)}) copy-start(f32[128]{0:T(128)} %copy-done.127) | copy-start | bytes 1540
  379.3 16.5 %copy-start.106 = (f32[128]{0:T(128)S(1)}, f32[128]{0:T(128)}, u32[]{:S(2)}) copy-start(f32[128]{0:T(128)} %copy-done.105) | copy-start | bytes 1540
  379.3 17.3 %copy-start.42 = (f32[128,768]{1,0:T(8,128)S(1)}, f32[128,768]{1,0:T(8,128)}, u32[]{:S(2)}) copy-start(f32[128,768]{1,0:T(8,128)} %get-tuple-element.296) | copy-start | bytes 1179652
  398.7 11.1 %copy-start.52 = (f32[512]{0:T(512)S(1)}, f32[512]{0:T(512)}, u32[]{:S(2)}) copy-start(f32[512]{0:T(512)} %copy-done.51) | copy-start | bytes 6148
  398.7 11.1 %copy-start.66 = (f32[512]{0:T(512)S(1)}, f32[512]{0:T(512)}, u32[]{:S(2)}) copy-start(f32[512]{0:T(512)} %copy-done.65) | copy-start | bytes 6148
  398.7 11.1 %copy-start.122 = (s32[512]{0:T(512)S(1)}, s32[512]{0:T(512)}, u32[]{:S(2)}) copy-start(s32[512]{0:T(512)} %iota_add_fusion) | copy-start | bytes 6148
  398.7 11.1 %copy-start.126 = (s32[256]{0:T(256)S(1)}, s32[256]{0:T(256)}, u32[]{:S(2)}) copy-start(s32[256]{0:T(256)} %pad_add_fusion.1) | copy-start | bytes 3076
  398.7 11.1 %copy-start.131 = (pred[512]{0:T(512)(128)(4,1)S(1)}, pred[512]{0:T(512)(128)(4,1)}, u32[]{:S(2)}) copy-start(pred[512]{0:T(512)(128)(4,1)} %iota_compare_fusion.6) | copy-start | bytes 1540
  411.9 7.1 slice-start.5
  443.9 330.2 %reduce-scatter.5.cloned.1.call-start = ((), (), s32[]{:S(2)}) async-start(), calls=%async_computation.6 | async-start | bytes 13271040 | tf_op jit(solution)/shard_map/reduce_scatter | solution.py:68
  557.2 71.6 %slice-start.3 = ((s8[7864320]{0:T(1024)(128)(4,1)}), s8[3670016]{0:T(1024)(128)(4,1)S(1)}, s32[]{:S(2)}) async-start(s8[7864320]{0:T(1024)(128)(4,1)} %bitcast.341), calls=%async_computation.10 | async-start | bytes 7340032
  592.3 36.5 %slice-start.4 = ((s8[7864320]{0:T(1024)(128)(4,1)}), s8[4194304]{0:T(1024)(128)(4,1)S(1)}, s32[]{:S(2)}) async-start(s8[7864320]{0:T(1024)(128)(4,1)} %bitcast.341), calls=%async_computation.11 | async-start | bytes 8388608
  710.0 39.3 %copy-start.46 = (bf16[192,768]{1,0:T(8,128)(2,1)S(1)}, bf16[192,768]{1,0:T(8,128)(2,1)}, u32[]{:S(2)}) copy-start(bf16[192,768]{1,0:T(8,128)(2,1)} %reduce-scatter.3.cloned.1.call-done) | copy-start | bytes 884740
  737.6 12.4 %copy-start.49 = (f32[4,6,192]{2,1,0:T(8,128)}, f32[4,6,192]{2,1,0:T(8,128)S(1)}, u32[]{:S(2)}) copy-start(f32[4,6,192]{2,1,0:T(8,128)S(1)} %reshape.969) | copy-start | bytes 55300
  793.0 7.3 copy-start.102
  793.0 7.3 copy-start.103
  793.0 8.0 copy-start.53
  793.0 8.0 copy-start.54
  793.0 10.7 %copy-start.43 = (f32[96,4,192]{2,1,0:T(4,128)S(1)}, f32[96,4,192]{2,1,0:T(4,128)}, u32[]{:S(2)}) copy-start(f32[96,4,192]{2,1,0:T(4,128)} %param.37) | copy-start | bytes 884740
  793.0 10.7 %copy-start.44 = (f32[96,4,192]{2,1,0:T(4,128)S(1)}, f32[96,4,192]{2,1,0:T(4,128)}, u32[]{:S(2)}) copy-start(f32[96,4,192]{2,1,0:T(4,128)} %param.38) | copy-start | bytes 884740
  797.6 7.8 copy-start.30
  (101 other events, 304.6 us)
Sparse Core Ops, SparseCore 0:
  11.5 72.8 all-gather.3
  88.0 103.6 all-gather.5
  195.3 92.4 all-gather.7
  444.0 157.5 reduce-scatter.2
  675.9 98.0 reduce-scatter.4

commit v4 on v3

--- a/solution.py
+++ b/solution.py
@@ -130,28 +130,44 @@
         return result
 
     def exchange(self, name, *moves):
-        outs, transfers = [], 0
+        outs, scratch = [], []
         for kind, axes, dim, _, value in moves:
             size = self.count(axes)
-            shape = value.shape
+            shape, sends, lands = value.shape, (size - 1,), (size - 1,)
             if kind == "gather":
                 shape = (size, *shape)
             elif kind == "swap":
                 shape = shape[:dim] + shape[dim + 1 :]
             elif kind == "spread":
                 shape = (size - 1, *shape[1:])
+            elif kind == "relay":
+                shape, sends = (size, *shape), (2, size - 1, shape[0])
+                lands = sends
+            elif kind == "plane":
+                shape, sends, lands = (2, 2, 2, *shape), (7 * shape[0],), (7, shape[0])
             outs.append(jax.ShapeDtypeStruct(shape, value.dtype))
-            transfers += size - 1
+            scratch += [
+                pltpu.SemaphoreType.DMA(sends),
+                pltpu.SemaphoreType.DMA(lands),
+                pltpu.SemaphoreType.DMA((1,)),
+            ]
         spaces = [m[3] for m in moves]
-        groups = list(dict.fromkeys(m[1] for m in moves))
+        groups = []
+        for kind, axes, *_ in moves:
+            groups += [(a,) for a in axes] if kind == "plane" else [axes]
+        groups = list(dict.fromkeys(groups))
 
         def kernel(*refs):
             ins, dests = refs[: len(moves)], refs[len(moves) : 2 * len(moves)]
-            sends, lands, own_sems = refs[2 * len(moves) :]
+            sems = refs[2 * len(moves) :]
             self.greet(groups)
-            started, slot = [], 0
-            for (kind, axes, dim, _, _), source, dest in zip(moves, ins, dests):
+            started, later = [], []
+            for i, ((kind, axes, dim, _, _), source, dest) in enumerate(zip(moves, ins, dests)):
+                sends, lands, own_sem = sems[3 * i : 3 * i + 3]
                 size, me = self.count(axes), self.place(axes)
+                if kind in ("relay", "plane"):
+                    act = self.relay if kind == "relay" else self.plane
+                    later.append(functools.partial(act, axes, source, dest, sends, lands))
                 for r in range(1, size):
                     peer = lax.rem(me + r, size)
                     if kind == "gather":
@@ -160,26 +176,33 @@
                         src, dst = source.at[(slice(None),) * dim + (peer,)], dest
                     elif kind == "spread":
                         src, dst = source.at[peer], dest.at[r - 1]
+                    elif kind == "trade":
+                        src, dst = source, dest
                     else:
-                        src, dst = source, dest
+                        continue
                     copy = pltpu.make_async_remote_copy(
                         src_ref=src,
                         dst_ref=dst,
-                        send_sem=sends.at[slot],
-                        recv_sem=lands.at[slot],
+                        send_sem=sends.at[r - 1],
+                        recv_sem=lands.at[r - 1],
                         device_id=self.target(axes, peer),
                         device_id_type=MESH,
                     )
                     copy.start()
                     started.append(copy)
-                    slot += 1
-            for number, ((kind, axes, _, _, _), source, dest) in enumerate(zip(moves, ins, dests)):
-                if kind == "gather":
-                    copy = pltpu.make_async_copy(
-                        source, dest.at[self.place(axes)], own_sems.at[number]
-                    )
+            runs = [act() for act in later]
+            for run in runs:
+                next(run)
+            for i, ((kind, axes, *_), source, dest) in enumerate(zip(moves, ins, dests)):
+                if kind in ("gather", "relay", "plane"):
+                    at = self.place(axes)
+                    if kind == "plane":
+                        at = tuple(lax.axis_index(a) for a in axes)
+                    copy = pltpu.make_async_copy(source, dest.at[at], sems[3 * i + 2].at[0])
                     copy.start()
                     started.append(copy)
+            for run in runs:
+                next(run, None)
             for copy in started:
                 copy.wait()
 
@@ -188,15 +211,132 @@
             outs,
             spaces,
             spaces,
-            [
-                pltpu.SemaphoreType.DMA((transfers,)),
-                pltpu.SemaphoreType.DMA((transfers,)),
-                pltpu.SemaphoreType.DMA((len(moves),)),
-            ],
+            scratch,
             [m[4] for m in moves],
             sum(2 * math.prod(o.shape) * o.dtype.itemsize for o in outs),
             name,
         )
+
+    def relay(self, axes, source, dest, sends, lands):
+        (axis,) = axes
+        size, parts = self.sizes[axis], source.shape[0]
+        me = lax.axis_index(axis)
+
+        def copy_of(way, hop, part):
+            step = 1 if way == 0 else -1
+            place = (me - step * hop, part)
+            return pltpu.make_async_remote_copy(
+                src_ref=source.at[part] if hop == 0 else dest.at[place],
+                dst_ref=dest.at[place],
+                send_sem=sends.at[way, hop, part],
+                recv_sem=lands.at[way, hop, part],
+                device_id={axis: me + step},
+                device_id_type=MESH,
+            )
+
+        def landing(way, hop, part):
+            step = 1 if way == 0 else -1
+            landed = dest.at[me - step * hop, part]
+            return pltpu.make_async_remote_copy(
+                src_ref=landed,
+                dst_ref=landed,
+                send_sem=sends.at[way, hop - 1, part],
+                recv_sem=lands.at[way, hop - 1, part],
+                device_id={axis: me - step},
+                device_id_type=MESH,
+            )
+
+        def held(way, hop):
+            return me - hop >= 0 if way == 0 else me + hop <= size - 1
+
+        def sending(way, hop):
+            return held(way, hop) & (me < size - 1 if way == 0 else me > 0)
+
+        for hop in range(size):
+            for part in range(parts):
+                for way in range(2):
+                    if hop > 0:
+
+                        @pl.when(held(way, hop))
+                        def _():
+                            landing(way, hop, part).wait_recv()
+
+                    if hop < size - 1:
+
+                        @pl.when(sending(way, hop))
+                        def _():
+                            copy_of(way, hop, part).start()
+
+            if hop == 0:
+                yield
+        for hop in range(size - 1):
+            for part in range(parts):
+                for way in range(2):
+
+                    @pl.when(sending(way, hop))
+                    def _():
+                        copy_of(way, hop, part).wait_send()
+
+    def plane(self, axes, own, out, sends, lands):
+        parts = own.shape[0]
+        head = (parts + 1) // 2
+        x, y, c = (lax.axis_index(a) for a in axes)
+        by_x, by_y, by_c = {"x": 1 - x}, {"y": 1 - y}, {"c": 1 - c}
+        started = []
+
+        def send(src, place, part, slot, peer):
+            copy = pltpu.make_async_remote_copy(
+                src_ref=src,
+                dst_ref=out.at[(*place, part)],
+                send_sem=sends.at[len(started)],
+                recv_sem=lands.at[slot, part],
+                device_id=peer,
+                device_id_type=MESH,
+            )
+            copy.start()
+            started.append(copy)
+
+        def arrived(place, part, slot):
+            landed = out.at[(*place, part)]
+            pltpu.make_async_remote_copy(
+                src_ref=landed,
+                dst_ref=landed,
+                send_sem=sends.at[0],
+                recv_sem=lands.at[slot, part],
+                device_id=by_c,
+                device_id_type=MESH,
+            ).wait_recv()
+            return landed
+
+        me, at_x, at_y, at_xy = (x, y, c), (1 - x, y, c), (x, 1 - y, c), (1 - x, 1 - y, c)
+        for part in range(parts):
+            send(own.at[part], me, part, 0, by_x)
+            send(own.at[part], me, part, 1, by_y)
+        for part in range(parts):
+            send(own.at[part], me, part, 3, by_c)
+        yield
+        for part in range(parts):
+            landed = arrived(at_x, part, 0)
+            if part < head:
+                send(landed, at_x, part, 2, by_y)
+            send(landed, at_x, part, 4, by_c)
+            landed = arrived(at_y, part, 1)
+            if part >= head:
+                send(landed, at_y, part, 2, by_x)
+            send(landed, at_y, part, 5, by_c)
+        for part in range(parts):
+            landed = arrived(at_xy, part, 2)
+            send(landed, at_xy, part, 6, by_c)
+        for slot, place in ((3, me), (4, at_x), (5, at_y), (6, at_xy)):
+            for part in range(parts):
+                arrived((place[0], place[1], 1 - c), part, slot)
+        for copy in started:
+            copy.wait_send()
+
+    def line_move(self, value, part_rows, memory):
+        parts = value.shape[0] // part_rows if value.shape[0] % part_rows == 0 else 1
+        kind = "relay" if self.sizes["z"] <= 8 else "gather"
+        return (kind, ("z",), 0, memory, value.reshape(parts, -1, value.shape[1]))
 
     def combine(self, name, value):
         pairs = [a for a in ("c", "x", "y") if self.sizes[a] > 1]
@@ -251,85 +391,6 @@
             name,
         )[0]
 
-    def gather_plane(self, name, value):
-        rows, width = value.shape
-        parts = 4 if rows % 64 == 0 else 1
-        head = (parts + 1) // 2
-        value = value.reshape(parts, rows // parts, width)
-        shape = (*(self.sizes[a] for a in ("x", "y", "c")), *value.shape)
-
-        def kernel(own, out, sends, lands, own_sem):
-            self.greet([("x",), ("y",), ("c",)])
-            x, y, c = (lax.axis_index(a) for a in ("x", "y", "c"))
-            by_x, by_y, by_c = {"x": 1 - x}, {"y": 1 - y}, {"c": 1 - c}
-            started = []
-
-            def send(src, place, part, slot, peer):
-                copy = pltpu.make_async_remote_copy(
-                    src_ref=src,
-                    dst_ref=out.at[(*place, part)],
-                    send_sem=sends.at[len(started)],
-                    recv_sem=lands.at[slot, part],
-                    device_id=peer,
-                    device_id_type=MESH,
-                )
-                copy.start()
-                started.append(copy)
-
-            def arrived(place, part, slot):
-                landed = out.at[(*place, part)]
-                pltpu.make_async_remote_copy(
-                    src_ref=landed,
-                    dst_ref=landed,
-                    send_sem=sends.at[0],
-                    recv_sem=lands.at[slot, part],
-                    device_id=by_c,
-                    device_id_type=MESH,
-                ).wait_recv()
-                return landed
-
-            me, at_x, at_y, at_xy = (x, y, c), (1 - x, y, c), (x, 1 - y, c), (1 - x, 1 - y, c)
-            for part in range(parts):
-                send(own.at[part], me, part, 0, by_x)
-                send(own.at[part], me, part, 1, by_y)
-            for part in range(parts):
-                send(own.at[part], me, part, 3, by_c)
-            local = pltpu.make_async_copy(own, out.at[me], own_sem.at[0])
-            local.start()
-            for part in range(parts):
-                landed = arrived(at_x, part, 0)
-                if part < head:
-                    send(landed, at_x, part, 2, by_y)
-                send(landed, at_x, part, 4, by_c)
-                landed = arrived(at_y, part, 1)
-                if part >= head:
-                    send(landed, at_y, part, 2, by_x)
-                send(landed, at_y, part, 5, by_c)
-            for part in range(parts):
-                landed = arrived(at_xy, part, 2)
-                send(landed, at_xy, part, 6, by_c)
-            for slot, place in ((3, me), (4, at_x), (5, at_y), (6, at_xy)):
-                for part in range(parts):
-                    arrived((place[0], place[1], 1 - c), part, slot)
-            for copy in started:
-                copy.wait_send()
-            local.wait()
-
-        return self.call(
-            kernel,
-            [jax.ShapeDtypeStruct(shape, value.dtype)],
-            [BIG],
-            [BIG],
-            [
-                pltpu.SemaphoreType.DMA((7 * parts,)),
-                pltpu.SemaphoreType.DMA((7, parts)),
-                pltpu.SemaphoreType.DMA((1,)),
-            ],
-            [value],
-            4 * math.prod(shape),
-            name,
-        )[0].reshape(-1, width)
-
 
 def row_major(value):
     return with_layout_constraint(value, Layout(major_to_minor=tuple(range(value.ndim))))
@@ -483,12 +544,11 @@
     first_core = (c_at == 0).astype(jnp.float32)
 
     side_rows = side_weight.shape[0] // mp_size
-    side_full = comm_all_gather(
-        lax.dynamic_slice_in_dim(side_weight.astype(low), mp_rank * side_rows, side_rows, 0), every
-    )
-    attn_blocks = comm_all_gather(
-        attn_weight.astype(low).reshape(rows_own, 4 * attn_cols), mp_first
-    ).reshape(mp_size, D, 4 * attn_cols)
+    side_own = lax.dynamic_slice_in_dim(side_weight, mp_rank * side_rows, side_rows, 0)
+    both = jnp.concatenate([attn_weight.reshape(rows_own, 4 * attn_cols), side_own]).astype(low)
+    both = comm_all_gather(both, mp_first).reshape(mp_size, dp_size, -1, D)
+    attn_blocks = both[:, :, :rows_own].reshape(mp_size, D, 4 * attn_cols)
+    side_full = both[:, :, rows_own:].transpose(1, 0, 2, 3).reshape(-1, D)
     ff_blocks = comm_all_gather(
         ff_weight.astype(low).reshape(rows_own, 2 * ff_cols), mp_first
     ).reshape(mp_size, D, 2 * ff_cols)
@@ -496,8 +556,10 @@
     stripe = vocab_own * x_size
     bias_mine = lax.dynamic_slice_in_dim(decoder_bias, z_at * stripe, stripe, 0)
     int_count = own_len + 2 * own_slots
-    ints, vec_parts, counts, mp_small = links.exchange(
-        "small_gather",
+    word_parts = 4 if vocab_own % 64 == 0 else 1
+    word_plane, ints, vec_parts, counts, mp_small = links.exchange(
+        "word_gather",
+        ("plane", plane, 0, BIG, word_table.astype(low).reshape(word_parts, -1, D)),
         ("gather", ("z",), 0, FAST, lanes(jnp.concatenate([own_ids, own_labels, own_valid]))),
         ("gather", ("z", "x"), 0, FAST, jnp.pad(vectors.astype(low), ((0, 0), (0, 128 - vec_cols)))),
         (
@@ -524,7 +586,7 @@
         .astype(jnp.float32)
     )
     mp_small = mp_small.reshape(mp_size, -1)
-    word_plane = links.gather_plane("word_gather", word_table.astype(low))
+    word_plane = word_plane.reshape(-1, D)
     bias_plane = (
         mp_small[:, :stripe].reshape(mp_size, x_size, vocab_own).transpose(1, 0, 2).reshape(-1)
     )
@@ -592,7 +654,7 @@
     dense_out = jnp.dot(picked_b, dense_w, preferred_element_type=jnp.float32) + vec_rows[8]
     act_dense = gelu_exact(dense_out)
     head_rows = layer_norm(act_dense, vec_rows[9], vec_rows[10])
-    (head_b,) = links.exchange("head_gather", ("gather", ("z",), 0, FAST, head_rows.astype(low)))
+    (head_b,) = links.exchange("head_gather", links.line_move(head_rows.astype(low), 32, FAST))
     head_b = head_b.reshape(-1, D)
     row_count = head_b.shape[0]
     logits = (
@@ -731,26 +793,27 @@
         "grad_swap_c",
         ("swap", ("c",), 1, BIG, attn_grad),
         ("swap", ("c",), 3, BIG, side_grad),
-        ("gather", ("z",), 0, BIG, x0_b[:cut_one]),
+        links.line_move(x0_b[:cut_one], 64, BIG),
     )
     attn_grad, side_grad = joined(attn_grad, c_at, 1, from_a), joined(side_grad, c_at, 3, from_s)
     from_a, from_s, x0_two = links.exchange(
         "grad_swap_xy",
         ("swap", ("x",), 2, BIG, attn_grad),
         ("swap", ("y",), 2, BIG, side_grad),
-        ("gather", ("z",), 0, BIG, x0_b[cut_one:cut_two]),
+        links.line_move(x0_b[cut_one:cut_two], 64, BIG),
     )
     attn_grad, side_grad = joined(attn_grad, x_at, 2, from_a), joined(side_grad, y_at, 2, from_s)
     from_a, from_s, x0_three = links.exchange(
         "grad_swap_yx",
         ("swap", ("y",), 0, BIG, attn_grad),
         ("swap", ("x",), 1, BIG, side_grad),
-        ("gather", ("z",), 0, BIG, x0_b[cut_two:]),
+        links.line_move(x0_b[cut_two:], 64, BIG),
     )
     attn_grad, side_grad = joined(attn_grad, y_at, 0, from_a), joined(side_grad, x_at, 1, from_s)
 
     ff_red, x0_three = lax.optimization_barrier((ff_red, x0_three))
-    all_x0 = jnp.concatenate([x0_one, x0_two, x0_three], axis=1).reshape(-1, D)
+    all_x0 = [x.reshape(z_size, -1, D) for x in (x0_one, x0_two, x0_three)]
+    all_x0 = jnp.concatenate(all_x0, axis=1).reshape(-1, D)
     onehot = (
         jnp.where(inside, at, -1)[None, :]
         == lax.broadcasted_iota(jnp.int32, (word_plane.shape[0], flat_ids.shape[0]), 0)
@@ -813,7 +876,7 @@
     word_f, attn_f, ff_f = (
         word_red,
         attn_red.reshape(attn_weight.shape),
-        lax.optimization_barrier(
+        row_major(
             ff_red.astype(jnp.float32).reshape(2, rows_own, ff_cols).transpose(1, 0, 2)
         ),
     )

time: 829 us -> 818 us (0.987)
  waiting for transfers between devices: 57.2 us -> 19.4 us
  Pallas kernels: 407 us -> 421 us
    all_gather x3 -> x2, waiting for transfers between devices: 37.2 us -> 0.02 us  [comm_all_gather(): return lax.all_gather(value, axes, axis=0, tiled=True)]
    pallas_call x17 -> x16, Pallas kernels: 361 us -> 375 us  [call(): pl.pallas_call(kernel, out_shape=outs, in_specs=[pl.BlockSpec(memory_spac...]
    dot_general x1, matrix products: 15 us -> 26.4 us  [step(): jnp.einsum('rd,vd->rv', head_b, word_plane, preferred_element_type=jnp.fl...]
    unnamed x304 -> x295, local copies, waits for them, and re-layouts: 37 us -> 34 us
  transfers between devices with their start and end apart: 5 -> 4, of which waited for: 2 -> 1; matrix products, arithmetic and copies ran while one was open for 17% -> 17% of each run, Pallas kernels for 43% -> 42%
where the time goes in v4:
time: 818 us; the launch traced here: 807 us
  Pallas kernels  421 us (51%)
  matrix products  135 us (17%)
  local copies, waits for them, and re-layouts  105 us (13%)
  other arithmetic  101 us (12%)
  between operations  25.4 us (3%)
  waiting for transfers between devices  19.4 us (2%)
    pallas_call x16, Pallas kernels, call(): pl.pallas_call(kernel, out_shape=outs, in_specs=[pl.BlockSpec(memory_spac...  375 us
    unnamed x295, local copies, waits for them, and re-layouts  34 us
    dot_general x1, matrix products, step(): jnp.dot(onehot, all_x0, preferred_element_type=jnp.float32)  33.9 us
    dot_general x1, matrix products, step(): jnp.einsum('rd,vd->rv', head_b, word_plane, preferred_element_type=jnp.fl...  26.4 us
    pallas_call x1, Pallas kernels, attention_backward(): pl.pallas_call(backward_kernel, grid=(pairs,), out_shape=[jax.ShapeDtypeS...  23.7 us
    pallas_call x1, Pallas kernels, attention_forward(): pl.pallas_call(forward_kernel, grid=(pairs,), out_shape=[jax.ShapeDtypeSt...  22.7 us
    reduce_scatter x2, waiting for transfers between devices, comm_scatter_sum(): return lax.psum_scatter(value, axes, scatter_dimension=0, tiled=True)  19.3 us
    sub x7, other arithmetic, adam_step(): return (weight - learn_rate * change, moment, square)  18 us
  transfers between devices with their start and end apart: 4, of which 1 were waited for; matrix products, arithmetic and copies ran while one was open for 17% of the time, Pallas kernels for 42%

profile of v4, /device:TPU:0, one launch (start us, length us, event | category | flops | bytes accessed | tf_op | source)
XLA Modules:
  0.0 807.3 jit_solution(17879602889596936656)
XLA Ops:
  17.1 76.4 %word_gather.1 = (bf16[2,2,2,4,240,768]{5,4,3,2,1,0:T(8,128)(2,1)S(1)}, s32[4,8,128]{2,1,0:T(8,128)S(1)}, bf16[8,16,128]{2,1,0:T(8,128)(2,1)S(1)}, f32[8,8,128]{2,1,0:T(8,128)S(1)}, f32[4,24,128]{2,1,0:T(8,128)S(1)}) custom-call(bf16[4,240,768]{2,1,0:T(8,128)(2,1)S(1)} %bitcast.351, s32[8,128]{1,0:T(8,128)S(1)} %pad_bitcast_fusion.refs_1_, ...), custom_call_target="tpu_custom_call" | custom-call | bytes 23855104 | tf_op jit(solution)/shard_map/word_gather/pallas_call | solution.py:116
  93.5 4.4 copy-done
  99.4 16.0 %gather_fusion = bf16[2048,768]{1,0:T(8,128)(2,1)} fusion(bf16[7680,768]{1,0:T(8,128)(2,1)} %bitcast.344, s32[2048]{0:T(1024)S(1)} %broadcast_clamp_fusion), kind=kCustom, calls=%fused_computation | custom fusion | bytes 6299648 | tf_op jit(solution)/shard_map/gather | solution.py:604
  117.6 67.4 %token_spread.1 = bf16[3,512,768]{2,1,0:T(8,128)(2,1)S(1)} custom-call(bf16[4,512,768]{2,1,0:T(8,128)(2,1)S(1)} %broadcast_select_fusion.refs_0_), custom_call_target="tpu_custom_call" | custom-call | bytes 4718592 | tf_op jit(solution)/shard_map/token_spread/pallas_call | solution.py:116
  198.4 3.3 convert_reduce_fusion.3
  201.7 3.9 slice.259
  205.7 4.1 slice_bitcast_fusion
  219.1 3.3 copy.229
  222.6 3.7 key_trade.1
  229.0 22.7 %attention_forward.1 = (bf16[512,768]{1,0:T(8,128)(2,1)}, f32[6,2,512]{2,1,0:T(2,128)}) custom-call(bf16[512,768]{1,0:T(8,128)(2,1)} %add_convert_fusion.5.q_ref, bf16[512,768]{1,0:T(8,128)(2,1)} %copy-done.2, bf16[512,768]{1,0:T(8,128)(2,1)} %copy-done.9, bf16[512,768]{1,0:T(8,128)(2,1)} %copy-done.3, bf16[512,768]{1,0:T(8,128)(2,1)} %copy-done.10), custom_call_target="tpu_custom_call" | custom-call | flops 3221225472 | bytes 6291456 | tf_op jit(solution)/shard_map/attention_forward/pallas_call | solution.py:444
  254.1 3.6 fusion.164
  258.1 6.9 fusion.11
  265.0 2.9 fusion.165
  278.0 46.9 %head_gather.1 = bf16[4,4,32,768]{3,2,1,0:T(8,128)(2,1)S(1)} custom-call(bf16[4,32,768]{2,1,0:T(8,128)(2,1)S(1)} %bitcast.359), custom_call_target="tpu_custom_call" | custom-call | bytes 1572864 | tf_op jit(solution)/shard_map/head_gather/pallas_call | solution.py:116
  324.9 26.4 %add_reduce_fusion = (f32[512]{0:T(512)}, f32[512,7680]{1,0:T(8,128)}) fusion(f32[7680]{0:T(1024)} %add.774, bf16[512,768]{1,0:T(8,128)(2,1)S(1)} %bitcast.357, bf16[7680,768]{1,0:T(8,128)(2,1)} %bitcast.345), kind=kOutput, calls=%fused_computation.11 | convolution fusion | flops 6047661568 | bytes 28344320 | tf_op jit(solution)/shard_map/rd,vd->rv/dot_general | solution.py:661
  351.3 9.5 %exponential_reduce_fusion = (f32[512]{0:T(512)S(1)}, f32[512]{0:T(512)S(1)}) fusion(f32[512,7680]{1,0:T(8,128)} %get-tuple-element.208, f32[512]{0:T(512)} %get-tuple-element.207, f32[7680]{0:T(1024)} %add.774, s32[512]{0:T(512)} %fusion.113), kind=kLoop, calls=%fused_computation.10 | loop fusion | flops 23591936 | bytes 15767552 | tf_op jit(solution)/shard_map/reduce_sum | solution.py:668
  360.8 5.7 stat_gather.1
  368.6 9.7 %convert_reduce_fusion = (f32[7680]{0:T(1024)}, bf16[512,7680]{1,0:T(8,128)(2,1)S(1)}) fusion(f32[512]{0:T(512)S(1)} %get-tuple-element.191, s32[512]{0:T(512)S(1)} %copy-done.71, f32[512]{0:T(512)S(1)} %get-tuple-element.174, f32[512,7680]{1,0:T(8,128)} %get-tuple-element.208, f32[7680]{0:T(1024)S(1)} %copy-done.49), kind=kLoop, calls=%fused_computation.6 | loop fusion | flops 35381760 | bytes 23660544 | tf_op jit(solution)/shard_map/reduce_sum | solution.py:682
  378.3 6.2 fusion.167
  384.6 15.5 %head_spread.1 = bf16[3,128,768]{2,1,0:T(8,128)(2,1)S(1)} custom-call(bf16[4,128,768]{2,1,0:T(8,128)(2,1)S(1)} %get-tuple-element.211.refs_0_), custom_call_target="tpu_custom_call" | custom-call | bytes 1179648 | tf_op jit(solution)/shard_map/head_spread/pallas_call | solution.py:116
  419.6 4.5 convolution_convert_fusion
  425.9 6.1 convert_reduce_fusion.1
  432.0 5.2 convolution_convert_fusion.1
  437.2 3.8 fusion.40
  440.9 8.2 %pad_maximum_fusion = bf16[32,2,96,768]{3,2,1,0:T(8,128)(2,1)} fusion(bf16[32,1,96,768]{3,2,1,0:T(8,128)(2,1)} %bitcast.383, bf16[32,1,96,768]{3,2,1,0:T(8,128)(2,1)} %bitcast.384), kind=kLoop, calls=%fused_computation.13 | loop fusion | flops 4718592 | bytes 18874368 | tf_op jit(solution)/shard_map/stack | solution.py:729
  450.5 3.2 slice.267
  455.4 3.3 multiply_reduce_fusion.1
  462.1 23.7 %attention_backward.1 = (bf16[512,768]{1,0:T(8,128)(2,1)}, f32[512,768]{1,0:T(8,128)}, f32[512,768]{1,0:T(8,128)}, f32[512,768]{1,0:T(8,128)}, f32[512,768]{1,0:T(8,128)}) custom-call(bf16[512,768]{1,0:T(8,128)(2,1)} %add_convert_fusion.5.q_ref, bf16[512,768]{1,0:T(8,128)(2,1)} %copy-done.2, bf16[512,768]{1,0:T(8,128)(2,1)} %copy-done.9, ...), custom_call_target="tpu_custom_call" | custom-call | flops 8053063680 | bytes 12582912 | tf_op jit(solution)/shard_map/attention_backward/pallas_call | solution.py:497
  488.8 6.6 key_grad_trade.1
  506.0 5.1 multiply_reduce_fusion.2
  514.3 4.1 convert_bitcast_fusion
  518.4 6.1 copy.251
  529.0 4.6 copy.253
  533.7 4.0 pad_maximum_fusion.1
  540.3 20.0 %grad_swap_c.1 = (bf16[2,4,2,96,768]{4,3,2,1,0:T(8,128)(2,1)S(1)}, bf16[4,2,2,80,768]{4,3,2,1,0:T(8,128)(2,1)S(1)}, bf16[4,1,64,768]{3,2,1,0:T(8,128)(2,1)S(1)}) custom-call(bf16[2,2,4,2,96,768]{5,4,3,2,1,0:T(8,128)(2,1)S(1)} %copy.254.refs_0_, bf16[4,2,2,2,80,768]{5,4,3,2,1,0:T(8,128)(2,1)S(1)} %bitcast.349, bf16[1,64,768]{2,1,0:T(8,128)(2,1)S(1)} %slice_bitcast_fusion.1.refs_2_), custom_call_target="tpu_custom_call" | custom-call | bytes 9437184 | tf_op jit(solution)/shard_map/grad_swap_c/pallas_call | solution.py:116
  564.1 36.6 %grad_swap_xy.1 = (bf16[2,4,96,768]{3,2,1,0:T(8,128)(2,1)S(1)}, bf16[4,2,80,768]{3,2,1,0:T(8,128)(2,1)S(1)}, bf16[4,4,64,768]{3,2,1,0:T(8,128)(2,1)S(1)}) custom-call(bf16[2,4,2,96,768]{4,3,2,1,0:T(8,128)(2,1)S(1)} %copy.258.refs_0_, bf16[4,2,2,80,768]{4,3,2,1,0:T(8,128)(2,1)S(1)} %copy.259.refs_1_, bf16[4,64,768]{2,1,0:T(8,128)(2,1)S(1)} %bitcast.352), custom_call_target="tpu_custom_call" | custom-call | bytes 7471104 | tf_op jit(solution)/shard_map/grad_swap_xy/pallas_call | solution.py:116
  601.3 22.0 %grad_swap_yx.1 = (bf16[4,96,768]{2,1,0:T(8,128)(2,1)S(1)}, bf16[4,80,768]{2,1,0:T(8,128)(2,1)S(1)}, bf16[4,3,64,768]{3,2,1,0:T(8,128)(2,1)S(1)}) custom-call(bf16[2,4,96,768]{3,2,1,0:T(8,128)(2,1)S(1)} %fusion.34.refs_0_, bf16[4,2,80,768]{3,2,1,0:T(8,128)(2,1)S(1)} %copy.261.refs_1_, bf16[3,64,768]{2,1,0:T(8,128)(2,1)S(1)} %bitcast.355), custom_call_target="tpu_custom_call" | custom-call | bytes 4521984 | tf_op jit(solution)/shard_map/grad_swap_yx/pallas_call | solution.py:116
  624.5 11.1 %fusion.170 = f32[7680,768]{1,0:T(8,128)} fusion(bf16[512,7680]{1,0:T(8,128)(2,1)S(1)} %bitcast.380, bf16[512,768]{1,0:T(8,128)(2,1)S(1)} %bitcast.358), kind=kOutput, calls=%fused_computation.399 | convolution fusion | flops 6039797760 | bytes 32243712 | tf_op jit(solution)/shard_map/rv,rd->vd/dot_general | solution.py:821
  637.1 33.9 %add_convert_fusion = bf16[7680,768]{1,0:T(8,128)(2,1)} fusion(f32[7680,768]{1,0:T(8,128)} %fusion.170, bf16[2048,768]{1,0:T(8,128)(2,1)S(1)} %bitcast.387, s32[2048]{0:T(1024)S(1)} %copy-done.102), kind=kOutput, calls=%fused_computation.5 | convolution fusion | flops 24186716160 | bytes 38543360 | tf_op jit(solution)/shard_map/dot_general | solution.py:822
  676.6 23.8 %grad_spread_z.1 = (bf16[3,96,768]{2,1,0:T(8,128)(2,1)S(1)}, bf16[3,80,768]{2,1,0:T(8,128)(2,1)S(1)}) custom-call(bf16[4,96,768]{2,1,0:T(8,128)(2,1)S(1)} %fusion.50.refs_0_, bf16[4,80,768]{2,1,0:T(8,128)(2,1)S(1)} %fusion.59.refs_1_), custom_call_target="tpu_custom_call" | custom-call | bytes 1622016 | tf_op jit(solution)/shard_map/grad_spread_z/pallas_call | solution.py:116
  700.5 23.8 %small_sum.1 = f32[4,192,128]{2,1,0:T(8,128)S(1)} custom-call(f32[192,128]{1,0:T(8,128)S(1)} %maximum_bitcast_fusion.x_ref), custom_call_target="tpu_custom_call" | custom-call | bytes 1572864 | tf_op jit(solution)/shard_map/small_sum/pallas_call | solution.py:116
  726.3 10.1 %side_gather.1 = bf16[4,80,768]{2,1,0:T(8,128)(2,1)S(1)} custom-call(bf16[80,768]{1,0:T(8,128)(2,1)S(1)} %convert_add_fusion.7.refs_0_), custom_call_target="tpu_custom_call" | custom-call | bytes 983040 | tf_op jit(solution)/shard_map/side_gather/pallas_call | solution.py:116
  743.1 19.3 %reduce-scatter.5.cloned.1.call-done = bf16[960,768]{1,0:T(8,128)(2,1)} async-done(((bf16[7680,768]{1,0:T(8,128)(2,1)}), bf16[960,768]{1,0:T(8,128)(2,1)}) %reduce-scatter.5.cloned.1.call-update) | async-done | bytes 1474576 | tf_op jit(solution)/shard_map/reduce_scatter | solution.py:68
  762.4 2.7 fusion.28
  767.2 12.5 %norm_sum.1 = f32[4,8,128]{2,1,0:T(8,128)S(1)} custom-call(f32[8,128]{1,0:T(8,128)S(1)} %iota.41.x_ref), custom_call_target="tpu_custom_call" | custom-call | bytes 65536 | tf_op jit(solution)/shard_map/norm_sum/pallas_call | solution.py:116
  784.3 4.9 multiply_subtract_fusion.2
  792.1 3.2 multiply_subtract_fusion.3
  795.2 4.3 multiply_subtract_fusion
  (519 shorter events, 126.9 us)
Async XLA Ops:
  7.2 194.5 %all-gather.3.cloned.1.call-start = ((), (), s32[]{:S(2)}) async-start(), calls=%async_computation.2 | async-start | bytes 8921088 | tf_op jit(solution)/shard_map/all_gather | solution.py:64
  10.3 247.7 %all-gather.5.cloned.1.call-start = ((), (), s32[]{:S(2)}) async-start(), calls=%async_computation.3 | async-start | bytes 9732096 | tf_op jit(solution)/shard_map/all_gather | solution.py:64
  11.3 624.2 %reduce-scatter.3.cloned.1.call-start = ((), (), s32[]{:S(2)}) async-start(), calls=%async_computation.4 | async-start | bytes 9732096 | tf_op jit(solution)/shard_map/reduce_scatter | solution.py:68
  98.0 99.8 %copy-start.53 = (s32[1,4,8,128]{3,1,2,0:T(4,128)}, s32[1,4,8,128]{3,1,2,0:T(4,128)S(1)}, u32[]{:S(2)}) copy-start(s32[1,4,8,128]{3,1,2,0:T(4,128)S(1)} %copy.322) | copy-start | bytes 49156
  117.6 75.8 %copy-start.127 = (s32[2]{0:T(128)S(1)}, s32[2]{0:T(128)}, u32[]{:S(2)}) copy-start(s32[2]{0:T(128)} %param.32) | copy-start | bytes 28
  117.6 78.2 %copy-start.122 = (s32[2,256]{1,0:T(2,128)S(1)}, s32[2,256]{1,0:T(2,128)}, u32[]{:S(2)}) copy-start(s32[2,256]{1,0:T(2,128)} %param.29) | copy-start | bytes 6148
  186.8 67.2 %copy-start.89 = (f32[768]{0:T(1024)}, f32[768]{0:T(1024)S(1)}, u32[]{:S(2)}) copy-start(f32[768]{0:T(1024)S(1)} %mul.790) | copy-start | bytes 9220
  186.9 67.2 %copy-start.110 = (f32[768]{0:T(1024)}, f32[768]{0:T(1024)S(1)}, u32[]{:S(2)}) copy-start(f32[768]{0:T(1024)S(1)} %add.732) | copy-start | bytes 9220
  187.4 77.6 %copy-start.112 = (f32[768]{0:T(1024)}, f32[768]{0:T(1024)S(1)}, u32[]{:S(2)}) copy-start(f32[768]{0:T(1024)S(1)} %add.746) | copy-start | bytes 9220
  189.6 68.5 %copy-start.95 = (f32[4,768]{1,0:T(4,128)}, f32[4,768]{1,0:T(4,128)S(1)}, u32[]{:S(2)}) copy-start(f32[4,768]{1,0:T(4,128)S(1)} %add.749) | copy-start | bytes 36868
  195.3 14.8 %copy-start.105 = (pred[512]{0:T(512)(128)(4,1)}, pred[512]{0:T(512)(128)(4,1)S(1)}, u32[]{:S(2)}) copy-start(pred[512]{0:T(512)(128)(4,1)S(1)} %get-tuple-element.131) | copy-start | bytes 1540
  212.0 42.1 %copy-start.65 = (f32[512]{0:T(512)}, f32[512]{0:T(512)S(1)}, u32[]{:S(2)}) copy-start(f32[512]{0:T(512)S(1)} %broadcast_multiply_fusion.3) | copy-start | bytes 6148
  212.3 41.8 %copy-start.99 = (f32[512]{0:T(512)}, f32[512]{0:T(512)S(1)}, u32[]{:S(2)}) copy-start(f32[512]{0:T(512)S(1)} %fusion.122) | copy-start | bytes 6148
  229.0 25.1 %copy-start.15 = (f32[512,768]{1,0:T(8,128)S(1)}, f32[512,768]{1,0:T(8,128)}, u32[]{:S(2)}) copy-start(f32[512,768]{1,0:T(8,128)} %copy-done.14) | copy-start | bytes 4718596
  257.7 7.4 copy-start.17
  324.9 26.4 %copy-start.7 = (bf16[4,4,32,768]{3,2,1,0:T(8,128)(2,1)}, bf16[4,4,32,768]{3,2,1,0:T(8,128)(2,1)S(1)}, u32[]{:S(2)}) copy-start(bf16[4,4,32,768]{3,2,1,0:T(8,128)(2,1)S(1)} %head_gather.1) | copy-start | bytes 2359300
  351.3 9.5 %copy-start.101 = (f32[512]{0:T(512)S(1)}, f32[512]{0:T(512)}, u32[]{:S(2)}) copy-start(f32[512]{0:T(512)} %get-tuple-element.207) | copy-start | bytes 6148
  351.3 17.3 %copy-start.49 = (f32[7680]{0:T(1024)S(1)}, f32[7680]{0:T(1024)}, u32[]{:S(2)}) copy-start(f32[7680]{0:T(1024)} %add.774) | copy-start | bytes 92164
  351.3 17.3 %copy-start.71 = (s32[512]{0:T(512)S(1)}, s32[512]{0:T(512)}, u32[]{:S(2)}) copy-start(s32[512]{0:T(512)} %fusion.113) | copy-start | bytes 6148
  351.3 27.0 %slice-start = ((s8[11796480]{0:T(1024)(128)(4,1)}), s8[4194304]{0:T(1024)(128)(4,1)S(1)}, s32[]{:S(2)}) async-start(s8[11796480]{0:T(1024)(128)(4,1)} %bitcast.346), calls=%async_computation.6 | async-start | bytes 8388608
  351.3 27.0 %slice-start.1 = ((s8[11796480]{0:T(1024)(128)(4,1)}), s8[3407872]{0:T(1024)(128)(4,1)S(1)}, s32[]{:S(2)}) async-start(s8[11796480]{0:T(1024)(128)(4,1)} %bitcast.346), calls=%async_computation.7 | async-start | bytes 6815744
  368.6 9.7 %slice-start.2 = ((s8[11796480]{0:T(1024)(128)(4,1)}), s8[4194304]{0:T(1024)(128)(4,1)S(1)}, s32[]{:S(2)}) async-start(s8[11796480]{0:T(1024)(128)(4,1)} %bitcast.346), calls=%async_computation.8 | async-start | bytes 8388608
  384.5 15.7 %copy-start.92 = (f32[128]{0:T(128)S(1)}, f32[128]{0:T(128)}, u32[]{:S(2)}) copy-start(f32[128]{0:T(128)} %copy-done.91) | copy-start | bytes 1540
  384.5 16.4 %copy-start.125 = (f32[128]{0:T(128)S(1)}, f32[128]{0:T(128)}, u32[]{:S(2)}) copy-start(f32[128]{0:T(128)} %copy-done.124) | copy-start | bytes 1540
  384.5 16.4 %copy-start.104 = (f32[128]{0:T(128)S(1)}, f32[128]{0:T(128)}, u32[]{:S(2)}) copy-start(f32[128]{0:T(128)} %copy-done.103) | copy-start | bytes 1540
  384.6 17.2 %copy-start.47 = (f32[128,768]{1,0:T(8,128)S(1)}, f32[128,768]{1,0:T(8,128)}, u32[]{:S(2)}) copy-start(f32[128,768]{1,0:T(8,128)} %get-tuple-element.206) | copy-start | bytes 1179652
  402.6 8.6 %copy-start.117 = (bf16[2,768]{1,0:T(2,128)(2,1)S(1)}, bf16[2,768]{1,0:T(2,128)(2,1)}, u32[]{:S(2)}) copy-start(bf16[2,768]{1,0:T(2,128)(2,1)} %slice.235) | copy-start | bytes 9220
  403.3 11.6 %copy-start.56 = (f32[512]{0:T(512)S(1)}, f32[512]{0:T(512)}, u32[]{:S(2)}) copy-start(f32[512]{0:T(512)} %copy-done.55) | copy-start | bytes 6148
  403.3 11.6 %copy-start.70 = (f32[512]{0:T(512)S(1)}, f32[512]{0:T(512)}, u32[]{:S(2)}) copy-start(f32[512]{0:T(512)} %copy-done.69) | copy-start | bytes 6148
  403.3 11.6 %copy-start.119 = (s32[512]{0:T(512)S(1)}, s32[512]{0:T(512)}, u32[]{:S(2)}) copy-start(s32[512]{0:T(512)} %iota_add_fusion) | copy-start | bytes 6148
  403.3 11.6 %copy-start.123 = (s32[256]{0:T(256)S(1)}, s32[256]{0:T(256)}, u32[]{:S(2)}) copy-start(s32[256]{0:T(256)} %pad_add_fusion.1) | copy-start | bytes 3076
  403.3 11.6 %copy-start.128 = (pred[512]{0:T(512)(128)(4,1)S(1)}, pred[512]{0:T(512)(128)(4,1)}, u32[]{:S(2)}) copy-start(pred[512]{0:T(512)(128)(4,1)} %iota_compare_fusion.6) | copy-start | bytes 1540
  417.0 7.1 slice-start.5
  449.2 313.2 %reduce-scatter.5.cloned.1.call-start = ((), (), s32[]{:S(2)}) async-start(), calls=%async_computation.5 | async-start | bytes 13271040 | tf_op jit(solution)/shard_map/reduce_scatter | solution.py:68
  564.1 60.4 %slice-start.3 = ((s8[7864320]{0:T(1024)(128)(4,1)}), s8[3670016]{0:T(1024)(128)(4,1)S(1)}, s32[]{:S(2)}) async-start(s8[7864320]{0:T(1024)(128)(4,1)} %bitcast.379), calls=%async_computation.9 | async-start | bytes 7340032
  600.9 23.5 %slice-start.4 = ((s8[7864320]{0:T(1024)(128)(4,1)}), s8[4194304]{0:T(1024)(128)(4,1)S(1)}, s32[]{:S(2)}) async-start(s8[7864320]{0:T(1024)(128)(4,1)} %bitcast.379), calls=%async_computation.10 | async-start | bytes 8388608
  601.3 23.2 %copy-start.8 = (bf16[4,4,32,768]{3,2,1,0:T(8,128)(2,1)S(1)}, bf16[4,4,32,768]{3,2,1,0:T(8,128)(2,1)}, u32[]{:S(2)}) copy-start(bf16[4,4,32,768]{3,2,1,0:T(8,128)(2,1)} %copy-done.7) | copy-start | bytes 2359300
  700.4 37.5 %copy-start.50 = (bf16[192,768]{1,0:T(8,128)(2,1)S(1)}, bf16[192,768]{1,0:T(8,128)(2,1)}, u32[]{:S(2)}) copy-start(bf16[192,768]{1,0:T(8,128)(2,1)} %reduce-scatter.3.cloned.1.call-done) | copy-start | bytes 884740
  725.0 13.0 %copy-start.52 = (f32[16,768]{1,0:T(8,128)}, f32[16,768]{1,0:T(8,128)S(1)}, u32[]{:S(2)}) copy-start(f32[16,768]{1,0:T(8,128)S(1)} %slice.243) | copy-start | bytes 147460
  738.3 43.0 %copy-start.60 = (f32[6,192]{1,0:T(8,128)S(1)}, f32[6,192]{1,0:T(8,128)}, u32[]{:S(2)}) copy-start(f32[6,192]{1,0:T(8,128)} %param.48) | copy-start | bytes 13828
  738.4 44.5 %copy-start.62 = (f32[16,96]{1,0:T(8,128)S(1)}, f32[16,96]{1,0:T(8,128)}, u32[]{:S(2)}) copy-start(f32[16,96]{1,0:T(8,128)} %param.45) | copy-start | bytes 18436
  781.2 8.0 copy-start.54
  781.2 8.0 copy-start.57
  781.3 8.0 copy-start.58
  781.3 8.7 %copy-start.40 = (f32[320,768]{1,0:T(8,128)S(1)}, f32[320,768]{1,0:T(8,128)}, u32[]{:S(2)}) copy-start(f32[320,768]{1,0:T(8,128)} %param.42) | copy-start | bytes 2949124
  781.4 8.6 %copy-start.41 = (f32[320,768]{1,0:T(8,128)S(1)}, f32[320,768]{1,0:T(8,128)}, u32[]{:S(2)}) copy-start(f32[320,768]{1,0:T(8,128)} %param.43) | copy-start | bytes 2949124
  781.4 8.6 %copy-start.42 = (f32[320,768]{1,0:T(8,128)S(1)}, f32[320,768]{1,0:T(8,128)}, u32[]{:S(2)}) copy-start(f32[320,768]{1,0:T(8,128)} %param.44) | copy-start | bytes 2949124
  784.3 10.9 %copy-start.34 = (f32[960,768]{1,0:T(8,128)S(1)}, f32[960,768]{1,0:T(8,128)}, u32[]{:S(2)}) copy-start(f32[960,768]{1,0:T(8,128)} %param.35) | copy-start | bytes 8847364
  (97 other events, 290.6 us)
Sparse Core Ops, SparseCore 0:
  11.6 97.6 all-gather.2
  112.9 122.9 all-gather.4
  449.3 141.4 reduce-scatter.2
  671.2 91.1 reduce-scatter.4

commit v5 on v4

--- a/solution.py
+++ b/solution.py
@@ -333,6 +333,90 @@
         for copy in started:
             copy.wait_send()
 
+    def fold(self, name, value):
+        size, parts = value.shape[:2]
+        block = value.shape[1:]
+
+        def kernel(source, out, land, sends, lands):
+            self.greet([("z",)])
+            me = lax.axis_index("z")
+
+            def beyond(way, hop):
+                return me + hop <= size - 1 if way == 0 else me - hop >= 0
+
+            def behind(way):
+                return me > 0 if way == 0 else me < size - 1
+
+            def copy_of(way, hop, part, src):
+                return pltpu.make_async_remote_copy(
+                    src_ref=src,
+                    dst_ref=land.at[way, hop - 1, part],
+                    send_sem=sends.at[way, hop - 1, part],
+                    recv_sem=lands.at[way, hop - 1, part],
+                    device_id={"z": me + (1 if way == 0 else -1)},
+                    device_id_type=MESH,
+                )
+
+            def landing(way, hop, part):
+                landed = land.at[way, hop, part]
+                return pltpu.make_async_remote_copy(
+                    src_ref=landed,
+                    dst_ref=landed,
+                    send_sem=sends.at[way, hop, part],
+                    recv_sem=lands.at[way, hop, part],
+                    device_id={"z": me - (1 if way == 0 else -1)},
+                    device_id_type=MESH,
+                )
+
+            for hop in range(size - 1, 0, -1):
+                for part in range(parts):
+                    for way in range(2):
+                        goal = me + hop if way == 0 else me - hop
+
+                        @pl.when(beyond(way, hop) & jnp.logical_not(behind(way)))
+                        def _():
+                            copy_of(way, hop, part, source.at[goal, part]).start()
+
+                        if hop < size - 1:
+
+                            @pl.when(beyond(way, hop) & behind(way))
+                            def _():
+                                landing(way, hop, part).wait_recv()
+                                land[way, hop, part] += source[goal, part]
+                                copy_of(way, hop, part, land.at[way, hop, part]).start()
+
+            for part in range(parts):
+                out[part] = source[me, part]
+                for way in range(2):
+
+                    @pl.when(behind(way))
+                    def _():
+                        landing(way, 0, part).wait_recv()
+                        out[part] += land[way, 0, part]
+
+            for hop in range(size - 1, 0, -1):
+                for part in range(parts):
+                    for way in range(2):
+
+                        @pl.when(beyond(way, hop))
+                        def _():
+                            copy_of(way, hop, part, source.at[0, part]).wait_send()
+
+        return self.call(
+            kernel,
+            [jax.ShapeDtypeStruct(block, value.dtype)],
+            [FAST],
+            [FAST],
+            [
+                pltpu.VMEM((2, size - 1, *block), value.dtype),
+                pltpu.SemaphoreType.DMA((2, size - 1, parts)),
+                pltpu.SemaphoreType.DMA((2, size - 1, parts)),
+            ],
+            [value],
+            4 * value.size,
+            name,
+        )[0]
+
     def line_move(self, value, part_rows, memory):
         parts = value.shape[0] // part_rows if value.shape[0] % part_rows == 0 else 1
         kind = "relay" if self.sizes["z"] <= 8 else "gather"
@@ -507,6 +591,110 @@
     )(queries, *keys, *values, log_norm, grad_mixed)
 
 
+def score_kernel(head_ref, word_ref, bias_ref, label_ref, stat_ref, top, total, target):
+    at, last = pl.program_id(1), pl.num_programs(1) - 1
+    logits = dots(head_ref[...], word_ref[...], 1, 1) + bias_ref[...]
+    column = at * logits.shape[1] + lax.broadcasted_iota(jnp.int32, logits.shape, 1)
+
+    @pl.when(at == 0)
+    def _():
+        top[...] = jnp.full(top.shape, -jnp.inf, jnp.float32)
+        total[...] = jnp.zeros(total.shape, jnp.float32)
+        target[...] = jnp.zeros(target.shape, jnp.float32)
+
+    old = top[...]
+    new = jnp.maximum(old, jnp.max(logits, axis=1, keepdims=True))
+    added = jnp.sum(jnp.exp(logits - new), axis=1, keepdims=True)
+    total[...] = total[...] * jnp.exp(old - new) + added
+    top[...] = new
+    hits = jnp.where(column == label_ref[...], logits, 0.0)
+    target[...] += jnp.sum(hits, axis=1, keepdims=True)
+
+    @pl.when(at == last)
+    def _():
+        lane = lax.broadcasted_iota(jnp.int32, stat_ref.shape, 1)
+        stat_ref[...] = jnp.where(
+            lane == 0, top[...], jnp.where(lane == 1, total[...], target[...])
+        )
+
+
+def slope_kernel(
+    head_ref, word_ref, bias_ref, label_ref, norm_ref, weight_ref, slope_ref, sum_ref, grad_ref
+):
+    at = pl.program_id(1)
+    logits = dots(head_ref[...], word_ref[...], 1, 1) + bias_ref[...]
+    column = at * logits.shape[1] + lax.broadcasted_iota(jnp.int32, logits.shape, 1)
+    hits = jnp.where(column == label_ref[...], 1.0, 0.0)
+    slope = ((jnp.exp(logits - norm_ref[...]) - hits) * weight_ref[...]).astype(jnp.bfloat16)
+    slope_ref[...] = slope
+    sum_ref[0] = jnp.sum(slope.astype(jnp.float32), axis=0, keepdims=True)
+    part = dots(slope, word_ref[...], 1, 0)
+
+    @pl.when(at == 0)
+    def _():
+        grad_ref[...] = part
+
+    @pl.when(at > 0)
+    def _():
+        grad_ref[...] += part
+
+
+def head_blocks(head, word, bias):
+    rows, vocab = head.shape[0], word.shape[0]
+    row_block = 512 if rows % 512 == 0 else rows
+    block = 768 if vocab % 768 == 0 else vocab
+    grid = (rows // row_block, vocab // block)
+    column = pl.BlockSpec((row_block, 1), lambda i, j: (i, 0))
+    specs = [
+        pl.BlockSpec((row_block, D), lambda i, j: (i, 0)),
+        pl.BlockSpec((block, D), lambda i, j: (j, 0)),
+        pl.BlockSpec((1, block), lambda i, j: (0, j)),
+        column,
+    ]
+    cost = pl.CostEstimate(
+        flops=2 * rows * vocab * D, bytes_accessed=2 * vocab * D, transcendentals=rows * vocab
+    )
+    return row_block, block, grid, column, specs, cost
+
+
+def head_scores(head, word, bias, labels):
+    row_block, _, grid, _, specs, cost = head_blocks(head, word, bias)
+    stats = pl.pallas_call(
+        score_kernel,
+        grid=grid,
+        out_shape=jax.ShapeDtypeStruct((head.shape[0], 128), jnp.float32),
+        in_specs=specs,
+        out_specs=pl.BlockSpec((row_block, 128), lambda i, j: (i, 0)),
+        scratch_shapes=[pltpu.VMEM((row_block, 1), jnp.float32)] * 3,
+        cost_estimate=cost,
+        name="head_scores",
+    )(head, word, bias[None], labels[:, None])
+    return stats[:, :3].T
+
+
+def head_slopes(head, word, bias, labels, norms, weights):
+    row_block, block, grid, column, specs, cost = head_blocks(head, word, bias)
+    rows, vocab = head.shape[0], word.shape[0]
+    slopes, sums, grad = pl.pallas_call(
+        slope_kernel,
+        grid=grid,
+        out_shape=[
+            jax.ShapeDtypeStruct((rows, vocab), head.dtype),
+            jax.ShapeDtypeStruct((grid[0], 1, vocab), jnp.float32),
+            jax.ShapeDtypeStruct((rows, D), jnp.float32),
+        ],
+        in_specs=specs + [column] * 2,
+        out_specs=[
+            pl.BlockSpec((row_block, block), lambda i, j: (i, j)),
+            pl.BlockSpec((1, 1, block), lambda i, j: (i, 0, j)),
+            pl.BlockSpec((row_block, D), lambda i, j: (i, 0)),
+        ],
+        cost_estimate=cost,
+        name="head_slopes",
+    )(head, word, bias[None], labels[:, None], norms[:, None], weights[:, None])
+    return slopes, jnp.sum(sums[:, 0], axis=0), grad
+
+
 def step(sizes, *args):
     (
         token_ids, type_ids, mask_pos, mask_valid, mlm_labels, nsp_labels,
@@ -602,10 +790,14 @@
     flat_ids = z_ids.reshape(-1)
     inside, at = plane_index(flat_ids)
     looked = jnp.where(inside[:, None], word_plane[jnp.where(inside, at, 0)], jnp.zeros((), low))
-    looked = looked.reshape(z_size, own_len, D)
-    (found,) = links.exchange("token_spread", ("spread", ("z",), 0, BIG, looked))
-    embedded = lax.dynamic_index_in_dim(looked, z_at, 0, False).astype(jnp.float32)
-    embedded = embedded + jnp.sum(found.astype(jnp.float32), axis=0)
+    if z_size <= 8:
+        looked = looked.reshape(z_size, 8, own_len // 8, D)
+        embedded = links.fold("token_fold", looked).reshape(own_len, D).astype(jnp.float32)
+    else:
+        looked = looked.reshape(z_size, own_len, D)
+        (found,) = links.exchange("token_spread", ("spread", ("z",), 0, BIG, looked))
+        embedded = lax.dynamic_index_in_dim(looked, z_at, 0, False).astype(jnp.float32)
+        embedded = embedded + jnp.sum(found.astype(jnp.float32), axis=0)
     position_rows = lax.dynamic_slice_in_dim(side_full, 2 * D + c_at * own_len, own_len, 0)
     embedded = (
         embedded
@@ -656,18 +848,9 @@
     head_rows = layer_norm(act_dense, vec_rows[9], vec_rows[10])
     (head_b,) = links.exchange("head_gather", links.line_move(head_rows.astype(low), 32, FAST))
     head_b = head_b.reshape(-1, D)
-    row_count = head_b.shape[0]
-    logits = (
-        jnp.einsum("rd,vd->rv", head_b, word_plane, preferred_element_type=jnp.float32)
-        + bias_plane
-    )
     label_in, label_at = plane_index(z_labels.reshape(-1))
     label_at = jnp.where(label_in, label_at, -1)
-    hit_rows = label_at[:, None] == lax.broadcasted_iota(jnp.int32, logits.shape, 1)
-    row_top = jnp.max(logits, axis=1)
-    row_total = jnp.sum(jnp.exp(logits - row_top[:, None]), axis=1)
-    row_target = jnp.sum(jnp.where(hit_rows, logits, 0.0), axis=1)
-    stats = jnp.pad(jnp.stack([row_top, row_total, row_target]), ((0, 5), (0, 0)))
+    stats = jnp.pad(head_scores(head_b, word_plane, bias_plane, label_at), ((0, 5), (0, 0)))
     (stats,) = links.exchange("stat_gather", ("gather", ("z",), 0, FAST, stats))
     top_all = jnp.max(stats[:, 0], axis=0)
     total_all = jnp.sum(stats[:, 1] * jnp.exp(stats[:, 0] - top_all), axis=0)
@@ -676,11 +859,9 @@
     valid_rows = z_valid.reshape(-1).astype(jnp.float32)
     mlm_sum = -jnp.sum(valid_rows * (target_all - log_total))
     weight_rows = valid_rows / total_count
-    grad_logits = (
-        (jnp.exp(logits - log_total[:, None]) - hit_rows.astype(jnp.float32)) * weight_rows[:, None]
-    ).astype(low)
-    decoder_part = jnp.sum(grad_logits.astype(jnp.float32), axis=0)
-    head_part = jnp.dot(grad_logits, word_plane, preferred_element_type=jnp.float32)
+    grad_logits, decoder_part, head_part = head_slopes(
+        head_b, word_plane, bias_plane, label_at, log_total, weight_rows
+    )
     head_part = head_part.reshape(z_size, own_slots, D)
     (head_others,) = links.exchange("head_spread", ("spread", ("z",), 0, FAST, head_part.astype(low)))
     grad_head = lax.dynamic_index_in_dim(head_part, z_at, 0, False) + jnp.sum(

time: 818 us -> 787 us (0.962)
  matrix products: 135 us -> 101 us
  Pallas kernels: 421 us -> 450 us
  other arithmetic: 101 us -> 81.7 us
    pallas_call x0 -> x2, Pallas kernels: none -> 39.8 us  [the longest x1 21.1 us: head_slopes(): pl.pallas_call(slope_kernel, grid=grid, out_shape=[jax.ShapeDtypeStruct((...]
    dot_general x2 -> x0, matrix products: 32.6 us -> none  [the longest x1 26.4 us: step(): jnp.einsum('rd,vd->rv', head_b, word_plane, preferred_element_type=jnp.fl...]
    reduce_sum x3 -> x0, other arithmetic: 22.5 us -> none  [the longest x1 9.69 us: step(): decoder_part = jnp.sum(grad_logits.astype(jnp.float32), axis=0)]
    pallas_call x16, Pallas kernels: 375 us -> 364 us  [call(): pl.pallas_call(kernel, out_shape=outs, in_specs=[pl.BlockSpec(memory_spac...]
    unnamed x295 -> x286, local copies, waits for them, and re-layouts: 34 us -> 31.9 us
  transfers between devices with their start and end apart: 4 -> 4, of which waited for: 1 -> 1; matrix products, arithmetic and copies ran while one was open for 17% -> 17% of each run, Pallas kernels for 42% -> 45%
where the time goes in v5:
time: 787 us; the launch traced here: 780 us
  Pallas kernels  450 us (57%)
  local copies, waits for them, and re-layouts  103 us (13%)
  matrix products  101 us (13%)
  other arithmetic  81.7 us (10%)
  between operations  25.7 us (3%)
  waiting for transfers between devices  18.7 us (2%)
    pallas_call x16, Pallas kernels, call(): pl.pallas_call(kernel, out_shape=outs, in_specs=[pl.BlockSpec(memory_spac...  364 us
    dot_general x1, matrix products, step(): jnp.dot(onehot, all_x0, preferred_element_type=jnp.float32)  33.9 us
    unnamed x286, local copies, waits for them, and re-layouts  31.9 us
    pallas_call x1, Pallas kernels, attention_backward(): pl.pallas_call(backward_kernel, grid=(pairs,), out_shape=[jax.ShapeDtypeS...  23.7 us
    pallas_call x1, Pallas kernels, attention_forward(): pl.pallas_call(forward_kernel, grid=(pairs,), out_shape=[jax.ShapeDtypeSt...  22.3 us
    pallas_call x1, Pallas kernels, head_slopes(): pl.pallas_call(slope_kernel, grid=grid, out_shape=[jax.ShapeDtypeStruct((...  21.1 us
    pallas_call x1, Pallas kernels, head_scores(): pl.pallas_call(score_kernel, grid=grid, out_shape=jax.ShapeDtypeStruct((h...  18.6 us
    reduce_scatter x2, waiting for transfers between devices, comm_scatter_sum(): return lax.psum_scatter(value, axes, scatter_dimension=0, tiled=True)  18.6 us
  transfers between devices with their start and end apart: 4, of which 1 were waited for; matrix products, arithmetic and copies ran while one was open for 17% of the time, Pallas kernels for 45%

profile of v5, /device:TPU:0, one launch (start us, length us, event | category | flops | bytes accessed | tf_op | source)
XLA Modules:
  0.0 780.5 jit_solution(2155102392064580371)
XLA Ops:
  17.1 76.4 %word_gather.1 = (bf16[2,2,2,4,240,768]{5,4,3,2,1,0:T(8,128)(2,1)S(1)}, s32[4,8,128]{2,1,0:T(8,128)S(1)}, bf16[8,16,128]{2,1,0:T(8,128)(2,1)S(1)}, f32[8,8,128]{2,1,0:T(8,128)S(1)}, f32[4,24,128]{2,1,0:T(8,128)S(1)}) custom-call(bf16[4,240,768]{2,1,0:T(8,128)(2,1)S(1)} %bitcast.332, s32[8,128]{1,0:T(8,128)S(1)} %pad_bitcast_fusion.refs_1_, ...), custom_call_target="tpu_custom_call" | custom-call | bytes 23855104 | tf_op jit(solution)/shard_map/word_gather/pallas_call | solution.py:116
  93.6 4.4 copy-done
  99.6 16.0 %gather_fusion = bf16[2048,768]{1,0:T(8,128)(2,1)} fusion(bf16[7680,768]{1,0:T(8,128)(2,1)} %bitcast.327, s32[2048]{0:T(1024)S(1)} %broadcast_clamp_fusion), kind=kCustom, calls=%fused_computation | custom fusion | bytes 6299648 | tf_op jit(solution)/shard_map/gather | solution.py:792
  117.7 85.2 %token_fold.1 = bf16[8,64,768]{2,1,0:T(8,128)(2,1)S(1)} custom-call(bf16[4,8,64,768]{3,2,1,0:T(8,128)(2,1)S(1)} %broadcast_select_fusion.source), custom_call_target="tpu_custom_call" | custom-call | bytes 6291456 | tf_op jit(solution)/shard_map/token_fold/pallas_call | solution.py:116
  214.6 2.6 slice.263
  217.3 4.1 slice_bitcast_fusion
  230.4 3.3 copy.223
  233.9 3.5 key_trade.1
  238.8 22.3 %attention_forward.1 = (bf16[512,768]{1,0:T(8,128)(2,1)}, f32[6,2,512]{2,1,0:T(2,128)}) custom-call(bf16[512,768]{1,0:T(8,128)(2,1)} %add_convert_fusion.5.q_ref, bf16[512,768]{1,0:T(8,128)(2,1)} %copy-done.1, bf16[512,768]{1,0:T(8,128)(2,1)} %copy-done.8, bf16[512,768]{1,0:T(8,128)(2,1)} %copy-done.2, bf16[512,768]{1,0:T(8,128)(2,1)} %copy-done.9), custom_call_target="tpu_custom_call" | custom-call | flops 3221225472 | bytes 6291456 | tf_op jit(solution)/shard_map/attention_forward/pallas_call | solution.py:528
  263.5 3.4 fusion.162
  267.3 7.0 fusion.11
  274.4 2.9 fusion.163
  281.5 2.6 gather_fusion.1
  286.4 19.0 %head_gather.1 = bf16[4,4,32,768]{3,2,1,0:T(8,128)(2,1)S(1)} custom-call(bf16[4,32,768]{2,1,0:T(8,128)(2,1)S(1)} %bitcast.341), custom_call_target="tpu_custom_call" | custom-call | bytes 1572864 | tf_op jit(solution)/shard_map/head_gather/pallas_call | solution.py:116
  306.2 18.6 %head_scores.1 = f32[512,128]{1,0:T(8,128)} custom-call(bf16[512,768]{1,0:T(8,128)(2,1)} %bitcast.338, bf16[7680,768]{1,0:T(8,128)(2,1)} %bitcast.328, f32[1,7680]{1,0:T(1,128)} %broadcast_in_dim_reshape.2.bias_ref, s32[512,1]{1,0:T(8,128)} %fusion.87.label_ref), custom_call_target="tpu_custom_call" | custom-call | flops 6039797760 | bytes 11796480 | tf_op jit(solution)/shard_map/head_scores/pallas_call | solution.py:662
  325.9 5.7 stat_gather.1
  335.4 21.1 %head_slopes.1 = (bf16[512,7680]{1,0:T(8,128)(2,1)}, f32[1,1,7680]{2,1,0:T(1,128)}, f32[512,768]{1,0:T(8,128)}) custom-call(bf16[512,768]{1,0:T(8,128)(2,1)} %bitcast.339, bf16[7680,768]{1,0:T(8,128)(2,1)} %bitcast.329, f32[1,7680]{1,0:T(1,128)} %broadcast_in_dim_reshape.2.bias_ref, s32[512,1]{1,0:T(8,128)} %fusion.87.label_ref, f32[512,1]{1,0:T(8,128)} %copy.242.norm_ref, ...), custom_call_target="tpu_custom_call" | custom-call | flops 6039797760 | bytes 11796480 | tf_op jit(solution)/shard_map/head_slopes/pallas_call | solution.py:678
  358.0 15.5 %head_spread.1 = bf16[3,128,768]{2,1,0:T(8,128)(2,1)S(1)} custom-call(bf16[4,128,768]{2,1,0:T(8,128)(2,1)S(1)} %bitcast_convert_fusion.refs_0_), custom_call_target="tpu_custom_call" | custom-call | bytes 1179648 | tf_op jit(solution)/shard_map/head_spread/pallas_call | solution.py:116
  393.7 4.4 convolution_convert_fusion
  400.2 6.0 convert_reduce_fusion
  406.3 5.1 convolution_convert_fusion.1
  411.4 3.8 fusion.39
  415.1 8.2 %pad_maximum_fusion = bf16[32,2,96,768]{3,2,1,0:T(8,128)(2,1)} fusion(bf16[32,1,96,768]{3,2,1,0:T(8,128)(2,1)} %bitcast.363, bf16[32,1,96,768]{3,2,1,0:T(8,128)(2,1)} %bitcast.364), kind=kLoop, calls=%fused_computation.7 | loop fusion | flops 4718592 | bytes 18874368 | tf_op jit(solution)/shard_map/stack | solution.py:910
  424.7 3.2 slice.271
  429.7 3.3 multiply_reduce_fusion.1
  436.3 23.7 %attention_backward.1 = (bf16[512,768]{1,0:T(8,128)(2,1)}, f32[512,768]{1,0:T(8,128)}, f32[512,768]{1,0:T(8,128)}, f32[512,768]{1,0:T(8,128)}, f32[512,768]{1,0:T(8,128)}) custom-call(bf16[512,768]{1,0:T(8,128)(2,1)} %add_convert_fusion.5.q_ref, bf16[512,768]{1,0:T(8,128)(2,1)} %copy-done.1, bf16[512,768]{1,0:T(8,128)(2,1)} %copy-done.8, ...), custom_call_target="tpu_custom_call" | custom-call | flops 8053063680 | bytes 12582912 | tf_op jit(solution)/shard_map/attention_backward/pallas_call | solution.py:581
  462.9 6.4 key_grad_trade.1
  471.8 2.4 add_convert_fusion.1
  480.2 5.0 multiply_reduce_fusion.2
  488.4 4.0 convert_bitcast_fusion
  492.3 6.0 copy.255
  500.3 2.6 concatenate.47
  502.9 4.6 copy.257
  507.5 4.0 pad_maximum_fusion.1
  514.1 19.0 %grad_swap_c.1 = (bf16[2,4,2,96,768]{4,3,2,1,0:T(8,128)(2,1)S(1)}, bf16[4,2,2,80,768]{4,3,2,1,0:T(8,128)(2,1)S(1)}, bf16[4,1,64,768]{3,2,1,0:T(8,128)(2,1)S(1)}) custom-call(bf16[2,2,4,2,96,768]{5,4,3,2,1,0:T(8,128)(2,1)S(1)} %copy.258.refs_0_, bf16[4,2,2,2,80,768]{5,4,3,2,1,0:T(8,128)(2,1)S(1)} %bitcast.330, bf16[1,64,768]{2,1,0:T(8,128)(2,1)S(1)} %slice_bitcast_fusion.1.refs_2_), custom_call_target="tpu_custom_call" | custom-call | bytes 9437184 | tf_op jit(solution)/shard_map/grad_swap_c/pallas_call | solution.py:116
  536.9 37.3 %grad_swap_xy.1 = (bf16[2,4,96,768]{3,2,1,0:T(8,128)(2,1)S(1)}, bf16[4,2,80,768]{3,2,1,0:T(8,128)(2,1)S(1)}, bf16[4,4,64,768]{3,2,1,0:T(8,128)(2,1)S(1)}) custom-call(bf16[2,4,2,96,768]{4,3,2,1,0:T(8,128)(2,1)S(1)} %copy.262.refs_0_, bf16[4,2,2,80,768]{4,3,2,1,0:T(8,128)(2,1)S(1)} %copy.263.refs_1_, bf16[4,64,768]{2,1,0:T(8,128)(2,1)S(1)} %bitcast.333), custom_call_target="tpu_custom_call" | custom-call | bytes 7471104 | tf_op jit(solution)/shard_map/grad_swap_xy/pallas_call | solution.py:116
  574.8 22.3 %grad_swap_yx.1 = (bf16[4,96,768]{2,1,0:T(8,128)(2,1)S(1)}, bf16[4,80,768]{2,1,0:T(8,128)(2,1)S(1)}, bf16[4,3,64,768]{3,2,1,0:T(8,128)(2,1)S(1)}) custom-call(bf16[2,4,96,768]{3,2,1,0:T(8,128)(2,1)S(1)} %fusion.34.refs_0_, bf16[4,2,80,768]{3,2,1,0:T(8,128)(2,1)S(1)} %copy.265.refs_1_, bf16[3,64,768]{2,1,0:T(8,128)(2,1)S(1)} %bitcast.336), custom_call_target="tpu_custom_call" | custom-call | bytes 4521984 | tf_op jit(solution)/shard_map/grad_swap_yx/pallas_call | solution.py:116
  598.6 11.1 %fusion.167 = f32[7680,768]{1,0:T(8,128)} fusion(bf16[512,7680]{1,0:T(8,128)(2,1)S(1)} %bitcast.420, bf16[512,768]{1,0:T(8,128)(2,1)S(1)} %bitcast.340), kind=kOutput, calls=%fused_computation.389 | convolution fusion | flops 6039797760 | bytes 32243712 | tf_op jit(solution)/shard_map/rv,rd->vd/dot_general | solution.py:1002
  611.2 33.9 %add_convert_fusion = bf16[7680,768]{1,0:T(8,128)(2,1)} fusion(f32[7680,768]{1,0:T(8,128)} %fusion.167, bf16[2048,768]{1,0:T(8,128)(2,1)S(1)} %bitcast.367, s32[2048]{0:T(1024)S(1)} %copy-done.102), kind=kOutput, calls=%fused_computation.5 | convolution fusion | flops 24186716160 | bytes 38543360 | tf_op jit(solution)/shard_map/dot_general | solution.py:1003
  650.7 24.0 %grad_spread_z.1 = (bf16[3,96,768]{2,1,0:T(8,128)(2,1)S(1)}, bf16[3,80,768]{2,1,0:T(8,128)(2,1)S(1)}) custom-call(bf16[4,96,768]{2,1,0:T(8,128)(2,1)S(1)} %fusion.51.refs_0_, bf16[4,80,768]{2,1,0:T(8,128)(2,1)S(1)} %fusion.60.refs_1_), custom_call_target="tpu_custom_call" | custom-call | bytes 1622016 | tf_op jit(solution)/shard_map/grad_spread_z/pallas_call | solution.py:116
  674.9 24.3 %small_sum.1 = f32[4,192,128]{2,1,0:T(8,128)S(1)} custom-call(f32[192,128]{1,0:T(8,128)S(1)} %maximum_bitcast_fusion.x_ref), custom_call_target="tpu_custom_call" | custom-call | bytes 1572864 | tf_op jit(solution)/shard_map/small_sum/pallas_call | solution.py:116
  701.3 8.8 %side_gather.1 = bf16[4,80,768]{2,1,0:T(8,128)(2,1)S(1)} custom-call(bf16[80,768]{1,0:T(8,128)(2,1)S(1)} %convert_add_fusion.7.refs_0_), custom_call_target="tpu_custom_call" | custom-call | bytes 983040 | tf_op jit(solution)/shard_map/side_gather/pallas_call | solution.py:116
  716.8 18.6 %reduce-scatter.5.cloned.1.call-done = bf16[960,768]{1,0:T(8,128)(2,1)} async-done(((bf16[7680,768]{1,0:T(8,128)(2,1)}), bf16[960,768]{1,0:T(8,128)(2,1)}) %reduce-scatter.5.cloned.1.call-update) | async-done | bytes 1474576 | tf_op jit(solution)/shard_map/reduce_scatter | solution.py:68
  735.4 2.7 fusion.28
  740.2 12.5 %norm_sum.1 = f32[4,8,128]{2,1,0:T(8,128)S(1)} custom-call(f32[8,128]{1,0:T(8,128)S(1)} %iota.35.x_ref), custom_call_target="tpu_custom_call" | custom-call | bytes 65536 | tf_op jit(solution)/shard_map/norm_sum/pallas_call | solution.py:116
  756.4 4.9 multiply_subtract_fusion.2
  762.0 3.8 multiply_subtract_fusion.1
  768.1 4.2 multiply_subtract_fusion
  (517 shorter events, 120.8 us)
Async XLA Ops:
  7.2 207.4 %all-gather.3.cloned.1.call-start = ((), (), s32[]{:S(2)}) async-start(), calls=%async_computation.2 | async-start | bytes 8921088 | tf_op jit(solution)/shard_map/all_gather | solution.py:64
  10.3 257.0 %all-gather.5.cloned.1.call-start = ((), (), s32[]{:S(2)}) async-start(), calls=%async_computation.3 | async-start | bytes 9732096 | tf_op jit(solution)/shard_map/all_gather | solution.py:64
  11.3 598.4 %reduce-scatter.3.cloned.1.call-start = ((), (), s32[]{:S(2)}) async-start(), calls=%async_computation.4 | async-start | bytes 9732096 | tf_op jit(solution)/shard_map/reduce_scatter | solution.py:68
  98.1 108.3 %copy-start.45 = (s32[1,4,8,128]{3,1,2,0:T(4,128)}, s32[1,4,8,128]{3,1,2,0:T(4,128)S(1)}, u32[]{:S(2)}) copy-start(s32[1,4,8,128]{3,1,2,0:T(4,128)S(1)} %copy.330) | copy-start | bytes 49156
  203.0 8.3 %copy-start.119 = (s32[2,256]{1,0:T(2,128)S(1)}, s32[2,256]{1,0:T(2,128)}, u32[]{:S(2)}) copy-start(s32[2,256]{1,0:T(2,128)} %param.29) | copy-start | bytes 6148
  203.4 60.1 %copy-start.84 = (f32[768]{0:T(1024)}, f32[768]{0:T(1024)S(1)}, u32[]{:S(2)}) copy-start(f32[768]{0:T(1024)S(1)} %mul.788) | copy-start | bytes 9220
  203.5 60.0 %copy-start.108 = (f32[768]{0:T(1024)}, f32[768]{0:T(1024)S(1)}, u32[]{:S(2)}) copy-start(f32[768]{0:T(1024)S(1)} %add.745) | copy-start | bytes 9220
  203.9 70.4 %copy-start.48 = (f32[768]{0:T(1024)}, f32[768]{0:T(1024)S(1)}, u32[]{:S(2)}) copy-start(f32[768]{0:T(1024)S(1)} %mul.794) | copy-start | bytes 9220
  204.0 70.4 %copy-start.110 = (f32[768]{0:T(1024)}, f32[768]{0:T(1024)S(1)}, u32[]{:S(2)}) copy-start(f32[768]{0:T(1024)S(1)} %add.759) | copy-start | bytes 9220
  204.4 62.9 %copy-start.90 = (f32[4,768]{1,0:T(4,128)}, f32[4,768]{1,0:T(4,128)S(1)}, u32[]{:S(2)}) copy-start(f32[4,768]{1,0:T(4,128)S(1)} %add.762) | copy-start | bytes 36868
  210.7 11.5 %copy-start.94 = (pred[512]{0:T(512)(128)(4,1)}, pred[512]{0:T(512)(128)(4,1)S(1)}, u32[]{:S(2)}) copy-start(pred[512]{0:T(512)(128)(4,1)S(1)} %get-tuple-element.135) | copy-start | bytes 1540
  217.2 6.5 copy-start.19
  223.7 39.8 %copy-start.96 = (f32[512]{0:T(512)}, f32[512]{0:T(512)S(1)}, u32[]{:S(2)}) copy-start(f32[512]{0:T(512)S(1)} %fusion.123) | copy-start | bytes 6148
  266.9 7.4 copy-start.13
  266.9 7.4 copy-start.50
  267.2 7.1 copy-start.67
  267.2 7.1 copy-start.62
  267.3 7.1 copy-start.123
  286.0 38.9 %copy-start.86 = (f32[128]{0:T(128)}, f32[128]{0:T(128)S(1)}, u32[]{:S(2)}) copy-start(f32[128]{0:T(128)S(1)} %broadcast_multiply_fusion.4) | copy-start | bytes 1540
  286.2 38.7 %copy-start.121 = (f32[128]{0:T(128)}, f32[128]{0:T(128)S(1)}, u32[]{:S(2)}) copy-start(f32[128]{0:T(128)S(1)} %multiply_reduce_fusion.11) | copy-start | bytes 1540
  286.2 38.7 %copy-start.103 = (f32[128]{0:T(128)}, f32[128]{0:T(128)S(1)}, u32[]{:S(2)}) copy-start(f32[128]{0:T(128)S(1)} %fusion.132) | copy-start | bytes 1540
  358.0 15.7 %copy-start.87 = (f32[128]{0:T(128)S(1)}, f32[128]{0:T(128)}, u32[]{:S(2)}) copy-start(f32[128]{0:T(128)} %copy-done.86) | copy-start | bytes 1540
  358.0 17.6 %copy-start.122 = (f32[128]{0:T(128)S(1)}, f32[128]{0:T(128)}, u32[]{:S(2)}) copy-start(f32[128]{0:T(128)} %copy-done.121) | copy-start | bytes 1540
  358.0 17.6 %copy-start.104 = (f32[128]{0:T(128)S(1)}, f32[128]{0:T(128)}, u32[]{:S(2)}) copy-start(f32[128]{0:T(128)} %copy-done.103) | copy-start | bytes 1540
  377.9 11.0 %copy-start.53 = (f32[512]{0:T(512)S(1)}, f32[512]{0:T(512)}, u32[]{:S(2)}) copy-start(f32[512]{0:T(512)} %copy-done.52) | copy-start | bytes 6148
  377.9 11.0 %copy-start.66 = (f32[512]{0:T(512)S(1)}, f32[512]{0:T(512)}, u32[]{:S(2)}) copy-start(f32[512]{0:T(512)} %copy-done.65) | copy-start | bytes 6148
  377.9 11.0 %copy-start.116 = (s32[512]{0:T(512)S(1)}, s32[512]{0:T(512)}, u32[]{:S(2)}) copy-start(s32[512]{0:T(512)} %iota_add_fusion) | copy-start | bytes 6148
  377.9 11.0 %copy-start.120 = (s32[256]{0:T(256)S(1)}, s32[256]{0:T(256)}, u32[]{:S(2)}) copy-start(s32[256]{0:T(256)} %pad_add_fusion.1) | copy-start | bytes 3076
  377.9 11.0 %copy-start.125 = (pred[512]{0:T(512)(128)(4,1)S(1)}, pred[512]{0:T(512)(128)(4,1)}, u32[]{:S(2)}) copy-start(pred[512]{0:T(512)(128)(4,1)} %iota_compare_fusion.4) | copy-start | bytes 1540
  391.7 6.4 copy-start.73
  393.6 6.5 slice-start.6
  400.2 6.1 copy-start.14
  400.2 6.1 copy-start.49
  400.2 6.1 copy-start.51
  400.2 6.1 copy-start.63
  423.4 312.0 %reduce-scatter.5.cloned.1.call-start = ((), (), s32[]{:S(2)}) async-start(), calls=%async_computation.5 | async-start | bytes 13271040 | tf_op jit(solution)/shard_map/reduce_scatter | solution.py:68
  462.9 6.5 copy-start.35
  536.8 61.2 %slice-start.3 = ((s8[7864320]{0:T(1024)(128)(4,1)}), s8[3670016]{0:T(1024)(128)(4,1)S(1)}, s32[]{:S(2)}) async-start(s8[7864320]{0:T(1024)(128)(4,1)} %bitcast.419), calls=%async_computation.9 | async-start | bytes 7340032
  574.4 23.7 %slice-start.4 = ((s8[7864320]{0:T(1024)(128)(4,1)}), s8[4194304]{0:T(1024)(128)(4,1)S(1)}, s32[]{:S(2)}) async-start(s8[7864320]{0:T(1024)(128)(4,1)} %bitcast.419), calls=%async_computation.10 | async-start | bytes 8388608
  699.2 12.4 %copy-start.44 = (bf16[192,768]{1,0:T(8,128)(2,1)S(1)}, bf16[192,768]{1,0:T(8,128)(2,1)}, u32[]{:S(2)}) copy-start(bf16[192,768]{1,0:T(8,128)(2,1)} %reduce-scatter.3.cloned.1.call-done) | copy-start | bytes 884740
  699.9 12.4 %copy-start.46 = (f32[4,6,192]{2,1,0:T(8,128)}, f32[4,6,192]{2,1,0:T(8,128)S(1)}, u32[]{:S(2)}) copy-start(f32[4,6,192]{2,1,0:T(8,128)S(1)} %reshape.1146) | copy-start | bytes 55300
  716.8 37.5 %copy-start.57 = (f32[6,192]{1,0:T(8,128)S(1)}, f32[6,192]{1,0:T(8,128)}, u32[]{:S(2)}) copy-start(f32[6,192]{1,0:T(8,128)} %param.48) | copy-start | bytes 13828
  716.8 37.5 %copy-start.98 = (f32[6,192]{1,0:T(8,128)S(1)}, f32[6,192]{1,0:T(8,128)}, u32[]{:S(2)}) copy-start(f32[6,192]{1,0:T(8,128)} %param.49) | copy-start | bytes 13828
  716.8 37.5 %copy-start.99 = (f32[6,192]{1,0:T(8,128)S(1)}, f32[6,192]{1,0:T(8,128)}, u32[]{:S(2)}) copy-start(f32[6,192]{1,0:T(8,128)} %param.50) | copy-start | bytes 13828
  716.8 38.8 %copy-start.59 = (f32[16,96]{1,0:T(8,128)S(1)}, f32[16,96]{1,0:T(8,128)}, u32[]{:S(2)}) copy-start(f32[16,96]{1,0:T(8,128)} %param.45) | copy-start | bytes 18436
  716.8 38.8 %copy-start.100 = (f32[16,96]{1,0:T(8,128)S(1)}, f32[16,96]{1,0:T(8,128)}, u32[]{:S(2)}) copy-start(f32[16,96]{1,0:T(8,128)} %param.46) | copy-start | bytes 18436
  716.8 38.8 %copy-start.101 = (f32[16,96]{1,0:T(8,128)S(1)}, f32[16,96]{1,0:T(8,128)}, u32[]{:S(2)}) copy-start(f32[16,96]{1,0:T(8,128)} %param.47) | copy-start | bytes 18436
  756.4 11.2 %copy-start.31 = (f32[960,768]{1,0:T(8,128)S(1)}, f32[960,768]{1,0:T(8,128)}, u32[]{:S(2)}) copy-start(f32[960,768]{1,0:T(8,128)} %param.35) | copy-start | bytes 8847364
  (91 other events, 246.9 us)
Sparse Core Ops, SparseCore 0:
  11.6 97.7 all-gather.2
  112.9 102.3 all-gather.4
  423.5 141.7 reduce-scatter.2
  645.2 90.1 reduce-scatter.4

commit v6 on v5

--- a/solution.py
+++ b/solution.py
@@ -591,6 +591,116 @@
     )(queries, *keys, *values, log_norm, grad_mixed)
 
 
+def project_kernel(hidden_ref, weight_ref, bias_ref, q_ref, k_ref, v_ref):
+    blocks, width = weight_ref.shape[0], weight_ref.shape[2] // 4
+    packed = [dots(hidden_ref[...], weight_ref[m], 1, 0) for m in range(blocks)]
+
+    def slot(at):
+        return jnp.concatenate([p[:, at * width : (at + 1) * width] for p in packed], axis=1)
+
+    q_ref[...] = (slot(0) + bias_ref[0:1]).astype(q_ref.dtype)
+    k_ref[...] = slot(1).astype(k_ref.dtype)
+    v_ref[...] = (slot(2) + bias_ref[1:2]).astype(v_ref.dtype)
+
+
+def project(hidden, blocks, biases):
+    rows = hidden.shape[0]
+    return pl.pallas_call(
+        project_kernel,
+        out_shape=[jax.ShapeDtypeStruct((rows, D), hidden.dtype)] * 3,
+        cost_estimate=pl.CostEstimate(
+            flops=8 * rows * D * D, bytes_accessed=8 * D * D, transcendentals=0
+        ),
+        name="project_heads",
+    )(hidden, blocks, biases)
+
+
+def mixed_grad_kernel(dy_ref, weight_ref, out_ref):
+    blocks, width = weight_ref.shape[0], weight_ref.shape[2] // 4
+    dy = dy_ref[...]
+    packed = [dots(dy, weight_ref[m][:, 3 * width :], 1, 0) for m in range(blocks)]
+    out_ref[...] = jnp.concatenate(packed, axis=1).astype(out_ref.dtype)
+
+
+def hidden_grad_kernel(dq_ref, dk_ref, dv_ref, weight_ref, out_ref):
+    blocks, width = weight_ref.shape[0], weight_ref.shape[2] // 4
+    grads = [r[...].astype(jnp.float32) for r in (dq_ref, dk_ref, dv_ref)]
+    empty = jnp.zeros((grads[0].shape[0], width), jnp.float32)
+    total = 0.0
+    for m in range(blocks):
+        block = [g[:, m * width : (m + 1) * width] for g in grads] + [empty]
+        block = jnp.concatenate(block, axis=1).astype(weight_ref.dtype)
+        total = total + dots(block, weight_ref[m], 1, 1)
+    out_ref[...] = total
+
+
+def projected(kernel, name, kind, *values):
+    rows = values[0].shape[0]
+    return pl.pallas_call(
+        kernel,
+        out_shape=jax.ShapeDtypeStruct((rows, D), kind),
+        cost_estimate=pl.CostEstimate(
+            flops=8 * rows * D * D, bytes_accessed=8 * D * D, transcendentals=0
+        ),
+        name=name,
+    )(*values)
+
+
+def attn_grad_kernel(hidden_ref, dq_ref, dk_ref, dv_ref, dy_ref, mixed_ref, out_ref):
+    blocks, width = out_ref.shape[0], out_ref.shape[2] // 4
+    hidden, dy = hidden_ref[...], dy_ref[...]
+    grads = [dots(hidden, r[...], 0, 0) for r in (dq_ref, dk_ref, dv_ref)]
+    grads.append(dots(dy, mixed_ref[...], 0, 0))
+    for m in range(blocks):
+        block = [g[:, m * width : (m + 1) * width] for g in grads]
+        out_ref[m] = jnp.concatenate(block, axis=1).astype(out_ref.dtype)
+
+
+def attn_weight_grad(blocks, *values):
+    rows = values[0].shape[0]
+    return pl.pallas_call(
+        attn_grad_kernel,
+        out_shape=jax.ShapeDtypeStruct((blocks, D, 4 * D // blocks), values[0].dtype),
+        cost_estimate=pl.CostEstimate(
+            flops=8 * rows * D * D, bytes_accessed=8 * D * D, transcendentals=0
+        ),
+        name="attn_weight_grad",
+    )(*values)
+
+
+def ff_grad_kernel(hidden_ref, dz_ref, up_ref, active_ref, out_ref):
+    def put(left, right):
+        grad = dots(left[...], right[0], 0, 0).astype(out_ref.dtype)
+        out_ref[0, :, 0] = grad.reshape(out_ref.shape[1], *out_ref.shape[3:])
+
+    @pl.when(pl.program_id(1) == 0)
+    def _():
+        put(hidden_ref, up_ref)
+
+    @pl.when(pl.program_id(1) == 1)
+    def _():
+        put(dz_ref, active_ref)
+
+
+def ff_weight_grad(shards, hidden, dz, grad_up, active):
+    blocks, rows, width = active.shape
+    whole = pl.BlockSpec((rows, D), lambda m, s: (0, 0))
+    block = pl.BlockSpec((1, rows, width), lambda m, s: (m, 0, 0))
+    return pl.pallas_call(
+        ff_grad_kernel,
+        grid=(blocks, 2),
+        out_shape=jax.ShapeDtypeStruct((blocks, shards, 2, D // shards, width), hidden.dtype),
+        in_specs=[whole, whole, block, block],
+        out_specs=pl.BlockSpec((1, shards, 1, D // shards, width), lambda m, s: (m, 0, s, 0, 0)),
+        cost_estimate=pl.CostEstimate(
+            flops=4 * rows * D * blocks * width,
+            bytes_accessed=4 * D * blocks * width,
+            transcendentals=0,
+        ),
+        name="ff_weight_grad",
+    )(hidden, dz, grad_up, active)
+
+
 def score_kernel(head_ref, word_ref, bias_ref, label_ref, stat_ref, top, total, target):
     at, last = pl.program_id(1), pl.num_programs(1) - 1
     logits = dots(head_ref[...], word_ref[...], 1, 1) + bias_ref[...]
@@ -732,14 +842,6 @@
     first_core = (c_at == 0).astype(jnp.float32)
 
     side_rows = side_weight.shape[0] // mp_size
-    side_own = lax.dynamic_slice_in_dim(side_weight, mp_rank * side_rows, side_rows, 0)
-    both = jnp.concatenate([attn_weight.reshape(rows_own, 4 * attn_cols), side_own]).astype(low)
-    both = comm_all_gather(both, mp_first).reshape(mp_size, dp_size, -1, D)
-    attn_blocks = both[:, :, :rows_own].reshape(mp_size, D, 4 * attn_cols)
-    side_full = both[:, :, rows_own:].transpose(1, 0, 2, 3).reshape(-1, D)
-    ff_blocks = comm_all_gather(
-        ff_weight.astype(low).reshape(rows_own, 2 * ff_cols), mp_first
-    ).reshape(mp_size, D, 2 * ff_cols)
     vec_cols = vectors.shape[1]
     stripe = vocab_own * x_size
     bias_mine = lax.dynamic_slice_in_dim(decoder_bias, z_at * stripe, stripe, 0)
@@ -775,6 +877,14 @@
     )
     mp_small = mp_small.reshape(mp_size, -1)
     word_plane = word_plane.reshape(-1, D)
+    side_own = lax.dynamic_slice_in_dim(side_weight, mp_rank * side_rows, side_rows, 0)
+    both = jnp.concatenate([attn_weight.reshape(rows_own, 4 * attn_cols), side_own]).astype(low)
+    ff_own = ff_weight.astype(low).reshape(rows_own, 2 * ff_cols)
+    word_plane, both, ff_own = lax.optimization_barrier((word_plane, both, ff_own))
+    both = comm_all_gather(both, mp_first).reshape(mp_size, dp_size, -1, D)
+    attn_blocks = both[:, :, :rows_own].reshape(mp_size, D, 4 * attn_cols)
+    side_full = both[:, :, rows_own:].transpose(1, 0, 2, 3).reshape(-1, D)
+    ff_blocks = comm_all_gather(ff_own, mp_first).reshape(mp_size, D, 2 * ff_cols)
     bias_plane = (
         mp_small[:, :stripe].reshape(mp_size, x_size, vocab_own).transpose(1, 0, 2).reshape(-1)
     )
@@ -807,13 +917,9 @@
     hidden0 = layer_norm(embedded, vec_rows[0], vec_rows[1])
     hidden0_b = hidden0.astype(low)
 
-    qkv_blocks = attn_blocks[:, :, : 3 * attn_cols]
     out_blocks = attn_blocks[:, :, 3 * attn_cols :]
-    packed = jnp.einsum("td,mde->tme", hidden0_b, qkv_blocks, preferred_element_type=jnp.float32)
-    packed = packed.reshape(own_len, mp_size, 3, attn_cols)
-    queries = (packed[:, :, 0] + split_full[:, 0]).astype(low).reshape(own_len, D)
-    own_keys = packed[:, :, 1].astype(low).reshape(own_len, D)
-    own_values = (packed[:, :, 2] + split_full[:, 1]).astype(low).reshape(own_len, D)
+    head_bias = split_full[:, :2].transpose(1, 0, 2).reshape(2, D)
+    queries, own_keys, own_values = project(hidden0_b, attn_blocks, head_bias)
     other_keys, other_values = links.exchange(
         "key_trade", ("trade", ("c",), 0, FAST, own_keys), ("trade", ("c",), 0, FAST, own_values)
     )
@@ -901,33 +1007,29 @@
     grad_r2, grad_g2, grad_s2 = norm_backward(resid2, vec_rows[6], vec_rows[7], grad_top)
     ffn_grad_b = grad_r2.astype(low)
     out_bias_two = jnp.sum(ffn_grad_b.astype(jnp.float32), axis=0)
-    ff_out_grad = jnp.einsum("td,mtf->mdf", ffn_grad_b, active, preferred_element_type=jnp.float32)
     grad_active = jnp.einsum("td,mdf->mtf", ffn_grad_b, ff_out, preferred_element_type=jnp.float32)
     grad_up = (grad_active * gelu_slope(upward)).astype(low)
     ff_bias_grad = jnp.sum(grad_up.astype(jnp.float32), axis=1)
-    ff_in_grad = jnp.einsum("td,mtf->mdf", hidden1_b, grad_up, preferred_element_type=jnp.float32)
     hidden1_part = jnp.einsum("mtf,mdf->td", grad_up, ff_in, preferred_element_type=jnp.float32)
-    ff_grad = jnp.stack(
-        [
-            row_major(g.astype(low)).reshape(mp_size * dp_size, rows_own, ff_cols)
-            for g in (ff_in_grad, ff_out_grad)
-        ],
-        axis=1,
-    )
+    if rows_own % 16 == 0:
+        ff_grad = ff_weight_grad(dp_size, hidden1_b, ffn_grad_b, grad_up, active)
+    else:
+        ff_grad = jnp.stack(
+            [
+                jnp.einsum("td,mtf->mdf", left, right, preferred_element_type=jnp.float32)
+                .astype(low)
+                .reshape(mp_size * dp_size, rows_own, ff_cols)
+                for left, right in ((hidden1_b, grad_up), (ffn_grad_b, active))
+            ],
+            axis=1,
+        )
     ff_grad, hidden1_part = lax.optimization_barrier((ff_grad, hidden1_part))
     ff_red = comm_scatter_sum(ff_grad.reshape(-1, ff_cols), mp_first)
     grad_h1 = grad_r2 + hidden1_part
     grad_r1, grad_g1, grad_s1 = norm_backward(resid1, vec_rows[3], vec_rows[4], grad_h1)
     attn_grad_b = grad_r1.astype(low)
     out_bias_one = jnp.sum(attn_grad_b.astype(jnp.float32), axis=0)
-    mixed_blocks = mixed.reshape(own_len, mp_size, attn_cols)
-    attn_grad_out = jnp.einsum(
-        "td,tme->mde", attn_grad_b, mixed_blocks, preferred_element_type=jnp.float32
-    )
-    grad_mixed = jnp.einsum(
-        "td,mde->tme", attn_grad_b, out_blocks, preferred_element_type=jnp.float32
-    )
-    grad_mixed = grad_mixed.astype(low).reshape(own_len, D)
+    grad_mixed = projected(mixed_grad_kernel, "mixed_grad", low, attn_grad_b, attn_blocks)
     grad_q, own_k, part_k, own_v, part_v = attention_backward(
         queries, keys, values, log_norm, grad_mixed
     )
@@ -938,22 +1040,17 @@
     )
     grad_k = (own_k + from_k).astype(low)
     grad_v = (own_v + from_v).astype(low)
-    grad_packed = jnp.stack(
+    packed_sums = jnp.stack(
         [
-            grad_q.reshape(own_len, mp_size, attn_cols),
-            grad_k.reshape(own_len, mp_size, attn_cols),
-            grad_v.reshape(own_len, mp_size, attn_cols),
+            jnp.sum(g.astype(jnp.float32), axis=0).reshape(mp_size, attn_cols)
+            for g in (grad_q, grad_v)
         ],
-        axis=2,
-    ).reshape(own_len, mp_size, 3 * attn_cols)
-    attn_grad_in = jnp.einsum(
-        "td,tme->mde", hidden0_b, grad_packed, preferred_element_type=jnp.float32
-    )
-    packed_sums = jnp.sum(grad_packed.astype(jnp.float32), axis=0).reshape(mp_size, 3, attn_cols)
-    hidden0_part = jnp.einsum(
-        "tme,mde->td", grad_packed, qkv_blocks, preferred_element_type=jnp.float32
-    )
-    attn_grad = jnp.concatenate([attn_grad_in, attn_grad_out], axis=2).astype(low)
+        axis=1,
+    )
+    hidden0_part = projected(
+        hidden_grad_kernel, "hidden_grad", jnp.float32, grad_q, grad_k, grad_v, attn_blocks
+    )
+    attn_grad = attn_weight_grad(mp_size, hidden0_b, grad_q, grad_k, grad_v, attn_grad_b, mixed)
     attn_grad = attn_grad.reshape(y_size, c_size, z_size, x_size, rows_own, 4 * attn_cols)
     grad_h0 = grad_r1 + hidden0_part
     grad_x0, grad_g0, grad_s0 = norm_backward(embedded, vec_rows[0], vec_rows[1], grad_h0)
@@ -1026,8 +1123,7 @@
     )
     split_grad = jnp.concatenate(
         [
-            packed_sums[:, 0:1],
-            packed_sums[:, 2:3],
+            packed_sums,
             ff_bias_grad.reshape(mp_size, attn_cols, 4).transpose(0, 2, 1),
         ],
         axis=1,

time: 787 us -> 776 us (0.986)
  local copies, waits for them, and re-layouts: 103 us -> 71.8 us
  Pallas kernels: 450 us -> 480 us
  waiting for transfers between devices: 18.7 us -> 40.2 us
  matrix products: 101 us -> 81.1 us
  other arithmetic: 81.7 us -> 71.9 us
    pallas_call x0 -> x5, Pallas kernels: none -> 38.3 us  [the longest x1 12.9 us: ff_weight_grad(): pl.pallas_call(ff_grad_kernel, grid=(blocks, 2), out_shape=jax.ShapeDtype...]
    dot_general x6 -> x0, matrix products: 22.6 us -> none  [the longest x1 5.08 us: step(): jnp.einsum('td,mtf->mdf', hidden1_b, grad_up, preferred_element_type=jnp....]
    all_gather x2, waiting for transfers between devices: 0.02 us -> 19.9 us  [comm_all_gather(): return lax.all_gather(value, axes, axis=0, tiled=True)]
    another operation x2 -> x1, other arithmetic: 9.34 us -> 0.07 us  [the longest x1 8.23 us: step(): jnp.stack([row_major(g.astype(low)).reshape(mp_size * dp_size, rows_own,...]
    pallas_call x16, Pallas kernels: 364 us -> 356 us  [call(): pl.pallas_call(kernel, out_shape=outs, in_specs=[pl.BlockSpec(memory_spac...]
    unnamed x286 -> x251, local copies, waits for them, and re-layouts: 31.9 us -> 27.8 us
  transfers between devices with their start and end apart: 4 -> 4, of which waited for: 1 -> 2; matrix products, arithmetic and copies ran while one was open for 17% -> 11% of each run, Pallas kernels for 45% -> 41%
where the time goes in v6:
time: 776 us; the launch traced here: 770 us
  Pallas kernels  480 us (62%)
  matrix products  81.1 us (10%)
  other arithmetic  71.9 us (9%)
  local copies, waits for them, and re-layouts  71.8 us (9%)
  waiting for transfers between devices  40.2 us (5%)
  between operations  25.1 us (3%)
    pallas_call x16, Pallas kernels, call(): pl.pallas_call(kernel, out_shape=outs, in_specs=[pl.BlockSpec(memory_spac...  356 us
    dot_general x1, matrix products, step(): jnp.dot(onehot, all_x0, preferred_element_type=jnp.float32)  34 us
    unnamed x251, local copies, waits for them, and re-layouts  27.8 us
    pallas_call x1, Pallas kernels, attention_backward(): pl.pallas_call(backward_kernel, grid=(pairs,), out_shape=[jax.ShapeDtypeS...  23.5 us
    pallas_call x1, Pallas kernels, attention_forward(): pl.pallas_call(forward_kernel, grid=(pairs,), out_shape=[jax.ShapeDtypeSt...  22.3 us
    pallas_call x1, Pallas kernels, head_slopes(): pl.pallas_call(slope_kernel, grid=grid, out_shape=[jax.ShapeDtypeStruct((...  21.1 us
    all_gather x2, waiting for transfers between devices, comm_all_gather(): return lax.all_gather(value, axes, axis=0, tiled=True)  19.9 us
    reduce_scatter x2, waiting for transfers between devices, comm_scatter_sum(): return lax.psum_scatter(value, axes, scatter_dimension=0, tiled=True)  19.6 us
  transfers between devices with their start and end apart: 4, of which 2 were waited for; matrix products, arithmetic and copies ran while one was open for 11% of the time, Pallas kernels for 41%

profile of v6, /device:TPU:0, one launch (start us, length us, event | category | flops | bytes accessed | tf_op | source)
XLA Modules:
  0.0 769.8 jit_solution(15719765357422673497)
XLA Ops:
  17.4 59.3 %word_gather.1 = (bf16[2,2,2,4,240,768]{5,4,3,2,1,0:T(8,128)(2,1)S(1)}, s32[4,8,128]{2,1,0:T(8,128)S(1)}, bf16[8,16,128]{2,1,0:T(8,128)(2,1)S(1)}, f32[8,8,128]{2,1,0:T(8,128)S(1)}, f32[4,24,128]{2,1,0:T(8,128)S(1)}) custom-call(bf16[4,240,768]{2,1,0:T(8,128)(2,1)S(1)} %bitcast.284, s32[8,128]{1,0:T(8,128)S(1)} %pad_bitcast_fusion.refs_1_, ...), custom_call_target="tpu_custom_call" | custom-call | bytes 23855104 | tf_op jit(solution)/shard_map/word_gather/pallas_call | solution.py:116
  76.7 4.4 copy-done
  83.5 16.1 %gather_fusion = bf16[2048,768]{1,0:T(8,128)(2,1)} fusion(bf16[7680,768]{1,0:T(8,128)(2,1)} %bitcast.275, s32[2048]{0:T(1024)S(1)} %broadcast_clamp_fusion), kind=kCustom, calls=%fused_computation | custom fusion | bytes 6299648 | tf_op jit(solution)/shard_map/gather | solution.py:902
  99.6 2.1 broadcast_select_fusion.source
  101.7 87.3 %token_fold.1 = bf16[8,64,768]{2,1,0:T(8,128)(2,1)S(1)} custom-call(bf16[4,8,64,768]{3,2,1,0:T(8,128)(2,1)S(1)} %broadcast_select_fusion.source), custom_call_target="tpu_custom_call" | custom-call | bytes 6291456 | tf_op jit(solution)/shard_map/token_fold/pallas_call | solution.py:116
  198.8 4.9 slice.234
  203.7 2.4 slice_bitcast_fusion
  210.0 6.3 project_heads.1
  218.7 3.5 key_trade.1
  224.0 22.3 %attention_forward.1 = (bf16[512,768]{1,0:T(8,128)(2,1)}, f32[6,2,512]{2,1,0:T(2,128)}) custom-call(bf16[512,768]{1,0:T(8,128)(2,1)} %get-tuple-element.74.q_ref, bf16[512,768]{1,0:T(8,128)(2,1)} %get-tuple-element.75.refs_0_.k0_ref, bf16[512,768]{1,0:T(8,128)(2,1)} %copy-done.8, bf16[512,768]{1,0:T(8,128)(2,1)} %get-tuple-element.76.refs_1_.v0_ref, ...), custom_call_target="tpu_custom_call" | custom-call | flops 3221225472 | bytes 6291456 | tf_op jit(solution)/shard_map/attention_forward/pallas_call | solution.py:528
  246.2 2.4 copy.185
  248.6 3.4 fusion.147
  252.7 19.9 %all-gather.5.cloned.1.call-done = bf16[3072,1536]{1,0:T(8,128)(2,1)} async-done(((bf16[96,1536]{1,0:T(8,128)(2,1)}), bf16[3072,1536]{1,0:T(8,128)(2,1)}) %all-gather.5.cloned.1.call-update) | async-done | bytes 9437200 | tf_op jit(solution)/shard_map/all_gather | solution.py:64
  272.6 6.8 fusion.11
  279.4 2.9 fusion.148
  283.8 2.4 hidden_trade.1
  286.2 2.2 fusion.151
  295.6 2.6 gather_fusion.1
  298.1 2.4 fusion.143
  300.9 16.4 %head_gather.1 = bf16[4,4,32,768]{3,2,1,0:T(8,128)(2,1)S(1)} custom-call(bf16[4,32,768]{2,1,0:T(8,128)(2,1)S(1)} %bitcast.293), custom_call_target="tpu_custom_call" | custom-call | bytes 1572864 | tf_op jit(solution)/shard_map/head_gather/pallas_call | solution.py:116
  318.1 18.8 %head_scores.1 = f32[512,128]{1,0:T(8,128)} custom-call(bf16[512,768]{1,0:T(8,128)(2,1)} %bitcast.290, bf16[7680,768]{1,0:T(8,128)(2,1)} %bitcast.276, f32[1,7680]{1,0:T(1,128)} %broadcast_in_dim_reshape.2.bias_ref, s32[512,1]{1,0:T(8,128)} %fusion.79.label_ref), custom_call_target="tpu_custom_call" | custom-call | flops 6039797760 | bytes 11796480 | tf_op jit(solution)/shard_map/head_scores/pallas_call | solution.py:772
  338.0 5.7 stat_gather.1
  346.7 21.1 %head_slopes.1 = (bf16[512,7680]{1,0:T(8,128)(2,1)}, f32[1,1,7680]{2,1,0:T(1,128)}, f32[512,768]{1,0:T(8,128)}) custom-call(bf16[512,768]{1,0:T(8,128)(2,1)} %bitcast.291, bf16[7680,768]{1,0:T(8,128)(2,1)} %bitcast.277, f32[1,7680]{1,0:T(1,128)} %broadcast_in_dim_reshape.2.bias_ref, s32[512,1]{1,0:T(8,128)} %fusion.79.label_ref, f32[512,1]{1,0:T(8,128)} %copy.198.norm_ref, ...), custom_call_target="tpu_custom_call" | custom-call | flops 6039797760 | bytes 11796480 | tf_op jit(solution)/shard_map/head_slopes/pallas_call | solution.py:788
  369.4 15.6 %head_spread.1 = bf16[3,128,768]{2,1,0:T(8,128)(2,1)S(1)} custom-call(bf16[4,128,768]{2,1,0:T(8,128)(2,1)S(1)} %bitcast_convert_fusion.refs_0_), custom_call_target="tpu_custom_call" | custom-call | bytes 1179648 | tf_op jit(solution)/shard_map/head_spread/pallas_call | solution.py:116
  396.4 8.6 %convert_reduce_fusion = (f32[4,768]{1,0:T(4,128)}, bf16[4,512,768]{2,1,0:T(8,128)(2,1)S(1)}) fusion(f32[4,768,512]{1,2,0:T(8,128)} %get-tuple-element.213, f32[4,768]{1,0:T(4,128)S(1)} %copy-done.87, bf16[4,768,1536]{2,1,0:T(8,128)(2,1)} %bitcast.348, bf16[512,768]{1,0:T(8,128)(2,1)S(1)} %get-tuple-element.170.dz_ref), kind=kOutput, calls=%fused_computation.19 | convolution fusion | flops 2436363264 | bytes 14966784 | tf_op jit(solution)/shard_map/td,mdf->mtf/dot_general | solution.py:1010
  406.7 3.8 fusion.35
  410.4 12.9 %ff_weight_grad.1 = bf16[4,8,2,96,768]{4,3,2,1,0:T(8,128)(2,1)} custom-call(bf16[512,768]{1,0:T(8,128)(2,1)} %copy-done.35, bf16[512,768]{1,0:T(8,128)(2,1)} %copy-done.36, bf16[4,512,768]{2,1,0:T(8,128)(2,1)} %copy-done.111, bf16[4,512,768]{2,1,0:T(8,128)(2,1)} %copy-done.110), custom_call_target="tpu_custom_call" | custom-call | flops 4831838208 | bytes 9437184 | tf_op jit(solution)/shard_map/ff_weight_grad/pallas_call | solution.py:689
  424.7 3.3 multiply_reduce_fusion.1
  431.5 4.9 mixed_grad.1.g_ref
  436.4 23.5 %attention_backward.1 = (bf16[512,768]{1,0:T(8,128)(2,1)}, f32[512,768]{1,0:T(8,128)}, f32[512,768]{1,0:T(8,128)}, f32[512,768]{1,0:T(8,128)}, f32[512,768]{1,0:T(8,128)}) custom-call(bf16[512,768]{1,0:T(8,128)(2,1)} %get-tuple-element.74.q_ref, bf16[512,768]{1,0:T(8,128)(2,1)} %get-tuple-element.75.refs_0_.k0_ref, bf16[512,768]{1,0:T(8,128)(2,1)} %copy-done.8, ...), custom_call_target="tpu_custom_call" | custom-call | flops 8053063680 | bytes 12582912 | tf_op jit(solution)/shard_map/attention_backward/pallas_call | solution.py:581
  462.9 6.3 key_grad_trade.1
  472.0 7.0 hidden_grad.1
  479.0 3.2 multiply_reduce_fusion.2
  485.0 7.2 attn_weight_grad.1
  495.3 19.2 %grad_swap_c.1 = (bf16[2,4,2,96,768]{4,3,2,1,0:T(8,128)(2,1)S(1)}, bf16[4,2,2,80,768]{4,3,2,1,0:T(8,128)(2,1)S(1)}, bf16[4,1,64,768]{3,2,1,0:T(8,128)(2,1)S(1)}) custom-call(bf16[2,2,4,2,96,768]{5,4,3,2,1,0:T(8,128)(2,1)S(1)} %bitcast.280, bf16[4,2,2,2,80,768]{5,4,3,2,1,0:T(8,128)(2,1)S(1)} %bitcast.282, bf16[1,64,768]{2,1,0:T(8,128)(2,1)S(1)} %slice_bitcast_fusion.1.refs_2_), custom_call_target="tpu_custom_call" | custom-call | bytes 9437184 | tf_op jit(solution)/shard_map/grad_swap_c/pallas_call | solution.py:116
  515.9 40.1 %grad_swap_xy.1 = (bf16[2,4,96,768]{3,2,1,0:T(8,128)(2,1)S(1)}, bf16[4,2,80,768]{3,2,1,0:T(8,128)(2,1)S(1)}, bf16[4,4,64,768]{3,2,1,0:T(8,128)(2,1)S(1)}) custom-call(bf16[2,4,2,96,768]{4,3,2,1,0:T(8,128)(2,1)S(1)} %copy.205.refs_0_, bf16[4,2,2,80,768]{4,3,2,1,0:T(8,128)(2,1)S(1)} %copy.206.refs_1_, bf16[4,64,768]{2,1,0:T(8,128)(2,1)S(1)} %bitcast.285), custom_call_target="tpu_custom_call" | custom-call | bytes 7471104 | tf_op jit(solution)/shard_map/grad_swap_xy/pallas_call | solution.py:116
  556.7 26.5 %grad_swap_yx.1 = (bf16[4,96,768]{2,1,0:T(8,128)(2,1)S(1)}, bf16[4,80,768]{2,1,0:T(8,128)(2,1)S(1)}, bf16[4,3,64,768]{3,2,1,0:T(8,128)(2,1)S(1)}) custom-call(bf16[2,4,96,768]{3,2,1,0:T(8,128)(2,1)S(1)} %fusion.28.refs_0_, bf16[4,2,80,768]{3,2,1,0:T(8,128)(2,1)S(1)} %copy.208.refs_1_, bf16[3,64,768]{2,1,0:T(8,128)(2,1)S(1)} %bitcast.288), custom_call_target="tpu_custom_call" | custom-call | bytes 4521984 | tf_op jit(solution)/shard_map/grad_swap_yx/pallas_call | solution.py:116
  584.8 11.1 %fusion.152 = f32[7680,768]{1,0:T(8,128)} fusion(bf16[512,7680]{1,0:T(8,128)(2,1)S(1)} %bitcast.354, bf16[512,768]{1,0:T(8,128)(2,1)S(1)} %bitcast.292), kind=kOutput, calls=%fused_computation.368 | convolution fusion | flops 6039797760 | bytes 32243712 | tf_op jit(solution)/shard_map/rv,rd->vd/dot_general | solution.py:1099
  597.3 34.0 %add_convert_fusion = bf16[7680,768]{1,0:T(8,128)(2,1)} fusion(f32[7680,768]{1,0:T(8,128)} %fusion.152, bf16[2048,768]{1,0:T(8,128)(2,1)S(1)} %bitcast.311, s32[2048]{0:T(1024)S(1)} %copy-done.96), kind=kOutput, calls=%fused_computation.5 | convolution fusion | flops 24186716160 | bytes 38543360 | tf_op jit(solution)/shard_map/dot_general | solution.py:1100
  637.4 22.1 %grad_spread_z.1 = (bf16[3,96,768]{2,1,0:T(8,128)(2,1)S(1)}, bf16[3,80,768]{2,1,0:T(8,128)(2,1)S(1)}) custom-call(bf16[4,96,768]{2,1,0:T(8,128)(2,1)S(1)} %fusion.46.refs_0_, bf16[4,80,768]{2,1,0:T(8,128)(2,1)S(1)} %fusion.55.refs_1_), custom_call_target="tpu_custom_call" | custom-call | bytes 1622016 | tf_op jit(solution)/shard_map/grad_spread_z/pallas_call | solution.py:116
  659.5 28.1 %small_sum.1 = f32[4,192,128]{2,1,0:T(8,128)S(1)} custom-call(f32[192,128]{1,0:T(8,128)S(1)} %maximum_bitcast_fusion.x_ref), custom_call_target="tpu_custom_call" | custom-call | bytes 1572864 | tf_op jit(solution)/shard_map/small_sum/pallas_call | solution.py:116
  689.7 8.9 %side_gather.1 = bf16[4,80,768]{2,1,0:T(8,128)(2,1)S(1)} custom-call(bf16[80,768]{1,0:T(8,128)(2,1)S(1)} %convert_add_fusion.7.refs_0_), custom_call_target="tpu_custom_call" | custom-call | bytes 983040 | tf_op jit(solution)/shard_map/side_gather/pallas_call | solution.py:116
  706.0 19.6 %reduce-scatter.5.cloned.1.call-done = bf16[960,768]{1,0:T(8,128)(2,1)} async-done(((bf16[7680,768]{1,0:T(8,128)(2,1)}), bf16[960,768]{1,0:T(8,128)(2,1)}) %reduce-scatter.5.cloned.1.call-update) | async-done | bytes 1474576 | tf_op jit(solution)/shard_map/reduce_scatter | solution.py:68
  725.7 2.7 fusion.24
  730.4 12.5 %norm_sum.1 = f32[4,8,128]{2,1,0:T(8,128)S(1)} custom-call(f32[8,128]{1,0:T(8,128)S(1)} %iota.35.x_ref), custom_call_target="tpu_custom_call" | custom-call | bytes 65536 | tf_op jit(solution)/shard_map/norm_sum/pallas_call | solution.py:116
  746.0 4.9 multiply_subtract_fusion.2
  751.6 3.8 multiply_subtract_fusion.1
  757.7 4.2 multiply_subtract_fusion
  (463 shorter events, 95.4 us)
Async XLA Ops:
  7.2 191.6 %all-gather.3.cloned.1.call-start = ((), (), s32[]{:S(2)}) async-start(), calls=%async_computation.2 | async-start | bytes 8921088 | tf_op jit(solution)/shard_map/all_gather | solution.py:64
  76.7 4.4 copy-start
  81.1 191.4 %all-gather.5.cloned.1.call-start = ((), (), s32[]{:S(2)}) async-start(), calls=%async_computation.3 | async-start | bytes 9732096 | tf_op jit(solution)/shard_map/all_gather | solution.py:64
  81.9 513.9 %reduce-scatter.3.cloned.1.call-start = ((), (), s32[]{:S(2)}) async-start(), calls=%async_computation.4 | async-start | bytes 9732096 | tf_op jit(solution)/shard_map/reduce_scatter | solution.py:68
  101.7 89.7 %copy-start.108 = (s32[2]{0:T(128)S(1)}, s32[2]{0:T(128)}, u32[]{:S(2)}) copy-start(s32[2]{0:T(128)} %param.32) | copy-start | bytes 28
  189.0 6.5 copy-start.105
  190.4 89.0 %copy-start.41 = (f32[768]{0:T(1024)}, f32[768]{0:T(1024)S(1)}, u32[]{:S(2)}) copy-start(f32[768]{0:T(1024)S(1)} %mul.794) | copy-start | bytes 9220
  191.0 81.6 %copy-start.86 = (f32[4,768]{1,0:T(4,128)}, f32[4,768]{1,0:T(4,128)S(1)}, u32[]{:S(2)}) copy-start(f32[4,768]{1,0:T(4,128)S(1)} %add.734) | copy-start | bytes 36868
  191.1 91.6 %copy-start.46 = (f32[768]{0:T(1024)}, f32[768]{0:T(1024)S(1)}, u32[]{:S(2)}) copy-start(f32[768]{0:T(1024)S(1)} %mul.803) | copy-start | bytes 9220
  194.9 12.1 %copy-start.90 = (pred[512]{0:T(512)(128)(4,1)}, pred[512]{0:T(512)(128)(4,1)S(1)}, u32[]{:S(2)}) copy-start(pred[512]{0:T(512)(128)(4,1)S(1)} %get-tuple-element.145) | copy-start | bytes 1540
  207.6 8.8 %copy-start.71 = (f32[512]{0:T(512)}, f32[512]{0:T(512)S(1)}, u32[]{:S(2)}) copy-start(f32[512]{0:T(512)S(1)} %get-tuple-element.190) | copy-start | bytes 6148
  207.6 41.0 %copy-start.58 = (f32[512]{0:T(512)}, f32[512]{0:T(512)S(1)}, u32[]{:S(2)}) copy-start(f32[512]{0:T(512)S(1)} %fusion.115) | copy-start | bytes 6148
  252.0 27.4 %copy-start.43 = (f32[512]{0:T(512)}, f32[512]{0:T(512)S(1)}, u32[]{:S(2)}) copy-start(f32[512]{0:T(512)S(1)} %broadcast_multiply_fusion.2) | copy-start | bytes 6148
  252.3 27.1 %copy-start.63 = (f32[512]{0:T(512)}, f32[512]{0:T(512)S(1)}, u32[]{:S(2)}) copy-start(f32[512]{0:T(512)S(1)} %multiply_reduce_fusion.7) | copy-start | bytes 6148
  252.4 27.1 %copy-start.48 = (f32[512]{0:T(512)}, f32[512]{0:T(512)S(1)}, u32[]{:S(2)}) copy-start(f32[512]{0:T(512)S(1)} %fusion.116) | copy-start | bytes 6148
  252.7 26.7 %copy-start.35 = (bf16[512,768]{1,0:T(8,128)(2,1)}, bf16[512,768]{1,0:T(8,128)(2,1)S(1)}, u32[]{:S(2)}) copy-start(bf16[512,768]{1,0:T(8,128)(2,1)S(1)} %fusion.43.hidden_ref) | copy-start | bytes 2359300
  272.6 6.9 copy-start.107
  300.5 86.5 %copy-start.84 = (f32[128]{0:T(128)}, f32[128]{0:T(128)S(1)}, u32[]{:S(2)}) copy-start(f32[128]{0:T(128)S(1)} %broadcast_multiply_fusion.4) | copy-start | bytes 1540
  300.7 86.3 %copy-start.97 = (f32[128]{0:T(128)}, f32[128]{0:T(128)S(1)}, u32[]{:S(2)}) copy-start(f32[128]{0:T(128)S(1)} %fusion.124) | copy-start | bytes 1540
  369.4 18.5 %copy-start.37 = (f32[128,768]{1,0:T(8,128)S(1)}, f32[128,768]{1,0:T(8,128)}, u32[]{:S(2)}) copy-start(f32[128,768]{1,0:T(8,128)} %get-tuple-element.216) | copy-start | bytes 1179652
  385.0 4.4 copy-start.14
  395.5 9.5 %copy-start.19 = (f32[512,768]{1,0:T(8,128)}, f32[512,768]{1,0:T(8,128)S(1)}, u32[]{:S(2)}) copy-start(f32[512,768]{1,0:T(8,128)S(1)} %get-tuple-element.184) | copy-start | bytes 4718596
  395.5 9.4 %copy-start.69 = (f32[512]{0:T(512)}, f32[512]{0:T(512)S(1)}, u32[]{:S(2)}) copy-start(f32[512]{0:T(512)S(1)} %negate_multiply_fusion.2) | copy-start | bytes 6148
  395.6 11.1 %slice-start.2 = ((s8[9437184]{0:T(1024)(128)(4,1)}), s8[4194304]{0:T(1024)(128)(4,1)S(1)}, s32[]{:S(2)}) async-start(s8[9437184]{0:T(1024)(128)(4,1)} %bitcast.350), calls=%async_computation.8 | async-start | bytes 8388608
  396.4 8.6 %copy-start.36 = (bf16[512,768]{1,0:T(8,128)(2,1)}, bf16[512,768]{1,0:T(8,128)(2,1)S(1)}, u32[]{:S(2)}) copy-start(bf16[512,768]{1,0:T(8,128)(2,1)S(1)} %get-tuple-element.170.dz_ref) | copy-start | bytes 2359300
  396.4 10.3 %slice-start.3 = ((s8[9437184]{0:T(1024)(128)(4,1)}), s8[4194304]{0:T(1024)(128)(4,1)S(1)}, s32[]{:S(2)}) async-start(s8[9437184]{0:T(1024)(128)(4,1)} %bitcast.350), calls=%async_computation.9 | async-start | bytes 8388608
  396.4 10.3 %slice-start.4 = ((s8[9437184]{0:T(1024)(128)(4,1)}), s8[1048576]{0:T(1024)(128)(4,1)S(1)}, s32[]{:S(2)}) async-start(s8[9437184]{0:T(1024)(128)(4,1)} %bitcast.350), calls=%async_computation.10 | async-start | bytes 2097152
  423.4 302.3 %reduce-scatter.5.cloned.1.call-start = ((), (), s32[]{:S(2)}) async-start(), calls=%async_computation.5 | async-start | bytes 13271040 | tf_op jit(solution)/shard_map/reduce_scatter | solution.py:68
  462.9 6.4 copy-start.29
  472.0 7.0 copy-start.12
  472.0 7.0 copy-start.59
  485.0 7.2 copy-start.98
  515.9 68.3 %slice-start.5 = ((s8[7864320]{0:T(1024)(128)(4,1)}), s8[3670016]{0:T(1024)(128)(4,1)S(1)}, s32[]{:S(2)}) async-start(s8[7864320]{0:T(1024)(128)(4,1)} %bitcast.353), calls=%async_computation.11 | async-start | bytes 7340032
  556.3 27.9 %slice-start.6 = ((s8[7864320]{0:T(1024)(128)(4,1)}), s8[4194304]{0:T(1024)(128)(4,1)S(1)}, s32[]{:S(2)}) async-start(s8[7864320]{0:T(1024)(128)(4,1)} %bitcast.353), calls=%async_computation.12 | async-start | bytes 8388608
  687.6 12.4 %copy-start.40 = (bf16[192,768]{1,0:T(8,128)(2,1)S(1)}, bf16[192,768]{1,0:T(8,128)(2,1)}, u32[]{:S(2)}) copy-start(bf16[192,768]{1,0:T(8,128)(2,1)} %reduce-scatter.3.cloned.1.call-done) | copy-start | bytes 884740
  706.0 38.6 %copy-start.54 = (f32[6,192]{1,0:T(8,128)S(1)}, f32[6,192]{1,0:T(8,128)}, u32[]{:S(2)}) copy-start(f32[6,192]{1,0:T(8,128)} %param.48) | copy-start | bytes 13828
  706.0 38.6 %copy-start.92 = (f32[6,192]{1,0:T(8,128)S(1)}, f32[6,192]{1,0:T(8,128)}, u32[]{:S(2)}) copy-start(f32[6,192]{1,0:T(8,128)} %param.49) | copy-start | bytes 13828
  706.0 38.6 %copy-start.93 = (f32[6,192]{1,0:T(8,128)S(1)}, f32[6,192]{1,0:T(8,128)}, u32[]{:S(2)}) copy-start(f32[6,192]{1,0:T(8,128)} %param.50) | copy-start | bytes 13828
  706.0 39.2 %copy-start.56 = (f32[16,96]{1,0:T(8,128)S(1)}, f32[16,96]{1,0:T(8,128)}, u32[]{:S(2)}) copy-start(f32[16,96]{1,0:T(8,128)} %param.45) | copy-start | bytes 18436
  706.0 39.2 %copy-start.94 = (f32[16,96]{1,0:T(8,128)S(1)}, f32[16,96]{1,0:T(8,128)}, u32[]{:S(2)}) copy-start(f32[16,96]{1,0:T(8,128)} %param.46) | copy-start | bytes 18436
  706.0 39.2 %copy-start.95 = (f32[16,96]{1,0:T(8,128)S(1)}, f32[16,96]{1,0:T(8,128)}, u32[]{:S(2)}) copy-start(f32[16,96]{1,0:T(8,128)} %param.47) | copy-start | bytes 18436
  745.9 5.0 copy-start.45
  745.9 5.0 copy-start.52
  745.9 5.0 copy-start.53
  745.9 5.6 copy-start.34
  745.9 11.2 %copy-start.27 = (f32[960,768]{1,0:T(8,128)S(1)}, f32[960,768]{1,0:T(8,128)}, u32[]{:S(2)}) copy-start(f32[960,768]{1,0:T(8,128)} %param.35) | copy-start | bytes 8847364
  751.6 5.5 copy-start.24
  751.6 5.5 copy-start.26
  (75 other events, 152.8 us)
Sparse Core Ops, SparseCore 0:
  81.3 102.0 all-gather.2
  187.0 85.5 all-gather.4
  423.5 152.1 reduce-scatter.2
  631.5 94.1 reduce-scatter.4

commit v7 on v6

--- a/solution.py
+++ b/solution.py
@@ -767,6 +767,51 @@
     return row_block, block, grid, column, specs, cost
 
 
+def word_grad_kernel(slope_ref, head_ref, at_ref, x0_ref, out_ref, total):
+    chunk, last = pl.program_id(1), pl.num_programs(1) - 1
+    first_row = pl.program_id(0) * total.shape[0]
+    rows = first_row + lax.broadcasted_iota(jnp.int32, (total.shape[0], at_ref.shape[1]), 0)
+    onehot = jnp.where(rows == at_ref[...], 1.0, 0.0).astype(jnp.bfloat16)
+    part = dots(onehot, x0_ref[...], 1, 0)
+
+    @pl.when(chunk == 0)
+    def _():
+        total[...] = part + dots(slope_ref[...], head_ref[...], 0, 0)
+
+    @pl.when(chunk > 0)
+    def _():
+        total[...] += part
+
+    @pl.when(chunk == last)
+    def _():
+        out_ref[...] = total[...].astype(out_ref.dtype)
+
+
+def word_weight_grad(slopes, head, at, x0):
+    (rows, vocab), tokens = slopes.shape, at.shape[0]
+    block = 768 if vocab % 768 == 0 else vocab
+    chunk = 2048 if tokens % 2048 == 0 else tokens
+    return pl.pallas_call(
+        word_grad_kernel,
+        grid=(vocab // block, tokens // chunk),
+        out_shape=jax.ShapeDtypeStruct((vocab, D), head.dtype),
+        in_specs=[
+            pl.BlockSpec((rows, block), lambda i, j: (0, i)),
+            pl.BlockSpec((rows, D), lambda i, j: (0, 0)),
+            pl.BlockSpec((1, chunk), lambda i, j: (0, j)),
+            pl.BlockSpec((chunk, D), lambda i, j: (j, 0)),
+        ],
+        out_specs=pl.BlockSpec((block, D), lambda i, j: (i, 0)),
+        scratch_shapes=[pltpu.VMEM((block, D), jnp.float32)],
+        cost_estimate=pl.CostEstimate(
+            flops=2 * (rows + tokens) * vocab * D,
+            bytes_accessed=2 * vocab * (rows + D),
+            transcendentals=0,
+        ),
+        name="word_weight_grad",
+    )(slopes, head, at[None], x0)
+
+
 def head_scores(head, word, bias, labels):
     row_block, _, grid, _, specs, cost = head_blocks(head, word, bias)
     stats = pl.pallas_call(
@@ -846,10 +891,13 @@
     stripe = vocab_own * x_size
     bias_mine = lax.dynamic_slice_in_dim(decoder_bias, z_at * stripe, stripe, 0)
     int_count = own_len + 2 * own_slots
+    side_own = lax.dynamic_slice_in_dim(side_weight, mp_rank * side_rows, side_rows, 0)
+    both = jnp.concatenate([attn_weight.reshape(rows_own, 4 * attn_cols), side_own]).astype(low)
     word_parts = 4 if vocab_own % 64 == 0 else 1
-    word_plane, ints, vec_parts, counts, mp_small = links.exchange(
+    word_plane, both, ints, vec_parts, counts, mp_small = links.exchange(
         "word_gather",
         ("plane", plane, 0, BIG, word_table.astype(low).reshape(word_parts, -1, D)),
+        links.line_move(both, 88, BIG),
         ("gather", ("z",), 0, FAST, lanes(jnp.concatenate([own_ids, own_labels, own_valid]))),
         ("gather", ("z", "x"), 0, FAST, jnp.pad(vectors.astype(low), ((0, 0), (0, 128 - vec_cols)))),
         (
@@ -877,13 +925,12 @@
     )
     mp_small = mp_small.reshape(mp_size, -1)
     word_plane = word_plane.reshape(-1, D)
-    side_own = lax.dynamic_slice_in_dim(side_weight, mp_rank * side_rows, side_rows, 0)
-    both = jnp.concatenate([attn_weight.reshape(rows_own, 4 * attn_cols), side_own]).astype(low)
     ff_own = ff_weight.astype(low).reshape(rows_own, 2 * ff_cols)
     word_plane, both, ff_own = lax.optimization_barrier((word_plane, both, ff_own))
-    both = comm_all_gather(both, mp_first).reshape(mp_size, dp_size, -1, D)
-    attn_blocks = both[:, :, :rows_own].reshape(mp_size, D, 4 * attn_cols)
-    side_full = both[:, :, rows_own:].transpose(1, 0, 2, 3).reshape(-1, D)
+    both = comm_all_gather(both.reshape(-1, D), ("y", "c", "x"))
+    both = both.reshape(mp_size, x_size, z_size, -1, D)
+    attn_blocks = both[:, :, :, :rows_own].transpose(0, 2, 1, 3, 4).reshape(mp_size, D, 4 * attn_cols)
+    side_full = both[:, :, :, rows_own:].transpose(2, 1, 0, 3, 4).reshape(-1, D)
     ff_blocks = comm_all_gather(ff_own, mp_first).reshape(mp_size, D, 2 * ff_cols)
     bias_plane = (
         mp_small[:, :stripe].reshape(mp_size, x_size, vocab_own).transpose(1, 0, 2).reshape(-1)
@@ -1092,14 +1139,9 @@
     ff_red, x0_three = lax.optimization_barrier((ff_red, x0_three))
     all_x0 = [x.reshape(z_size, -1, D) for x in (x0_one, x0_two, x0_three)]
     all_x0 = jnp.concatenate(all_x0, axis=1).reshape(-1, D)
-    onehot = (
-        jnp.where(inside, at, -1)[None, :]
-        == lax.broadcasted_iota(jnp.int32, (word_plane.shape[0], flat_ids.shape[0]), 0)
-    ).astype(low)
-    word_grad = jnp.einsum("rv,rd->vd", grad_logits, head_b, preferred_element_type=jnp.float32)
-    word_grad = word_grad + jnp.dot(onehot, all_x0, preferred_element_type=jnp.float32)
+    word_grad = word_weight_grad(grad_logits, head_b, jnp.where(inside, at, -1), all_x0)
     word_grad, attn_grad, side_grad = lax.optimization_barrier(
-        (word_grad.astype(low), attn_grad, side_grad)
+        (word_grad, attn_grad, side_grad)
     )
     word_red = comm_scatter_sum(word_grad, plane).astype(jnp.float32)
     from_a, from_s = links.exchange(

time: 776 us -> 728 us (0.938)
  matrix products: 81.1 us -> 37.9 us
  Pallas kernels: 480 us -> 502 us
  waiting for transfers between devices: 40.2 us -> 20.2 us
    dot_general x2 -> x0, matrix products: 45.1 us -> none  [the longest x1 34 us: step(): jnp.dot(onehot, all_x0, preferred_element_type=jnp.float32)]
    pallas_call x0 -> x1, Pallas kernels: none -> 35.8 us  [word_weight_grad(): pl.pallas_call(word_grad_kernel, grid=(vocab // block, tokens // chunk),...]
    all_gather x2, waiting for transfers between devices: 19.9 us -> 0.02 us  [comm_all_gather(): return lax.all_gather(value, axes, axis=0, tiled=True)]
    pallas_call x16, Pallas kernels: 356 us -> 342 us  [call(): pl.pallas_call(kernel, out_shape=outs, in_specs=[pl.BlockSpec(memory_spac...]
    unnamed x251 -> x202, local copies, waits for them, and re-layouts: 27.8 us -> 23.1 us
  transfers between devices with their start and end apart: 4 -> 4, of which waited for: 2 -> 1; matrix products, arithmetic and copies ran while one was open for 11% -> 10% of each run, Pallas kernels for 41% -> 39%
where the time goes in v7:
time: 728 us; the launch traced here: 721 us
  Pallas kernels  502 us (69%)
  local copies, waits for them, and re-layouts  68.4 us (9%)
  other arithmetic  67.9 us (9%)
  matrix products  37.9 us (5%)
  between operations  25.3 us (3%)
  waiting for transfers between devices  20.2 us (3%)
    pallas_call x16, Pallas kernels, call(): pl.pallas_call(kernel, out_shape=outs, in_specs=[pl.BlockSpec(memory_spac...  342 us
    pallas_call x1, Pallas kernels, word_weight_grad(): pl.pallas_call(word_grad_kernel, grid=(vocab // block, tokens // chunk),...  35.8 us
    pallas_call x1, Pallas kernels, attention_backward(): pl.pallas_call(backward_kernel, grid=(pairs,), out_shape=[jax.ShapeDtypeS...  23.5 us
    unnamed x202, local copies, waits for them, and re-layouts  23.1 us
    pallas_call x1, Pallas kernels, attention_forward(): pl.pallas_call(forward_kernel, grid=(pairs,), out_shape=[jax.ShapeDtypeSt...  22.4 us
    pallas_call x1, Pallas kernels, head_slopes(): pl.pallas_call(slope_kernel, grid=grid, out_shape=[jax.ShapeDtypeStruct((...  21.2 us
    reduce_scatter x2, waiting for transfers between devices, comm_scatter_sum(): return lax.psum_scatter(value, axes, scatter_dimension=0, tiled=True)  19.4 us
    pallas_call x1, Pallas kernels, head_scores(): pl.pallas_call(score_kernel, grid=grid, out_shape=jax.ShapeDtypeStruct((h...  18.9 us
  transfers between devices with their start and end apart: 4, of which 1 were waited for; matrix products, arithmetic and copies ran while one was open for 10% of the time, Pallas kernels for 39%

profile of v7, /device:TPU:0, one launch (start us, length us, event | category | flops | bytes accessed | tf_op | source)
XLA Modules:
  0.0 721.4 jit_solution(12372093813624693037)
XLA Ops:
  7.3 2.1 convert_element_type.230
  15.3 73.8 %word_gather.1 = (bf16[2,2,2,4,240,768]{5,4,3,2,1,0:T(8,128)(2,1)}, bf16[4,2,88,768]{3,2,1,0:T(8,128)(2,1)}, s32[4,8,128]{2,1,0:T(8,128)S(1)}, bf16[8,16,128]{2,...) custom-call(bf16[4,240,768]{2,1,0:T(8,128)(2,1)S(1)} %bitcast.284, ...), custom_call_target="tpu_custom_call" | custom-call | bytes 26017792 | tf_op jit(solution)/shard_map/word_gather/pallas_call | solution.py:116
  93.2 15.2 %gather_fusion = bf16[2048,768]{1,0:T(8,128)(2,1)S(1)} fusion(bf16[7680,768]{1,0:T(8,128)(2,1)} %bitcast.298, s32[2048]{0:T(1024)S(1)} %broadcast_clamp_fusion), kind=kCustom, calls=%fused_computation | custom fusion | bytes 6299648 | tf_op jit(solution)/shard_map/gather | solution.py:949
  109.0 58.3 %token_fold.1 = bf16[8,64,768]{2,1,0:T(8,128)(2,1)S(1)} custom-call(bf16[4,8,64,768]{3,2,1,0:T(8,128)(2,1)S(1)} %broadcast_select_fusion.source), custom_call_target="tpu_custom_call" | custom-call | bytes 6291456 | tf_op jit(solution)/shard_map/token_fold/pallas_call | solution.py:116
  177.9 2.6 slice_bitcast_fusion.1
  183.3 2.8 copy.188
  189.4 6.3 project_heads.1
  198.2 3.6 key_trade.1
  203.7 22.4 %attention_forward.1 = (bf16[512,768]{1,0:T(8,128)(2,1)}, f32[6,2,512]{2,1,0:T(2,128)}) custom-call(bf16[512,768]{1,0:T(8,128)(2,1)} %get-tuple-element.76.q_ref, bf16[512,768]{1,0:T(8,128)(2,1)} %get-tuple-element.77.refs_0_.k0_ref, bf16[512,768]{1,0:T(8,128)(2,1)} %copy-done.6, bf16[512,768]{1,0:T(8,128)(2,1)} %get-tuple-element.78.refs_1_.v0_ref, ...), custom_call_target="tpu_custom_call" | custom-call | flops 3221225472 | bytes 6291456 | tf_op jit(solution)/shard_map/attention_forward/pallas_call | solution.py:528
  227.5 3.6 fusion.135
  232.1 6.8 fusion.9
  239.0 2.9 fusion.136
  243.3 2.4 hidden_trade.1
  247.0 2.6 gather_fusion.1
  251.8 18.5 %head_gather.1 = bf16[4,4,32,768]{3,2,1,0:T(8,128)(2,1)S(1)} custom-call(bf16[4,32,768]{2,1,0:T(8,128)(2,1)S(1)} %bitcast.294), custom_call_target="tpu_custom_call" | custom-call | bytes 1572864 | tf_op jit(solution)/shard_map/head_gather/pallas_call | solution.py:116
  271.2 18.9 %head_scores.1 = f32[512,128]{1,0:T(8,128)} custom-call(bf16[512,768]{1,0:T(8,128)(2,1)} %bitcast.291, bf16[7680,768]{1,0:T(8,128)(2,1)} %bitcast.299, f32[1,7680]{1,0:T(1,128)} %broadcast_in_dim_reshape.2.bias_ref, s32[512,1]{1,0:T(8,128)} %fusion.77.label_ref), custom_call_target="tpu_custom_call" | custom-call | flops 6039797760 | bytes 11796480 | tf_op jit(solution)/shard_map/head_scores/pallas_call | solution.py:817
  291.2 5.7 stat_gather.1
  301.2 1.9 fusion.99
  304.9 1.9 fusion.108
  306.9 2.3 convolution_reduce_fusion
  309.3 21.2 %head_slopes.1 = (bf16[512,7680]{1,0:T(8,128)(2,1)}, f32[1,1,7680]{2,1,0:T(1,128)}, f32[512,768]{1,0:T(8,128)}) custom-call(bf16[512,768]{1,0:T(8,128)(2,1)} %bitcast.292, bf16[7680,768]{1,0:T(8,128)(2,1)} %bitcast.300, f32[1,7680]{1,0:T(1,128)} %broadcast_in_dim_reshape.2.bias_ref, s32[512,1]{1,0:T(8,128)} %fusion.77.label_ref, f32[512,1]{1,0:T(8,128)} %copy.203.norm_ref, ...), custom_call_target="tpu_custom_call" | custom-call | flops 6039797760 | bytes 11796480 | tf_op jit(solution)/shard_map/head_slopes/pallas_call | solution.py:833
  331.9 15.5 %head_spread.1 = bf16[3,128,768]{2,1,0:T(8,128)(2,1)S(1)} custom-call(bf16[4,128,768]{2,1,0:T(8,128)(2,1)S(1)} %bitcast_convert_fusion.refs_0_), custom_call_target="tpu_custom_call" | custom-call | bytes 1179648 | tf_op jit(solution)/shard_map/head_spread/pallas_call | solution.py:116
  350.0 1.9 fusion.48.refs_0_
  352.0 1.8 picked_trade.1
  356.6 7.2 convert_reduce_fusion
  363.8 12.9 %ff_weight_grad.1 = bf16[4,8,2,96,768]{4,3,2,1,0:T(8,128)(2,1)} custom-call(bf16[512,768]{1,0:T(8,128)(2,1)} %copy-done.31, bf16[512,768]{1,0:T(8,128)(2,1)} %copy-done.32, bf16[4,512,768]{2,1,0:T(8,128)(2,1)} %get-tuple-element.224.up_ref, bf16[4,512,768]{2,1,0:T(8,128)(2,1)} %copy-done.88), custom_call_target="tpu_custom_call" | custom-call | flops 4831838208 | bytes 9437184 | tf_op jit(solution)/shard_map/ff_weight_grad/pallas_call | solution.py:689
  376.7 7.1 fusion.33
  385.3 2.7 multiply_reduce_fusion.1
  390.9 4.9 mixed_grad.1.g_ref
  395.8 23.5 %attention_backward.1 = (bf16[512,768]{1,0:T(8,128)(2,1)}, f32[512,768]{1,0:T(8,128)}, f32[512,768]{1,0:T(8,128)}, f32[512,768]{1,0:T(8,128)}, f32[512,768]{1,0:T(8,128)}) custom-call(bf16[512,768]{1,0:T(8,128)(2,1)} %get-tuple-element.76.q_ref, bf16[512,768]{1,0:T(8,128)(2,1)} %get-tuple-element.77.refs_0_.k0_ref, bf16[512,768]{1,0:T(8,128)(2,1)} %copy-done.6, ...), custom_call_target="tpu_custom_call" | custom-call | flops 8053063680 | bytes 12582912 | tf_op jit(solution)/shard_map/attention_backward/pallas_call | solution.py:581
  422.3 6.2 key_grad_trade.1
  431.4 7.0 hidden_grad.1
  438.3 2.6 multiply_reduce_fusion.2
  443.5 7.2 %attn_weight_grad.1 = bf16[4,768,768]{2,1,0:T(8,128)(2,1)} custom-call(bf16[512,768]{1,0:T(8,128)(2,1)} %fusion.40.hidden_ref, bf16[512,768]{1,0:T(8,128)(2,1)} %get-tuple-element.88.dq_ref, bf16[512,768]{1,0:T(8,128)(2,1)} %add_convert_fusion.1.dk_ref, bf16[512,768]{1,0:T(8,128)(2,1)} %get-tuple-element.176.dv_ref, ...), custom_call_target="tpu_custom_call" | custom-call | flops 2415919104 | bytes 4718592 | tf_op jit(solution)/shard_map/attn_weight_grad/pallas_call | solution.py:661
  454.3 19.4 %grad_swap_c.1 = (bf16[2,4,2,96,768]{4,3,2,1,0:T(8,128)(2,1)S(1)}, bf16[4,2,2,80,768]{4,3,2,1,0:T(8,128)(2,1)S(1)}, bf16[4,1,64,768]{3,2,1,0:T(8,128)(2,1)S(1)}) custom-call(bf16[2,2,4,2,96,768]{5,4,3,2,1,0:T(8,128)(2,1)S(1)} %bitcast.280, bf16[4,2,2,2,80,768]{5,4,3,2,1,0:T(8,128)(2,1)S(1)} %bitcast.282, bf16[1,64,768]{2,1,0:T(8,128)(2,1)S(1)} %slice_bitcast_fusion.2.refs_2_), custom_call_target="tpu_custom_call" | custom-call | bytes 9437184 | tf_op jit(solution)/shard_map/grad_swap_c/pallas_call | solution.py:116
  475.3 39.9 %grad_swap_xy.1 = (bf16[2,4,96,768]{3,2,1,0:T(8,128)(2,1)S(1)}, bf16[4,2,80,768]{3,2,1,0:T(8,128)(2,1)S(1)}, bf16[4,4,64,768]{3,2,1,0:T(8,128)(2,1)S(1)}) custom-call(bf16[2,4,2,96,768]{4,3,2,1,0:T(8,128)(2,1)S(1)} %copy.210.refs_0_, bf16[4,2,2,80,768]{4,3,2,1,0:T(8,128)(2,1)S(1)} %copy.211.refs_1_, bf16[4,64,768]{2,1,0:T(8,128)(2,1)S(1)} %bitcast.285), custom_call_target="tpu_custom_call" | custom-call | bytes 7471104 | tf_op jit(solution)/shard_map/grad_swap_xy/pallas_call | solution.py:116
  515.8 26.4 %grad_swap_yx.1 = (bf16[4,96,768]{2,1,0:T(8,128)(2,1)S(1)}, bf16[4,80,768]{2,1,0:T(8,128)(2,1)S(1)}, bf16[4,3,64,768]{3,2,1,0:T(8,128)(2,1)S(1)}) custom-call(bf16[2,4,96,768]{3,2,1,0:T(8,128)(2,1)S(1)} %fusion.26.refs_0_, bf16[4,2,80,768]{3,2,1,0:T(8,128)(2,1)S(1)} %copy.213.refs_1_, bf16[3,64,768]{2,1,0:T(8,128)(2,1)S(1)} %bitcast.288), custom_call_target="tpu_custom_call" | custom-call | bytes 4521984 | tf_op jit(solution)/shard_map/grad_swap_yx/pallas_call | solution.py:116
  543.4 3.1 pad_maximum_fusion.1
  546.5 35.8 %word_weight_grad.1 = bf16[7680,768]{1,0:T(8,128)(2,1)} custom-call(bf16[512,7680]{1,0:T(8,128)(2,1)} %get-tuple-element.84.slope_ref, bf16[512,768]{1,0:T(8,128)(2,1)} %bitcast.293, s32[1,2048]{1,0:T(1,128)} %compare_select_fusion.1.at_ref, bf16[2048,768]{1,0:T(8,128)(2,1)} %bitcast.317), custom_call_target="tpu_custom_call" | custom-call | flops 30198988800 | bytes 19660800 | tf_op jit(solution)/shard_map/word_weight_grad/pallas_call | solution.py:794
  589.7 21.8 %grad_spread_z.1 = (bf16[3,96,768]{2,1,0:T(8,128)(2,1)S(1)}, bf16[3,80,768]{2,1,0:T(8,128)(2,1)S(1)}) custom-call(bf16[4,96,768]{2,1,0:T(8,128)(2,1)S(1)} %fusion.44.refs_0_, bf16[4,80,768]{2,1,0:T(8,128)(2,1)S(1)} %fusion.53.refs_1_), custom_call_target="tpu_custom_call" | custom-call | bytes 1622016 | tf_op jit(solution)/shard_map/grad_spread_z/pallas_call | solution.py:116
  611.5 24.9 %small_sum.1 = f32[4,192,128]{2,1,0:T(8,128)S(1)} custom-call(f32[192,128]{1,0:T(8,128)S(1)} %maximum_bitcast_fusion.x_ref), custom_call_target="tpu_custom_call" | custom-call | bytes 1572864 | tf_op jit(solution)/shard_map/small_sum/pallas_call | solution.py:116
  637.0 10.8 %side_gather.1 = bf16[4,80,768]{2,1,0:T(8,128)(2,1)S(1)} custom-call(bf16[80,768]{1,0:T(8,128)(2,1)S(1)} %convert_add_fusion.7.refs_0_), custom_call_target="tpu_custom_call" | custom-call | bytes 983040 | tf_op jit(solution)/shard_map/side_gather/pallas_call | solution.py:116
  656.1 19.4 %reduce-scatter.5.cloned.1.call-done = bf16[960,768]{1,0:T(8,128)(2,1)} async-done(((bf16[7680,768]{1,0:T(8,128)(2,1)}), bf16[960,768]{1,0:T(8,128)(2,1)}) %reduce-scatter.5.cloned.1.call-update) | async-done | bytes 1474576 | tf_op jit(solution)/shard_map/reduce_scatter | solution.py:68
  675.4 2.7 fusion.22
  680.2 12.5 %norm_sum.1 = f32[4,8,128]{2,1,0:T(8,128)S(1)} custom-call(f32[8,128]{1,0:T(8,128)S(1)} %iota.29.x_ref), custom_call_target="tpu_custom_call" | custom-call | bytes 65536 | tf_op jit(solution)/shard_map/norm_sum/pallas_call | solution.py:116
  695.3 4.9 multiply_subtract_fusion.2
  702.4 3.8 multiply_subtract_fusion.1
  709.1 4.2 multiply_subtract_fusion
  (414 shorter events, 90.2 us)
Async XLA Ops:
  7.2 170.7 %all-gather.3.cloned.1.call-start = ((), (), s32[]{:S(2)}) async-start(), calls=%async_computation.2 | async-start | bytes 9732096 | tf_op jit(solution)/shard_map/all_gather | solution.py:64
  7.3 4.5 copy-start.56
  7.3 4.5 copy-start.58
  7.3 4.6 copy-start.23
  89.1 142.7 %all-gather.5.cloned.1.call-start = ((), (), s32[]{:S(2)}) async-start(), calls=%async_computation.3 | async-start | bytes 9732096 | tf_op jit(solution)/shard_map/all_gather | solution.py:64
  89.9 453.5 %reduce-scatter.3.cloned.1.call-start = ((), (), s32[]{:S(2)}) async-start(), calls=%async_computation.4 | async-start | bytes 9732096 | tf_op jit(solution)/shard_map/reduce_scatter | solution.py:68
  92.7 77.8 %copy-start.39 = (s32[1,4,8,128]{3,1,2,0:T(4,128)}, s32[1,4,8,128]{3,1,2,0:T(4,128)S(1)}, u32[]{:S(2)}) copy-start(s32[1,4,8,128]{3,1,2,0:T(4,128)S(1)} %copy.268) | copy-start | bytes 49156
  92.8 15.7 %copy-start.41 = (s32[1,1,4,512]{3,1,2,0:T(1,128)}, s32[1,1,4,512]{3,1,2,0:T(1,128)S(1)}, u32[]{:S(2)}) copy-start(s32[1,1,4,512]{3,1,2,0:T(1,128)S(1)} %copy.229) | copy-start | bytes 24580
  92.9 15.6 %copy-start.43 = (s32[1,1,4,512]{3,1,2,0:T(1,128)}, s32[1,1,4,512]{3,1,2,0:T(1,128)S(1)}, u32[]{:S(2)}) copy-start(s32[1,1,4,512]{3,1,2,0:T(1,128)S(1)} %copy.230) | copy-start | bytes 24580
  109.0 61.8 %copy-start.86 = (s32[2]{0:T(128)S(1)}, s32[2]{0:T(128)}, u32[]{:S(2)}) copy-start(s32[2]{0:T(128)} %param.32) | copy-start | bytes 28
  109.0 65.6 %copy-start.83 = (s32[2,256]{1,0:T(2,128)S(1)}, s32[2,256]{1,0:T(2,128)}, u32[]{:S(2)}) copy-start(s32[2,256]{1,0:T(2,128)} %param.29) | copy-start | bytes 6148
  168.4 70.5 %copy-start.45 = (f32[768]{0:T(1024)}, f32[768]{0:T(1024)S(1)}, u32[]{:S(2)}) copy-start(f32[768]{0:T(1024)S(1)} %mul.800) | copy-start | bytes 9220
  168.6 73.6 %copy-start.50 = (f32[768]{0:T(1024)}, f32[768]{0:T(1024)S(1)}, u32[]{:S(2)}) copy-start(f32[768]{0:T(1024)S(1)} %mul.809) | copy-start | bytes 9220
  174.0 12.5 %copy-start.71 = (pred[512]{0:T(512)(128)(4,1)}, pred[512]{0:T(512)(128)(4,1)S(1)}, u32[]{:S(2)}) copy-start(pred[512]{0:T(512)(128)(4,1)S(1)} %get-tuple-element.147) | copy-start | bytes 1540
  177.9 4.7 slice-start.3
  187.2 8.6 %copy-start.65 = (f32[512]{0:T(512)}, f32[512]{0:T(512)S(1)}, u32[]{:S(2)}) copy-start(f32[512]{0:T(512)S(1)} %get-tuple-element.192) | copy-start | bytes 6148
  187.2 40.3 %copy-start.60 = (f32[512]{0:T(512)}, f32[512]{0:T(512)S(1)}, u32[]{:S(2)}) copy-start(f32[512]{0:T(512)S(1)} %fusion.103) | copy-start | bytes 6148
  231.1 7.8 %copy-start.47 = (f32[512]{0:T(512)}, f32[512]{0:T(512)S(1)}, u32[]{:S(2)}) copy-start(f32[512]{0:T(512)S(1)} %broadcast_multiply_fusion.2) | copy-start | bytes 6148
  231.4 7.5 %copy-start.63 = (f32[512]{0:T(512)}, f32[512]{0:T(512)S(1)}, u32[]{:S(2)}) copy-start(f32[512]{0:T(512)S(1)} %multiply_reduce_fusion.7) | copy-start | bytes 6148
  231.5 7.5 %copy-start.52 = (f32[512]{0:T(512)}, f32[512]{0:T(512)S(1)}, u32[]{:S(2)}) copy-start(f32[512]{0:T(512)S(1)} %fusion.104) | copy-start | bytes 6148
  231.8 7.1 copy-start.31
  232.1 6.8 copy-start.78
  232.1 6.9 copy-start.85
  271.2 25.7 %copy-start.68 = (f32[1,768]{1,0:T(1,128)S(1)}, f32[1,768]{1,0:T(1,128)}, u32[]{:S(2)}) copy-start(f32[1,768]{1,0:T(1,128)} %slice.210) | copy-start | bytes 9220
  290.1 8.4 %copy-start.80 = (bf16[2,768]{1,0:T(2,128)(2,1)S(1)}, bf16[2,768]{1,0:T(2,128)(2,1)}, u32[]{:S(2)}) copy-start(bf16[2,768]{1,0:T(2,128)(2,1)} %slice.212) | copy-start | bytes 9220
  350.0 6.1 slice-start.5
  355.9 7.9 %copy-start.15 = (f32[512,768]{1,0:T(8,128)}, f32[512,768]{1,0:T(8,128)S(1)}, u32[]{:S(2)}) copy-start(f32[512,768]{1,0:T(8,128)S(1)} %get-tuple-element.186) | copy-start | bytes 4718596
  356.1 7.7 %copy-start.32 = (bf16[512,768]{1,0:T(8,128)(2,1)}, bf16[512,768]{1,0:T(8,128)(2,1)S(1)}, u32[]{:S(2)}) copy-start(bf16[512,768]{1,0:T(8,128)(2,1)S(1)} %get-tuple-element.172.dz_ref) | copy-start | bytes 2359300
  383.8 291.6 %reduce-scatter.5.cloned.1.call-start = ((), (), s32[]{:S(2)}) async-start(), calls=%async_computation.5 | async-start | bytes 13271040 | tf_op jit(solution)/shard_map/reduce_scatter | solution.py:68
  422.3 6.3 copy-start.27
  431.3 7.0 copy-start.9
  431.4 7.0 copy-start.61
  443.5 8.3 %copy-start.25 = (bf16[128,768]{1,0:T(8,128)(2,1)S(1)}, bf16[128,768]{1,0:T(8,128)(2,1)}, u32[]{:S(2)}) copy-start(bf16[128,768]{1,0:T(8,128)(2,1)} %copy-done.24) | copy-start | bytes 589828
  443.5 8.3 %copy-start.34 = (bf16[128,768]{1,0:T(8,128)(2,1)S(1)}, bf16[128,768]{1,0:T(8,128)(2,1)}, u32[]{:S(2)}) copy-start(bf16[128,768]{1,0:T(8,128)(2,1)} %copy-done.33) | copy-start | bytes 589828
  611.4 25.5 %copy-start.37 = (bf16[192,768]{1,0:T(8,128)(2,1)S(1)}, bf16[192,768]{1,0:T(8,128)(2,1)}, u32[]{:S(2)}) copy-start(bf16[192,768]{1,0:T(8,128)(2,1)} %reduce-scatter.3.cloned.1.call-done) | copy-start | bytes 884740
  650.9 5.2 copy-start.38
  695.2 5.0 copy-start.57
  695.2 5.0 copy-start.73
  695.2 5.0 copy-start.74
  695.2 5.7 copy-start.59
  695.3 5.7 copy-start.75
  695.3 5.7 copy-start.76
  695.3 7.0 copy-start.30
  695.3 13.2 %copy-start.22 = (f32[960,768]{1,0:T(8,128)S(1)}, f32[960,768]{1,0:T(8,128)}, u32[]{:S(2)}) copy-start(f32[960,768]{1,0:T(8,128)} %param.35) | copy-start | bytes 8847364
  702.3 4.5 copy-start.29
  702.3 4.5 copy-start.35
  702.4 6.2 copy-start.18
  702.4 6.2 copy-start.21
  (52 other events, 116.8 us)
Sparse Core Ops, SparseCore 0:
  89.3 53.1 all-gather.2
  146.0 82.7 all-gather.4
  384.0 150.8 reduce-scatter.2
  582.5 92.9 reduce-scatter.4

commit v8 on v7

--- a/solution.py
+++ b/solution.py
@@ -201,8 +201,8 @@
                     copy = pltpu.make_async_copy(source, dest.at[at], sems[3 * i + 2].at[0])
                     copy.start()
                     started.append(copy)
-            for run in runs:
-                next(run, None)
+            while runs:
+                runs = [run for run in runs if next(run, run) is None]
             for copy in started:
                 copy.wait()
 
@@ -267,8 +267,7 @@
                         def _():
                             copy_of(way, hop, part).start()
 
-            if hop == 0:
-                yield
+            yield
         for hop in range(size - 1):
             for part in range(parts):
                 for way in range(2):
@@ -324,9 +323,11 @@
             if part >= head:
                 send(landed, at_y, part, 2, by_x)
             send(landed, at_y, part, 5, by_c)
+            yield
         for part in range(parts):
             landed = arrived(at_xy, part, 2)
             send(landed, at_xy, part, 6, by_c)
+        yield
         for slot, place in ((3, me), (4, at_x), (5, at_y), (6, at_xy)):
             for part in range(parts):
                 arrived((place[0], place[1], 1 - c), part, slot)
@@ -671,7 +672,10 @@
 def ff_grad_kernel(hidden_ref, dz_ref, up_ref, active_ref, out_ref):
     def put(left, right):
         grad = dots(left[...], right[0], 0, 0).astype(out_ref.dtype)
-        out_ref[0, :, 0] = grad.reshape(out_ref.shape[1], *out_ref.shape[3:])
+        _, wide, deep, _, rows, width = out_ref.shape
+        grad = grad.reshape(deep, wide, rows, width)
+        for x in range(wide):
+            out_ref[0, x, :, 0] = grad[:, x]
 
     @pl.when(pl.program_id(1) == 0)
     def _():
@@ -682,16 +686,17 @@
         put(dz_ref, active_ref)
 
 
-def ff_weight_grad(shards, hidden, dz, grad_up, active):
+def ff_weight_grad(deep, wide, hidden, dz, grad_up, active):
     blocks, rows, width = active.shape
+    piece = (wide, deep, 2, D // (deep * wide), width)
     whole = pl.BlockSpec((rows, D), lambda m, s: (0, 0))
     block = pl.BlockSpec((1, rows, width), lambda m, s: (m, 0, 0))
     return pl.pallas_call(
         ff_grad_kernel,
         grid=(blocks, 2),
-        out_shape=jax.ShapeDtypeStruct((blocks, shards, 2, D // shards, width), hidden.dtype),
+        out_shape=jax.ShapeDtypeStruct((blocks, *piece), hidden.dtype),
         in_specs=[whole, whole, block, block],
-        out_specs=pl.BlockSpec((1, shards, 1, D // shards, width), lambda m, s: (m, 0, s, 0, 0)),
+        out_specs=pl.BlockSpec((1, wide, deep, 1, *piece[3:]), lambda m, s: (m, 0, 0, s, 0, 0)),
         cost_estimate=pl.CostEstimate(
             flops=4 * rows * D * blocks * width,
             bytes_accessed=4 * D * blocks * width,
@@ -1059,19 +1064,21 @@
     ff_bias_grad = jnp.sum(grad_up.astype(jnp.float32), axis=1)
     hidden1_part = jnp.einsum("mtf,mdf->td", grad_up, ff_in, preferred_element_type=jnp.float32)
     if rows_own % 16 == 0:
-        ff_grad = ff_weight_grad(dp_size, hidden1_b, ffn_grad_b, grad_up, active)
+        ff_grad = ff_weight_grad(z_size, x_size, hidden1_b, ffn_grad_b, grad_up, active)
     else:
         ff_grad = jnp.stack(
             [
                 jnp.einsum("td,mtf->mdf", left, right, preferred_element_type=jnp.float32)
                 .astype(low)
-                .reshape(mp_size * dp_size, rows_own, ff_cols)
+                .reshape(mp_size, z_size, x_size, rows_own, ff_cols)
+                .transpose(0, 2, 1, 3, 4)
                 for left, right in ((hidden1_b, grad_up), (ffn_grad_b, active))
             ],
-            axis=1,
+            axis=3,
         )
     ff_grad, hidden1_part = lax.optimization_barrier((ff_grad, hidden1_part))
-    ff_red = comm_scatter_sum(ff_grad.reshape(-1, ff_cols), mp_first)
+    ff_red = comm_scatter_sum(ff_grad.reshape(-1, ff_cols), ("y", "c", "x"))
+    ff_red = ff_red.reshape(z_size, 2 * rows_own, ff_cols)
     grad_h1 = grad_r2 + hidden1_part
     grad_r1, grad_g1, grad_s1 = norm_backward(resid1, vec_rows[3], vec_rows[4], grad_h1)
     attn_grad_b = grad_r1.astype(low)
@@ -1144,8 +1151,11 @@
         (word_grad, attn_grad, side_grad)
     )
     word_red = comm_scatter_sum(word_grad, plane).astype(jnp.float32)
-    from_a, from_s = links.exchange(
-        "grad_spread_z", ("spread", ("z",), 0, BIG, attn_grad), ("spread", ("z",), 0, BIG, side_grad)
+    from_a, from_s, from_f = links.exchange(
+        "grad_spread_z",
+        ("spread", ("z",), 0, BIG, attn_grad),
+        ("spread", ("z",), 0, BIG, side_grad),
+        ("spread", ("z",), 0, BIG, ff_red),
     )
 
     def total(value, received):
@@ -1153,6 +1163,7 @@
         return kept + jnp.sum(received.astype(jnp.float32), axis=0)
 
     attn_red, side_quarter = total(attn_grad, from_a), total(side_grad, from_s)
+    ff_red = total(ff_red, from_f)
     type_zero = jnp.sum(jnp.where(own_types[:, None] == 0, grad_x0, 0.0), axis=0)
     type_one = jnp.sum(jnp.where(own_types[:, None] == 1, grad_x0, 0.0), axis=0)
     vec_grad = jnp.stack(
@@ -1196,7 +1207,7 @@
         word_red,
         attn_red.reshape(attn_weight.shape),
         row_major(
-            ff_red.astype(jnp.float32).reshape(2, rows_own, ff_cols).transpose(1, 0, 2)
+            ff_red.reshape(2, rows_own, ff_cols).transpose(1, 0, 2)
         ),
     )
     own_square = (

time: 728 us -> 701 us (0.963)
  waiting for transfers between devices: 20.2 us -> 0.79 us
  Pallas kernels: 502 us -> 490 us
    reduce_scatter x2, waiting for transfers between devices: 19.4 us -> 0.02 us  [comm_scatter_sum(): return lax.psum_scatter(value, axes, scatter_dimension=0, tiled=True)]
    pallas_call x16, Pallas kernels: 342 us -> 330 us  [call(): pl.pallas_call(kernel, out_shape=outs, in_specs=[pl.BlockSpec(memory_spac...]
    unnamed x202 -> x204, local copies, waits for them, and re-layouts: 23.1 us -> 23.9 us
  transfers between devices with their start and end apart: 4 -> 4, of which waited for: 1 -> 0; matrix products, arithmetic and copies ran while one was open for 10% -> 11% of each run, Pallas kernels for 39% -> 41%
where the time goes in v8:
time: 701 us; the launch traced here: 694 us
  Pallas kernels  490 us (70%)
  local copies, waits for them, and re-layouts  69.9 us (10%)
  other arithmetic  69.9 us (10%)
  matrix products  37.9 us (5%)
  between operations  25.3 us (4%)
    pallas_call x16, Pallas kernels, call(): pl.pallas_call(kernel, out_shape=outs, in_specs=[pl.BlockSpec(memory_spac...  330 us
    pallas_call x1, Pallas kernels, word_weight_grad(): pl.pallas_call(word_grad_kernel, grid=(vocab // block, tokens // chunk),...  35.8 us
    unnamed x204, local copies, waits for them, and re-layouts  23.9 us
    pallas_call x1, Pallas kernels, attention_backward(): pl.pallas_call(backward_kernel, grid=(pairs,), out_shape=[jax.ShapeDtypeS...  23.6 us
    pallas_call x1, Pallas kernels, attention_forward(): pl.pallas_call(forward_kernel, grid=(pairs,), out_shape=[jax.ShapeDtypeSt...  22.3 us
    pallas_call x1, Pallas kernels, head_slopes(): pl.pallas_call(slope_kernel, grid=grid, out_shape=[jax.ShapeDtypeStruct((...  21.2 us
    pallas_call x1, Pallas kernels, head_scores(): pl.pallas_call(score_kernel, grid=grid, out_shape=jax.ShapeDtypeStruct((h...  18.9 us
    sub x7, other arithmetic, adam_step(): return (weight - learn_rate * change, moment, square)  16.4 us
  transfers between devices with their start and end apart: 4, of which 0 were waited for; matrix products, arithmetic and copies ran while one was open for 11% of the time, Pallas kernels for 41%

profile of v8, /device:TPU:0, one launch (start us, length us, event | category | flops | bytes accessed | tf_op | source)
XLA Modules:
  0.0 693.9 jit_solution(16567215706679583699)
XLA Ops:
  7.3 2.1 convert_element_type.239
  15.3 60.0 %word_gather.1 = (bf16[2,2,2,4,240,768]{5,4,3,2,1,0:T(8,128)(2,1)}, bf16[4,2,88,768]{3,2,1,0:T(8,128)(2,1)}, s32[4,8,128]{2,1,0:T(8,128)S(1)}, bf16[8,16,128]{2,...) custom-call(bf16[4,240,768]{2,1,0:T(8,128)(2,1)S(1)} %bitcast.286, ...), custom_call_target="tpu_custom_call" | custom-call | bytes 26017792 | tf_op jit(solution)/shard_map/word_gather/pallas_call | solution.py:116
  79.4 15.3 %gather_fusion = bf16[2048,768]{1,0:T(8,128)(2,1)S(1)} fusion(bf16[7680,768]{1,0:T(8,128)(2,1)} %bitcast.302, s32[2048]{0:T(1024)S(1)} %broadcast_clamp_fusion), kind=kCustom, calls=%fused_computation | custom fusion | bytes 6299648 | tf_op jit(solution)/shard_map/gather | solution.py:954
  95.3 58.4 %token_fold.1 = bf16[8,64,768]{2,1,0:T(8,128)(2,1)S(1)} custom-call(bf16[4,8,64,768]{3,2,1,0:T(8,128)(2,1)S(1)} %broadcast_select_fusion.source), custom_call_target="tpu_custom_call" | custom-call | bytes 6291456 | tf_op jit(solution)/shard_map/token_fold/pallas_call | solution.py:116
  164.2 2.6 slice_bitcast_fusion.1
  169.6 2.7 copy.192
  175.7 6.3 project_heads.1
  184.5 4.1 key_trade.1
  190.5 22.3 %attention_forward.1 = (bf16[512,768]{1,0:T(8,128)(2,1)}, f32[6,2,512]{2,1,0:T(2,128)}) custom-call(bf16[512,768]{1,0:T(8,128)(2,1)} %get-tuple-element.77.q_ref, bf16[512,768]{1,0:T(8,128)(2,1)} %get-tuple-element.78.refs_0_.k0_ref, bf16[512,768]{1,0:T(8,128)(2,1)} %copy-done.8, bf16[512,768]{1,0:T(8,128)(2,1)} %get-tuple-element.79.refs_1_.v0_ref, ...), custom_call_target="tpu_custom_call" | custom-call | flops 3221225472 | bytes 6291456 | tf_op jit(solution)/shard_map/attention_forward/pallas_call | solution.py:529
  214.3 3.6 fusion.135
  218.9 6.8 fusion.9
  225.8 2.9 fusion.136
  230.1 2.4 hidden_trade.1
  233.7 2.6 gather_fusion.1
  238.5 18.2 %head_gather.1 = bf16[4,4,32,768]{3,2,1,0:T(8,128)(2,1)S(1)} custom-call(bf16[4,32,768]{2,1,0:T(8,128)(2,1)S(1)} %bitcast.298), custom_call_target="tpu_custom_call" | custom-call | bytes 1572864 | tf_op jit(solution)/shard_map/head_gather/pallas_call | solution.py:116
  257.7 18.9 %head_scores.1 = f32[512,128]{1,0:T(8,128)} custom-call(bf16[512,768]{1,0:T(8,128)(2,1)} %bitcast.295, bf16[7680,768]{1,0:T(8,128)(2,1)} %bitcast.303, f32[1,7680]{1,0:T(1,128)} %broadcast_in_dim_reshape.2.bias_ref, s32[512,1]{1,0:T(8,128)} %fusion.77.label_ref), custom_call_target="tpu_custom_call" | custom-call | flops 6039797760 | bytes 11796480 | tf_op jit(solution)/shard_map/head_scores/pallas_call | solution.py:822
  277.7 5.7 stat_gather.1
  287.7 1.9 fusion.99
  291.4 1.9 fusion.108
  293.4 2.3 convolution_reduce_fusion
  295.7 21.2 %head_slopes.1 = (bf16[512,7680]{1,0:T(8,128)(2,1)}, f32[1,1,7680]{2,1,0:T(1,128)}, f32[512,768]{1,0:T(8,128)}) custom-call(bf16[512,768]{1,0:T(8,128)(2,1)} %bitcast.296, bf16[7680,768]{1,0:T(8,128)(2,1)} %bitcast.304, f32[1,7680]{1,0:T(1,128)} %broadcast_in_dim_reshape.2.bias_ref, s32[512,1]{1,0:T(8,128)} %fusion.77.label_ref, f32[512,1]{1,0:T(8,128)} %copy.207.norm_ref, ...), custom_call_target="tpu_custom_call" | custom-call | flops 6039797760 | bytes 11796480 | tf_op jit(solution)/shard_map/head_slopes/pallas_call | solution.py:838
  318.4 15.6 %head_spread.1 = bf16[3,128,768]{2,1,0:T(8,128)(2,1)S(1)} custom-call(bf16[4,128,768]{2,1,0:T(8,128)(2,1)S(1)} %bitcast_convert_fusion.refs_0_), custom_call_target="tpu_custom_call" | custom-call | bytes 1179648 | tf_op jit(solution)/shard_map/head_spread/pallas_call | solution.py:116
  336.5 2.0 fusion.48.refs_0_
  338.5 1.8 picked_trade.1
  343.1 7.2 %convert_reduce_fusion = (f32[4,768]{1,0:T(4,128)S(1)}, bf16[4,512,768]{2,1,0:T(8,128)(2,1)}) fusion(f32[4,768,512]{1,2,0:T(8,128)S(1)} %bitcast.361, f32[4,768]{1,0:T(4,128)S(1)} %copy-done.71, bf16[4,768,1536]{2,1,0:T(8,128)(2,1)} %bitcast.357, bf16[512,768]{1,0:T(8,128)(2,1)S(1)} %get-tuple-element.174.dz_ref), kind=kOutput, calls=%fused_computation.15 | convolution fusion | flops 2436363264 | bytes 14966784 | tf_op jit(solution)/shard_map/td,mdf->mtf/dot_general | solution.py:1062
  350.3 12.9 %ff_weight_grad.1 = bf16[4,2,4,2,96,768]{5,4,3,2,1,0:T(8,128)(2,1)} custom-call(bf16[512,768]{1,0:T(8,128)(2,1)} %copy-done.35, bf16[512,768]{1,0:T(8,128)(2,1)} %copy-done.36, bf16[4,512,768]{2,1,0:T(8,128)(2,1)} %get-tuple-element.226.up_ref, bf16[4,512,768]{2,1,0:T(8,128)(2,1)} %copy-done.89), custom_call_target="tpu_custom_call" | custom-call | flops 4831838208 | bytes 9437184 | tf_op jit(solution)/shard_map/ff_weight_grad/pallas_call | solution.py:694
  363.2 7.1 %fusion.33 = f32[512,768]{1,0:T(8,128)} fusion(bf16[4,512,768]{2,1,0:T(8,128)(2,1)} %get-tuple-element.226.up_ref, bf16[4,768,1536]{2,1,0:T(8,128)(2,1)} %bitcast.358), kind=kOutput, calls=%fused_computation.83 | convolution fusion | flops 2415919104 | bytes 9437184 | tf_op jit(solution)/shard_map/mtf,mdf->td/dot_general | solution.py:1065
  371.8 2.7 multiply_reduce_fusion.1
  377.4 4.7 mixed_grad.1.g_ref
  382.1 23.6 %attention_backward.1 = (bf16[512,768]{1,0:T(8,128)(2,1)}, f32[512,768]{1,0:T(8,128)}, f32[512,768]{1,0:T(8,128)}, f32[512,768]{1,0:T(8,128)}, f32[512,768]{1,0:T(8,128)}) custom-call(bf16[512,768]{1,0:T(8,128)(2,1)} %get-tuple-element.77.q_ref, bf16[512,768]{1,0:T(8,128)(2,1)} %get-tuple-element.78.refs_0_.k0_ref, bf16[512,768]{1,0:T(8,128)(2,1)} %copy-done.8, ...), custom_call_target="tpu_custom_call" | custom-call | flops 8053063680 | bytes 12582912 | tf_op jit(solution)/shard_map/attention_backward/pallas_call | solution.py:582
  408.6 5.7 key_grad_trade.1
  417.2 7.0 %hidden_grad.1 = f32[512,768]{1,0:T(8,128)} custom-call(bf16[512,768]{1,0:T(8,128)(2,1)} %get-tuple-element.89.dq_ref, bf16[512,768]{1,0:T(8,128)(2,1)} %add_convert_fusion.1.dk_ref, bf16[512,768]{1,0:T(8,128)(2,1)} %get-tuple-element.178.dv_ref, bf16[4,768,768]{2,1,0:T(8,128)(2,1)} %bitcast.320), custom_call_target="tpu_custom_call" | custom-call | flops 2415919104 | bytes 4718592 | tf_op jit(solution)/shard_map/hidden_grad/pallas_call | solution.py:640
  424.2 2.6 multiply_reduce_fusion.2
  429.4 7.2 %attn_weight_grad.1 = bf16[4,768,768]{2,1,0:T(8,128)(2,1)} custom-call(bf16[512,768]{1,0:T(8,128)(2,1)} %fusion.40.hidden_ref, bf16[512,768]{1,0:T(8,128)(2,1)} %get-tuple-element.89.dq_ref, bf16[512,768]{1,0:T(8,128)(2,1)} %add_convert_fusion.1.dk_ref, bf16[512,768]{1,0:T(8,128)(2,1)} %get-tuple-element.178.dv_ref, ...), custom_call_target="tpu_custom_call" | custom-call | flops 2415919104 | bytes 4718592 | tf_op jit(solution)/shard_map/attn_weight_grad/pallas_call | solution.py:662
  440.3 17.4 %grad_swap_c.1 = (bf16[2,4,2,96,768]{4,3,2,1,0:T(8,128)(2,1)S(1)}, bf16[4,2,2,80,768]{4,3,2,1,0:T(8,128)(2,1)S(1)}, bf16[4,1,64,768]{3,2,1,0:T(8,128)(2,1)S(1)}) custom-call(bf16[2,2,4,2,96,768]{5,4,3,2,1,0:T(8,128)(2,1)S(1)} %bitcast.282, bf16[4,2,2,2,80,768]{5,4,3,2,1,0:T(8,128)(2,1)S(1)} %bitcast.284, bf16[1,64,768]{2,1,0:T(8,128)(2,1)S(1)} %slice_bitcast_fusion.2.refs_2_), custom_call_target="tpu_custom_call" | custom-call | bytes 9437184 | tf_op jit(solution)/shard_map/grad_swap_c/pallas_call | solution.py:116
  459.2 26.9 %grad_swap_xy.1 = (bf16[2,4,96,768]{3,2,1,0:T(8,128)(2,1)S(1)}, bf16[4,2,80,768]{3,2,1,0:T(8,128)(2,1)S(1)}, bf16[4,4,64,768]{3,2,1,0:T(8,128)(2,1)S(1)}) custom-call(bf16[2,4,2,96,768]{4,3,2,1,0:T(8,128)(2,1)S(1)} %copy.214.refs_0_, bf16[4,2,2,80,768]{4,3,2,1,0:T(8,128)(2,1)S(1)} %copy.215.refs_1_, bf16[4,64,768]{2,1,0:T(8,128)(2,1)S(1)} %bitcast.289), custom_call_target="tpu_custom_call" | custom-call | bytes 7471104 | tf_op jit(solution)/shard_map/grad_swap_xy/pallas_call | solution.py:116
  486.8 19.1 %grad_swap_yx.1 = (bf16[4,96,768]{2,1,0:T(8,128)(2,1)S(1)}, bf16[4,80,768]{2,1,0:T(8,128)(2,1)S(1)}, bf16[4,3,64,768]{3,2,1,0:T(8,128)(2,1)S(1)}) custom-call(bf16[2,4,96,768]{3,2,1,0:T(8,128)(2,1)S(1)} %fusion.26.refs_0_, bf16[4,2,80,768]{3,2,1,0:T(8,128)(2,1)S(1)} %copy.217.refs_1_, bf16[3,64,768]{2,1,0:T(8,128)(2,1)S(1)} %bitcast.292), custom_call_target="tpu_custom_call" | custom-call | bytes 4521984 | tf_op jit(solution)/shard_map/grad_swap_yx/pallas_call | solution.py:116
  507.1 3.1 pad_maximum_fusion.1
  510.3 35.8 %word_weight_grad.1 = bf16[7680,768]{1,0:T(8,128)(2,1)} custom-call(bf16[512,7680]{1,0:T(8,128)(2,1)} %get-tuple-element.85.slope_ref, bf16[512,768]{1,0:T(8,128)(2,1)} %bitcast.297, s32[1,2048]{1,0:T(1,128)} %compare_select_fusion.1.at_ref, bf16[2048,768]{1,0:T(8,128)(2,1)} %bitcast.321), custom_call_target="tpu_custom_call" | custom-call | flops 30198988800 | bytes 19660800 | tf_op jit(solution)/shard_map/word_weight_grad/pallas_call | solution.py:799
  550.0 2.4 select_reduce_fusion
  552.7 43.7 %grad_spread_z.1 = (bf16[3,96,768]{2,1,0:T(8,128)(2,1)S(1)}, bf16[3,80,768]{2,1,0:T(8,128)(2,1)S(1)}, bf16[3,192,768]{2,1,0:T(8,128)(2,1)S(1)}) custom-call(bf16[4,96,768]{2,1,0:T(8,128)(2,1)S(1)} %fusion.44.refs_0_, bf16[4,80,768]{2,1,0:T(8,128)(2,1)S(1)} %fusion.53.refs_1_, bf16[4,192,768]{2,1,0:T(8,128)(2,1)S(1)} %bitcast.287), custom_call_target="tpu_custom_call" | custom-call | bytes 3391488 | tf_op jit(solution)/shard_map/grad_spread_z/pallas_call | solution.py:116
  597.3 25.5 %small_sum.1 = f32[4,192,128]{2,1,0:T(8,128)S(1)} custom-call(f32[192,128]{1,0:T(8,128)S(1)} %maximum_bitcast_fusion.x_ref), custom_call_target="tpu_custom_call" | custom-call | bytes 1572864 | tf_op jit(solution)/shard_map/small_sum/pallas_call | solution.py:116
  623.3 12.7 %side_gather.1 = bf16[4,80,768]{2,1,0:T(8,128)(2,1)S(1)} custom-call(bf16[80,768]{1,0:T(8,128)(2,1)S(1)} %convert_add_fusion.8.refs_0_), custom_call_target="tpu_custom_call" | custom-call | bytes 983040 | tf_op jit(solution)/shard_map/side_gather/pallas_call | solution.py:116
  648.5 2.8 fusion.22
  653.4 12.6 %norm_sum.1 = f32[4,8,128]{2,1,0:T(8,128)S(1)} custom-call(f32[8,128]{1,0:T(8,128)S(1)} %iota.29.x_ref), custom_call_target="tpu_custom_call" | custom-call | bytes 65536 | tf_op jit(solution)/shard_map/norm_sum/pallas_call | solution.py:116
  668.6 4.8 multiply_subtract_fusion.2
  674.8 3.8 multiply_subtract_fusion.1
  681.5 4.2 multiply_subtract_fusion
  (418 shorter events, 91.4 us)
Async XLA Ops:
  7.2 157.0 %all-gather.3.cloned.1.call-start = ((), (), s32[]{:S(2)}) async-start(), calls=%async_computation.2 | async-start | bytes 9732096 | tf_op jit(solution)/shard_map/all_gather | solution.py:64
  7.3 4.5 copy-start.57
  7.3 4.5 copy-start.59
  7.3 4.6 copy-start.24
  75.4 143.2 %all-gather.5.cloned.1.call-start = ((), (), s32[]{:S(2)}) async-start(), calls=%async_computation.3 | async-start | bytes 9732096 | tf_op jit(solution)/shard_map/all_gather | solution.py:64
  76.1 431.0 %reduce-scatter.3.cloned.1.call-start = ((), (), s32[]{:S(2)}) async-start(), calls=%async_computation.4 | async-start | bytes 10616832 | tf_op jit(solution)/shard_map/reduce_scatter | solution.py:68
  78.9 77.9 %copy-start.41 = (s32[1,4,8,128]{3,1,2,0:T(4,128)}, s32[1,4,8,128]{3,1,2,0:T(4,128)S(1)}, u32[]{:S(2)}) copy-start(s32[1,4,8,128]{3,1,2,0:T(4,128)S(1)} %copy.272) | copy-start | bytes 49156
  79.0 15.7 %copy-start.42 = (s32[1,1,4,512]{3,1,2,0:T(1,128)}, s32[1,1,4,512]{3,1,2,0:T(1,128)S(1)}, u32[]{:S(2)}) copy-start(s32[1,1,4,512]{3,1,2,0:T(1,128)S(1)} %copy.233) | copy-start | bytes 24580
  79.1 15.6 %copy-start.44 = (s32[1,1,4,512]{3,1,2,0:T(1,128)}, s32[1,1,4,512]{3,1,2,0:T(1,128)S(1)}, u32[]{:S(2)}) copy-start(s32[1,1,4,512]{3,1,2,0:T(1,128)S(1)} %copy.234) | copy-start | bytes 24580
  95.2 61.8 %copy-start.87 = (s32[2]{0:T(128)S(1)}, s32[2]{0:T(128)}, u32[]{:S(2)}) copy-start(s32[2]{0:T(128)} %param.32) | copy-start | bytes 28
  95.2 65.7 %copy-start.84 = (s32[2,256]{1,0:T(2,128)S(1)}, s32[2,256]{1,0:T(2,128)}, u32[]{:S(2)}) copy-start(s32[2,256]{1,0:T(2,128)} %param.29) | copy-start | bytes 6148
  154.8 70.9 %copy-start.46 = (f32[768]{0:T(1024)}, f32[768]{0:T(1024)S(1)}, u32[]{:S(2)}) copy-start(f32[768]{0:T(1024)S(1)} %mul.800) | copy-start | bytes 9220
  154.9 74.1 %copy-start.51 = (f32[768]{0:T(1024)}, f32[768]{0:T(1024)S(1)}, u32[]{:S(2)}) copy-start(f32[768]{0:T(1024)S(1)} %mul.809) | copy-start | bytes 9220
  160.4 12.5 %copy-start.72 = (pred[512]{0:T(512)(128)(4,1)}, pred[512]{0:T(512)(128)(4,1)S(1)}, u32[]{:S(2)}) copy-start(pred[512]{0:T(512)(128)(4,1)S(1)} %get-tuple-element.149) | copy-start | bytes 1540
  164.2 4.7 slice-start.3
  173.5 8.6 %copy-start.66 = (f32[512]{0:T(512)}, f32[512]{0:T(512)S(1)}, u32[]{:S(2)}) copy-start(f32[512]{0:T(512)S(1)} %get-tuple-element.194) | copy-start | bytes 6148
  173.5 40.8 %copy-start.61 = (f32[512]{0:T(512)}, f32[512]{0:T(512)S(1)}, u32[]{:S(2)}) copy-start(f32[512]{0:T(512)S(1)} %fusion.103) | copy-start | bytes 6148
  217.9 7.8 %copy-start.48 = (f32[512]{0:T(512)}, f32[512]{0:T(512)S(1)}, u32[]{:S(2)}) copy-start(f32[512]{0:T(512)S(1)} %broadcast_multiply_fusion.2) | copy-start | bytes 6148
  218.2 7.5 %copy-start.64 = (f32[512]{0:T(512)}, f32[512]{0:T(512)S(1)}, u32[]{:S(2)}) copy-start(f32[512]{0:T(512)S(1)} %multiply_reduce_fusion.7) | copy-start | bytes 6148
  218.2 7.5 %copy-start.53 = (f32[512]{0:T(512)}, f32[512]{0:T(512)S(1)}, u32[]{:S(2)}) copy-start(f32[512]{0:T(512)S(1)} %fusion.104) | copy-start | bytes 6148
  218.6 7.1 %copy-start.35 = (bf16[512,768]{1,0:T(8,128)(2,1)}, bf16[512,768]{1,0:T(8,128)(2,1)S(1)}, u32[]{:S(2)}) copy-start(bf16[512,768]{1,0:T(8,128)(2,1)S(1)} %fusion.41.hidden_ref) | copy-start | bytes 2359300
  218.9 6.8 copy-start.79
  218.9 6.9 copy-start.86
  257.7 25.7 %copy-start.69 = (f32[1,768]{1,0:T(1,128)S(1)}, f32[1,768]{1,0:T(1,128)}, u32[]{:S(2)}) copy-start(f32[1,768]{1,0:T(1,128)} %slice.210) | copy-start | bytes 9220
  276.6 8.4 %copy-start.81 = (bf16[2,768]{1,0:T(2,128)(2,1)S(1)}, bf16[2,768]{1,0:T(2,128)(2,1)}, u32[]{:S(2)}) copy-start(bf16[2,768]{1,0:T(2,128)(2,1)} %slice.212) | copy-start | bytes 9220
  336.5 6.1 slice-start.5
  342.4 7.9 %copy-start.16 = (f32[512,768]{1,0:T(8,128)}, f32[512,768]{1,0:T(8,128)S(1)}, u32[]{:S(2)}) copy-start(f32[512,768]{1,0:T(8,128)S(1)} %get-tuple-element.188) | copy-start | bytes 4718596
  342.6 7.7 %copy-start.36 = (bf16[512,768]{1,0:T(8,128)(2,1)}, bf16[512,768]{1,0:T(8,128)(2,1)S(1)}, u32[]{:S(2)}) copy-start(bf16[512,768]{1,0:T(8,128)(2,1)S(1)} %get-tuple-element.174.dz_ref) | copy-start | bytes 2359300
  370.3 278.2 %reduce-scatter.5.cloned.1.call-start = ((), (), s32[]{:S(2)}) async-start(), calls=%async_computation.5 | async-start | bytes 13271040 | tf_op jit(solution)/shard_map/reduce_scatter | solution.py:68
  408.6 5.7 copy-start.29
  417.2 7.0 %copy-start.11 = (f32[512,768]{1,0:T(8,128)S(1)}, f32[512,768]{1,0:T(8,128)}, u32[]{:S(2)}) copy-start(f32[512,768]{1,0:T(8,128)} %copy-done.10) | copy-start | bytes 4718596
  417.2 7.0 %copy-start.62 = (f32[512]{0:T(512)S(1)}, f32[512]{0:T(512)}, u32[]{:S(2)}) copy-start(f32[512]{0:T(512)} %copy-done.61) | copy-start | bytes 6148
  429.4 8.3 %copy-start.27 = (bf16[128,768]{1,0:T(8,128)(2,1)S(1)}, bf16[128,768]{1,0:T(8,128)(2,1)}, u32[]{:S(2)}) copy-start(bf16[128,768]{1,0:T(8,128)(2,1)} %copy-done.26) | copy-start | bytes 589828
  429.4 8.3 %copy-start.38 = (bf16[128,768]{1,0:T(8,128)(2,1)S(1)}, bf16[128,768]{1,0:T(8,128)(2,1)}, u32[]{:S(2)}) copy-start(bf16[128,768]{1,0:T(8,128)(2,1)} %copy-done.37) | copy-start | bytes 589828
  648.5 19.9 %copy-start.25 = (f32[96,2,768]{2,1,0:T(2,128)S(1)}, f32[96,2,768]{2,1,0:T(2,128)}, u32[]{:S(2)}) copy-start(f32[96,2,768]{2,1,0:T(2,128)} %param.39) | copy-start | bytes 1769476
  668.5 4.9 copy-start.58
  668.5 4.8 copy-start.74
  668.5 4.8 copy-start.75
  668.5 5.5 copy-start.60
  668.5 5.5 copy-start.76
  668.5 5.5 copy-start.77
  668.5 6.1 copy-start.34
  668.5 12.4 %copy-start.23 = (f32[960,768]{1,0:T(8,128)S(1)}, f32[960,768]{1,0:T(8,128)}, u32[]{:S(2)}) copy-start(f32[960,768]{1,0:T(8,128)} %param.35) | copy-start | bytes 8847364
  674.7 4.5 copy-start.31
  674.7 4.5 copy-start.32
  674.7 4.5 copy-start.33
  674.7 6.2 copy-start.19
  674.8 6.2 copy-start.22
  (53 other events, 117.0 us)
Sparse Core Ops, SparseCore 0:
  75.5 53.3 all-gather.2
  132.4 83.3 all-gather.4
  370.5 78.1 reduce-scatter.2
  546.2 94.3 reduce-scatter.4

commit v9 on v8

--- a/solution.py
+++ b/solution.py
@@ -423,14 +423,38 @@
         kind = "relay" if self.sizes["z"] <= 8 else "gather"
         return (kind, ("z",), 0, memory, value.reshape(parts, -1, value.shape[1]))
 
-    def combine(self, name, value):
+    def combine(self, name, value, extra=None, axes=()):
         pairs = [a for a in ("c", "x", "y") if self.sizes[a] > 1]
         depth = self.sizes["z"]
         steps = len(pairs)
 
-        def kernel(x_ref, out_ref, sums, land, sends, lands):
-            self.greet([(a,) for a in pairs] + [("z",)])
+        more = [] if extra is None else [extra]
+        peers = self.count(axes) - 1
+
+        def kernel(x_ref, *refs):
+            if more:
+                e_ref, out_ref, all_ref, sums, land, sends, lands, e_sends, e_lands, e_own = refs
+            else:
+                out_ref, sums, land, sends, lands = refs
+            self.greet([(a,) for a in pairs] + [("z",)] + ([axes] if more else []))
             me = lax.axis_index("z")
+            beside = []
+            for r in range(1, peers + 1) if more else ():
+                at = self.place(axes)
+                copy = pltpu.make_async_remote_copy(
+                    src_ref=e_ref,
+                    dst_ref=all_ref.at[at],
+                    send_sem=e_sends.at[r - 1],
+                    recv_sem=e_lands.at[r - 1],
+                    device_id=self.target(axes, lax.rem(at + r, peers + 1)),
+                    device_id_type=MESH,
+                )
+                copy.start()
+                beside.append(copy)
+            if more:
+                copy = pltpu.make_async_copy(e_ref, all_ref.at[self.place(axes)], e_own.at[0])
+                copy.start()
+                beside.append(copy)
             for i, a in enumerate(pairs):
                 source = x_ref if i == 0 else sums.at[i - 1]
                 copy = pltpu.make_async_remote_copy(
@@ -457,24 +481,32 @@
                 )
                 copy.start()
                 started.append(copy)
-            for copy in started:
+            for copy in started + beside:
                 copy.wait()
 
+        outs = [jax.ShapeDtypeStruct((depth, *value.shape), value.dtype)]
+        outs += [jax.ShapeDtypeStruct((peers + 1, *v.shape), v.dtype) for v in more]
+        more_sems = [
+            pltpu.SemaphoreType.DMA((peers,)),
+            pltpu.SemaphoreType.DMA((peers,)),
+            pltpu.SemaphoreType.DMA((1,)),
+        ]
         return self.call(
             kernel,
-            [jax.ShapeDtypeStruct((depth, *value.shape), value.dtype)],
-            [FAST],
-            [FAST],
+            outs,
+            [FAST] * len(outs),
+            [FAST] * len(outs),
             [
                 pltpu.VMEM((steps, *value.shape), value.dtype),
                 pltpu.VMEM((steps, *value.shape), value.dtype),
                 pltpu.SemaphoreType.DMA((steps + depth - 1,)),
                 pltpu.SemaphoreType.DMA((steps + depth - 1,)),
+                *(more_sems if more else []),
             ],
-            [value],
+            [value, *more],
             16 * value.size * 4,
             name,
-        )[0]
+        )
 
 
 def row_major(value):
@@ -1183,13 +1215,8 @@
     )
     late = lanes(jnp.concatenate([vec_grad.reshape(-1), split_grad.reshape(-1), decoder_part]))
     late, side_quarter = lax.optimization_barrier((late, side_quarter))
-    small = links.combine(
-        "small_sum",
-        late,
-    ).reshape(z_size, -1)
-    (side_red,) = links.exchange(
-        "side_gather", ("gather", ("y", "c"), 0, FAST, side_quarter.astype(low))
-    )
+    small, side_red = links.combine("small_sum", late, side_quarter.astype(low), ("y", "c"))
+    small = small.reshape(z_size, -1)
     side_red = side_red.reshape(side_weight.shape).astype(jnp.float32)
     narrow = vec_grad.size + split_grad.size
     summed = jnp.sum(small[:, :narrow], axis=0)
@@ -1222,7 +1249,7 @@
     ends = jnp.where(
         lax.broadcasted_iota(jnp.int32, (8, 128), 0) == 0, own_square, loss_part
     )
-    ends = jnp.sum(links.combine("norm_sum", ends), axis=0)
+    ends = jnp.sum(links.combine("norm_sum", ends)[0], axis=0)
     grad_square, total_loss = ends[0, 0], ends[1, 0]
     grad_norm = jnp.sqrt(grad_square)
     clip_scale = max_norm / jnp.maximum(grad_norm, max_norm)

time: 701 us -> 693 us (0.989)
  Pallas kernels: 490 us -> 481 us
    pallas_call x16 -> x15, Pallas kernels: 330 us -> 320 us  [call(): pl.pallas_call(kernel, out_shape=outs, in_specs=[pl.BlockSpec(memory_spac...]
    unnamed x204 -> x142, local copies, waits for them, and re-layouts: 23.9 us -> 20.7 us
  transfers between devices with their start and end apart: 4 -> 4, of which waited for: 0 -> 0; matrix products, arithmetic and copies ran while one was open for 11% -> 11% of each run, Pallas kernels for 41% -> 40%
where the time goes in v9:
time: 693 us; the launch traced here: 687 us
  Pallas kernels  481 us (69%)
  other arithmetic  74.7 us (11%)
  local copies, waits for them, and re-layouts  66 us (10%)
  matrix products  39.2 us (6%)
  between operations  25 us (4%)
    pallas_call x15, Pallas kernels, call(): pl.pallas_call(kernel, out_shape=outs, in_specs=[pl.BlockSpec(memory_spac...  320 us
    pallas_call x1, Pallas kernels, word_weight_grad(): pl.pallas_call(word_grad_kernel, grid=(vocab // block, tokens // chunk),...  35.8 us
    pallas_call x1, Pallas kernels, attention_backward(): pl.pallas_call(backward_kernel, grid=(pairs,), out_shape=[jax.ShapeDtypeS...  23.7 us
    pallas_call x1, Pallas kernels, attention_forward(): pl.pallas_call(forward_kernel, grid=(pairs,), out_shape=[jax.ShapeDtypeSt...  22.4 us
    pallas_call x1, Pallas kernels, head_slopes(): pl.pallas_call(slope_kernel, grid=grid, out_shape=[jax.ShapeDtypeStruct((...  21.2 us
    unnamed x142, local copies, waits for them, and re-layouts  20.7 us
    pallas_call x1, Pallas kernels, head_scores(): pl.pallas_call(score_kernel, grid=grid, out_shape=jax.ShapeDtypeStruct((h...  18.9 us
    gather x1, local copies, waits for them, and re-layouts, step(): word_plane[jnp.where(inside, at, 0)]  16.7 us
  transfers between devices with their start and end apart: 4, of which 0 were waited for; matrix products, arithmetic and copies ran while one was open for 11% of the time, Pallas kernels for 40%

profile of v9, /device:TPU:0, one launch (start us, length us, event | category | flops | bytes accessed | tf_op | source)
XLA Modules:
  0.0 686.5 jit_solution(16577917378503834727)
XLA Ops:
  7.3 2.1 convert_element_type.239
  15.3 60.0 %word_gather.1 = (bf16[2,2,2,4,240,768]{5,4,3,2,1,0:T(8,128)(2,1)}, bf16[4,2,88,768]{3,2,1,0:T(8,128)(2,1)}, s32[4,8,128]{2,1,0:T(8,128)S(1)}, bf16[8,16,128]{2,...) custom-call(bf16[4,240,768]{2,1,0:T(8,128)(2,1)S(1)} %bitcast.286, ...), custom_call_target="tpu_custom_call" | custom-call | bytes 26017792 | tf_op jit(solution)/shard_map/word_gather/pallas_call | solution.py:116
  77.6 16.7 %gather_fusion = bf16[2048,768]{1,0:T(8,128)(2,1)} fusion(bf16[7680,768]{1,0:T(8,128)(2,1)} %bitcast.302, s32[2048]{0:T(1024)S(1)} %broadcast_clamp_fusion), kind=kCustom, calls=%fused_computation | custom fusion | bytes 6299648 | tf_op jit(solution)/shard_map/gather | solution.py:986
  94.4 2.1 broadcast_select_fusion.source
  96.5 58.6 %token_fold.1 = bf16[8,64,768]{2,1,0:T(8,128)(2,1)S(1)} custom-call(bf16[4,8,64,768]{3,2,1,0:T(8,128)(2,1)S(1)} %broadcast_select_fusion.source), custom_call_target="tpu_custom_call" | custom-call | bytes 6291456 | tf_op jit(solution)/shard_map/token_fold/pallas_call | solution.py:116
  162.2 2.6 slice_bitcast_fusion.1
  167.6 2.8 copy.192
  172.6 2.6 fusion.40.hidden_ref
  175.1 6.3 project_heads.1
  183.7 5.6 key_trade.1
  191.1 22.4 %attention_forward.1 = (bf16[512,768]{1,0:T(8,128)(2,1)}, f32[6,2,512]{2,1,0:T(2,128)}) custom-call(bf16[512,768]{1,0:T(8,128)(2,1)} %get-tuple-element.79.q_ref, bf16[512,768]{1,0:T(8,128)(2,1)} %get-tuple-element.80.refs_0_.k0_ref, bf16[512,768]{1,0:T(8,128)(2,1)} %copy-done.8, bf16[512,768]{1,0:T(8,128)(2,1)} %get-tuple-element.81.refs_1_.v0_ref, ...), custom_call_target="tpu_custom_call" | custom-call | flops 3221225472 | bytes 6291456 | tf_op jit(solution)/shard_map/attention_forward/pallas_call | solution.py:561
  214.9 3.6 fusion.135
  219.3 6.9 %fusion.9 = (bf16[4,512,768]{2,1,0:T(8,128)(2,1)S(1)}, f32[4,768,512]{1,2,0:T(8,128)}) fusion(f32[4,768]{1,0:T(4,128)S(1)} %add.761, bf16[4,768,1536]{2,1,0:T(8,128)(2,1)} %bitcast.356, bf16[512,768]{1,0:T(8,128)(2,1)S(1)} %fusion.41.hidden_ref), kind=kOutput, calls=%fused_computation.14 | convolution fusion | flops 2425356288 | bytes 14954496 | tf_op jit(solution)/shard_map/td,mdf->mtf/dot_general | solution.py:1023
  226.6 2.9 fusion.136
  230.9 2.4 hidden_trade.1
  234.5 2.6 gather_fusion.1
  237.1 2.4 fusion.131
  239.8 18.0 %head_gather.1 = bf16[4,4,32,768]{3,2,1,0:T(8,128)(2,1)S(1)} custom-call(bf16[4,32,768]{2,1,0:T(8,128)(2,1)S(1)} %bitcast.297), custom_call_target="tpu_custom_call" | custom-call | bytes 1572864 | tf_op jit(solution)/shard_map/head_gather/pallas_call | solution.py:116
  258.8 18.9 %head_scores.1 = f32[512,128]{1,0:T(8,128)} custom-call(bf16[512,768]{1,0:T(8,128)(2,1)} %bitcast.294, bf16[7680,768]{1,0:T(8,128)(2,1)} %bitcast.303, f32[1,7680]{1,0:T(1,128)} %broadcast_in_dim_reshape.2.bias_ref, s32[512,1]{1,0:T(8,128)} %fusion.77.label_ref), custom_call_target="tpu_custom_call" | custom-call | flops 6039797760 | bytes 11796480 | tf_op jit(solution)/shard_map/head_scores/pallas_call | solution.py:854
  278.8 5.7 stat_gather.1
  293.8 2.3 convolution_reduce_fusion
  296.1 21.2 %head_slopes.1 = (bf16[512,7680]{1,0:T(8,128)(2,1)}, f32[1,1,7680]{2,1,0:T(1,128)}, f32[512,768]{1,0:T(8,128)}) custom-call(bf16[512,768]{1,0:T(8,128)(2,1)} %bitcast.295, bf16[7680,768]{1,0:T(8,128)(2,1)} %bitcast.304, f32[1,7680]{1,0:T(1,128)} %broadcast_in_dim_reshape.2.bias_ref, s32[512,1]{1,0:T(8,128)} %fusion.77.label_ref, f32[512,1]{1,0:T(8,128)} %copy.207.norm_ref, ...), custom_call_target="tpu_custom_call" | custom-call | flops 6039797760 | bytes 11796480 | tf_op jit(solution)/shard_map/head_slopes/pallas_call | solution.py:870
  318.8 15.6 %head_spread.1 = bf16[3,128,768]{2,1,0:T(8,128)(2,1)S(1)} custom-call(bf16[4,128,768]{2,1,0:T(8,128)(2,1)S(1)} %bitcast_convert_fusion.refs_0_), custom_call_target="tpu_custom_call" | custom-call | bytes 1179648 | tf_op jit(solution)/shard_map/head_spread/pallas_call | solution.py:116
  342.4 7.7 %convert_reduce_fusion = (f32[4,768]{1,0:T(4,128)S(1)}, bf16[4,512,768]{2,1,0:T(8,128)(2,1)}) fusion(f32[4,768,512]{1,2,0:T(8,128)S(1)} %bitcast.361, f32[4,768]{1,0:T(4,128)S(1)} %add.761, bf16[4,768,1536]{2,1,0:T(8,128)(2,1)} %bitcast.357, bf16[512,768]{1,0:T(8,128)(2,1)S(1)} %get-tuple-element.178.dz_ref), kind=kOutput, calls=%fused_computation.15 | convolution fusion | flops 2436363264 | bytes 14966784 | tf_op jit(solution)/shard_map/td,mdf->mtf/dot_general | solution.py:1094
  350.1 12.9 %ff_weight_grad.1 = bf16[4,2,4,2,96,768]{5,4,3,2,1,0:T(8,128)(2,1)} custom-call(bf16[512,768]{1,0:T(8,128)(2,1)} %copy-done.32, bf16[512,768]{1,0:T(8,128)(2,1)} %copy-done.33, bf16[4,512,768]{2,1,0:T(8,128)(2,1)} %get-tuple-element.230.up_ref, bf16[4,512,768]{2,1,0:T(8,128)(2,1)} %copy-done.58), custom_call_target="tpu_custom_call" | custom-call | flops 4831838208 | bytes 9437184 | tf_op jit(solution)/shard_map/ff_weight_grad/pallas_call | solution.py:726
  363.1 7.1 %fusion.33 = f32[512,768]{1,0:T(8,128)} fusion(bf16[4,512,768]{2,1,0:T(8,128)(2,1)} %get-tuple-element.230.up_ref, bf16[4,768,1536]{2,1,0:T(8,128)(2,1)} %bitcast.358), kind=kOutput, calls=%fused_computation.83 | convolution fusion | flops 2415919104 | bytes 9437184 | tf_op jit(solution)/shard_map/mtf,mdf->td/dot_general | solution.py:1097
  371.0 2.7 multiply_reduce_fusion.1
  376.7 4.9 mixed_grad.1.g_ref
  381.5 23.7 %attention_backward.1 = (bf16[512,768]{1,0:T(8,128)(2,1)}, f32[512,768]{1,0:T(8,128)}, f32[512,768]{1,0:T(8,128)}, f32[512,768]{1,0:T(8,128)}, f32[512,768]{1,0:T(8,128)}) custom-call(bf16[512,768]{1,0:T(8,128)(2,1)} %get-tuple-element.79.q_ref, bf16[512,768]{1,0:T(8,128)(2,1)} %get-tuple-element.80.refs_0_.k0_ref, bf16[512,768]{1,0:T(8,128)(2,1)} %copy-done.8, ...), custom_call_target="tpu_custom_call" | custom-call | flops 8053063680 | bytes 12582912 | tf_op jit(solution)/shard_map/attention_backward/pallas_call | solution.py:614
  408.1 5.9 key_grad_trade.1
  416.9 7.0 %hidden_grad.1 = f32[512,768]{1,0:T(8,128)} custom-call(bf16[512,768]{1,0:T(8,128)(2,1)} %get-tuple-element.91.dq_ref, bf16[512,768]{1,0:T(8,128)(2,1)} %add_convert_fusion.1.dk_ref, bf16[512,768]{1,0:T(8,128)(2,1)} %get-tuple-element.182.dv_ref, bf16[4,768,768]{2,1,0:T(8,128)(2,1)} %bitcast.320), custom_call_target="tpu_custom_call" | custom-call | flops 2415919104 | bytes 4718592 | tf_op jit(solution)/shard_map/hidden_grad/pallas_call | solution.py:672
  424.0 2.6 multiply_reduce_fusion.2
  430.6 8.0 %attn_weight_grad.1 = bf16[4,768,768]{2,1,0:T(8,128)(2,1)} custom-call(bf16[512,768]{1,0:T(8,128)(2,1)} %fusion.40.hidden_ref, bf16[512,768]{1,0:T(8,128)(2,1)} %get-tuple-element.91.dq_ref, bf16[512,768]{1,0:T(8,128)(2,1)} %add_convert_fusion.1.dk_ref, bf16[512,768]{1,0:T(8,128)(2,1)} %get-tuple-element.182.dv_ref, ...), custom_call_target="tpu_custom_call" | custom-call | flops 2415919104 | bytes 4718592 | tf_op jit(solution)/shard_map/attn_weight_grad/pallas_call | solution.py:694
  442.1 15.5 %grad_swap_c.1 = (bf16[2,4,2,96,768]{4,3,2,1,0:T(8,128)(2,1)S(1)}, bf16[4,2,2,80,768]{4,3,2,1,0:T(8,128)(2,1)S(1)}, bf16[4,1,64,768]{3,2,1,0:T(8,128)(2,1)S(1)}) custom-call(bf16[2,2,4,2,96,768]{5,4,3,2,1,0:T(8,128)(2,1)S(1)} %bitcast.282, bf16[4,2,2,2,80,768]{5,4,3,2,1,0:T(8,128)(2,1)S(1)} %bitcast.284, bf16[1,64,768]{2,1,0:T(8,128)(2,1)S(1)} %slice_bitcast_fusion.2.refs_2_), custom_call_target="tpu_custom_call" | custom-call | bytes 9437184 | tf_op jit(solution)/shard_map/grad_swap_c/pallas_call | solution.py:116
  459.1 27.0 %grad_swap_xy.1 = (bf16[2,4,96,768]{3,2,1,0:T(8,128)(2,1)S(1)}, bf16[4,2,80,768]{3,2,1,0:T(8,128)(2,1)S(1)}, bf16[4,4,64,768]{3,2,1,0:T(8,128)(2,1)S(1)}) custom-call(bf16[2,4,2,96,768]{4,3,2,1,0:T(8,128)(2,1)S(1)} %copy.214.refs_0_, bf16[4,2,2,80,768]{4,3,2,1,0:T(8,128)(2,1)S(1)} %copy.215.refs_1_, bf16[4,64,768]{2,1,0:T(8,128)(2,1)S(1)} %bitcast.289), custom_call_target="tpu_custom_call" | custom-call | bytes 7471104 | tf_op jit(solution)/shard_map/grad_swap_xy/pallas_call | solution.py:116
  486.8 20.5 %grad_swap_yx.1 = (bf16[4,96,768]{2,1,0:T(8,128)(2,1)S(1)}, bf16[4,80,768]{2,1,0:T(8,128)(2,1)S(1)}, bf16[4,3,64,768]{3,2,1,0:T(8,128)(2,1)S(1)}) custom-call(bf16[2,4,96,768]{3,2,1,0:T(8,128)(2,1)S(1)} %fusion.26.refs_0_, bf16[4,2,80,768]{3,2,1,0:T(8,128)(2,1)S(1)} %copy.217.refs_1_, bf16[3,64,768]{2,1,0:T(8,128)(2,1)S(1)} %bitcast.291), custom_call_target="tpu_custom_call" | custom-call | bytes 4521984 | tf_op jit(solution)/shard_map/grad_swap_yx/pallas_call | solution.py:116
  508.5 3.2 pad_maximum_fusion.1
  511.7 35.8 %word_weight_grad.1 = bf16[7680,768]{1,0:T(8,128)(2,1)} custom-call(bf16[512,7680]{1,0:T(8,128)(2,1)} %get-tuple-element.87.slope_ref, bf16[512,768]{1,0:T(8,128)(2,1)} %bitcast.296, s32[1,2048]{1,0:T(1,128)} %compare_select_fusion.1.at_ref, bf16[2048,768]{1,0:T(8,128)(2,1)} %bitcast.321), custom_call_target="tpu_custom_call" | custom-call | flops 30198988800 | bytes 19660800 | tf_op jit(solution)/shard_map/word_weight_grad/pallas_call | solution.py:831
  551.5 2.4 select_reduce_fusion
  554.2 43.7 %grad_spread_z.1 = (bf16[3,96,768]{2,1,0:T(8,128)(2,1)S(1)}, bf16[3,80,768]{2,1,0:T(8,128)(2,1)S(1)}, bf16[3,192,768]{2,1,0:T(8,128)(2,1)S(1)}) custom-call(bf16[4,96,768]{2,1,0:T(8,128)(2,1)S(1)} %fusion.44.refs_0_, bf16[4,80,768]{2,1,0:T(8,128)(2,1)S(1)} %fusion.53.refs_1_, bf16[4,192,768]{2,1,0:T(8,128)(2,1)S(1)} %bitcast.287), custom_call_target="tpu_custom_call" | custom-call | bytes 3391488 | tf_op jit(solution)/shard_map/grad_spread_z/pallas_call | solution.py:116
  598.7 27.4 %small_sum.1 = (f32[4,192,128]{2,1,0:T(8,128)S(1)}, bf16[4,80,768]{2,1,0:T(8,128)(2,1)S(1)}) custom-call(f32[192,128]{1,0:T(8,128)S(1)} %maximum_bitcast_fusion.x_ref, bf16[80,768]{1,0:T(8,128)(2,1)S(1)} %convert_add_fusion.8.refs_0_), custom_call_target="tpu_custom_call" | custom-call | bytes 1572864 | tf_op jit(solution)/shard_map/small_sum/pallas_call | solution.py:116
  630.5 2.0 reshape.1250
  634.3 2.0 reduce_sum.629
  642.0 2.8 fusion.22
  646.8 12.0 %norm_sum.1 = f32[4,8,128]{2,1,0:T(8,128)S(1)} custom-call(f32[8,128]{1,0:T(8,128)S(1)} %iota.29.x_ref), custom_call_target="tpu_custom_call" | custom-call | bytes 65536 | tf_op jit(solution)/shard_map/norm_sum/pallas_call | solution.py:116
  661.4 4.6 multiply_subtract_fusion.2
  667.5 3.8 multiply_subtract_fusion.1
  674.2 4.2 multiply_subtract_fusion
  (355 shorter events, 87.8 us)
Async XLA Ops:
  7.2 155.0 %all-gather.3.cloned.1.call-start = ((), (), s32[]{:S(2)}) async-start(), calls=%async_computation.2 | async-start | bytes 9732096 | tf_op jit(solution)/shard_map/all_gather | solution.py:64
  7.3 2.4 copy-start.53
  7.3 4.5 copy-start.42
  7.3 4.6 copy-start.44
  7.3 4.6 copy-start.23
  75.4 143.9 %all-gather.5.cloned.1.call-start = ((), (), s32[]{:S(2)}) async-start(), calls=%async_computation.3 | async-start | bytes 9732096 | tf_op jit(solution)/shard_map/all_gather | solution.py:64
  76.1 432.4 %reduce-scatter.3.cloned.1.call-start = ((), (), s32[]{:S(2)}) async-start(), calls=%async_computation.4 | async-start | bytes 10616832 | tf_op jit(solution)/shard_map/reduce_scatter | solution.py:68
  96.5 61.5 %copy-start.57 = (s32[2]{0:T(128)S(1)}, s32[2]{0:T(128)}, u32[]{:S(2)}) copy-start(s32[2]{0:T(128)} %param.32) | copy-start | bytes 28
  96.5 63.5 %copy-start.55 = (s32[2,256]{1,0:T(2,128)S(1)}, s32[2,256]{1,0:T(2,128)}, u32[]{:S(2)}) copy-start(s32[2,256]{1,0:T(2,128)} %param.29) | copy-start | bytes 6148
  160.0 10.8 %copy-start.47 = (pred[512]{0:T(512)(128)(4,1)}, pred[512]{0:T(512)(128)(4,1)S(1)}, u32[]{:S(2)}) copy-start(pred[512]{0:T(512)(128)(4,1)S(1)} %get-tuple-element.153) | copy-start | bytes 1540
  162.2 3.4 slice-start.2
  162.2 4.7 slice-start.3
  167.0 3.9 copy-start.10
  219.2 6.9 %copy-start.32 = (bf16[512,768]{1,0:T(8,128)(2,1)}, bf16[512,768]{1,0:T(8,128)(2,1)S(1)}, u32[]{:S(2)}) copy-start(bf16[512,768]{1,0:T(8,128)(2,1)S(1)} %fusion.41.hidden_ref) | copy-start | bytes 2359300
  219.3 7.4 %copy-start.56 = (bf16[3072,1536]{1,0:T(8,128)(2,1)S(1)}, bf16[3072,1536]{1,0:T(8,128)(2,1)}, u32[]{:S(2)}) copy-start(bf16[3072,1536]{1,0:T(8,128)(2,1)} %all-gather.5.cloned.1.call-done) | copy-start | bytes 28311556
  226.1 3.3 copy-start.58
  336.3 3.8 copy-start.12
  336.3 6.1 slice-start.5
  340.1 2.3 slice-start.6
  342.1 8.0 %copy-start.14 = (f32[512,768]{1,0:T(8,128)}, f32[512,768]{1,0:T(8,128)S(1)}, u32[]{:S(2)}) copy-start(f32[512,768]{1,0:T(8,128)S(1)} %get-tuple-element.192) | copy-start | bytes 4718596
  342.3 7.8 %copy-start.33 = (bf16[512,768]{1,0:T(8,128)(2,1)}, bf16[512,768]{1,0:T(8,128)(2,1)S(1)}, u32[]{:S(2)}) copy-start(bf16[512,768]{1,0:T(8,128)(2,1)S(1)} %get-tuple-element.178.dz_ref) | copy-start | bytes 2359300
  370.2 271.8 %reduce-scatter.5.cloned.1.call-start = ((), (), s32[]{:S(2)}) async-start(), calls=%async_computation.5 | async-start | bytes 13271040 | tf_op jit(solution)/shard_map/reduce_scatter | solution.py:68
  408.1 5.9 copy-start.26
  416.9 7.1 %copy-start.16 = (f32[512,768]{1,0:T(8,128)S(1)}, f32[512,768]{1,0:T(8,128)}, u32[]{:S(2)}) copy-start(f32[512,768]{1,0:T(8,128)} %copy-done.15) | copy-start | bytes 4718596
  547.5 2.8 copy-start.19
  551.0 3.1 copy-start.46
  551.1 3.2 copy-start
  629.7 9.2 %copy-start.38 = (f32[4,2,4,960]{3,2,1,0:T(4,128)}, f32[4,2,4,960]{3,2,1,0:T(4,128)S(1)}, u32[]{:S(2)}) copy-start(f32[4,2,4,960]{3,2,1,0:T(4,128)S(1)} %reshape.1239) | copy-start | bytes 368644
  642.0 19.4 %copy-start.24 = (f32[96,2,768]{2,1,0:T(2,128)S(1)}, f32[96,2,768]{2,1,0:T(2,128)}, u32[]{:S(2)}) copy-start(f32[96,2,768]{2,1,0:T(2,128)} %param.39) | copy-start | bytes 1769476
  642.0 19.4 %copy-start.34 = (f32[96,2,768]{2,1,0:T(2,128)S(1)}, f32[96,2,768]{2,1,0:T(2,128)}, u32[]{:S(2)}) copy-start(f32[96,2,768]{2,1,0:T(2,128)} %param.40) | copy-start | bytes 1769476
  661.3 4.7 copy-start.43
  661.3 4.7 copy-start.49
  661.3 4.7 copy-start.50
  661.4 5.4 copy-start.45
  661.4 5.4 copy-start.51
  661.4 5.3 copy-start.52
  661.4 6.0 copy-start.31
  661.4 12.2 %copy-start.22 = (f32[960,768]{1,0:T(8,128)S(1)}, f32[960,768]{1,0:T(8,128)}, u32[]{:S(2)}) copy-start(f32[960,768]{1,0:T(8,128)} %param.35) | copy-start | bytes 8847364
  667.4 3.9 copy-start.39
  667.4 3.9 copy-start.40
  667.4 3.9 copy-start.41
  667.4 4.5 copy-start.28
  667.4 4.5 copy-start.29
  667.4 4.5 copy-start.30
  667.4 4.5 copy-start.36
  667.4 4.5 copy-start.37
  667.4 6.2 copy-start.18
  667.5 6.2 copy-start.21
  (22 other events, 30.4 us)
Sparse Core Ops, SparseCore 0:
  75.5 53.3 all-gather.2
  132.4 83.9 all-gather.4
  370.3 78.2 reduce-scatter.2
  547.7 91.1 reduce-scatter.4
